TPU v7x, 32 devices: a whole 2x2x4 slice. The times are simulated.
32 devices in a mesh: row: 4 (over x, core), col: 8 (over z, y).
Axes of the slice: x: 2, y: 2, z: 4, core: 2. Of those that a mesh axis runs over, the one named last changes fastest.
Arguments:
- hidden_in: bfloat16 [6144, 2048], P('row', 'col'), may hold values from -6 to 6
- token_order: int32 [4, 1536], P('row'), may hold values from 0 to 1535, each once within a row
- lengths: int32 [4, 3], P('row'), may hold values from 1 to 1024, 1536 in all within a row
- key_mask: int32 [6144], P('row'), may hold values 0 or 1
- routes: int32 [6144, 8], P('row'), may hold values from 0 to 63, all different within a row; in each aligned block of 1536 rows (0 to 1535, 1536 to 3071, ...) at most 240 rows name the same one
- norm1_gain: float32 [2048], P('col'), may hold values from 0.5 to 1.5
- query_gain: float32 [128], replicated, may hold values from 1.1 to 2.2
- key_gain: float32 [128], replicated, may hold values from 1.1 to 2.2
- w_query: bfloat16 [2048, 2048], P('row', 'col'), may hold values from -0.125 to 0.125
- w_key: bfloat16 [2048, 2048], P('row', 'col'), may hold values from -0.125 to 0.125
- w_value: bfloat16 [2048, 2048], P('row', 'col'), may hold values from -0.125 to 0.125
- w_out: bfloat16 [2048, 2048], P('row', 'col'), may hold values from -1 to 1
- norm2_gain: float32 [2048], P('col'), may hold values from 0.5 to 1.5
- router: bfloat16 [64, 2048], P(None, 'row'), may hold values from -0.0625 to 0.0625
- w_gate: bfloat16 [64, 2048, 1024], P('col', 'row'), may hold values from -0.125 to 0.125
- w_up: bfloat16 [64, 2048, 1024], P('col', 'row'), may hold values from -0.125 to 0.125
- w_down: bfloat16 [64, 2048, 1024], P('col', 'row'), may hold values from -0.5 to 0.5
- cotangent: bfloat16 [6144, 2048], P('row', 'col'), may hold values from -6 to 6
Outputs:
- output: bfloat16 [6144, 2048], P('row', 'col')
- grad_input: float32 [6144, 2048], P('row', 'col')
- grad_norm1: float32 [2048], P('col')
- grad_query_gain: float32 [128], replicated
- grad_key_gain: float32 [128], replicated
- grad_w_query: float32 [2048, 2048], P('row', 'col')
- grad_w_key: float32 [2048, 2048], P('row', 'col')
- grad_w_value: float32 [2048, 2048], P('row', 'col')
- grad_w_out: float32 [2048, 2048], P('row', 'col')
- grad_norm2: float32 [2048], P('col')
- grad_router: float32 [64, 2048], P(None, 'row')
- grad_w_gate: float32 [64, 2048, 1024], P('col', 'row')
- grad_w_up: float32 [64, 2048, 1024], P('col', 'row')
- grad_w_down: float32 [64, 2048, 1024], P('col', 'row')
Inputs may be any that keep to these rules, and one draw needn't show every extreme that they name: Each row of token_order holds every number of 0 to 1535 once. `lengths`: each row sums to 1536; its largest entry is 1024. `routes`: a row names 8 different experts; within the rows of one group no expert is named by more than 240 rows, a bound that some block reaches.
All inputs are finite; a program needn't handle non-finite values. No bound on the sum of `key_mask` on one device may be relied on, other than what follows from the above.
Results may differ from a plain program's by a relative error of at most 0.015.
The roundings to bfloat16 on the way count: a program that leaves them out, or rounds other values in their place, can miss the bound.
Values may be sent and summed in bfloat16 or wider, within the bound.
No kernel may reach another device: no remote copies, remote signals or barrier semaphores. Data moves between devices by JAX's collectives and lax.ppermute only.
A program may use at most 512 MiB of HBM per device.

v0:
```python
import jax
import jax.numpy as jnp
from jax import lax
from jax.sharding import PartitionSpec as P

D = 2048
DH = 128
E = 64
TOP = 8


EPSILON = 1e-06
ROPE_BASE = 10000.0


def layout(seq_lengths, tok_count):
    seq_ends = jnp.cumsum(seq_lengths)
    seq_starts = seq_ends - seq_lengths
    places = jnp.arange(tok_count, dtype=jnp.int32)
    segment = jnp.sum((places[:, None] >= seq_ends[None, :]).astype(jnp.int32), axis=1)
    member = segment[:, None] == jnp.arange(seq_lengths.shape[0], dtype=jnp.int32)[None, :]
    offset = jnp.sum(jnp.where(member, seq_starts[None, :], 0), axis=1)
    return (segment, places - offset)


def rotate(values, position):
    half_dim = values.shape[-1] // 2
    frequency = ROPE_BASE ** (-2.0 * jnp.arange(half_dim, dtype=jnp.float32) / values.shape[-1])
    angles = position.astype(jnp.float32)[:, None] * frequency[None, :]
    cosine = jnp.cos(angles)[:, None, :]
    sine_part = jnp.sin(angles)[:, None, :]
    first_half = values[..., :half_dim]
    second_half = values[..., half_dim:]
    return jnp.concatenate(
        [
            first_half * cosine - second_half * sine_part,
            second_half * cosine + first_half * sine_part,
        ],
        axis=-1,
    )


def head_norm(values, gain_vec):
    return (
        values * lax.rsqrt(jnp.mean(values * values, axis=-1, keepdims=True) + EPSILON) * gain_vec
    )


def slot_table(route_rows, experts, first_id, capacity):
    tok_count, top_count = route_rows.shape
    flat_routes = route_rows.reshape(-1)
    expert_ids = first_id + jnp.arange(experts, dtype=jnp.int32)
    hit_table = (flat_routes[:, None] == expert_ids[None, :]).astype(jnp.int32)
    rank_table = jnp.cumsum(hit_table, axis=0) - 1
    slot_place = jnp.sum(rank_table * hit_table, axis=1)
    local_id = flat_routes - first_id
    inside = (local_id >= 0) & (local_id < experts)
    target = jnp.where(inside, local_id, experts)
    entries = jnp.arange(tok_count * top_count, dtype=jnp.int32)
    slot_ids = jnp.full((experts, capacity), tok_count * top_count, jnp.int32)
    slot_ids = slot_ids.at[target, slot_place].set(entries, mode="drop")
    return (slot_ids // top_count, slot_ids % top_count)


def feature_sum(partial_rows):
    return lax.psum(partial_rows, "col")


def gather_features(local_rows):
    return lax.all_gather(local_rows, "col", axis=1, tiled=True)


def scatter_partial(partial_rows):
    return lax.psum_scatter(partial_rows, "col", scatter_dimension=1, tiled=True)


def contract_last(left_op, right_op):
    return lax.dot_general(
        left_op, right_op, (((1,), (1,)), ((), ())), preferred_element_type=jnp.float32
    )


def contract_first(left_op, right_op):
    return lax.dot_general(
        left_op, right_op, (((0,), (0,)), ((), ())), preferred_element_type=jnp.float32
    )


def plain_dot(left_op, right_op):
    return jnp.dot(left_op, right_op, preferred_element_type=jnp.float32)


def body(
    hidden_in,
    token_order,
    lengths,
    key_mask,
    routes,
    norm1_gain,
    query_gain,
    key_gain,
    w_query,
    w_key,
    w_value,
    w_out,
    norm2_gain,
    router,
    w_gate,
    w_up,
    w_down,
    cotangent,
):
    tok_count, feat_local = hidden_in.shape
    places = jnp.arange(tok_count, dtype=jnp.int32)
    order_row = token_order[0]
    inverse = jnp.zeros((tok_count,), jnp.int32).at[order_row].set(places)
    segment, position = layout(lengths[0], tok_count)
    packed = hidden_in[order_row].astype(jnp.float32)
    grad_packed = cotangent[order_row]
    w_query_all, w_key_all, w_value_all, w_out_all = (
        lax.all_gather(w_query, "row", axis=0, tiled=True),
        lax.all_gather(w_key, "row", axis=0, tiled=True),
        lax.all_gather(w_value, "row", axis=0, tiled=True),
        lax.all_gather(w_out, "row", axis=0, tiled=True),
    )
    width_local = w_query_all.shape[1]
    head_count = width_local // DH
    scale_in = lax.rsqrt(feature_sum(jnp.sum(packed * packed, axis=1)) / D + EPSILON)[:, None]
    unit_in = packed * scale_in
    normed1 = gather_features((unit_in * norm1_gain).astype(jnp.bfloat16))
    queries = plain_dot(normed1, w_query_all).reshape(tok_count, head_count, DH)
    keys_raw = plain_dot(normed1, w_key_all).reshape(tok_count, head_count, DH)
    values_b = (
        plain_dot(normed1, w_value_all).astype(jnp.bfloat16).reshape(tok_count, head_count, DH)
    )

    def post_heads(raw_rows, gain_vec):
        return rotate(head_norm(raw_rows, gain_vec), position)

    query_post, query_pull = jax.vjp(post_heads, queries, query_gain)
    key_post, key_pull = jax.vjp(post_heads, keys_raw, key_gain)
    query_rot = query_post.astype(jnp.bfloat16)
    key_rot = key_post.astype(jnp.bfloat16)
    score_scale = DH ** (-0.5)
    block_rows = 512
    starts = jnp.arange(tok_count // block_rows, dtype=jnp.int32) * block_rows

    def allowed_at(block_start):
        rows_here = block_start + jnp.arange(block_rows, dtype=jnp.int32)
        segment_here = lax.dynamic_slice_in_dim(segment, block_start, block_rows, 0)
        return (segment_here[:, None] == segment[None, :]) & (
            (key_mask[None, :] == 1) | (rows_here[:, None] == places[None, :])
        )

    def scores_at(block_start):
        query_rows = lax.dynamic_slice_in_dim(query_rot, block_start, block_rows, 0)
        scores = (
            jnp.einsum("qhd,khd->hqk", query_rows, key_rot, preferred_element_type=jnp.float32)
            * score_scale
        )
        return (query_rows, jnp.where(allowed_at(block_start)[None], scores, -1e30))

    def forward_block(block_start):
        query_rows, scores = scores_at(block_start)
        row_max = jnp.max(scores, axis=-1, keepdims=True)
        exp_terms = jnp.exp(scores - row_max)
        row_total = jnp.sum(exp_terms, axis=-1, keepdims=True)
        weights = (exp_terms / row_total).astype(jnp.bfloat16)
        attended = jnp.einsum("hqk,khd->qhd", weights, values_b, preferred_element_type=jnp.float32)
        return (attended, (row_max + jnp.log(row_total))[..., 0])

    attended_blocks, log_totals = lax.map(forward_block, starts)
    attended_b = attended_blocks.reshape(tok_count, width_local).astype(jnp.bfloat16)
    branch = scatter_partial(contract_last(attended_b, w_out_all))
    mixed = packed + branch
    scale_mid = lax.rsqrt(feature_sum(jnp.sum(mixed * mixed, axis=1)) / D + EPSILON)[:, None]
    unit_mid = mixed * scale_mid
    normed2 = gather_features((unit_mid * norm2_gain).astype(jnp.bfloat16))
    w_gate_all, w_up_all, w_down_all, router_all = (
        lax.all_gather(w_gate, "row", axis=1, tiled=True),
        lax.all_gather(w_up, "row", axis=1, tiled=True),
        lax.all_gather(w_down, "row", axis=1, tiled=True),
        lax.all_gather(router, "row", axis=1, tiled=True),
    )
    logits = contract_last(normed2, router_all)
    gate_probs = jax.nn.softmax(jnp.take_along_axis(logits, routes, axis=1), axis=-1)
    local_experts = w_gate.shape[0]
    capacity = 5 * tok_count * TOP // (4 * E)
    slot_token, slot_pick = slot_table(
        routes, local_experts, lax.axis_index("col") * local_experts, capacity
    )
    slot_rows = jnp.concatenate([normed2, jnp.zeros((1, D), jnp.bfloat16)], axis=0)[slot_token]
    slot_gate = jnp.concatenate([gate_probs, jnp.zeros((1, TOP), jnp.float32)], axis=0)[
        slot_token, slot_pick
    ]
    gate_pre = jnp.einsum("ecd,edf->ecf", slot_rows, w_gate_all, preferred_element_type=jnp.float32)
    up_pre = jnp.einsum("ecd,edf->ecf", slot_rows, w_up_all, preferred_element_type=jnp.float32)
    sigmoid_gate = jax.nn.sigmoid(gate_pre)
    silu_gate = gate_pre * sigmoid_gate
    activation = (silu_gate * up_pre).astype(jnp.bfloat16)
    expert_out = jnp.einsum(
        "ecf,edf->ecd", activation, w_down_all, preferred_element_type=jnp.float32
    )
    weighted = slot_gate[..., None] * expert_out
    combined = jnp.zeros((tok_count + 1, D), jnp.float32).at[slot_token].add(weighted)[:tok_count]
    combined_part = scatter_partial(combined)
    mixed_out = mixed + combined_part
    output = mixed_out.astype(jnp.bfloat16)[inverse]
    grad_rows = grad_packed.astype(jnp.float32)
    grad_moe = gather_features(grad_packed)
    grad_slot = jnp.concatenate([grad_moe, jnp.zeros((1, D), jnp.bfloat16)], axis=0)[slot_token]
    grad_expert = (slot_gate[..., None] * grad_slot).astype(jnp.bfloat16)
    grad_gate_slot = jnp.sum(grad_slot * expert_out, axis=-1)
    grad_activation = jnp.einsum(
        "ecd,edf->ecf", grad_expert, w_down_all, preferred_element_type=jnp.float32
    )
    grad_gate_pre = (
        grad_activation * up_pre * sigmoid_gate * (1.0 + gate_pre * (1.0 - sigmoid_gate))
    ).astype(jnp.bfloat16)
    grad_up_pre = (grad_activation * silu_gate).astype(jnp.bfloat16)
    grad_w_down = jnp.einsum(
        "ecd,ecf->edf", grad_expert, activation, preferred_element_type=jnp.float32
    )
    grad_w_gate = jnp.einsum(
        "ecd,ecf->edf", slot_rows, grad_gate_pre, preferred_element_type=jnp.float32
    )
    grad_w_up = jnp.einsum(
        "ecd,ecf->edf", slot_rows, grad_up_pre, preferred_element_type=jnp.float32
    )
    grad_slot_rows = jnp.einsum(
        "ecf,edf->ecd", grad_gate_pre, w_gate_all, preferred_element_type=jnp.float32
    ) + jnp.einsum("ecf,edf->ecd", grad_up_pre, w_up_all, preferred_element_type=jnp.float32)
    gate_table = (
        jnp.zeros((tok_count + 1, TOP), jnp.float32)
        .at[slot_token, slot_pick]
        .add(grad_gate_slot)[:tok_count]
    )
    grad_gates = lax.psum(gate_table, "col")
    grad_chosen = gate_probs * (
        grad_gates - jnp.sum(gate_probs * grad_gates, axis=1, keepdims=True)
    )
    expert_ids = jnp.arange(E, dtype=jnp.int32)
    grad_logits = jnp.sum(
        jnp.where(routes[:, :, None] == expert_ids[None, None, :], grad_chosen[:, :, None], 0.0),
        axis=1,
    ).astype(jnp.bfloat16)
    grad_router = contract_first(grad_logits, normed2)
    column_start = lax.axis_index("col") * feat_local
    router_local = lax.dynamic_slice_in_dim(router_all, column_start, feat_local, 1)
    grad_normed2 = (
        jnp.zeros((tok_count + 1, D), jnp.float32).at[slot_token].add(grad_slot_rows)[:tok_count]
    )
    grad_normed2_part = scatter_partial(grad_normed2)
    grad_unit_mid = grad_normed2_part + plain_dot(grad_logits, router_local)
    grad_norm2_part = jnp.sum(grad_unit_mid * unit_mid, axis=0)
    scaled_mid = grad_unit_mid * norm2_gain
    inner_mid = feature_sum(jnp.sum(scaled_mid * unit_mid, axis=1))[:, None] / D
    grad_mixed = grad_rows + scale_mid * (scaled_mid - unit_mid * inner_mid)
    grad_branch = gather_features(grad_mixed.astype(jnp.bfloat16))
    grad_w_out = contract_first(grad_branch, attended_b)
    grad_attended = (
        plain_dot(grad_branch, w_out_all).astype(jnp.bfloat16).reshape(tok_count, head_count, DH)
    )

    def backward_block(carried, inputs):
        grad_keys, grad_values = carried
        block_start, log_total = inputs
        query_rows, scores = scores_at(block_start)
        prob_rows = jnp.exp(scores - log_total[..., None])
        grad_out_rows = lax.dynamic_slice_in_dim(grad_attended, block_start, block_rows, 0)
        grad_values = grad_values + jnp.einsum(
            "hqk,qhd->khd",
            prob_rows.astype(jnp.bfloat16),
            grad_out_rows,
            preferred_element_type=jnp.float32,
        )
        grad_probs = jnp.einsum(
            "qhd,khd->hqk", grad_out_rows, values_b, preferred_element_type=jnp.float32
        )
        grad_scores = (
            prob_rows * (grad_probs - jnp.sum(prob_rows * grad_probs, axis=-1, keepdims=True))
        ).astype(jnp.bfloat16)
        grad_query_rows = (
            jnp.einsum("hqk,khd->qhd", grad_scores, key_rot, preferred_element_type=jnp.float32)
            * score_scale
        )
        grad_keys = (
            grad_keys
            + jnp.einsum(
                "hqk,qhd->khd", grad_scores, query_rows, preferred_element_type=jnp.float32
            )
            * score_scale
        )
        return ((grad_keys, grad_values), grad_query_rows)

    zero_heads = jnp.zeros((tok_count, head_count, DH), jnp.float32)
    (grad_key_rot, grad_values), grad_query_rot = lax.scan(
        backward_block, (zero_heads, zero_heads), (starts, log_totals)
    )
    grad_queries, grad_query_gain = query_pull(grad_query_rot.reshape(tok_count, head_count, DH))
    grad_keys_raw, grad_key_gain = key_pull(grad_key_rot)
    grad_query_b = grad_queries.reshape(tok_count, width_local).astype(jnp.bfloat16)
    grad_key_b = grad_keys_raw.reshape(tok_count, width_local).astype(jnp.bfloat16)
    grad_value_b = grad_values.reshape(tok_count, width_local).astype(jnp.bfloat16)
    grad_w_query = contract_first(normed1, grad_query_b)
    grad_w_key = contract_first(normed1, grad_key_b)
    grad_w_value = contract_first(normed1, grad_value_b)
    grad_normed1 = (
        contract_last(grad_query_b, w_query_all)
        + contract_last(grad_key_b, w_key_all)
        + contract_last(grad_value_b, w_value_all)
    )
    grad_unit_in = scatter_partial(grad_normed1)
    grad_norm1_part = jnp.sum(grad_unit_in * unit_in, axis=0)
    scaled_in = grad_unit_in * norm1_gain
    inner_in = feature_sum(jnp.sum(scaled_in * unit_in, axis=1))[:, None] / D
    grad_input = (grad_mixed + scale_in * (scaled_in - unit_in * inner_in))[inverse]
    grad_w_query, grad_w_key, grad_w_value, grad_w_out = (
        lax.psum_scatter(grad_w_query, "row", scatter_dimension=0, tiled=True),
        lax.psum_scatter(grad_w_key, "row", scatter_dimension=0, tiled=True),
        lax.psum_scatter(grad_w_value, "row", scatter_dimension=0, tiled=True),
        lax.psum_scatter(grad_w_out, "row", scatter_dimension=0, tiled=True),
    )
    grad_w_gate, grad_w_up, grad_w_down, grad_router = (
        lax.psum_scatter(grad_w_gate, "row", scatter_dimension=1, tiled=True),
        lax.psum_scatter(grad_w_up, "row", scatter_dimension=1, tiled=True),
        lax.psum_scatter(grad_w_down, "row", scatter_dimension=1, tiled=True),
        lax.psum_scatter(grad_router, "row", scatter_dimension=1, tiled=True),
    )
    grad_norm1, grad_norm2 = lax.psum((grad_norm1_part, grad_norm2_part), "row")
    grad_query_gain, grad_key_gain = lax.psum((grad_query_gain, grad_key_gain), ("row", "col"))
    return (
        output,
        grad_input,
        grad_norm1,
        grad_query_gain,
        grad_key_gain,
        grad_w_query,
        grad_w_key,
        grad_w_value,
        grad_w_out,
        grad_norm2,
        grad_router,
        grad_w_gate,
        grad_w_up,
        grad_w_down,
    )


def solution(mesh):
    return jax.shard_map(
        body,
        mesh=mesh,
        in_specs=(
            P("row", "col"),
            P("row", None),
            P("row", None),
            P("row"),
            P("row", None),
            P("col"),
            P(),
            P(),
            P("row", "col"),
            P("row", "col"),
            P("row", "col"),
            P("row", "col"),
            P("col"),
            P(None, "row"),
            P("col", "row", None),
            P("col", "row", None),
            P("col", "row", None),
            P("row", "col"),
        ),
        out_specs=(
            P("row", "col"),
            P("row", "col"),
            P("col"),
            P(),
            P(),
            P("row", "col"),
            P("row", "col"),
            P("row", "col"),
            P("row", "col"),
            P("col"),
            P(None, "row"),
            P("col", "row", None),
            P("col", "row", None),
            P("col", "row", None),
        ),
        check_vma=False,
    )
```

profile of v0, /device:TPU:0, one launch (start us, length us, event | category | flops | bytes accessed | tf_op | source)
XLA Modules:
  0.0 3827.1 jit_solution(5890505354712891399)
XLA Ops:
  14.4 23.4 psum.63
  45.6 90.8 %all-gather.13.cloned.1.call-done = bf16[1536,2048]{1,0:T(8,128)(2,1)} async-done(((bf16[1536,256]{1,0:T(8,128)(2,1)}), bf16[1536,2048]{1,0:T(8,128)(2,1)}) %all-gather.13.cloned.1.call-update) | async-done | bytes 6291472 | tf_op jit(solution)/shard_map/all_gather | solution.py:70
  142.4 10.5 all-gather.17.cloned.1.call-done
  159.4 11.6 all-gather.15.cloned.1.call-done
  184.0 38.1 while.28
  239.4 201.5 %reduce-scatter.13.cloned.1.call-done = f32[1536,256]{1,0:T(8,128)} async-done(((f32[1536,2048]{1,0:T(8,128)}), f32[1536,256]{1,0:T(8,128)}) %reduce-scatter.13.cloned.1.call-update) | async-done | bytes 1572880 | tf_op jit(solution)/shard_map/reduce_scatter | solution.py:74
  442.6 20.1 psum.64
  473.1 45.4 %scatter_custom_fusion.3 = s32[1920]{0:T(1024)S(1)} fusion(s32[12288]{0:T(1024)S(1)} %broadcast_select_fusion, s32[12288]{0:T(1024)S(1)} %iota.57, s32[]{:T(128)} %constant.91.clone.1), kind=kCustom, calls=%fused_computation.199 | custom fusion | bytes 7684
  526.0 16.5 all-gather.33.cloned.1.call-done
  549.2 20.4 gather_fusion.5
  569.5 73.8 %all-gather.23.cloned.1.call-done = bf16[1536,2048]{1,0:T(8,128)(2,1)} async-done(((bf16[1536,256]{1,0:T(8,128)(2,1)}), bf16[1536,2048]{1,0:T(8,128)(2,1)}) %all-gather.23.cloned.1.call-update) | async-done | bytes 6291472 | tf_op jit(solution)/shard_map/all_gather | solution.py:70
  648.1 98.1 %gather_fusion.7 = f32[12288]{0:T(1024)S(1)} fusion(f32[1536,64]{0,1:T(8,128)S(1)} %fusion.94, s32[12288]{0:T(1024)S(1)} %reshape.539), kind=kCustom, calls=%fused_computation.7 | custom fusion | bytes 196608 | tf_op jit(solution)/shard_map/jit(take_along_axis)/gather | solution.py:186
  753.5 19.9 gather_fusion.2
  773.6 71.1 %all-gather.25.cloned.1.call-done = bf16[8,2048,1024]{2,1,0:T(8,128)(2,1)} async-done(((bf16[8,512,1024]{2,1,0:T(8,128)(2,1)}), bf16[8,2048,1024]{2,1,0:T(8,128)(2,1)}) %all-gather.25.cloned.1.call-update) | async-done | bytes 33554448 | tf_op jit(solution)/shard_map/all_gather | solution.py:180
  844.6 27.2 fusion.95
  871.8 175.9 %all-gather.27.cloned.1.call-done = bf16[8,2048,1024]{2,1,0:T(8,128)(2,1)} async-done(((bf16[8,512,1024]{2,1,0:T(8,128)(2,1)}), bf16[8,2048,1024]{2,1,0:T(8,128)(2,1)}) %all-gather.27.cloned.1.call-update) | async-done | bytes 33554448 | tf_op jit(solution)/shard_map/all_gather | solution.py:181
  1047.7 36.5 multiply_convert_fusion.3
  1084.1 166.7 %all-gather.29.cloned.1.call-done = bf16[8,2048,1024]{2,1,0:T(8,128)(2,1)} async-done(((bf16[8,512,1024]{2,1,0:T(8,128)(2,1)}), bf16[8,2048,1024]{2,1,0:T(8,128)(2,1)}) %all-gather.29.cloned.1.call-update) | async-done | bytes 33554448 | tf_op jit(solution)/shard_map/all_gather | solution.py:182
  1250.8 21.6 fusion.40
  1272.5 12.7 scatter_custom_fusion.4
  1285.3 37.3 psum.65
  1322.7 10.9 gather_fusion.1
  1333.7 23.7 multiply_convert_fusion.1
  1357.4 19.9 fusion.96
  1377.2 23.6 convolution_add_fusion
  1400.9 32.9 scatter_custom_fusion.2
  1433.8 11.5 slice.58
  1445.8 203.7 %reduce-scatter.17.cloned.1.call-done = f32[1536,256]{1,0:T(8,128)} async-done(((f32[1536,2048]{1,0:T(8,128)}), f32[1536,256]{1,0:T(8,128)}) %reduce-scatter.17.cloned.1.call-update) | async-done | bytes 1572880 | tf_op jit(solution)/shard_map/reduce_scatter | solution.py:74
  1653.3 19.7 psum.66
  1676.4 96.8 %all-gather.31.cloned.1.call-done = bf16[1536,2048]{1,0:T(8,128)(2,1)} async-done(((bf16[1536,256]{1,0:T(8,128)(2,1)}), bf16[1536,2048]{1,0:T(8,128)(2,1)}) %all-gather.31.cloned.1.call-update) | async-done | bytes 6291472 | tf_op jit(solution)/shard_map/all_gather | solution.py:70
  1779.0 52.3 %while.29 = (s32[]{:T(128)}, f32[1536,2,128]{0,2,1:T(8,128)}, f32[1536,2,128]{0,2,1:T(8,128)}, f32[3,512,2,128]{3,1,0,2:T(8,128)}, s32[3]{0:T(128)S(1)}, /*index...) while((s32[]{:T(128)}, f32[1536,2,128]{0,2,1:T(8,128)}, ...), condition=%wide.region_34.35_spmd.clone, body=%wide.region_32.34_spmd.clone.sunk | while | flops 2032665600 | bytes 71611680 | solution.py:297
  1862.1 11.5 add_add_fusion
  1874.3 11.3 broadcast_multiply_fusion
  1885.6 32.7 scatter_custom_fusion
  1918.3 11.5 slice.57
  1960.2 28.2 fusion.42
  1988.6 28.0 fusion.103
  2016.7 28.3 fusion.102
  2051.6 42.2 %all-reduce.7 = (f32[128]{0:T(128)}, f32[128]{0:T(128)}) all-reduce(f32[128]{0:T(128)S(1)} %copy-done.77, f32[128]{0:T(128)S(1)} %copy-done.76), channel_id=1, replica_groups=mesh['row'=4,'col'=8] {'row','col'}, use_global_device_ids=true, to_apply=%region_43.44 | all-reduce | flops 256 | bytes 2048 | tf_op jit(solution)/shard_map/psum | solution.py:331
  2096.0 22.9 psum.67
  2118.9 172.4 %reduce-scatter.15.cloned.1.call-done = f32[1536,256]{1,0:T(8,128)} async-done(((f32[1536,2048]{1,0:T(8,128)}), f32[1536,256]{1,0:T(8,128)}) %reduce-scatter.15.cloned.1.call-update) | async-done | bytes 1572880 | tf_op jit(solution)/shard_map/reduce_scatter | solution.py:74
  2315.1 34.5 reduce-scatter.27.cloned.1.call-done
  2349.6 34.4 reduce-scatter.21.cloned.1.call-done
  2384.0 34.7 reduce-scatter.25.cloned.1.call-done
  2418.7 34.4 reduce-scatter.23.cloned.1.call-done
  2453.2 455.8 %reduce-scatter.35.cloned.1.call-done = f32[8,512,1024]{2,1,0:T(8,128)} async-done(((f32[8,2048,1024]{2,1,0:T(8,128)}), f32[8,512,1024]{2,1,0:T(8,128)}) %reduce-scatter.35.cloned.1.call-update) | async-done | bytes 16777232 | tf_op jit(solution)/shard_map/reduce_scatter | solution.py:327
  2908.9 455.6 %reduce-scatter.33.cloned.1.call-done = f32[8,512,1024]{2,1,0:T(8,128)} async-done(((f32[8,2048,1024]{2,1,0:T(8,128)}), f32[8,512,1024]{2,1,0:T(8,128)}) %reduce-scatter.33.cloned.1.call-update) | async-done | bytes 16777232 | tf_op jit(solution)/shard_map/reduce_scatter | solution.py:326
  3364.5 455.8 %reduce-scatter.31.cloned.1.call-done = f32[8,512,1024]{2,1,0:T(8,128)} async-done(((f32[8,2048,1024]{2,1,0:T(8,128)}), f32[8,512,1024]{2,1,0:T(8,128)}) %reduce-scatter.31.cloned.1.call-update) | async-done | bytes 16777232 | tf_op jit(solution)/shard_map/reduce_scatter | solution.py:325
  (407 shorter events, 281.2 us)
Async XLA Ops:
  7.2 38.4 %all-gather.19.cloned.1.call-start = ((), (), s32[]{:S(2)}) async-start(), calls=%async_computation.15 | async-start | bytes 1310720 | tf_op jit(solution)/shard_map/all_gather | solution.py:123
  7.9 128.4 %all-gather.13.cloned.1.call-start = ((), (), s32[]{:S(2)}) async-start(), calls=%async_computation.12 | async-start | bytes 7077888 | tf_op jit(solution)/shard_map/all_gather | solution.py:70
  14.1 426.8 %copy-start.13 = (bf16[1536,256]{1,0:T(8,128)(2,1)}, bf16[1536,256]{1,0:T(8,128)(2,1)S(1)}, u32[]{:S(2)}) copy-start(bf16[1536,256]{1,0:T(8,128)(2,1)S(1)} %gather_fusion) | copy-start | bytes 2359300
  39.0 113.9 %all-gather.17.cloned.1.call-start = ((), (), s32[]{:S(2)}) async-start(), calls=%async_computation.14 | async-start | bytes 1310720 | tf_op jit(solution)/shard_map/all_gather | solution.py:122
  39.7 131.3 %all-gather.15.cloned.1.call-start = ((), (), s32[]{:S(2)}) async-start(), calls=%async_computation.13 | async-start | bytes 1310720 | tf_op jit(solution)/shard_map/all_gather | solution.py:121
  40.3 184.4 %all-gather.21.cloned.1.call-start = ((), (), s32[]{:S(2)}) async-start(), calls=%async_computation.16 | async-start | bytes 1310720 | tf_op jit(solution)/shard_map/all_gather | solution.py:124
  40.9 400.0 %reduce-scatter.13.cloned.1.call-start = ((), (), s32[]{:S(2)}) async-start(), calls=%async_computation.17 | async-start | bytes 14155776 | tf_op jit(solution)/shard_map/reduce_scatter | solution.py:74
  45.6 136.5 %copy-start.21 = (f32[1536,64]{1,0:T(8,128)}, f32[1536,64]{1,0:T(8,128)S(1)}, u32[]{:S(2)}) copy-start(f32[1536,64]{1,0:T(8,128)S(1)} %get-tuple-element.366) | copy-start | bytes 1179652
  232.9 309.7 %all-gather.33.cloned.1.call-start = ((), (), s32[]{:S(2)}) async-start(), calls=%async_computation.34 | async-start | bytes 7077888 | tf_op jit(solution)/shard_map/all_gather | solution.py:70
  239.3 223.4 %copy-start.62 = (f32[256]{0:T(256)S(1)}, f32[256]{0:T(256)}, u32[]{:S(2)}) copy-start(f32[256]{0:T(256)} %param.34) | copy-start | bytes 3076
  239.3 404.0 %all-gather.23.cloned.1.call-start = ((), (), s32[]{:S(2)}) async-start(), calls=%async_computation.18 | async-start | bytes 7077888 | tf_op jit(solution)/shard_map/all_gather | solution.py:70
  463.9 380.7 %all-gather.25.cloned.1.call-start = ((), (), s32[]{:S(2)}) async-start(), calls=%async_computation.19 | async-start | bytes 41943040 | tf_op jit(solution)/shard_map/all_gather | solution.py:180
  464.7 583.0 %all-gather.27.cloned.1.call-start = ((), (), s32[]{:S(2)}) async-start(), calls=%async_computation.20 | async-start | bytes 41943040 | tf_op jit(solution)/shard_map/all_gather | solution.py:181
  465.3 785.5 %all-gather.29.cloned.1.call-start = ((), (), s32[]{:S(2)}) async-start(), calls=%async_computation.21 | async-start | bytes 41943040 | tf_op jit(solution)/shard_map/all_gather | solution.py:182
  466.0 1183.4 %reduce-scatter.17.cloned.1.call-start = ((), (), s32[]{:S(2)}) async-start(), calls=%async_computation.23 | async-start | bytes 14155776 | tf_op jit(solution)/shard_map/reduce_scatter | solution.py:74
  467.4 52.0 %copy-start.75 = (s32[2]{0:T(128)S(1)}, s32[2]{0:T(128)}, u32[]{:S(2)}) copy-start(s32[2]{0:T(128)} %constant.179) | copy-start | bytes 28
  467.4 52.0 %copy-start.74 = (s32[2]{0:T(128)S(1)}, s32[2]{0:T(128)}, u32[]{:S(2)}) copy-start(s32[2]{0:T(128)} %constant.182) | copy-start | bytes 28
  467.4 52.8 %copy-start.55 = (bf16[64,512]{1,0:T(8,128)(2,1)S(1)}, bf16[64,512]{1,0:T(8,128)(2,1)}, u32[]{:S(2)}) copy-start(bf16[64,512]{1,0:T(8,128)(2,1)} %param.35) | copy-start | bytes 196612
  519.3 29.8 copy-start.61
  526.0 117.3 %copy-start.34 = (bf16[64,2048]{1,0:T(8,128)(2,1)}, bf16[64,2048]{1,0:T(8,128)(2,1)S(1)}, u32[]{:S(2)}) copy-start(bf16[64,2048]{1,0:T(8,128)(2,1)S(1)} %all_gather.42) | copy-start | bytes 786436
  1250.8 71.8 %copy-start.4 = (s32[1920]{0:T(1024)S(1)}, s32[1920]{0:T(1024)}, u32[]{:S(2)}) copy-start(s32[1920]{0:T(1024)} %reshape.493) | copy-start | bytes 23044
  1445.3 204.2 %copy-start.10 = (f32[1536,256]{1,0:T(8,128)S(1)}, f32[1536,256]{1,0:T(8,128)}, u32[]{:S(2)}) copy-start(f32[1536,256]{1,0:T(8,128)} %copy-done.9) | copy-start | bytes 4718596
  1445.3 204.2 %copy-start.43 = (f32[1536]{0:T(1024)S(1)}, f32[1536]{0:T(1024)}, u32[]{:S(2)}) copy-start(f32[1536]{0:T(1024)} %copy-done.42) | copy-start | bytes 18436
  1445.3 204.2 %copy-start.63 = (f32[256]{0:T(256)S(1)}, f32[256]{0:T(256)}, u32[]{:S(2)}) copy-start(f32[256]{0:T(256)} %param.34) | copy-start | bytes 3076
  1445.3 227.7 %copy-start.20 = (bf16[1536,256]{1,0:T(8,128)(2,1)S(1)}, bf16[1536,256]{1,0:T(8,128)(2,1)}, u32[]{:S(2)}) copy-start(bf16[1536,256]{1,0:T(8,128)(2,1)} %gather_fusion.4) | copy-start | bytes 2359300
  1445.3 327.8 %all-gather.31.cloned.1.call-start = ((), (), s32[]{:S(2)}) async-start(), calls=%async_computation.24 | async-start | bytes 7077888 | tf_op jit(solution)/shard_map/all_gather | solution.py:70
  1675.9 418.0 %reduce-scatter.19.cloned.1.call-start = ((), (), s32[]{:S(2)}) async-start(), calls=%async_computation.25 | async-start | bytes 14155776 | tf_op jit(solution)/shard_map/reduce_scatter | solution.py:74
  1676.4 102.6 %copy-start.3 = (bf16[1536,2,128]{2,0,1:T(8,128)(2,1)S(1)}, bf16[1536,2,128]{2,0,1:T(8,128)(2,1)}, u32[]{:S(2)}) copy-start(bf16[1536,2,128]{2,0,1:T(8,128)(2,1)} %copy-done.2) | copy-start | bytes 2359300
  1676.4 102.6 %copy-start.12 = (bf16[1536,2,128]{2,0,1:T(8,128)(2,1)S(1)}, bf16[1536,2,128]{2,0,1:T(8,128)(2,1)}, u32[]{:S(2)}) copy-start(bf16[1536,2,128]{2,0,1:T(8,128)(2,1)} %copy-done.11) | copy-start | bytes 2359300
  1676.4 102.6 %copy-start.33 = (s32[1536]{0:T(1024)S(1)}, s32[1536]{0:T(1024)}, u32[]{:S(2)}) copy-start(s32[1536]{0:T(1024)} %copy-done.32) | copy-start | bytes 18436
  1676.4 102.6 %copy-start.37 = (s32[1536]{0:T(1024)S(1)}, s32[1536]{0:T(1024)}, u32[]{:S(2)}) copy-start(s32[1536]{0:T(1024)} %param.25) | copy-start | bytes 18436
  1676.4 102.6 %copy-start.80 = (s32[3]{0:T(128)S(1)}, s32[3]{0:T(128)}, u32[]{:S(2)}) copy-start(s32[3]{0:T(128)} %copy-done.79) | copy-start | bytes 40
  1873.7 417.7 %reduce-scatter.15.cloned.1.call-start = ((), (), s32[]{:S(2)}) async-start(), calls=%async_computation.22 | async-start | bytes 14155776 | tf_op jit(solution)/shard_map/reduce_scatter | solution.py:74
  1929.8 385.2 %reduce-scatter.29.cloned.1.call-start = ((), (), s32[]{:S(2)}) async-start(), calls=%async_computation.30 | async-start | bytes 655360 | tf_op jit(solution)/shard_map/reduce_scatter | solution.py:328
  1935.1 414.4 %reduce-scatter.27.cloned.1.call-start = ((), (), s32[]{:S(2)}) async-start(), calls=%async_computation.29 | async-start | bytes 2621440 | tf_op jit(solution)/shard_map/reduce_scatter | solution.py:322
  1941.7 442.4 %reduce-scatter.21.cloned.1.call-start = ((), (), s32[]{:S(2)}) async-start(), calls=%async_computation.26 | async-start | bytes 2621440 | tf_op jit(solution)/shard_map/reduce_scatter | solution.py:319
  1947.9 470.9 %reduce-scatter.25.cloned.1.call-start = ((), (), s32[]{:S(2)}) async-start(), calls=%async_computation.28 | async-start | bytes 2621440 | tf_op jit(solution)/shard_map/reduce_scatter | solution.py:321
  1953.9 499.2 %reduce-scatter.23.cloned.1.call-start = ((), (), s32[]{:S(2)}) async-start(), calls=%async_computation.27 | async-start | bytes 2621440 | tf_op jit(solution)/shard_map/reduce_scatter | solution.py:320
  1960.1 948.8 %reduce-scatter.35.cloned.1.call-start = ((), (), s32[]{:S(2)}) async-start(), calls=%async_computation.33 | async-start | bytes 83886080 | tf_op jit(solution)/shard_map/reduce_scatter | solution.py:327
  1988.4 1376.2 %reduce-scatter.33.cloned.1.call-start = ((), (), s32[]{:S(2)}) async-start(), calls=%async_computation.32 | async-start | bytes 83886080 | tf_op jit(solution)/shard_map/reduce_scatter | solution.py:326
  2016.6 1803.7 %reduce-scatter.31.cloned.1.call-start = ((), (), s32[]{:S(2)}) async-start(), calls=%async_computation.31 | async-start | bytes 83886080 | tf_op jit(solution)/shard_map/reduce_scatter | solution.py:325
  2045.0 48.9 %copy-start.14 = (bf16[1536,256]{1,0:T(8,128)(2,1)S(1)}, bf16[1536,256]{1,0:T(8,128)(2,1)}, u32[]{:S(2)}) copy-start(bf16[1536,256]{1,0:T(8,128)(2,1)} %copy-done.13) | copy-start | bytes 2359300
  2045.0 48.9 %copy-start.50 = (f32[1536]{0:T(1024)S(1)}, f32[1536]{0:T(1024)}, u32[]{:S(2)}) copy-start(f32[1536]{0:T(1024)} %copy-done.49) | copy-start | bytes 18436
  2045.0 48.8 %copy-start.66 = (f32[256]{0:T(256)S(1)}, f32[256]{0:T(256)}, u32[]{:S(2)}) copy-start(f32[256]{0:T(256)} %param.27) | copy-start | bytes 3076
  2045.0 246.3 %copy-start.44 = (f32[1536]{0:T(1024)S(1)}, f32[1536]{0:T(1024)}, u32[]{:S(2)}) copy-start(f32[1536]{0:T(1024)} %copy-done.42) | copy-start | bytes 18436
  2045.0 246.3 %copy-start.54 = (f32[1536]{0:T(1024)S(1)}, f32[1536]{0:T(1024)}, u32[]{:S(2)}) copy-start(f32[1536]{0:T(1024)} %copy-done.53) | copy-start | bytes 18436
  2045.1 246.3 %copy-start.64 = (f32[256]{0:T(256)S(1)}, f32[256]{0:T(256)}, u32[]{:S(2)}) copy-start(f32[256]{0:T(256)} %param.34) | copy-start | bytes 3076
  2299.7 1520.6 %copy-start.1 = (bf16[1536,256]{1,0:T(8,128)(2,1)S(1)}, bf16[1536,256]{1,0:T(8,128)(2,1)}, u32[]{:S(2)}) copy-start(bf16[1536,256]{1,0:T(8,128)(2,1)} %param.22) | copy-start | bytes 2359300
  (64 other events, 382.8 us)
Sparse Core Ops, SparseCore 0:
  9.6 19.4 all-gather.18
  39.1 97.1 all-gather.12
  137.9 14.8 all-gather.16
  154.3 16.7 all-gather.14
  172.4 16.7 all-gather.20
  233.0 207.8 reduce-scatter.12
  442.9 99.5 all-gather.32
  545.1 98.1 all-gather.22
  644.9 199.7 all-gather.24
  846.1 201.5 all-gather.26
  1049.2 201.5 all-gather.28
  1445.5 203.9 reduce-scatter.16
  1676.0 97.1 all-gather.30
  1873.8 206.6 reduce-scatter.18
  2083.9 207.3 reduce-scatter.14
  2294.3 20.7 reduce-scatter.28
  2318.2 31.3 reduce-scatter.26
  2352.5 31.4 reduce-scatter.20
  2387.3 31.4 reduce-scatter.24
  2421.7 31.4 reduce-scatter.22
  2456.5 452.3 reduce-scatter.34
  2912.1 452.3 reduce-scatter.32
  3367.9 452.4 reduce-scatter.30
where the time goes:
time: 3840 us; the launch traced here: 3830 us
  waiting for transfers between devices  2800 us (73%)
  matrix products  377 us (10%)
  local copies, waits for them, and re-layouts  282 us (7%)
  blocking collectives  179 us (5%)
  other arithmetic  155 us (4%)
    reduce_scatter x4, waiting for transfers between devices, scatter_partial(): lax.psum_scatter(partial_rows, 'col', scatter_dimension=1, tiled=True)  578 us
    reduce_scatter x1, waiting for transfers between devices, body(): lax.psum_scatter(grad_w_gate, 'row', scatter_dimension=1, tiled=True)  456 us
    reduce_scatter x1, waiting for transfers between devices, body(): lax.psum_scatter(grad_w_down, 'row', scatter_dimension=1, tiled=True)  456 us
    reduce_scatter x1, waiting for transfers between devices, body(): lax.psum_scatter(grad_w_up, 'row', scatter_dimension=1, tiled=True)  456 us
    all_gather x4, waiting for transfers between devices, gather_features(): return lax.all_gather(local_rows, 'col', axis=1, tiled=True)  278 us
    all_gather x1, waiting for transfers between devices, body(): lax.all_gather(w_up, 'row', axis=1, tiled=True)  176 us
    all_gather x1, waiting for transfers between devices, body(): lax.all_gather(w_down, 'row', axis=1, tiled=True)  167 us
    gather x5, local copies, waits for them, and re-layouts, body(): jnp.take_along_axis(logits, routes, axis=1)  99.4 us
  transfers between devices with their start and end apart: 23, of which 20 were waited for; matrix products, arithmetic and copies ran while one was open for 14% of the time, Pallas kernels for 0%

commit v1 on v0

v1 whole, which is shorter than its diff:
```python
import jax
import jax.numpy as jnp
from jax import lax
from jax.sharding import PartitionSpec as P

D = 2048
DH = 128
E = 64
TOP = 8


EPSILON = 1e-06
ROPE_BASE = 10000.0
BF16 = jnp.bfloat16
F32 = jnp.float32


def layout(seq_lengths, tok_count):
    seq_ends = jnp.cumsum(seq_lengths)
    seq_starts = seq_ends - seq_lengths
    places = jnp.arange(tok_count, dtype=jnp.int32)
    segment = jnp.sum((places[:, None] >= seq_ends[None, :]).astype(jnp.int32), axis=1)
    member = segment[:, None] == jnp.arange(seq_lengths.shape[0], dtype=jnp.int32)[None, :]
    offset = jnp.sum(jnp.where(member, seq_starts[None, :], 0), axis=1)
    return (segment, places - offset)


def rotate(values, position):
    half_dim = values.shape[-1] // 2
    frequency = ROPE_BASE ** (-2.0 * jnp.arange(half_dim, dtype=jnp.float32) / values.shape[-1])
    angles = position.astype(jnp.float32)[:, None] * frequency[None, :]
    cosine = jnp.cos(angles)[:, None, :]
    sine_part = jnp.sin(angles)[:, None, :]
    first_half = values[..., :half_dim]
    second_half = values[..., half_dim:]
    return jnp.concatenate(
        [
            first_half * cosine - second_half * sine_part,
            second_half * cosine + first_half * sine_part,
        ],
        axis=-1,
    )


def head_norm(values, gain_vec):
    return (
        values * lax.rsqrt(jnp.mean(values * values, axis=-1, keepdims=True) + EPSILON) * gain_vec
    )


def gather_features(local_rows):
    return lax.all_gather(local_rows, "col", axis=1, tiled=True)


def scatter_partial(partial_rows):
    return lax.psum_scatter(partial_rows, "col", scatter_dimension=1, tiled=True)


def swap_rows(pieces):
    return lax.all_to_all(pieces, "row", 0, 0, tiled=True)


def contract_last(left_op, right_op, kind=F32):
    return lax.dot_general(
        left_op, right_op, (((1,), (1,)), ((), ())), preferred_element_type=F32
    ).astype(kind)


def contract_first(left_op, right_op, kind=F32):
    return lax.dot_general(
        left_op, right_op, (((0,), (0,)), ((), ())), preferred_element_type=F32
    ).astype(kind)


def plain_dot(left_op, right_op, kind=F32):
    return jnp.dot(left_op, right_op, preferred_element_type=F32).astype(kind)


def after(value, *earlier):
    return lax.optimization_barrier((value, *earlier))[0]


def body(
    hidden_in,
    token_order,
    lengths,
    key_mask,
    routes,
    norm1_gain,
    query_gain,
    key_gain,
    w_query,
    w_key,
    w_value,
    w_out,
    norm2_gain,
    router,
    w_gate,
    w_up,
    w_down,
    cotangent,
):
    tok_count, feat_local = hidden_in.shape
    n_row = D // w_query.shape[0]
    local_experts, _, hidden_units = w_gate.shape
    per_device = max(1, local_experts // n_row)
    unit_split = max(1, n_row // local_experts)
    capacity = 5 * tok_count * TOP // (4 * E)
    col = lax.axis_index("col")
    core = lax.axis_index("row") % 2
    places = jnp.arange(tok_count, dtype=jnp.int32)
    order_row = token_order[0]
    inverse = jnp.zeros((tok_count,), jnp.int32).at[order_row].set(places)
    segment, position = layout(lengths[0], tok_count)

    packed_b = hidden_in[order_row]
    packed_all_b = gather_features(packed_b)
    cot_b = cotangent[order_row]

    width_local = w_query.shape[1]
    head_count = width_local // DH
    weight_rows = jnp.concatenate([w_query, w_key, w_value, w_out], axis=1)
    weight_heads = swap_rows(
        jnp.broadcast_to(weight_rows[None], (n_row,) + weight_rows.shape)
    ).reshape(D, 4 * width_local)
    w_qkv = weight_heads[:, : 3 * width_local]
    w_out_own = weight_heads[:, 3 * width_local :]

    def to_owner(weight, e):
        if unit_split == 1:
            pieces = weight.reshape(n_row, per_device, *weight.shape[1:])[:, e]
        else:
            pieces = weight.reshape(local_experts, -1, unit_split, hidden_units // unit_split)
            pieces = pieces.transpose(0, 2, 1, 3).reshape(
                n_row, -1, hidden_units // unit_split
            )
        return swap_rows(pieces).reshape(D, hidden_units // unit_split)

    experts = [
        tuple(to_owner(weight, e) for weight in (w_gate, w_up, w_down)) for e in range(per_device)
    ]

    gains = lax.all_gather(jnp.stack([norm1_gain, norm2_gain]), "col", axis=1, tiled=True)
    router_all = lax.all_gather(router, "row", axis=1, tiled=True)

    expert_ids = jnp.arange(E, dtype=jnp.int32)
    routes_t = routes.T
    chosen = jnp.any(routes_t[None] == expert_ids[:, None, None], axis=1)
    own_ids = col * local_experts + jnp.arange(local_experts, dtype=jnp.int32)
    own_chosen = jnp.any(routes_t[None] == own_ids[:, None, None], axis=1)
    earlier = (places[:, None] < places[None, :]).astype(BF16)
    rank = plain_dot(own_chosen.astype(BF16), earlier).astype(jnp.int32)
    slot_rank = jnp.where(own_chosen, rank, -1)
    slots = jnp.arange(capacity, dtype=jnp.int32)

    def slot_matrix(e):
        if unit_split == 1:
            mine = slot_rank.reshape(n_row, per_device, tok_count)[:, e]
        else:
            mine = jnp.repeat(slot_rank, unit_split, axis=0)
        hits = mine[:, None, :] == slots[None, :, None]
        return hits

    hits = [slot_matrix(e) for e in range(per_device)]
    picks = [h.astype(BF16).reshape(n_row * capacity, tok_count) for h in hits]

    packed_all = packed_all_b.astype(F32)
    scale_in = lax.rsqrt(jnp.mean(packed_all * packed_all, axis=1, keepdims=True) + EPSILON)
    normed1 = (packed_all * scale_in * gains[0]).astype(BF16)
    qkv = plain_dot(normed1, w_qkv)
    queries, keys_raw, values_raw = (
        qkv[:, i * width_local : (i + 1) * width_local].reshape(tok_count, head_count, DH)
        for i in range(3)
    )
    values_b = values_raw.astype(BF16)

    def post_heads(raw_rows, gain_vec):
        return rotate(head_norm(raw_rows, gain_vec), position)

    query_post, query_pull = jax.vjp(post_heads, queries, query_gain)
    key_post, key_pull = jax.vjp(post_heads, keys_raw, key_gain)
    query_rot = query_post.astype(BF16)
    key_rot = key_post.astype(BF16)
    score_scale = DH ** (-0.5)
    block_rows = 512
    starts = jnp.arange(tok_count // block_rows, dtype=jnp.int32) * block_rows

    def allowed_at(block_start):
        rows_here = block_start + jnp.arange(block_rows, dtype=jnp.int32)
        segment_here = lax.dynamic_slice_in_dim(segment, block_start, block_rows, 0)
        return (segment_here[:, None] == segment[None, :]) & (
            (key_mask[None, :] == 1) | (rows_here[:, None] == places[None, :])
        )

    def scores_at(block_start):
        query_rows = lax.dynamic_slice_in_dim(query_rot, block_start, block_rows, 0)
        scores = (
            jnp.einsum("qhd,khd->hqk", query_rows, key_rot, preferred_element_type=F32)
            * score_scale
        )
        return (query_rows, jnp.where(allowed_at(block_start)[None], scores, -1e30))

    def forward_block(block_start):
        query_rows, scores = scores_at(block_start)
        row_max = jnp.max(scores, axis=-1, keepdims=True)
        exp_terms = jnp.exp(scores - row_max)
        row_total = jnp.sum(exp_terms, axis=-1, keepdims=True)
        weights = (exp_terms / row_total).astype(BF16)
        attended = jnp.einsum("hqk,khd->qhd", weights, values_b, preferred_element_type=F32)
        return (attended, (row_max + jnp.log(row_total))[..., 0])

    attended_blocks, log_totals = lax.map(forward_block, starts)
    attended_b = attended_blocks.reshape(tok_count, width_local).astype(BF16)

    half = D // 2
    out_half = lax.dynamic_slice_in_dim(w_out_own, core * half, half, 0)
    out_half_all = gather_features(after(out_half, packed_all_b))
    other_half = lax.ppermute(out_half_all, "row", [(r, r ^ 1) for r in range(n_row)])
    first_core = core == 0
    w_out_all = jnp.concatenate(
        [
            jnp.where(first_core, out_half_all, other_half),
            jnp.where(first_core, other_half, out_half_all),
        ],
        axis=0,
    )
    attended_all = gather_features(after(attended_b, out_half_all))
    cot_all = gather_features(after(cot_b, attended_all))
    mixed_all = packed_all + contract_last(attended_all, w_out_all)
    scale_mid = lax.rsqrt(jnp.mean(mixed_all * mixed_all, axis=1, keepdims=True) + EPSILON)
    normed2 = (mixed_all * scale_mid * gains[1]).astype(BF16)
    column_start = col * feat_local
    mixed = lax.dynamic_slice_in_dim(mixed_all, column_start, feat_local, 1)

    logits = contract_last(router_all, normed2)
    top_logit = jnp.max(jnp.where(chosen, logits, -jnp.inf), axis=0, keepdims=True)
    raised = jnp.where(chosen, jnp.exp(logits - top_logit), 0.0)
    gate_probs = raised / jnp.sum(raised, axis=0, keepdims=True)
    own_probs = lax.dynamic_slice_in_dim(gate_probs, col * local_experts, local_experts, 0)

    def of_rows(table, e):
        if unit_split == 1:
            return table.reshape(n_row, per_device, *table.shape[1:])[:, e]
        return jnp.repeat(table, unit_split, axis=0)

    branch_back, grads_back, scalars_back, weight_grads = [], [], [], []
    for e in range(per_device):
        w_gate_e, w_up_e, w_down_e = experts[e]
        rows = swap_rows(plain_dot(picks[e], normed2, BF16).reshape(n_row, capacity, D))
        rows = rows.reshape(n_row * capacity, D)
        slot_gate = jnp.sum(jnp.where(hits[e], of_rows(own_probs, e)[:, None, :], 0.0), axis=2)
        slot_gate = swap_rows(slot_gate).reshape(n_row * capacity, 1)
        grad_rows = swap_rows(plain_dot(picks[e], cot_all, BF16).reshape(n_row, capacity, D))
        grad_rows = grad_rows.reshape(n_row * capacity, D)
        gate_pre = plain_dot(rows, w_gate_e)
        up_pre = plain_dot(rows, w_up_e)
        sigmoid_gate = jax.nn.sigmoid(gate_pre)
        silu_gate = gate_pre * sigmoid_gate
        activation = silu_gate * up_pre
        scaled_activation = (slot_gate * activation).astype(BF16)
        grad_unscaled = plain_dot(grad_rows, w_down_e)
        grad_gate = jnp.sum(activation * grad_unscaled, axis=1)
        grad_activation = slot_gate * grad_unscaled
        grad_gate_pre = (
            grad_activation * up_pre * sigmoid_gate * (1.0 + gate_pre * (1.0 - sigmoid_gate))
        ).astype(BF16)
        grad_up_pre = (grad_activation * silu_gate).astype(BF16)
        inner = jnp.sum(
            grad_gate_pre.astype(F32) * gate_pre + grad_up_pre.astype(F32) * up_pre, axis=1
        )
        scalars = jnp.stack([grad_gate, inner]).reshape(2, n_row, capacity).transpose(1, 0, 2)
        scalars_back.append(swap_rows(scalars))
        grad_slot_rows = (
            contract_last(grad_gate_pre, w_gate_e) + contract_last(grad_up_pre, w_up_e)
        ).astype(BF16)
        grads_back.append(swap_rows(grad_slot_rows.reshape(n_row, capacity, D)))
        expert_out = contract_last(scaled_activation, w_down_e, BF16)
        branch_back.append(swap_rows(expert_out.reshape(n_row, capacity, D)))
        weight_grads.append(
            (
                contract_first(rows, grad_gate_pre, BF16),
                contract_first(rows, grad_up_pre, BF16),
                contract_first(grad_rows, scaled_activation, BF16),
            )
        )

    def to_tokens(back):
        total = 0.0
        for e in range(per_device):
            total = total + contract_first(picks[e], back[e].reshape(n_row * capacity, D))
        return total.astype(BF16)

    grad_normed2 = scatter_partial(to_tokens(grads_back)).astype(F32)

    def of_experts(e, which):
        spread = jnp.where(hits[e], scalars_back[e][:, which, :, None], 0.0)
        return jnp.sum(spread, axis=1)

    def over_experts(which):
        table = jnp.stack([of_experts(e, which) for e in range(per_device)], axis=1)
        if unit_split == 1:
            return table.reshape(local_experts, tok_count)
        return jnp.sum(table.reshape(local_experts, unit_split, tok_count), axis=1)

    small = jnp.concatenate([over_experts(0), jnp.sum(over_experts(1), axis=0)[None]], axis=0)
    small = lax.all_gather(small, "col", axis=0)
    grad_gates = small[:, :local_experts].reshape(E, tok_count)
    grad_logits = gate_probs * (
        grad_gates - jnp.sum(gate_probs * grad_gates, axis=0, keepdims=True)
    )
    grad_logits = grad_logits.astype(BF16)
    inner_mid = jnp.sum(small[:, local_experts], axis=0) + jnp.sum(
        grad_logits.astype(F32) * logits, axis=0
    )
    inner_mid = (inner_mid / D)[:, None]
    grad_router = plain_dot(grad_logits, normed2)
    router_local = lax.dynamic_slice_in_dim(router_all, column_start, feat_local, 1)
    grad_unit_mid = grad_normed2 + contract_first(grad_logits, router_local)
    unit_mid = mixed * scale_mid
    grad_norm2 = jnp.sum(grad_unit_mid * unit_mid, axis=0)
    scaled_mid = grad_unit_mid * norm2_gain
    grad_mixed = cot_b.astype(F32) + scale_mid * (scaled_mid - unit_mid * inner_mid)
    grad_branch = gather_features(grad_mixed.astype(BF16))

    combined = scatter_partial(after(to_tokens(branch_back), grad_branch))
    output = (mixed + combined.astype(F32)).astype(BF16)[inverse]

    grad_w_out = contract_first(grad_branch, attended_b, BF16)
    grad_attended = plain_dot(grad_branch, w_out_own, BF16).reshape(tok_count, head_count, DH)

    def backward_block(carried, inputs):
        grad_keys, grad_values = carried
        block_start, log_total = inputs
        query_rows, scores = scores_at(block_start)
        prob_rows = jnp.exp(scores - log_total[..., None])
        grad_out_rows = lax.dynamic_slice_in_dim(grad_attended, block_start, block_rows, 0)
        grad_values = grad_values + jnp.einsum(
            "hqk,qhd->khd", prob_rows.astype(BF16), grad_out_rows, preferred_element_type=F32
        )
        grad_probs = jnp.einsum(
            "qhd,khd->hqk", grad_out_rows, values_b, preferred_element_type=F32
        )
        grad_scores = (
            prob_rows * (grad_probs - jnp.sum(prob_rows * grad_probs, axis=-1, keepdims=True))
        ).astype(BF16)
        grad_query_rows = (
            jnp.einsum("hqk,khd->qhd", grad_scores, key_rot, preferred_element_type=F32)
            * score_scale
        )
        grad_keys = (
            grad_keys
            + jnp.einsum("hqk,qhd->khd", grad_scores, query_rows, preferred_element_type=F32)
            * score_scale
        )
        return ((grad_keys, grad_values), grad_query_rows)

    zero_heads = jnp.zeros((tok_count, head_count, DH), F32)
    (grad_key_rot, grad_values), grad_query_rot = lax.scan(
        backward_block, (zero_heads, zero_heads), (starts, log_totals)
    )
    grad_queries, grad_query_gain = query_pull(grad_query_rot.reshape(tok_count, head_count, DH))
    grad_keys_raw, grad_key_gain = key_pull(grad_key_rot)
    grad_qkv = jnp.concatenate(
        [
            grad.reshape(tok_count, width_local).astype(BF16)
            for grad in (grad_queries, grad_keys_raw, grad_values)
        ],
        axis=1,
    )
    grad_normed1_part = contract_last(grad_qkv, w_qkv, BF16)
    grad_unit_in = scatter_partial(grad_normed1_part).astype(F32)
    inner_in = lax.psum(jnp.sum(grad_qkv.astype(F32) * qkv, axis=1), "col")[:, None] / D
    packed = packed_b.astype(F32)
    unit_in = packed * scale_in
    grad_norm1 = jnp.sum(grad_normed1_part.astype(F32) * (packed_all * scale_in), axis=0)
    scaled_in = grad_unit_in * norm1_gain
    grad_input = (grad_mixed + scale_in * (scaled_in - unit_in * inner_in))[inverse]

    grad_heads = jnp.concatenate(
        [contract_first(normed1, grad_qkv, BF16), grad_w_out], axis=1
    ).reshape(n_row, D // n_row, 4 * width_local)
    grad_heads = jnp.sum(swap_rows(grad_heads).astype(F32), axis=0)
    grad_w_query, grad_w_key, grad_w_value, grad_w_out = (
        grad_heads[:, i * width_local : (i + 1) * width_local] for i in range(4)
    )
    grad_router = grad_router.reshape(E, n_row, D // n_row).transpose(1, 0, 2)
    grad_router = jnp.sum(swap_rows(grad_router), axis=0)

    def to_rows(which):
        parts = []
        for e in range(per_device):
            grad = weight_grads[e][which].reshape(n_row, D // n_row, hidden_units // unit_split)
            parts.append(swap_rows(grad).astype(F32))
        if unit_split == 1:
            return jnp.stack(parts, axis=1).reshape(local_experts, D // n_row, hidden_units)
        grad = parts[0].reshape(local_experts, unit_split, D // n_row, -1)
        return grad.transpose(0, 2, 1, 3).reshape(local_experts, D // n_row, hidden_units)

    grad_w_gate, grad_w_up, grad_w_down = (to_rows(which) for which in range(3))

    vectors = jnp.concatenate(
        [
            grad_norm1,
            lax.dynamic_update_slice_in_dim(jnp.zeros((D,), F32), grad_norm2, column_start, 0),
            grad_query_gain,
            grad_key_gain,
        ]
    )
    vectors = lax.psum(vectors, ("row", "col"))
    grad_norm1 = lax.dynamic_slice_in_dim(vectors, column_start, feat_local, 0)
    grad_norm2 = lax.dynamic_slice_in_dim(vectors, D + column_start, feat_local, 0)
    grad_query_gain = vectors[2 * D : 2 * D + DH]
    grad_key_gain = vectors[2 * D + DH :]
    return (
        output,
        grad_input,
        grad_norm1,
        grad_query_gain,
        grad_key_gain,
        grad_w_query,
        grad_w_key,
        grad_w_value,
        grad_w_out,
        grad_norm2,
        grad_router,
        grad_w_gate,
        grad_w_up,
        grad_w_down,
    )


def solution(mesh):
    return jax.shard_map(
        body,
        mesh=mesh,
        in_specs=(
            P("row", "col"),
            P("row", None),
            P("row", None),
            P("row"),
            P("row", None),
            P("col"),
            P(),
            P(),
            P("row", "col"),
            P("row", "col"),
            P("row", "col"),
            P("row", "col"),
            P("col"),
            P(None, "row"),
            P("col", "row", None),
            P("col", "row", None),
            P("col", "row", None),
            P("row", "col"),
        ),
        out_specs=(
            P("row", "col"),
            P("row", "col"),
            P("col"),
            P(),
            P(),
            P("row", "col"),
            P("row", "col"),
            P("row", "col"),
            P("row", "col"),
            P("col"),
            P(None, "row"),
            P("col", "row", None),
            P("col", "row", None),
            P("col", "row", None),
        ),
        check_vma=False,
    )
```

time: 3840 us -> 1750 us (0.46)
  waiting for transfers between devices: 2800 us -> 777 us
  local copies, waits for them, and re-layouts: 282 us -> 135 us
  starting transfers between devices: 1.91 us -> 129 us
  other arithmetic: 155 us -> 115 us
    reduce_scatter x8 -> x0, waiting for transfers between devices: 1510 us -> none  [the longest x1 456 us: body(): lax.psum_scatter(grad_w_gate, 'row', scatter_dimension=1, tiled=True)]
    all_to_all x0 -> x27, waiting for transfers between devices: none -> 563 us  [swap_rows(): return lax.all_to_all(pieces, 'row', 0, 0, tiled=True)]
    reduce_scatter x4 -> x3, waiting for transfers between devices: 578 us -> 67.7 us  [scatter_partial(): lax.psum_scatter(partial_rows, 'col', scatter_dimension=1, tiled=True)]
    all_gather x7 -> x0, waiting for transfers between devices: 436 us -> none  [the longest x1 176 us: body(): lax.all_gather(w_up, 'row', axis=1, tiled=True)]
    gather x12 -> x3, local copies, waits for them, and re-layouts: 166 us -> 16.1 us  [the longest x1 5.37 us: body(): packed_b = hidden_in[order_row]]
    dot_general x29, matrix products: 303 us -> 169 us  [the longest x14 120 us: plain_dot(): return jnp.dot(left_op, right_op, preferred_element_type=F32).astype(kind)]
    all_gather x4 -> x5, waiting for transfers between devices: 278 us -> 146 us  [gather_features(): return lax.all_gather(local_rows, 'col', axis=1, tiled=True)]
    all_to_all x0 -> x27, starting transfers between devices: none -> 127 us  [swap_rows(): return lax.all_to_all(pieces, 'row', 0, 0, tiled=True)]
  transfers between devices with their start and end apart: 23 -> 36, of which waited for: 20 -> 26; matrix products, arithmetic and copies ran while one was open for 14% -> 32% of each run, Pallas kernels for 0% -> 0%
where the time goes in v1:
time: 1750 us; the launch traced here: 1730 us
  waiting for transfers between devices  777 us (44%)
  matrix products  386 us (22%)
  blocking collectives  163 us (9%)
  local copies, waits for them, and re-layouts  135 us (8%)
  starting transfers between devices  129 us (7%)
  other arithmetic  115 us (7%)
    all_to_all x27, waiting for transfers between devices, swap_rows(): return lax.all_to_all(pieces, 'row', 0, 0, tiled=True)  563 us
    all_gather x5, waiting for transfers between devices, gather_features(): return lax.all_gather(local_rows, 'col', axis=1, tiled=True)  146 us
    all_to_all x27, starting transfers between devices, swap_rows(): return lax.all_to_all(pieces, 'row', 0, 0, tiled=True)  127 us
    dot_general x14, matrix products, plain_dot(): return jnp.dot(left_op, right_op, preferred_element_type=F32).astype(kind)  120 us
    dot_general x13, matrix products, contract_first(): lax.dot_general(left_op, right_op, (((0,), (0,)), ((), ())), preferred_el...  111 us
    dot_general x9, matrix products, contract_last(): lax.dot_general(left_op, right_op, (((1,), (1,)), ((), ())), preferred_el...  88.3 us
    reduce_scatter x3, waiting for transfers between devices, scatter_partial(): lax.psum_scatter(partial_rows, 'col', scatter_dimension=1, tiled=True)  67.7 us
    all_gather x1, blocking collectives, body(): router_all = lax.all_gather(router, 'row', axis=1, tiled=True)  42.3 us
  transfers between devices with their start and end apart: 36, of which 26 were waited for; matrix products, arithmetic and copies ran while one was open for 32% of the time, Pallas kernels for 0%

profile of v1, /device:TPU:0, one launch (start us, length us, event | category | flops | bytes accessed | tf_op | source)
XLA Modules:
  0.0 1732.5 jit_solution(4854338868310501398)
XLA Ops:
  22.2 28.2 %all_gather.28 = f32[2,2048]{1,0:T(2,128)S(1)} all-gather(f32[2,256]{1,0:T(2,128)S(1)} %pad_maximum_fusion.7), channel_id=1, replica_groups=mesh['row'=4,'col'=8] {'col'}, dimensions={1}, use_global_device_ids=true | all-gather | bytes 18432 | tf_op jit(solution)/shard_map/all_gather | solution.py:143
  55.5 15.2 all-to-all-done
  72.9 44.3 %all-gather.17.cloned.1.call-done = bf16[1536,2048]{1,0:T(8,128)(2,1)} async-done(((bf16[1536,256]{1,0:T(8,128)(2,1)}), bf16[1536,2048]{1,0:T(8,128)(2,1)}) %all-gather.17.cloned.1.call-update) | async-done | bytes 6291472 | tf_op jit(solution)/shard_map/all_gather | solution.py:52
  144.8 40.4 %while.28 = (s32[]{:T(128)}, bf16[3,512,2,128]{3,1,2,0:T(8,128)(2,1)S(1)}, f32[3,2,512]{2,1,0:T(2,128)}, s32[3]{0:T(128)S(1)}, s32[1536]{0:T(1024)S(1)}, /*index...) while((s32[]{:T(128)}, ...), condition=%wide.region_9.10_spmd.clone, body=%wide.region_6.9_spmd.clone.sunk | while | flops 827327488 | bytes 24437952 | solution.py:212
  187.9 25.5 %all-gather.9.cloned.1.call-done = bf16[1024,2048]{1,0:T(8,128)(2,1)} async-done(((bf16[1024,256]{1,0:T(8,128)(2,1)}), bf16[1024,2048]{1,0:T(8,128)(2,1)}) %all-gather.9.cloned.1.call-update) | async-done | bytes 4194320 | tf_op jit(solution)/shard_map/all_gather | solution.py:52
  230.4 42.2 %all-to-all-done.4 = bf16[4,512,1024]{2,1,0:T(8,128)(2,1)} async-done(((bf16[4,512,1024]{2,1,0:T(8,128)(2,1)}), bf16[4,512,1024]{2,1,0:T(8,128)(2,1)}, u32[]{:S(2)}, u32[]{:S(2)}) %all-to-all-start.4) | async-done | bytes 4194336 | tf_op jit(solution)/shard_map/all_to_all | solution.py:60
  284.0 41.7 %all-to-all-done.3 = bf16[4,512,1024]{2,1,0:T(8,128)(2,1)} async-done(((bf16[4,512,1024]{2,1,0:T(8,128)(2,1)}), bf16[4,512,1024]{2,1,0:T(8,128)(2,1)}, u32[]{:S(2)}, u32[]{:S(2)}) %all-to-all-start.3) | async-done | bytes 4194336 | tf_op jit(solution)/shard_map/all_to_all | solution.py:60
  338.9 42.3 %all_gather.31 = bf16[64,2048]{1,0:T(8,128)(2,1)S(1)} all-gather(bf16[64,512]{1,0:T(8,128)(2,1)S(1)} %copy-done.67), channel_id=1, replica_groups=mesh['row'=4,'col'=8] {'row'}, dimensions={1}, use_global_device_ids=true | all-gather | bytes 327680 | tf_op jit(solution)/shard_map/all_gather | solution.py:144
  393.4 22.3 %multiply_reduce_fusion.1 = (f32[1536]{0:T(1024)S(1)}, f32[1536,2048]{1,0:T(8,128)}) fusion(bf16[1536,2048]{1,0:T(8,128)(2,1)} %all-gather.11.cloned.1.call-done, bf16[1024,2048]{1,0:T(8,128)(2,1)} %get-tuple-element.398, bf16[1024,2048]{1,0:T(8,128)(2,1)} %get-tuple-element.397, bf16[1536,2048]{1,0:T(8,128)(2,1)} %all-gather.17.cloned.1.call-done), kind=kOutput, calls=%fused_computation.67 | convolution fusion | flops 12914259968 | bytes 33560576 | tf_op jit(solution)/shard_map/dot_general | solution.py:64
  415.7 20.0 %all-to-all-done.10 = bf16[4,512,1024]{2,1,0:T(8,128)(2,1)} async-done(((bf16[4,512,1024]{2,1,0:T(8,128)(2,1)}), bf16[4,512,1024]{2,1,0:T(8,128)(2,1)}, u32[]{:S(2)}, u32[]{:S(2)}) %all-to-all-start.10) | async-done | bytes 4194336 | tf_op jit(solution)/shard_map/all_to_all | solution.py:60
  457.4 31.8 %all-to-all-done.9 = bf16[4,512,1024]{2,1,0:T(8,128)(2,1)} async-done(((bf16[4,512,1024]{2,1,0:T(8,128)(2,1)}), bf16[4,512,1024]{2,1,0:T(8,128)(2,1)}, u32[]{:S(2)}, u32[]{:S(2)}) %all-to-all-start.9) | async-done | bytes 4194336 | tf_op jit(solution)/shard_map/all_to_all | solution.py:60
  499.4 10.5 convolution_convert_fusion.10
  514.8 10.5 convolution_convert_fusion.9
  525.3 34.9 %all-to-all-done.2 = bf16[4,240,2048]{2,1,0:T(8,128)(2,1)} async-done(((bf16[4,240,2048]{2,1,0:T(8,128)(2,1)}), bf16[4,240,2048]{2,1,0:T(8,128)(2,1)}, u32[]{:S(2)}, u32[]{:S(2)}) %all-to-all-start.2) | async-done | bytes 3932192 | tf_op jit(solution)/shard_map/all_to_all | solution.py:60
  575.1 35.7 %all-to-all-done.8 = bf16[4,240,2048]{2,1,0:T(8,128)(2,1)} async-done(((bf16[4,240,2048]{2,1,0:T(8,128)(2,1)}), bf16[4,240,2048]{2,1,0:T(8,128)(2,1)}, u32[]{:S(2)}, u32[]{:S(2)}) %all-to-all-start.8) | async-done | bytes 3932192 | tf_op jit(solution)/shard_map/all_to_all | solution.py:60
  634.6 10.6 convolution_convert_fusion.8
  645.3 18.6 %all-to-all-done.11 = bf16[4,512,1024]{2,1,0:T(8,128)(2,1)} async-done(((bf16[4,512,1024]{2,1,0:T(8,128)(2,1)}), bf16[4,512,1024]{2,1,0:T(8,128)(2,1)}, u32[]{:S(2)}, u32[]{:S(2)}) %all-to-all-start.11) | async-done | bytes 4194336 | tf_op jit(solution)/shard_map/all_to_all | solution.py:60
  678.4 10.5 convolution_convert_fusion.7
  688.9 25.4 %all-to-all-done.13 = bf16[4,240,2048]{2,1,0:T(8,128)(2,1)} async-done(((bf16[4,240,2048]{2,1,0:T(8,128)(2,1)}), bf16[4,240,2048]{2,1,0:T(8,128)(2,1)}, u32[]{:S(2)}, u32[]{:S(2)}) %all-to-all-start.13) | async-done | bytes 3932192 | tf_op jit(solution)/shard_map/all_to_all | solution.py:60
  719.3 12.3 multiply_reduce_fusion.4
  747.3 17.4 %all-to-all-done.15 = bf16[4,240,2048]{2,1,0:T(8,128)(2,1)} async-done(((bf16[4,240,2048]{2,1,0:T(8,128)(2,1)}), bf16[4,240,2048]{2,1,0:T(8,128)(2,1)}, u32[]{:S(2)}, u32[]{:S(2)}) %all-to-all-start.15) | async-done | bytes 3932192 | tf_op jit(solution)/shard_map/all_to_all | solution.py:60
  769.8 12.4 multiply_reduce_fusion.3
  797.9 17.4 %all-to-all-done.14 = bf16[4,240,2048]{2,1,0:T(8,128)(2,1)} async-done(((bf16[4,240,2048]{2,1,0:T(8,128)(2,1)}), bf16[4,240,2048]{2,1,0:T(8,128)(2,1)}, u32[]{:S(2)}, u32[]{:S(2)}) %all-to-all-start.14) | async-done | bytes 3932192 | tf_op jit(solution)/shard_map/all_to_all | solution.py:60
  820.7 11.4 fusion.50
  832.1 33.5 %all-to-all-done.16 = bf16[4,240,2048]{2,1,0:T(8,128)(2,1)} async-done(((bf16[4,240,2048]{2,1,0:T(8,128)(2,1)}), bf16[4,240,2048]{2,1,0:T(8,128)(2,1)}, u32[]{:S(2)}, u32[]{:S(2)}) %all-to-all-start.16) | async-done | bytes 3932192 | tf_op jit(solution)/shard_map/all_to_all | solution.py:60
  865.6 12.6 fusion.44
  897.0 35.5 %all-gather.2 = f32[8,9,1536]{2,1,0:T(8,128)S(1)} all-gather(f32[1,9,1536]{2,1,0:T(8,128)S(1)} %maximum_bitcast_fusion), channel_id=3, replica_groups=mesh['row'=4,'col'=8] {'col'}, dimensions={0}, use_global_device_ids=true | all-gather | bytes 497664 | tf_op jit(solution)/shard_map/all_gather | solution.py:306
  932.8 67.7 %reduce-scatter.4.cloned.1.call-done = bf16[1536,256]{1,0:T(8,128)(2,1)} async-done(((bf16[1536,2048]{1,0:T(8,128)(2,1)}), bf16[1536,256]{1,0:T(8,128)(2,1)}) %reduce-scatter.4.cloned.1.call-update) | async-done | bytes 786448 | tf_op jit(solution)/shard_map/reduce_scatter | solution.py:56
  1027.1 76.3 %all-gather.15.cloned.1.call-done = bf16[1536,2048]{1,0:T(8,128)(2,1)} async-done(((bf16[1536,256]{1,0:T(8,128)(2,1)}), bf16[1536,2048]{1,0:T(8,128)(2,1)}) %all-gather.15.cloned.1.call-update) | async-done | bytes 6291472 | tf_op jit(solution)/shard_map/all_gather | solution.py:52
  1115.0 70.3 %while.29 = (s32[]{:T(128)}, f32[1536,2,128]{0,2,1:T(8,128)}, f32[1536,2,128]{0,2,1:T(8,128)}, f32[3,512,2,128]{3,1,0,2:T(8,128)}, s32[3]{0:T(128)S(1)}, /*index...) while((s32[]{:T(128)}, f32[1536,2,128]{0,2,1:T(8,128)}, ...), condition=%wide.region_33.34_spmd.clone, body=%wide.region_31.33_spmd.clone.sunk | while | flops 2032665600 | bytes 109360416 | solution.py:358
  1211.0 12.5 fusion.42
  1233.3 11.3 all-to-all-done.12
  1257.9 39.9 %all-to-all-done.22 = bf16[4,512,1024]{2,1,0:T(8,128)(2,1)} async-done(((bf16[4,512,1024]{2,1,0:T(8,128)(2,1)}), bf16[4,512,1024]{2,1,0:T(8,128)(2,1)}, u32[]{:S(2)}, u32[]{:S(2)}) %all-to-all-start.22) | async-done | bytes 4194336 | tf_op jit(solution)/shard_map/all_to_all | solution.py:60
  1311.3 39.9 %all-to-all-done.21 = bf16[4,512,1024]{2,1,0:T(8,128)(2,1)} async-done(((bf16[4,512,1024]{2,1,0:T(8,128)(2,1)}), bf16[4,512,1024]{2,1,0:T(8,128)(2,1)}, u32[]{:S(2)}, u32[]{:S(2)}) %all-to-all-start.21) | async-done | bytes 4194336 | tf_op jit(solution)/shard_map/all_to_all | solution.py:60
  1364.5 11.4 fusion.51
  1375.9 28.6 %all-to-all-done.24 = bf16[4,512,1024]{2,1,0:T(8,128)(2,1)} async-done(((bf16[4,512,1024]{2,1,0:T(8,128)(2,1)}), bf16[4,512,1024]{2,1,0:T(8,128)(2,1)}, u32[]{:S(2)}, u32[]{:S(2)}) %all-to-all-start.24) | async-done | bytes 4194336 | tf_op jit(solution)/shard_map/all_to_all | solution.py:60
  1409.8 12.6 fusion.45
  1432.1 25.6 %all-to-all-done.23 = bf16[4,512,1024]{2,1,0:T(8,128)(2,1)} async-done(((bf16[4,512,1024]{2,1,0:T(8,128)(2,1)}), bf16[4,512,1024]{2,1,0:T(8,128)(2,1)}, u32[]{:S(2)}, u32[]{:S(2)}) %all-to-all-start.23) | async-done | bytes 4194336 | tf_op jit(solution)/shard_map/all_to_all | solution.py:60
  1471.0 40.0 %all-to-all-done.26 = bf16[4,512,1024]{2,1,0:T(8,128)(2,1)} async-done(((bf16[4,512,1024]{2,1,0:T(8,128)(2,1)}), bf16[4,512,1024]{2,1,0:T(8,128)(2,1)}, u32[]{:S(2)}, u32[]{:S(2)}) %all-to-all-start.26) | async-done | bytes 4194336 | tf_op jit(solution)/shard_map/all_to_all | solution.py:60
  1529.4 35.1 %all-to-all-done.25 = bf16[4,512,1024]{2,1,0:T(8,128)(2,1)} async-done(((bf16[4,512,1024]{2,1,0:T(8,128)(2,1)}), bf16[4,512,1024]{2,1,0:T(8,128)(2,1)}, u32[]{:S(2)}, u32[]{:S(2)}) %all-to-all-start.25) | async-done | bytes 4194336 | tf_op jit(solution)/shard_map/all_to_all | solution.py:60
  1576.9 10.7 maximum_convert_fusion
  1587.6 12.0 copy.111
  1599.6 10.7 maximum_convert_fusion.1
  1610.3 12.0 copy.112
  1622.3 10.4 maximum_convert_fusion.2
  1632.7 13.0 copy.113
  1646.6 18.9 %psum.14 = f32[1536]{0:T(1024)S(1)} all-reduce(f32[1536]{0:T(1024)S(1)} %multiply_reduce_fusion.2), channel_id=1, replica_groups=mesh['row'=4,'col'=8] {'col'}, use_global_device_ids=true, to_apply=%region_38.39 | all-reduce | flops 1536 | bytes 12288 | tf_op jit(solution)/shard_map/psum | solution.py:372
  1686.5 37.5 %psum.15 = f32[4352]{0:T(1024)S(1)} all-reduce(f32[4352]{0:T(1024)S(1)} %pad_maximum_fusion.6), channel_id=1, replica_groups=mesh['row'=4,'col'=8] {'row','col'}, use_global_device_ids=true, to_apply=%region_43.44 | all-reduce | flops 4352 | bytes 34816 | tf_op jit(solution)/shard_map/psum | solution.py:409
  (497 shorter events, 555.4 us)
Async XLA Ops:
  7.2 110.0 %all-gather.17.cloned.1.call-start = ((), (), s32[]{:S(2)}) async-start(), calls=%async_computation.37 | async-start | bytes 7077888 | tf_op jit(solution)/shard_map/all_gather | solution.py:52
  16.9 53.8 %all-to-all-start = ((bf16[4,512,1024]{2,1,0:T(8,128)(2,1)}), bf16[4,512,1024]{2,1,0:T(8,128)(2,1)}, u32[]{:S(2)}, u32[]{:S(2)}) async-start(bf16[4,512,1024]{2,1,0:T(8,128)(2,1)} %broadcast_in_dim.192), calls=%async_computation | async-start | bytes 8388608 | tf_op jit(solution)/shard_map/all_to_all | solution.py:60
  21.9 191.5 %all-gather.9.cloned.1.call-start = ((), (), s32[]{:S(2)}) async-start(), calls=%async_computation.30 | async-start | bytes 4718592 | tf_op jit(solution)/shard_map/all_gather | solution.py:52
  51.2 70.2 %copy-start.76 = (f32[1,2048]{1,0:T(1,128)}, f32[1,2048]{1,0:T(1,128)S(1)}, u32[]{:S(2)}) copy-start(f32[1,2048]{1,0:T(1,128)S(1)} %get-tuple-element.428) | copy-start | bytes 24580
  139.1 254.3 %all-gather.11.cloned.1.call-start = ((), (), s32[]{:S(2)}) async-start(), calls=%async_computation.31 | async-start | bytes 7077888 | tf_op jit(solution)/shard_map/all_gather | solution.py:52
  219.4 53.1 %all-to-all-start.4 = ((bf16[4,512,1024]{2,1,0:T(8,128)(2,1)}), bf16[4,512,1024]{2,1,0:T(8,128)(2,1)}, u32[]{:S(2)}, u32[]{:S(2)}) async-start(bf16[4,512,1024]{2,1,0:T(8,128)(2,1)} %get-tuple-element.396), calls=%async_computation.4 | async-start | bytes 8388608 | tf_op jit(solution)/shard_map/all_to_all | solution.py:60
  272.6 53.1 %all-to-all-start.3 = ((bf16[4,512,1024]{2,1,0:T(8,128)(2,1)}), bf16[4,512,1024]{2,1,0:T(8,128)(2,1)}, u32[]{:S(2)}, u32[]{:S(2)}) async-start(bf16[4,512,1024]{2,1,0:T(8,128)(2,1)} %get-tuple-element.394), calls=%async_computation.3 | async-start | bytes 8388608 | tf_op jit(solution)/shard_map/all_to_all | solution.py:60
  277.5 110.1 %collective-permute-start = (bf16[1024,2048]{1,0:T(8,128)(2,1)}, bf16[1024,2048]{1,0:T(8,128)(2,1)}, u32[]{:S(2)}, u32[]{:S(2)}) collective-permute-start(bf16[1024,2048]{1,0:T(8,128)(2,1)} %all-gather.9.cloned.1.call-done), channel_id=1, source_target_pairs={{0,8},{8,0},{16,24},{24,16},{1,9},{9,1},{17,25},{25,17},{2,10},{10... | collective-permute-start | bytes 12582920 | tf_op jit(solution)/shard_map/ppermute | solution.py:218
  325.7 56.9 %all-to-all-start.5 = ((bf16[4,512,1024]{2,1,0:T(8,128)(2,1)}), bf16[4,512,1024]{2,1,0:T(8,128)(2,1)}, u32[]{:S(2)}, u32[]{:S(2)}) async-start(bf16[4,512,1024]{2,1,0:T(8,128)(2,1)} %get-tuple-element.392), calls=%async_computation.5 | async-start | bytes 8388608 | tf_op jit(solution)/shard_map/all_to_all | solution.py:60
  331.8 160.6 %copy-start.43 = (s32[4,1,1536]{2,0,1:T(4,128)}, s32[4,1,1536]{2,0,1:T(4,128)S(1)}, u32[]{:S(2)}) copy-start(s32[4,1,1536]{2,0,1:T(4,128)S(1)} %copy.186) | copy-start | bytes 73732
  331.9 124.1 %copy-start.46 = (s32[4,1,1536]{2,0,1:T(4,128)}, s32[4,1,1536]{2,0,1:T(4,128)S(1)}, u32[]{:S(2)}) copy-start(s32[4,1,1536]{2,0,1:T(4,128)S(1)} %copy.188) | copy-start | bytes 73732
  381.3 68.2 %copy-start.39 = (bf16[64,2048]{1,0:T(8,128)(2,1)}, bf16[64,2048]{1,0:T(8,128)(2,1)S(1)}, u32[]{:S(2)}) copy-start(bf16[64,2048]{1,0:T(8,128)(2,1)S(1)} %all_gather.31) | copy-start | bytes 786436
  382.6 53.1 %all-to-all-start.10 = ((bf16[4,512,1024]{2,1,0:T(8,128)(2,1)}), bf16[4,512,1024]{2,1,0:T(8,128)(2,1)}, u32[]{:S(2)}, u32[]{:S(2)}) async-start(bf16[4,512,1024]{2,1,0:T(8,128)(2,1)} %get-tuple-element.395), calls=%async_computation.10 | async-start | bytes 8388608 | tf_op jit(solution)/shard_map/all_to_all | solution.py:60
  387.5 247.1 %all-gather.13.cloned.1.call-start = ((), (), s32[]{:S(2)}) async-start(), calls=%async_computation.32 | async-start | bytes 7077888 | tf_op jit(solution)/shard_map/all_gather | solution.py:52
  435.7 53.5 %all-to-all-start.9 = ((bf16[4,512,1024]{2,1,0:T(8,128)(2,1)}), bf16[4,512,1024]{2,1,0:T(8,128)(2,1)}, u32[]{:S(2)}, u32[]{:S(2)}) async-start(bf16[4,512,1024]{2,1,0:T(8,128)(2,1)} %get-tuple-element.393), calls=%async_computation.9 | async-start | bytes 8388608 | tf_op jit(solution)/shard_map/all_to_all | solution.py:60
  489.2 7.0 all-to-all-start.1
  496.2 13.8 all-to-all-start.7
  509.9 50.2 %all-to-all-start.2 = ((bf16[4,240,2048]{2,1,0:T(8,128)(2,1)}), bf16[4,240,2048]{2,1,0:T(8,128)(2,1)}, u32[]{:S(2)}, u32[]{:S(2)}) async-start(bf16[4,240,2048]{2,1,0:T(8,128)(2,1)} %bitcast.298), calls=%async_computation.2 | async-start | bytes 7864320 | tf_op jit(solution)/shard_map/all_to_all | solution.py:60
  560.2 50.6 %all-to-all-start.8 = ((bf16[4,240,2048]{2,1,0:T(8,128)(2,1)}), bf16[4,240,2048]{2,1,0:T(8,128)(2,1)}, u32[]{:S(2)}, u32[]{:S(2)}) async-start(bf16[4,240,2048]{2,1,0:T(8,128)(2,1)} %bitcast.295), calls=%async_computation.8 | async-start | bytes 7864320 | tf_op jit(solution)/shard_map/all_to_all | solution.py:60
  610.8 53.1 %all-to-all-start.11 = ((bf16[4,512,1024]{2,1,0:T(8,128)(2,1)}), bf16[4,512,1024]{2,1,0:T(8,128)(2,1)}, u32[]{:S(2)}, u32[]{:S(2)}) async-start(bf16[4,512,1024]{2,1,0:T(8,128)(2,1)} %get-tuple-element.391), calls=%async_computation.11 | async-start | bytes 8388608 | tf_op jit(solution)/shard_map/all_to_all | solution.py:60
  663.9 50.4 %all-to-all-start.13 = ((bf16[4,240,2048]{2,1,0:T(8,128)(2,1)}), bf16[4,240,2048]{2,1,0:T(8,128)(2,1)}, u32[]{:S(2)}, u32[]{:S(2)}) async-start(bf16[4,240,2048]{2,1,0:T(8,128)(2,1)} %bitcast.297), calls=%async_computation.13 | async-start | bytes 7864320 | tf_op jit(solution)/shard_map/all_to_all | solution.py:60
  714.3 50.4 %all-to-all-start.15 = ((bf16[4,240,2048]{2,1,0:T(8,128)(2,1)}), bf16[4,240,2048]{2,1,0:T(8,128)(2,1)}, u32[]{:S(2)}, u32[]{:S(2)}) async-start(bf16[4,240,2048]{2,1,0:T(8,128)(2,1)} %bitcast.293), calls=%async_computation.15 | async-start | bytes 7864320 | tf_op jit(solution)/shard_map/all_to_all | solution.py:60
  764.7 50.5 %all-to-all-start.14 = ((bf16[4,240,2048]{2,1,0:T(8,128)(2,1)}), bf16[4,240,2048]{2,1,0:T(8,128)(2,1)}, u32[]{:S(2)}, u32[]{:S(2)}) async-start(bf16[4,240,2048]{2,1,0:T(8,128)(2,1)} %bitcast.294), calls=%async_computation.14 | async-start | bytes 7864320 | tf_op jit(solution)/shard_map/all_to_all | solution.py:60
  815.2 50.4 %all-to-all-start.16 = ((bf16[4,240,2048]{2,1,0:T(8,128)(2,1)}), bf16[4,240,2048]{2,1,0:T(8,128)(2,1)}, u32[]{:S(2)}, u32[]{:S(2)}) async-start(bf16[4,240,2048]{2,1,0:T(8,128)(2,1)} %bitcast.296), calls=%async_computation.16 | async-start | bytes 7864320 | tf_op jit(solution)/shard_map/all_to_all | solution.py:60
  820.2 45.4 %copy-start.44 = (s32[4,1,1536]{2,0,1:T(4,128)S(1)}, s32[4,1,1536]{2,0,1:T(4,128)}, u32[]{:S(2)}) copy-start(s32[4,1,1536]{2,0,1:T(4,128)} %copy-done.43) | copy-start | bytes 73732
  820.2 180.3 %reduce-scatter.4.cloned.1.call-start = ((), (), s32[]{:S(2)}) async-start(), calls=%async_computation.33 | async-start | bytes 7077888 | tf_op jit(solution)/shard_map/reduce_scatter | solution.py:56
  878.2 54.4 %copy-start.24 = (f32[64,1536]{1,0:T(8,128)S(1)}, f32[64,1536]{1,0:T(8,128)}, u32[]{:S(2)}) copy-start(f32[64,1536]{1,0:T(8,128)} %copy-done.23) | copy-start | bytes 1179652
  878.2 54.5 %copy-start.22 = (f32[64,1536]{1,0:T(8,128)S(1)}, f32[64,1536]{1,0:T(8,128)}, u32[]{:S(2)}) copy-start(f32[64,1536]{1,0:T(8,128)} %copy-done.21) | copy-start | bytes 1179652
  878.2 122.3 %copy-start.15 = (bf16[1536,256]{1,0:T(8,128)(2,1)S(1)}, bf16[1536,256]{1,0:T(8,128)(2,1)}, u32[]{:S(2)}) copy-start(bf16[1536,256]{1,0:T(8,128)(2,1)} %gather_fusion.1) | copy-start | bytes 2359300
  878.2 122.3 %copy-start.59 = (f32[1536]{0:T(1024)S(1)}, f32[1536]{0:T(1024)}, u32[]{:S(2)}) copy-start(f32[1536]{0:T(1024)} %copy-done.58) | copy-start | bytes 18436
  878.2 122.3 %copy-start.73 = (f32[256]{0:T(256)S(1)}, f32[256]{0:T(256)}, u32[]{:S(2)}) copy-start(f32[256]{0:T(256)} %param.34) | copy-start | bytes 3076
  879.0 7.0 all-to-all-start.17
  886.1 7.0 all-to-all-start.18
  889.3 214.1 %all-gather.15.cloned.1.call-start = ((), (), s32[]{:S(2)}) async-start(), calls=%async_computation.34 | async-start | bytes 7077888 | tf_op jit(solution)/shard_map/all_gather | solution.py:52
  932.8 80.5 %copy-start.65 = (f32[1536]{0:T(1024)}, f32[1536]{0:T(1024)S(1)}, u32[]{:S(2)}) copy-start(f32[1536]{0:T(1024)S(1)} %add_multiply_fusion) | copy-start | bytes 18436
  1023.6 85.5 %all-to-all-start.20 = ((f32[4,64,512]{2,1,0:T(8,128)}), f32[4,64,512]{2,1,0:T(8,128)S(1)}, u32[]{:S(2)}, u32[]{:S(2)}) async-start(f32[4,64,512]{2,1,0:T(8,128)} %bitcast.229), calls=%async_computation.23 | async-start | bytes 1048576 | tf_op jit(solution)/shard_map/all_to_all | solution.py:60
  1109.9 84.4 %all-to-all-start.6 = ((bf16[4,240,2048]{2,1,0:T(8,128)(2,1)}), bf16[4,240,2048]{2,1,0:T(8,128)(2,1)}, u32[]{:S(2)}, u32[]{:S(2)}) async-start(bf16[4,240,2048]{2,1,0:T(8,128)(2,1)} %bitcast.292), calls=%async_computation.6 | async-start | bytes 7864320 | tf_op jit(solution)/shard_map/all_to_all | solution.py:60
  1194.4 50.3 %all-to-all-start.12 = ((bf16[4,240,2048]{2,1,0:T(8,128)(2,1)}), bf16[4,240,2048]{2,1,0:T(8,128)(2,1)}, u32[]{:S(2)}, u32[]{:S(2)}) async-start(bf16[4,240,2048]{2,1,0:T(8,128)(2,1)} %bitcast.291), calls=%async_computation.12 | async-start | bytes 7864320 | tf_op jit(solution)/shard_map/all_to_all | solution.py:60
  1199.2 473.7 %reduce-scatter.8.cloned.1.call-start = ((), (), s32[]{:S(2)}) async-start(), calls=%async_computation.36 | async-start | bytes 7077888 | tf_op jit(solution)/shard_map/reduce_scatter | solution.py:56
  1244.6 53.2 %all-to-all-start.22 = ((bf16[4,512,1024]{2,1,0:T(8,128)(2,1)}), bf16[4,512,1024]{2,1,0:T(8,128)(2,1)}, u32[]{:S(2)}, u32[]{:S(2)}) async-start(bf16[4,512,1024]{2,1,0:T(8,128)(2,1)} %bitcast.290), calls=%async_computation.25 | async-start | bytes 8388608 | tf_op jit(solution)/shard_map/all_to_all | solution.py:60
  1297.9 53.4 %all-to-all-start.21 = ((bf16[4,512,1024]{2,1,0:T(8,128)(2,1)}), bf16[4,512,1024]{2,1,0:T(8,128)(2,1)}, u32[]{:S(2)}, u32[]{:S(2)}) async-start(bf16[4,512,1024]{2,1,0:T(8,128)(2,1)} %bitcast.289), calls=%async_computation.24 | async-start | bytes 8388608 | tf_op jit(solution)/shard_map/all_to_all | solution.py:60
  1351.2 53.2 %all-to-all-start.24 = ((bf16[4,512,1024]{2,1,0:T(8,128)(2,1)}), bf16[4,512,1024]{2,1,0:T(8,128)(2,1)}, u32[]{:S(2)}, u32[]{:S(2)}) async-start(bf16[4,512,1024]{2,1,0:T(8,128)(2,1)} %bitcast.287), calls=%async_computation.27 | async-start | bytes 8388608 | tf_op jit(solution)/shard_map/all_to_all | solution.py:60
  1404.5 53.3 %all-to-all-start.23 = ((bf16[4,512,1024]{2,1,0:T(8,128)(2,1)}), bf16[4,512,1024]{2,1,0:T(8,128)(2,1)}, u32[]{:S(2)}, u32[]{:S(2)}) async-start(bf16[4,512,1024]{2,1,0:T(8,128)(2,1)} %bitcast.285), calls=%async_computation.26 | async-start | bytes 8388608 | tf_op jit(solution)/shard_map/all_to_all | solution.py:60
  1409.5 263.4 %reduce-scatter.6.cloned.1.call-start = ((), (), s32[]{:S(2)}) async-start(), calls=%async_computation.35 | async-start | bytes 7077888 | tf_op jit(solution)/shard_map/reduce_scatter | solution.py:56
  1457.7 53.2 %all-to-all-start.26 = ((bf16[4,512,1024]{2,1,0:T(8,128)(2,1)}), bf16[4,512,1024]{2,1,0:T(8,128)(2,1)}, u32[]{:S(2)}, u32[]{:S(2)}) async-start(bf16[4,512,1024]{2,1,0:T(8,128)(2,1)} %bitcast.288), calls=%async_computation.29 | async-start | bytes 8388608 | tf_op jit(solution)/shard_map/all_to_all | solution.py:60
  1510.9 53.6 %all-to-all-start.25 = ((bf16[4,512,1024]{2,1,0:T(8,128)(2,1)}), bf16[4,512,1024]{2,1,0:T(8,128)(2,1)}, u32[]{:S(2)}, u32[]{:S(2)}) async-start(bf16[4,512,1024]{2,1,0:T(8,128)(2,1)} %bitcast.286), calls=%async_computation.28 | async-start | bytes 8388608 | tf_op jit(solution)/shard_map/all_to_all | solution.py:60
  1564.6 101.0 %all-to-all-start.19 = ((bf16[4,512,1024]{1,2,0:T(8,128)(2,1)}), bf16[4,512,1024]{1,2,0:T(8,128)(2,1)}, u32[]{:S(2)}, u32[]{:S(2)}) async-start(bf16[4,512,1024]{1,2,0:T(8,128)(2,1)} %bitcast.275), calls=%async_computation.22 | async-start | bytes 8388608 | tf_op jit(solution)/shard_map/all_to_all | solution.py:60
  1681.6 43.5 %copy-start.1 = (bf16[1536,256]{1,0:T(8,128)(2,1)S(1)}, bf16[1536,256]{1,0:T(8,128)(2,1)}, u32[]{:S(2)}) copy-start(bf16[1536,256]{1,0:T(8,128)(2,1)} %param.22) | copy-start | bytes 2359300
  (98 other events, 615.9 us)
Sparse Core Ops, SparseCore 0:
  14.2 102.9 all-gather.16
  139.2 74.0 all-gather.8
  216.0 97.2 all-gather.10
  393.5 97.6 all-gather.12
  878.4 122.0 reduce-scatter.3
  1004.3 99.0 all-gather.14
  1223.7 117.0 reduce-scatter.7
  1422.5 117.0 reduce-scatter.5

commit v2 on v1

v2 whole, which is shorter than its diff:
```python
import jax
import jax.numpy as jnp
from jax import lax
from jax.experimental import pallas as pl
from jax.experimental.pallas import tpu as pltpu
from jax.sharding import PartitionSpec as P

D = 2048
DH = 128
E = 64
TOP = 8


EPSILON = 1e-06
ROPE_BASE = 10000.0
BF16 = jnp.bfloat16
F32 = jnp.float32


def layout(seq_lengths, tok_count):
    seq_ends = jnp.cumsum(seq_lengths)
    seq_starts = seq_ends - seq_lengths
    places = jnp.arange(tok_count, dtype=jnp.int32)
    segment = jnp.sum((places[:, None] >= seq_ends[None, :]).astype(jnp.int32), axis=1)
    member = segment[:, None] == jnp.arange(seq_lengths.shape[0], dtype=jnp.int32)[None, :]
    offset = jnp.sum(jnp.where(member, seq_starts[None, :], 0), axis=1)
    return (segment, places - offset)


def rope_tables(position):
    half_dim = DH // 2
    frequency = ROPE_BASE ** (-2.0 * jnp.arange(half_dim, dtype=F32) / DH)
    angles = position.astype(F32)[:, None] * frequency[None, :]
    cosine, sine = jnp.cos(angles), jnp.sin(angles)
    return jnp.concatenate([cosine, cosine], 1), jnp.concatenate([-sine, sine], 1)


def gather_features(local_rows):
    return lax.all_gather(local_rows, "col", axis=1, tiled=True)


def scatter_partial(partial_rows):
    return lax.psum_scatter(partial_rows, "col", scatter_dimension=1, tiled=True)


def trade(value, step, n_row):
    if step == 0:
        return value
    return lax.ppermute(value, "row", [(r, r ^ step) for r in range(n_row)])


def trade_all(pieces):
    return [trade(piece, step, len(pieces)) for step, piece in enumerate(pieces)]


def contract_last(left_op, right_op, kind=F32):
    return lax.dot_general(
        left_op, right_op, (((1,), (1,)), ((), ())), preferred_element_type=F32
    ).astype(kind)


def contract_first(left_op, right_op, kind=F32):
    return lax.dot_general(
        left_op, right_op, (((0,), (0,)), ((), ())), preferred_element_type=F32
    ).astype(kind)


def plain_dot(left_op, right_op, kind=F32):
    return jnp.dot(left_op, right_op, preferred_element_type=F32).astype(kind)


def after(value, *earlier):
    return lax.optimization_barrier((value, *earlier))[0]


def thirds(values):
    high = lax.reduce_precision(values, 8, 7)
    middle = lax.reduce_precision(values - high, 8, 7)
    return jnp.stack([high, middle, values - high - middle]).astype(BF16)


def cost(flops, moved):
    return pl.CostEstimate(flops=flops, bytes_accessed=moved, transcendentals=0)


def rope(values, cosine, sine):
    return values * cosine + pltpu.roll(values, DH // 2, 1) * sine


def rope_back(grad, cosine, sine):
    return grad * cosine + pltpu.roll(grad * sine, DH // 2, 1)


def project_kernel(x_ref, gain_ref, w_ref, qg_ref, kg_ref, cos_ref, sin_ref, *outs):
    normed_ref, scale_ref, raw_ref, q_ref, k_ref, v_ref = outs
    x = x_ref[...].astype(F32)
    scale = lax.rsqrt(jnp.mean(x * x, axis=1, keepdims=True) + EPSILON)
    normed = (x * scale * gain_ref[...]).astype(BF16)
    normed_ref[...] = normed
    scale_ref[...] = scale
    width = q_ref.shape[1]
    qkv = jnp.dot(normed, w_ref[:, : 3 * width], preferred_element_type=F32)
    raw_ref[...] = qkv[:, : 2 * width]
    v_ref[...] = qkv[:, 2 * width :].astype(BF16)
    cosine, sine = cos_ref[...], sin_ref[...]
    for part, gain, out in ((0, qg_ref, q_ref), (1, kg_ref, k_ref)):
        for h in range(width // DH):
            head = qkv[:, part * width + h * DH : part * width + (h + 1) * DH]
            size = lax.rsqrt(jnp.mean(head * head, axis=1, keepdims=True) + EPSILON)
            out[:, h * DH : (h + 1) * DH] = rope(head * size * gain[...], cosine, sine).astype(BF16)


def project(x, gain, w, q_gain, k_gain, cosine, sine, width, block=256):
    rows = cosine.shape[0]
    by_rows = lambda n: pl.BlockSpec((block, n), lambda i: (i, 0))
    whole = lambda a: pl.BlockSpec(a.shape, lambda i: (0, 0))
    return pl.pallas_call(
        project_kernel,
        name="project",
        grid=(rows // block,),
        in_specs=[
            by_rows(D),
            whole(gain),
            whole(w),
            whole(q_gain),
            whole(k_gain),
            by_rows(DH),
            by_rows(DH),
        ],
        out_specs=[by_rows(n) for n in (D, 1, 2 * width, width, width, width)],
        out_shape=[
            jax.ShapeDtypeStruct((rows, D), BF16),
            jax.ShapeDtypeStruct((rows, 1), F32),
            jax.ShapeDtypeStruct((rows, 2 * width), F32),
            jax.ShapeDtypeStruct((rows, width), BF16),
            jax.ShapeDtypeStruct((rows, width), BF16),
            jax.ShapeDtypeStruct((rows, width), BF16),
        ],
        cost_estimate=cost(1000, 1000),
    )(x, gain, w, q_gain, k_gain, cosine, sine)


def masked_scores(q, k, seg_q, seg_k, first):
    scores = lax.dot_general(q, k, (((1,), (1,)), ((), ())), preferred_element_type=F32)
    rows = first + lax.broadcasted_iota(jnp.int32, scores.shape, 0)
    columns = lax.broadcasted_iota(jnp.int32, scores.shape, 1)
    allowed = (seg_q == seg_k) | (rows == columns)
    return jnp.where(allowed, scores * DH ** (-0.5), -1e30)


def attend_kernel(q_ref, k_ref, v_ref, seg_q_ref, seg_k_ref, out_ref, log_ref):
    first = pl.program_id(1) * q_ref.shape[0]
    scores = masked_scores(q_ref[...], k_ref[...], seg_q_ref[...], seg_k_ref[...], first)
    top = jnp.max(scores, axis=1, keepdims=True)
    terms = jnp.exp(scores - top)
    total = jnp.sum(terms, axis=1, keepdims=True)
    weights = (terms * (1.0 / total)).astype(BF16)
    out_ref[...] = jnp.dot(weights, v_ref[...], preferred_element_type=F32).astype(BF16)
    log_ref[0] = top + jnp.log(total)


def attend(q, k, v, seg_q, seg_k, block=256):
    rows, width = q.shape
    heads = width // DH
    by_rows = pl.BlockSpec((block, DH), lambda h, i: (i, h))
    whole = pl.BlockSpec((rows, DH), lambda h, i: (0, h))
    return pl.pallas_call(
        attend_kernel,
        name="attend",
        grid=(heads, rows // block),
        in_specs=[
            by_rows,
            whole,
            whole,
            pl.BlockSpec((block, 1), lambda h, i: (i, 0)),
            pl.BlockSpec((1, rows), lambda h, i: (0, 0)),
        ],
        out_specs=[by_rows, pl.BlockSpec((1, block, 1), lambda h, i: (h, i, 0))],
        out_shape=[
            jax.ShapeDtypeStruct((rows, width), BF16),
            jax.ShapeDtypeStruct((heads, rows, 1), F32),
        ],
        cost_estimate=cost(1000, 1000),
    )(q, k, v, seg_q, seg_k)


def head_back(grad, raw, gain, cosine, sine):
    grad = rope_back(grad, cosine, sine)
    size = lax.rsqrt(jnp.mean(raw * raw, axis=1, keepdims=True) + EPSILON)
    unit = raw * size
    grad_gain = jnp.sum(grad * unit, axis=0, keepdims=True)
    grad = grad * gain
    return size * (grad - unit * jnp.mean(grad * unit, axis=1, keepdims=True)), grad_gain


def attend_back_kernel(
    q_ref, k_ref, v_ref, grad_ref, log_ref, seg_q_ref, seg_k_ref, raw_q_ref, raw_k_ref,
    qg_ref, kg_ref, cos_q_ref, sin_q_ref, cos_ref, sin_ref,
    dq_ref, dk_ref, dv_ref, dqg_ref, dkg_ref, sum_k, sum_v,
):
    head, i = pl.program_id(0), pl.program_id(1)

    @pl.when((head == 0) & (i == 0))
    def _():
        dqg_ref[...] = jnp.zeros_like(dqg_ref)
        dkg_ref[...] = jnp.zeros_like(dkg_ref)

    @pl.when(i == 0)
    def _():
        sum_k[...] = jnp.zeros_like(sum_k)
        sum_v[...] = jnp.zeros_like(sum_v)

    q, k, grad = q_ref[...], k_ref[...], grad_ref[...]
    scores = masked_scores(q, k, seg_q_ref[...], seg_k_ref[...], i * q.shape[0])
    probs = jnp.exp(scores - log_ref[0])
    sum_v[...] += lax.dot_general(
        probs.astype(BF16), grad, (((0,), (0,)), ((), ())), preferred_element_type=F32
    )
    grad_probs = lax.dot_general(
        grad, v_ref[...], (((1,), (1,)), ((), ())), preferred_element_type=F32
    )
    inner = jnp.sum(probs * grad_probs, axis=1, keepdims=True)
    grad_scores = (probs * (grad_probs - inner)).astype(BF16)
    sum_k[...] += lax.dot_general(
        grad_scores, q, (((0,), (0,)), ((), ())), preferred_element_type=F32
    )
    grad_q = jnp.dot(grad_scores, k, preferred_element_type=F32) * DH ** (-0.5)
    grad_q, grad_gain = head_back(
        grad_q, raw_q_ref[...], qg_ref[...], cos_q_ref[...], sin_q_ref[...]
    )
    dq_ref[...] = grad_q.astype(BF16)
    dqg_ref[...] += grad_gain

    @pl.when(i == pl.num_programs(1) - 1)
    def _():
        grad_k, gain_k = head_back(
            sum_k[...] * DH ** (-0.5), raw_k_ref[...], kg_ref[...], cos_ref[...], sin_ref[...]
        )
        dk_ref[...] = grad_k.astype(BF16)
        dkg_ref[...] += gain_k
        dv_ref[...] = sum_v[...].astype(BF16)


def attend_back(q, k, v, grad, logs, seg_q, seg_k, raw, q_gain, k_gain, cosine, sine, block=256):
    rows, width = q.shape
    heads = width // DH
    by_rows = pl.BlockSpec((block, DH), lambda h, i: (i, h))
    whole = pl.BlockSpec((rows, DH), lambda h, i: (0, h))
    gain = pl.BlockSpec((1, DH), lambda h, i: (0, 0))
    return pl.pallas_call(
        attend_back_kernel,
        name="attend_back",
        grid=(heads, rows // block),
        in_specs=[
            by_rows,
            whole,
            whole,
            by_rows,
            pl.BlockSpec((1, block, 1), lambda h, i: (h, i, 0)),
            pl.BlockSpec((block, 1), lambda h, i: (i, 0)),
            pl.BlockSpec((1, rows), lambda h, i: (0, 0)),
            by_rows,
            pl.BlockSpec((rows, DH), lambda h, i: (0, heads + h)),
            gain,
            gain,
            pl.BlockSpec((block, DH), lambda h, i: (i, 0)),
            pl.BlockSpec((block, DH), lambda h, i: (i, 0)),
            pl.BlockSpec((rows, DH), lambda h, i: (0, 0)),
            pl.BlockSpec((rows, DH), lambda h, i: (0, 0)),
        ],
        out_specs=[by_rows, whole, whole, gain, gain],
        out_shape=[
            jax.ShapeDtypeStruct((rows, width), BF16),
            jax.ShapeDtypeStruct((rows, width), BF16),
            jax.ShapeDtypeStruct((rows, width), BF16),
            jax.ShapeDtypeStruct((1, DH), F32),
            jax.ShapeDtypeStruct((1, DH), F32),
        ],
        scratch_shapes=[pltpu.VMEM((rows, DH), F32), pltpu.VMEM((rows, DH), F32)],
        cost_estimate=cost(1000, 1000),
    )(q, k, v, grad, logs, seg_q, seg_k, raw, raw, q_gain, k_gain, cosine, sine, cosine, sine)


def branch_kernel(
    at_ref, x_ref, att_ref, own_ref, other_ref, gain_ref, normed_ref, scale_ref, mixed_ref, total
):
    half = own_ref.shape[0]
    own = contract_last(att_ref[...], own_ref[...])
    other = contract_last(att_ref[...], other_ref[...])
    second = at_ref[0] == 1
    total[:, :half] = x_ref[:, :half].astype(F32) + jnp.where(second, other, own)
    total[:, half:] = x_ref[:, half:].astype(F32) + jnp.where(second, own, other)
    mixed = total[...]
    scale = lax.rsqrt(jnp.mean(mixed * mixed, axis=1, keepdims=True) + EPSILON)
    normed_ref[...] = (mixed * scale * gain_ref[...]).astype(BF16)
    scale_ref[...] = scale
    width = mixed_ref.shape[1]
    mixed_ref[...] = total[:, pl.ds(pl.multiple_of(at_ref[1] * width, 128), width)]


def run_branch(core, col, x, attended, own, other, gain, width, block=256):
    rows = attended.shape[0]
    by_rows = lambda n: pl.BlockSpec((block, n), lambda i, at: (i, 0))
    whole = lambda a: pl.BlockSpec(a.shape, lambda i, at: (0, 0))
    return pl.pallas_call(
        branch_kernel,
        name="branch",
        grid_spec=pltpu.PrefetchScalarGridSpec(
            num_scalar_prefetch=1,
            grid=(rows // block,),
            in_specs=[by_rows(D), by_rows(D), whole(own), whole(other), whole(gain)],
            out_specs=[by_rows(D), by_rows(1), by_rows(width)],
            scratch_shapes=[pltpu.VMEM((block, D), F32)],
        ),
        out_shape=[
            jax.ShapeDtypeStruct((rows, D), BF16),
            jax.ShapeDtypeStruct((rows, 1), F32),
            jax.ShapeDtypeStruct((rows, width), F32),
        ],
        cost_estimate=cost(1000, 1000),
    )(jnp.stack([core, col]), x, attended, own, other, gain)


def expert_kernel(x_ref, c_ref, gate_ref, w_ref, wd_ref, act_ref, grad_ref, sums_ref, dx_ref):
    width = act_ref.shape[1]
    slot_gate = gate_ref[...]
    pre = jnp.dot(x_ref[...], w_ref[...], preferred_element_type=F32)
    gate, up = pre[:, :width], pre[:, width:]
    grad = jnp.dot(c_ref[...], wd_ref[...], preferred_element_type=F32)
    opened = 1.0 / (1.0 + jnp.exp(-gate))
    silu = gate * opened
    act = silu * up
    act_ref[...] = (slot_gate * act).astype(BF16)
    grad_gate = jnp.sum(act * grad, axis=1, keepdims=True)
    grad = slot_gate * grad
    dgate = (grad * up * opened * (1.0 + gate * (1.0 - opened))).astype(BF16)
    dup = (grad * silu).astype(BF16)
    grad_ref[:, :width] = dgate
    grad_ref[:, width:] = dup
    inner = jnp.sum(dgate.astype(F32) * gate + dup.astype(F32) * up, axis=1, keepdims=True)
    sums_ref[:, 0:1] = grad_gate
    sums_ref[:, 1:2] = inner
    dx_ref[...] = contract_last(grad_ref[...], w_ref[...], BF16)


def run_expert(x, c, slot_gate, w, wd, block):
    rows, width = x.shape[0], wd.shape[1]
    by_rows = lambda n: pl.BlockSpec((block, n), lambda i: (i, 0))
    whole = lambda a: pl.BlockSpec(a.shape, lambda i: (0, 0), pipeline_mode=pl.Buffered(1))
    return pl.pallas_call(
        expert_kernel,
        name="expert",
        grid=(rows // block,),
        in_specs=[by_rows(D), by_rows(D), by_rows(1), whole(w), whole(wd)],
        out_specs=[by_rows(width), by_rows(2 * width), by_rows(2), by_rows(D)],
        out_shape=[
            jax.ShapeDtypeStruct((rows, width), BF16),
            jax.ShapeDtypeStruct((rows, 2 * width), BF16),
            jax.ShapeDtypeStruct((rows, 2), F32),
            jax.ShapeDtypeStruct((rows, D), BF16),
        ],
        cost_estimate=cost(1000, 1000),
    )(x, c, slot_gate, w, wd)


def body(
    hidden_in,
    token_order,
    lengths,
    key_mask,
    routes,
    norm1_gain,
    query_gain,
    key_gain,
    w_query,
    w_key,
    w_value,
    w_out,
    norm2_gain,
    router,
    w_gate,
    w_up,
    w_down,
    cotangent,
):
    tok_count, feat_local = hidden_in.shape
    n_row = D // w_query.shape[0]
    n_col = D // feat_local
    local_experts, _, hidden_units = w_gate.shape
    per_device = max(1, local_experts // n_row)
    unit_split = max(1, n_row // local_experts)
    capacity = 5 * tok_count * TOP // (4 * E)
    col = lax.axis_index("col")
    row = lax.axis_index("row")
    core = row % 2
    steps = range(n_row)
    peers = [row ^ step for step in steps]
    rows_local = D // n_row
    unit_count = hidden_units // unit_split
    places = jnp.arange(tok_count, dtype=jnp.int32)
    order_row = token_order[0]
    inverse = jnp.zeros((tok_count,), jnp.int32).at[order_row].set(places)
    segment, position = layout(lengths[0], tok_count)

    packed_b = hidden_in[order_row]
    gains_b = jnp.concatenate([thirds(norm1_gain), thirds(norm2_gain)])
    gathered = gather_features(jnp.concatenate([packed_b, jnp.pad(gains_b, ((0, 10), (0, 0)))]))
    cot_b = cotangent[order_row]

    width_local = w_query.shape[1]
    head_count = width_local // DH
    weight_rows = jnp.concatenate([w_query, w_key, w_value, w_out, router.T], axis=1)
    weight_pieces = {step: trade(weight_rows, step, n_row) for step in steps if step % 2 == 0}
    for step in steps:
        if step % 2 == 1:
            weight_pieces[step] = trade(weight_pieces[step ^ 1], 1, n_row)
    weight_heads = jnp.zeros((D, weight_rows.shape[1]), BF16)
    for step in steps:
        weight_heads = lax.dynamic_update_slice(
            weight_heads, weight_pieces[step], (peers[step] * rows_local, 0)
        )
    w_qkv = weight_heads[:, : 3 * width_local]
    w_out_own = weight_heads[:, 3 * width_local : 4 * width_local]
    router_all = weight_heads[:, 4 * width_local :]

    def owned_at(peer):
        return (peer * per_device // unit_split, 0, (peer % unit_split) * unit_count)

    all_weights = (w_gate, w_up, w_down)
    all_parts = [(which, e) for which in range(3) for e in range(per_device)]
    owned = {}
    w_in = [jnp.zeros((D, 2 * unit_count), BF16) for e in range(per_device)]
    w_back = [jnp.zeros((D, unit_count), BF16) for e in range(per_device)]

    def slices(parts):
        pieces = []
        for step in steps if parts else ():
            first, _, unit = owned_at(peers[step])
            held = [
                lax.dynamic_slice(
                    all_weights[which], (first + e, 0, unit), (1, rows_local, unit_count)
                )
                for which, e in parts
            ]
            pieces.append(jnp.concatenate(held))
        return pieces

    def to_owner(parts, pieces, *earlier):
        pieces = trade_all(after(pieces, *earlier))
        for i, (which, e) in enumerate(parts):
            for step in steps:
                at = (peers[step] * rows_local, unit_count if which == 1 else 0)
                if which < 2:
                    w_in[e] = lax.dynamic_update_slice(w_in[e], pieces[step][i], at)
                else:
                    w_back[e] = lax.dynamic_update_slice(w_back[e], pieces[step][i], at)

    def tied(value):
        value, w_in[:], w_back[:] = lax.optimization_barrier((value, w_in[:], w_back[:]))
        return value

    first_parts, second_parts = all_parts[:per_device], all_parts[per_device : per_device + 1]
    third_parts = all_parts[per_device + 1 : 2 * per_device + 1]
    last_parts = all_parts[2 * per_device + 1 :]
    to_owner(first_parts, slices(first_parts))
    second_pieces = after(slices(second_parts), *w_in)
    later = [slices(parts) for parts in (third_parts, last_parts)]
    gathered, second_pieces, later = tied((gathered, second_pieces, later))
    gains = gathered[tok_count : tok_count + 6].astype(F32).reshape(2, 3, D).sum(axis=1)

    expert_ids = jnp.arange(E, dtype=jnp.int32)
    routes_t = routes.T
    chosen = jnp.any(routes_t[None] == expert_ids[:, None, None], axis=1)
    own_ids = col * local_experts + jnp.arange(local_experts, dtype=jnp.int32)
    own_chosen = jnp.any(routes_t[None] == own_ids[:, None, None], axis=1)
    earlier = (places[:, None] < places[None, :]).astype(BF16)
    rank = plain_dot(own_chosen.astype(BF16), earlier).astype(jnp.int32)
    slot_rank = jnp.where(own_chosen, rank, -1)
    slots = jnp.arange(capacity, dtype=jnp.int32)

    def of_peer(table, step, e):
        return lax.dynamic_slice_in_dim(table, owned_at(peers[step])[0] + e, 1, 0)

    hits = [
        [of_peer(slot_rank, step, e) == slots[:, None] for step in steps]
        for e in range(per_device)
    ]
    picks = [[hit.astype(BF16) for hit in hits[e]] for e in range(per_device)]

    def swap_small(pieces):
        table = jnp.zeros((n_row,) + pieces[0].shape, pieces[0].dtype)
        for step in steps:
            table = jnp.where(
                jnp.arange(n_row).reshape((-1,) + (1,) * pieces[0].ndim) == peers[step],
                pieces[step][None],
                table,
            )
        table = lax.all_to_all(table, "row", 0, 0, tiled=True)
        return [lax.dynamic_index_in_dim(table, peers[step], 0, False) for step in steps]

    cosine, sine = rope_tables(position)
    q_gain, k_gain = query_gain[None], key_gain[None]
    normed1, scale_in, raw_qk, query_rot, key_rot, values_b = project(
        gathered, gains[:1], weight_heads, q_gain, k_gain, cosine, sine, width_local
    )
    seg_q, seg_k = segment[:, None], jnp.where(key_mask == 1, segment, -1)[None]
    attended_b, log_totals = attend(query_rot, key_rot, values_b, seg_q, seg_k)

    half = D // 2
    out_half = lax.dynamic_slice_in_dim(w_out_own, core * half, half, 0)
    out_half_all = gather_features(after(out_half, *w_in))

    to_owner(second_parts, second_pieces)
    attended_b = tied(attended_b)
    attended_all = gather_features(attended_b)
    to_owner(third_parts, later[0], attended_b)
    other_half = trade(after(out_half_all, *w_back), 1, n_row)
    cot_all = gather_features(after(cot_b, attended_all))
    attended_all = tied(attended_all)
    if last_parts:
        to_owner(last_parts, later[1], w_back[0])
    normed2, scale_mid, mixed = run_branch(
        core, col, gathered, attended_all, out_half_all, other_half, gains[1:], feat_local
    )
    column_start = col * feat_local

    def chosen_rows(e, values):
        return [plain_dot(picks[e][step], values, BF16) for step in steps]

    sent_rows = [chosen_rows(e, normed2) for e in range(per_device)]
    sent_rows[0] = tied(sent_rows[0])
    all_rows = [trade_all(pieces) for pieces in sent_rows]
    sent_grads = [chosen_rows(e, cot_all) for e in range(per_device)]
    all_rows, sent_grads = lax.optimization_barrier((all_rows, sent_grads))
    all_grad_rows = [trade_all(pieces) for pieces in sent_grads]

    logits = lax.dot_general(
        router_all, normed2, (((0,), (1,)), ((), ())), preferred_element_type=F32
    )
    top_logit = jnp.max(jnp.where(chosen, logits, -jnp.inf), axis=0, keepdims=True)
    raised = jnp.where(chosen, jnp.exp(logits - top_logit), 0.0)
    gate_probs = raised / jnp.sum(raised, axis=0, keepdims=True)
    own_probs = lax.dynamic_slice_in_dim(gate_probs, col * local_experts, local_experts, 0)

    slot_gates = []
    for step in steps:
        held = [
            jnp.sum(jnp.where(hits[e][step], of_peer(own_probs, step, e), 0.0), axis=1)
            for e in range(per_device)
        ]
        slot_gates.append(jnp.stack(held))
    slot_gates = swap_small(slot_gates)

    near, far = list(steps)[:2], list(steps)[2:]
    branch_back, grads_back, scalars, weight_grads = [], [], [], []
    for e in range(per_device):
        rows, grad_rows, act, grad_pre, sums, grad_slot_rows = [], [], [], [], [], []
        for held in (near, far):
            rows.append(jnp.concatenate([all_rows[e][step] for step in held]))
            grad_rows.append(jnp.concatenate([all_grad_rows[e][step] for step in held]))
            slot_gate = jnp.concatenate([slot_gates[step][e] for step in held])[:, None]
            results = run_expert(
                rows[-1], grad_rows[-1], slot_gate, w_in[e], w_back[e], 2 * capacity
            )
            for total, result in zip((act, grad_pre, sums), results):
                total.append(result)
            grad_slot_rows += [
                results[3][i * capacity : (i + 1) * capacity] for i in range(len(held))
            ]
        rows, grad_rows, act, grad_pre, sums = (
            jnp.concatenate(parts) for parts in (rows, grad_rows, act, grad_pre, sums)
        )
        scalars.append(sums)
        grads_back.append(trade_all(grad_slot_rows))
        branch_back.append(contract_last(act, w_back[e], BF16))
        grad_in = contract_first(rows, grad_pre, BF16)
        weight_grads.append(
            (
                grad_in[:, :unit_count],
                grad_in[:, unit_count:],
                contract_first(grad_rows, act, BF16),
            )
        )
    scalars = jnp.stack(scalars)
    scalars_back = swap_small(
        [scalars[:, step * capacity : (step + 1) * capacity] for step in steps]
    )
    branch_back = jnp.stack(branch_back)
    out_pieces = [branch_back[:, step * capacity : (step + 1) * capacity] for step in steps]

    def to_tokens(back, which):
        return contract_first(
            jnp.concatenate([picks[e][step] for e, step in which]),
            jnp.concatenate([back[e][step] for e, step in which]),
        )

    every = [(e, step) for e in range(per_device) for step in steps]
    late = [(per_device - 1, step) for step in far]
    early = [pair for pair in every if pair not in late]
    grad_normed2_part = to_tokens(grads_back, early)
    grads_back, out_pieces, grad_normed2_part = lax.optimization_barrier(
        (grads_back, out_pieces, grad_normed2_part)
    )
    grad_normed2_part = (grad_normed2_part + to_tokens(grads_back, late)).astype(BF16)
    branch_back = trade_all(out_pieces)
    branch_back = [[piece[e] for piece in branch_back] for e in range(per_device)]
    grad_normed2 = scatter_partial(grad_normed2_part).astype(F32)

    grad_own = jnp.zeros((local_experts, tok_count), F32)
    inner_own = jnp.zeros((1, tok_count), F32)
    own_rows = jnp.arange(local_experts, dtype=jnp.int32)[:, None]
    for e in range(per_device):
        for step in steps:
            expert = owned_at(peers[step])[0] + e
            back = scalars_back[step][e]
            spread = jnp.sum(jnp.where(hits[e][step], back[:, :1], 0.0), axis=0, keepdims=True)
            grad_own = grad_own + jnp.where(own_rows == expert, spread, 0.0)
            inner_own = inner_own + jnp.sum(
                jnp.where(hits[e][step], back[:, 1:], 0.0), axis=0, keepdims=True
            )
    small = jnp.concatenate([grad_own, inner_own], axis=0)
    small = lax.all_to_all(
        jnp.broadcast_to(small[None], (n_col,) + small.shape), "col", 0, 0, tiled=True
    )
    grad_gates = small[:, :local_experts].reshape(E, tok_count)
    grad_logits = gate_probs * (
        grad_gates - jnp.sum(gate_probs * grad_gates, axis=0, keepdims=True)
    )
    grad_logits = grad_logits.astype(BF16)
    inner_mid = jnp.sum(small[:, local_experts], axis=0) + jnp.sum(
        grad_logits.astype(F32) * logits, axis=0
    )
    inner_mid = (inner_mid / D)[:, None]
    grad_router = lax.dot_general(
        normed2, grad_logits, (((0,), (1,)), ((), ())), preferred_element_type=F32
    )
    router_local = lax.dynamic_slice_in_dim(router_all, column_start, feat_local, 0)
    grad_unit_mid = grad_normed2 + lax.dot_general(
        grad_logits, router_local, (((0,), (1,)), ((), ())), preferred_element_type=F32
    )
    unit_mid = mixed * scale_mid
    grad_norm2 = jnp.sum(grad_unit_mid * unit_mid, axis=0)
    scaled_mid = grad_unit_mid * norm2_gain
    grad_mixed = cot_b.astype(F32) + scale_mid * (scaled_mid - unit_mid * inner_mid)
    def held_slices(which):
        return [
            jnp.stack(
                [
                    lax.dynamic_slice_in_dim(
                        weight_grads[e][which], peers[step] * rows_local, rows_local, 0
                    )
                    for e in range(per_device)
                ]
            )
            for step in steps
        ]

    gate_slices, up_slices = held_slices(0), held_slices(1)
    grad_mixed_b, branch_back, gate_slices, up_slices = lax.optimization_barrier(
        (grad_mixed.astype(BF16), branch_back, gate_slices, up_slices)
    )
    grad_branch = gather_features(grad_mixed_b)

    def to_holders(pieces, *earlier):
        return trade_all(after(pieces, *earlier))

    def to_rows(pieces):
        grad = jnp.zeros((local_experts, rows_local, hidden_units), F32)
        for step in steps:
            grad = lax.dynamic_update_slice(grad, pieces[step].astype(F32), owned_at(peers[step]))
        return grad

    def sum_groups(grad, *earlier):
        parts = [
            lax.dynamic_slice_in_dim(grad, peers[step] * rows_local, rows_local, 0)
            for step in steps
        ]
        return sum(part.astype(F32) for part in to_holders(parts, *earlier))

    gate_pieces = to_holders(gate_slices)
    combined_part = to_tokens(branch_back, every).astype(BF16)
    grad_branch, gate_pieces, combined_part = lax.optimization_barrier(
        (grad_branch, gate_pieces, combined_part)
    )
    up_pieces = to_holders(up_slices, gate_pieces)

    combined = scatter_partial(combined_part)

    grad_w_out = contract_first(grad_branch, attended_b, BF16)
    grad_attended = plain_dot(grad_branch, w_out_own, BF16)
    grad_q, grad_k, grad_v, grad_query_gain, grad_key_gain = attend_back(
        query_rot, key_rot, values_b, grad_attended, log_totals, seg_q, seg_k, raw_qk,
        q_gain, k_gain, cosine, sine,
    )
    grad_qkv = jnp.concatenate([grad_q, grad_k, grad_v], axis=1)
    grad_w_out = sum_groups(grad_w_out, up_pieces)
    grad_router = sum_groups(grad_router, up_pieces).T
    down_pieces = held_slices(2)
    grad_qkv, up_pieces, combined, down_pieces, grad_w_out, grad_router = (
        lax.optimization_barrier(
            (grad_qkv, up_pieces, combined, down_pieces, grad_w_out, grad_router)
        )
    )
    grad_normed1_part = contract_last(grad_qkv, w_qkv, BF16)
    grad_unit_in = scatter_partial(grad_normed1_part)
    inner_in = jnp.sum(
        grad_qkv.astype(F32) * jnp.concatenate([raw_qk, values_b.astype(F32)], axis=1), axis=1
    )
    packed = packed_b.astype(F32)
    unit_in = packed * scale_in
    unit_all = gathered[:tok_count].astype(F32) * scale_in
    grad_norm1 = jnp.sum(grad_normed1_part.astype(F32) * unit_all, axis=0)
    down_pieces = to_holders(down_pieces, grad_normed1_part)
    def for_all(vector):
        return jnp.broadcast_to(vector[None], (n_col,) + vector.shape)

    vectors = jnp.concatenate(
        [
            for_all(inner_in),
            for_all(grad_query_gain[0]),
            for_all(grad_key_gain[0]),
            grad_norm1.reshape(n_col, feat_local),
        ],
        axis=1,
    )
    vectors = jnp.sum(lax.all_to_all(vectors, "col", 0, 0, tiled=True), axis=0)
    inner_in = vectors[:tok_count, None] / D
    vectors = jnp.concatenate([vectors[tok_count:], grad_norm2])
    vectors = sum(trade(vectors, step, n_row) for step in steps)
    grad_unit_in, vectors, inner_in = lax.optimization_barrier(
        (grad_unit_in, vectors, inner_in)
    )
    grad_unit_in = grad_unit_in.astype(F32)
    scaled_in = grad_unit_in * norm1_gain
    grad_input = (grad_mixed + scale_in * (scaled_in - unit_in * inner_in))[inverse]

    output = (mixed + combined.astype(F32)).astype(BF16)[inverse]

    grad_heads = sum_groups(contract_first(normed1, grad_qkv, BF16), down_pieces)
    grad_w_query, grad_w_key, grad_w_value = (
        grad_heads[:, i * width_local : (i + 1) * width_local] for i in range(3)
    )
    grad_w_gate, grad_w_up, grad_w_down = (
        to_rows(pieces) for pieces in (gate_pieces, up_pieces, down_pieces)
    )

    grad_query_gain, grad_key_gain = vectors[:DH], vectors[DH : 2 * DH]
    grad_norm1 = vectors[2 * DH : 2 * DH + feat_local]
    grad_norm2 = vectors[2 * DH + feat_local :]
    return (
        output,
        grad_input,
        grad_norm1,
        grad_query_gain,
        grad_key_gain,
        grad_w_query,
        grad_w_key,
        grad_w_value,
        grad_w_out,
        grad_norm2,
        grad_router,
        grad_w_gate,
        grad_w_up,
        grad_w_down,
    )


def solution(mesh):
    return jax.shard_map(
        body,
        mesh=mesh,
        in_specs=(
            P("row", "col"),
            P("row", None),
            P("row", None),
            P("row"),
            P("row", None),
            P("col"),
            P(),
            P(),
            P("row", "col"),
            P("row", "col"),
            P("row", "col"),
            P("row", "col"),
            P("col"),
            P(None, "row"),
            P("col", "row", None),
            P("col", "row", None),
            P("col", "row", None),
            P("row", "col"),
        ),
        out_specs=(
            P("row", "col"),
            P("row", "col"),
            P("col"),
            P(),
            P(),
            P("row", "col"),
            P("row", "col"),
            P("row", "col"),
            P("row", "col"),
            P("col"),
            P(None, "row"),
            P("col", "row", None),
            P("col", "row", None),
            P("col", "row", None),
        ),
        check_vma=False,
    )
```

time: 1750 us -> 1290 us (0.74)
  waiting for transfers between devices: 777 us -> 556 us
  matrix products: 386 us -> 169 us
  blocking collectives: 163 us -> 0 us
  Pallas kernels: 0 us -> 154 us
  starting transfers between devices: 129 us -> 59.9 us
  local copies, waits for them, and re-layouts: 135 us -> 181 us
  other arithmetic: 115 us -> 141 us
    all_to_all x27 -> x4, waiting for transfers between devices: 563 us -> 31.3 us  [the longest x1 24.7 us: body(): lax.all_to_all(jnp.broadcast_to(small[None], (n_col,) + small.shape), 'co...]
    ppermute x1 -> x58, waiting for transfers between devices: 0.01 us -> 487 us  [trade(): return lax.ppermute(value, 'row', [(r, r ^ step) for r in range(n_row)])]
    pallas_call x0 -> x8, Pallas kernels: none -> 154 us  [the longest x4 72.7 us: run_expert(): pl.pallas_call(expert_kernel, name='expert', grid=(rows // block,), in_sp...]
    all_to_all x27 -> x4, starting transfers between devices: 127 us -> 13.6 us  [the longest x2 6.5 us: swap_small(): table = lax.all_to_all(table, 'row', 0, 0, tiled=True)]
    all_gather x5, waiting for transfers between devices: 146 us -> 37.3 us  [gather_features(): return lax.all_gather(local_rows, 'col', axis=1, tiled=True)]
    all_gather x3 -> x0, blocking collectives: 106 us -> none  [the longest x1 42.3 us: body(): router_all = lax.all_gather(router, 'row', axis=1, tiled=True)]
    reduce_scatter x3, waiting for transfers between devices: 67.7 us -> 0.01 us  [scatter_partial(): lax.psum_scatter(partial_rows, 'col', scatter_dimension=1, tiled=True)]
    dot_general x14 -> x18, matrix products: 120 us -> 53.1 us  [plain_dot(): return jnp.dot(left_op, right_op, preferred_element_type=F32).astype(kind)]
  transfers between devices with their start and end apart: 36 -> 70, of which waited for: 26 -> 30; matrix products, arithmetic and copies ran while one was open for 32% -> 35% of each run, Pallas kernels for 0% -> 11%
where the time goes in v2:
time: 1290 us; the launch traced here: 1280 us
  waiting for transfers between devices  556 us (43%)
  local copies, waits for them, and re-layouts  181 us (14%)
  matrix products  169 us (13%)
  Pallas kernels  154 us (12%)
  other arithmetic  141 us (11%)
  starting transfers between devices  59.9 us (5%)
  between operations  16.4 us (1%)
    ppermute x58, waiting for transfers between devices, trade(): return lax.ppermute(value, 'row', [(r, r ^ step) for r in range(n_row)])  487 us
    dot_general x9, matrix products, contract_first(): lax.dot_general(left_op, right_op, (((0,), (0,)), ((), ())), preferred_el...  87.1 us
    pallas_call x4, Pallas kernels, run_expert(): pl.pallas_call(expert_kernel, name='expert', grid=(rows // block,), in_sp...  72.7 us
    dot_general x18, matrix products, plain_dot(): return jnp.dot(left_op, right_op, preferred_element_type=F32).astype(kind)  53.1 us
    ppermute x58, starting transfers between devices, trade(): return lax.ppermute(value, 'row', [(r, r ^ step) for r in range(n_row)])  44.3 us
    all_gather x5, waiting for transfers between devices, gather_features(): return lax.all_gather(local_rows, 'col', axis=1, tiled=True)  37.3 us
    dynamic_update_slice x12, other arithmetic, to_rows(): lax.dynamic_update_slice(grad, pieces[step].astype(F32), owned_at(peers[s...  36.7 us
    another operation x6, local copies, waits for them, and re-layouts  28.2 us
  transfers between devices with their start and end apart: 70, of which 30 were waited for; matrix products, arithmetic and copies ran while one was open for 35% of the time, Pallas kernels for 11%

profile of v2, /device:TPU:0, one launch (start us, length us, event | category | flops | bytes accessed | tf_op | source)
XLA Modules:
  0.0 1277.4 jit_solution(13245665268930212488)
XLA Ops:
  66.6 24.1 %collective-permute-done.1 = bf16[2,512,1024]{2,1,0:T(8,128)(2,1)} collective-permute-done((bf16[2,512,1024]{2,1,0:T(8,128)(2,1)}, bf16[2,512,1024]{2,1,0:T(8,128)(2,1)}, u32[]{:S(2)}, u32[]{:S(2)}) %collective-permute-start.1) | collective-permute-done | bytes 2097184 | tf_op jit(solution)/shard_map/ppermute | solution.py:49
  93.7 41.5 %collective-permute-done.2 = bf16[2,512,1024]{2,1,0:T(8,128)(2,1)} collective-permute-done((bf16[2,512,1024]{2,1,0:T(8,128)(2,1)}, bf16[2,512,1024]{2,1,0:T(8,128)(2,1)}, u32[]{:S(2)}, u32[]{:S(2)}) %collective-permute-start.2) | collective-permute-done | bytes 2097184 | tf_op jit(solution)/shard_map/ppermute | solution.py:49
  153.9 13.9 %project.1 = (bf16[1536,2048]{1,0:T(8,128)(2,1)}, f32[1536,1]{1,0:T(8,128)}, f32[1536,512]{1,0:T(8,128)}, bf16[1536,256]{1,0:T(8,128)(2,1)}, bf16[1536,256]{1,0:T(8,128)(2,1)}, /*index=5*/bf16[1536,256]{1,0:T(8,128)(2,1)}) custom-call(bf16[1552,2048]{1,0:T(8,128)(2,1)} %all-gather.6.cloned.1.call-done.x_ref, f32[1,2048]{1,0:T(1,128)} %get-tuple-element.516.gain_ref, ...), custom_call_target="tpu_custom_call" | custom-call | flops 1000 | bytes 1000 | tf_op jit(solution)/shard_map/project/pallas_call | solution.py:117
  167.8 16.7 %attend.1 = (bf16[1536,256]{1,0:T(8,128)(2,1)}, f32[2,1536,1]{2,1,0:T(8,128)}) custom-call(bf16[1536,256]{1,0:T(8,128)(2,1)} %get-tuple-element.198.q_ref, bf16[1536,256]{1,0:T(8,128)(2,1)} %get-tuple-element.199.k_ref, bf16[1536,256]{1,0:T(8,128)(2,1)} %get-tuple-element.200.v_ref, s32[1536,1]{1,0:T(8,128)} %broadcast_in_dim.646.seg_q_ref, ...), custom_call_target="tpu_custom_call" | custom-call | flops 1000 | bytes 1000 | tf_op jit(solution)/shard_map/attend/pallas_call | solution.py:167
  190.2 8.2 collective-permute-done.8
  203.1 5.4 gather_fusion.1
  217.9 32.5 %collective-permute-done.10 = bf16[2,512,1024]{2,1,0:T(8,128)(2,1)} collective-permute-done((bf16[2,512,1024]{2,1,0:T(8,128)(2,1)}, bf16[2,512,1024]{2,1,0:T(8,128)(2,1)}, u32[]{:S(2)}, u32[]{:S(2)}) %collective-permute-start.10) | collective-permute-done | bytes 2097184 | tf_op jit(solution)/shard_map/ppermute | solution.py:49
  253.4 40.1 %collective-permute-done.11 = bf16[2,512,1024]{2,1,0:T(8,128)(2,1)S(1)} collective-permute-done((bf16[2,512,1024]{2,1,0:T(8,128)(2,1)}, bf16[2,512,1024]{2,1,0:T(8,128)(2,1)S(1)}, u32[]{:S(2)}, u32[]{:S(2)}) %collective-permute-start.11) | collective-permute-done | bytes 2097184 | tf_op jit(solution)/shard_map/ppermute | solution.py:49
  302.8 17.1 %all-gather.8.cloned.1.call-done.att_ref = bf16[1536,2048]{1,0:T(8,128)(2,1)} async-done(((bf16[1536,256]{1,0:T(8,128)(2,1)}), bf16[1536,2048]{1,0:T(8,128)(2,1)}) %all-gather.8.cloned.1.call-update) | async-done | bytes 6291472 | tf_op jit(solution)/shard_map/all_gather | solution.py:39
  330.4 22.9 %branch.1 = (bf16[1536,2048]{1,0:T(8,128)(2,1)}, f32[1536,1]{1,0:T(8,128)}, f32[1536,256]{1,0:T(8,128)}) custom-call(s32[2]{0:T(128)} %pad_add_fusion.at_ref, bf16[1552,2048]{1,0:T(8,128)(2,1)} %all-gather.6.cloned.1.call-done.x_ref, bf16[1536,2048]{1,0:T(8,128)(2,1)} %all-gather.8.cloned.1.call-done.att_ref, ...), custom_call_target="tpu_custom_call" | custom-call | flops 1000 | bytes 1000 | tf_op jit(solution)/shard_map/branch/pallas_call | solution.py:305
  353.3 5.6 convolution_convert_fusion.17
  391.4 6.6 all-to-all-done
  407.2 12.8 %all-gather.12.cloned.1.call-done = bf16[1536,2048]{1,0:T(8,128)(2,1)} async-done(((bf16[1536,256]{1,0:T(8,128)(2,1)}), bf16[1536,2048]{1,0:T(8,128)(2,1)}) %all-gather.12.cloned.1.call-update) | async-done | bytes 6291472 | tf_op jit(solution)/shard_map/all_gather | solution.py:39
  444.0 20.4 %collective-permute-done.18 = bf16[240,2048]{1,0:T(8,128)(2,1)} collective-permute-done((bf16[240,2048]{1,0:T(8,128)(2,1)S(1)}, bf16[240,2048]{1,0:T(8,128)(2,1)}, u32[]{:S(2)}, u32[]{:S(2)}) %collective-permute-start.18) | collective-permute-done | bytes 983072 | tf_op jit(solution)/shard_map/ppermute | solution.py:49
  481.1 7.3 collective-permute-done.25
  491.6 18.5 %collective-permute-done.24 = bf16[240,2048]{1,0:T(8,128)(2,1)S(1)} collective-permute-done((bf16[240,2048]{1,0:T(8,128)(2,1)}, bf16[240,2048]{1,0:T(8,128)(2,1)S(1)}, u32[]{:S(2)}, u32[]{:S(2)}) %collective-permute-start.24) | collective-permute-done | bytes 983072 | tf_op jit(solution)/shard_map/ppermute | solution.py:49
  516.1 18.0 %expert.5 = (bf16[480,1024]{1,0:T(8,128)(2,1)}, bf16[480,2048]{1,0:T(8,128)(2,1)}, f32[480,2]{1,0:T(8,128)}, bf16[480,2048]{1,0:T(8,128)(2,1)}) custom-call(bf16[480,2048]{1,0:T(8,128)(2,1)} %pad_maximum_fusion.24.x_ref, bf16[480,2048]{1,0:T(8,128)(2,1)} %pad_maximum_fusion.25.c_ref, f32[480,1]{1,0:T(8,128)} %copy.68.gate_ref, ...), custom_call_target="tpu_custom_call" | custom-call | flops 1000 | bytes 1000 | tf_op jit(solution)/shard_map/expert/pallas_call | solution.py:350
  534.1 18.2 %expert.4 = (bf16[480,1024]{1,0:T(8,128)(2,1)}, bf16[480,2048]{1,0:T(8,128)(2,1)}, f32[480,2]{1,0:T(8,128)}, bf16[480,2048]{1,0:T(8,128)(2,1)}) custom-call(bf16[480,2048]{1,0:T(8,128)(2,1)} %pad_maximum_fusion.22.x_ref, bf16[480,2048]{1,0:T(8,128)(2,1)} %pad_maximum_fusion.23.c_ref, f32[480,1]{1,0:T(8,128)} %copy.67.gate_ref, ...), custom_call_target="tpu_custom_call" | custom-call | flops 1000 | bytes 1000 | tf_op jit(solution)/shard_map/expert/pallas_call | solution.py:350
  555.4 18.3 %expert.7 = (bf16[480,1024]{1,0:T(8,128)(2,1)}, bf16[480,2048]{1,0:T(8,128)(2,1)}, f32[480,2]{1,0:T(8,128)}, bf16[480,2048]{1,0:T(8,128)(2,1)}) custom-call(bf16[480,2048]{1,0:T(8,128)(2,1)} %pad_maximum_fusion.28.x_ref, bf16[480,2048]{1,0:T(8,128)(2,1)} %pad_maximum_fusion.29.c_ref, f32[480,1]{1,0:T(8,128)} %copy.70.gate_ref, ...), custom_call_target="tpu_custom_call" | custom-call | flops 1000 | bytes 1000 | tf_op jit(solution)/shard_map/expert/pallas_call | solution.py:350
  576.7 18.1 %expert.6 = (bf16[480,1024]{1,0:T(8,128)(2,1)}, bf16[480,2048]{1,0:T(8,128)(2,1)}, f32[480,2]{1,0:T(8,128)}, bf16[480,2048]{1,0:T(8,128)(2,1)}) custom-call(bf16[480,2048]{1,0:T(8,128)(2,1)} %pad_maximum_fusion.26.x_ref, bf16[480,2048]{1,0:T(8,128)(2,1)} %pad_maximum_fusion.27.c_ref, f32[480,1]{1,0:T(8,128)} %copy.69.gate_ref, ...), custom_call_target="tpu_custom_call" | custom-call | flops 1000 | bytes 1000 | tf_op jit(solution)/shard_map/expert/pallas_call | solution.py:350
  609.9 14.1 %convolution_convert_fusion.2 = bf16[2048,2048]{1,0:T(8,128)(2,1)} fusion(bf16[240,2048]{1,0:T(8,128)(2,1)} %collective-permute-done.21, bf16[240,2048]{1,0:T(8,128)(2,1)} %collective-permute-done.20, bf16[240,2048]{1,0:T(8,128)(2,1)} %collective-permute-done.19, bf16[240,2048]{1,0:T(8,128)(2,1)S(1)} %copy-done.60, bf16[480,2048]{1,0:T(8,128)(2,1)S(1)} %copy-done.112, ...), kind=kOutput, calls=%fused_computation.17 | convolution fusion | flops 8080850944 | bytes 16252928 | tf_op jit(solution)/shard_map/dot_general | solution.py:63
  630.8 19.3 %collective-permute-done.27 = bf16[240,2048]{1,0:T(8,128)(2,1)S(1)} collective-permute-done((bf16[240,2048]{1,0:T(8,128)(2,1)S(1)}, bf16[240,2048]{1,0:T(8,128)(2,1)S(1)}, u32[]{:S(2)}, u32[]{:S(2)}) %collective-permute-start.27) | collective-permute-done | bytes 983072 | tf_op jit(solution)/shard_map/ppermute | solution.py:49
  652.8 6.8 convert_bitcast_fusion.1
  663.5 13.8 %fusion.173 = f32[1536,2048]{1,0:T(8,128)S(1)} fusion(bf16[1440,1536]{1,0:T(8,128)(2,1)} %get-tuple-element.521, bf16[1440,2048]{1,0:T(8,128)(2,1)} %constant_dynamic-update-slice_fusion.8), kind=kOutput, calls=%fused_computation.520 | convolution fusion | flops 9059696640 | bytes 22904832 | tf_op jit(solution)/shard_map/dot_general | solution.py:63
  677.2 14.6 %collective-permute-done.33 = bf16[240,2048]{1,0:T(8,128)(2,1)} collective-permute-done((bf16[240,2048]{1,0:T(8,128)(2,1)S(1)}, bf16[240,2048]{1,0:T(8,128)(2,1)}, u32[]{:S(2)}, u32[]{:S(2)}) %collective-permute-start.33) | collective-permute-done | bytes 983072 | tf_op jit(solution)/shard_map/ppermute | solution.py:49
  691.9 5.0 fusion.51
  706.5 12.2 convolution_convert_fusion.3
  752.1 24.7 %all-to-all-done.2 = f32[8,9,1536]{2,1,0:T(8,128)S(1)} async-done(((f32[8,9,1536]{2,1,0:T(8,128)}), f32[8,9,1536]{2,1,0:T(8,128)S(1)}, u32[]{:S(2)}, u32[]{:S(2)}) %all-to-all-start.2) | async-done | bytes 442400 | tf_op jit(solution)/shard_map/all_to_all | solution.py:622
  783.5 9.8 collective-permute-done.35
  796.3 37.5 %collective-permute-done.36 = bf16[2,240,2048]{2,1,0:T(8,128)(2,1)S(1)} collective-permute-done((bf16[2,240,2048]{2,1,0:T(8,128)(2,1)}, bf16[2,240,2048]{2,1,0:T(8,128)(2,1)S(1)}, u32[]{:S(2)}, u32[]{:S(2)}) %collective-permute-start.36) | collective-permute-done | bytes 1966112 | tf_op jit(solution)/shard_map/ppermute | solution.py:49
  847.3 17.3 %convolution_convert_fusion.1 = bf16[1536,2048]{1,0:T(8,128)(2,1)} fusion(bf16[1920,1536]{1,0:T(8,128)(2,1)} %fusion.112, bf16[1920,2048]{1,0:T(8,128)(2,1)S(1)} %constant_dynamic-update-slice_fusion.14), kind=kOutput, calls=%fused_computation.16 | convolution fusion | flops 12082741248 | bytes 20054016 | tf_op jit(solution)/shard_map/dot_general | solution.py:63
  864.6 25.3 %collective-permute-done.38 = bf16[2,512,1024]{2,1,0:T(8,128)(2,1)} collective-permute-done((bf16[2,512,1024]{2,1,0:T(8,128)(2,1)}, bf16[2,512,1024]{2,1,0:T(8,128)(2,1)}, u32[]{:S(2)}, u32[]{:S(2)}) %collective-permute-start.38) | collective-permute-done | bytes 2097184 | tf_op jit(solution)/shard_map/ppermute | solution.py:49
  889.9 43.3 %collective-permute-done.39 = bf16[2,512,1024]{2,1,0:T(8,128)(2,1)} collective-permute-done((bf16[2,512,1024]{2,1,0:T(8,128)(2,1)}, bf16[2,512,1024]{2,1,0:T(8,128)(2,1)}, u32[]{:S(2)}, u32[]{:S(2)}) %collective-permute-start.39) | collective-permute-done | bytes 2097184 | tf_op jit(solution)/shard_map/ppermute | solution.py:49
  933.2 7.3 all-gather.14.cloned.1.call-done
  942.2 7.0 fusion.38
  952.1 5.8 fusion.41
  973.1 27.6 %attend_back.1 = (bf16[1536,256]{1,0:T(8,128)(2,1)}, bf16[1536,256]{1,0:T(8,128)(2,1)}, bf16[1536,256]{1,0:T(8,128)(2,1)}, f32[1,128]{1,0:T(1,128)}, f32[1,128]{1,0:T(1,128)}) custom-call(bf16[1536,256]{1,0:T(8,128)(2,1)} %get-tuple-element.198.q_ref, bf16[1536,256]{1,0:T(8,128)(2,1)} %get-tuple-element.199.k_ref, ...), custom_call_target="tpu_custom_call" | custom-call | flops 1000 | bytes 1000 | tf_op jit(solution)/shard_map/attend_back/pallas_call | solution.py:250
  1010.2 44.2 %collective-permute-done.42 = bf16[2,512,1024]{2,1,0:T(8,128)(2,1)} collective-permute-done((bf16[2,512,1024]{2,1,0:T(8,128)(2,1)}, bf16[2,512,1024]{2,1,0:T(8,128)(2,1)}, u32[]{:S(2)}, u32[]{:S(2)}) %collective-permute-start.42) | collective-permute-done | bytes 2097184 | tf_op jit(solution)/shard_map/ppermute | solution.py:49
  1062.5 11.7 collective-permute-done.47
  1075.8 10.4 multiply_reduce_fusion
  1086.2 6.5 scatter_custom_fusion
  1092.8 8.3 broadcast.177.clone
  1135.1 7.1 convolution_convert_fusion.4
  1142.2 8.3 broadcast.177.clone.2
  1157.2 59.2 %collective-permute-done.51 = f32[768]{0:T(1024)S(1)} collective-permute-done((f32[768]{0:T(1024)S(1)}, f32[768]{0:T(1024)S(1)}, u32[]{:S(2)}, u32[]{:S(2)}) %collective-permute-start.51) | collective-permute-done | bytes 3104 | tf_op jit(solution)/shard_map/ppermute | solution.py:49
  1231.9 5.2 collective-permute-done.57
  1237.1 17.3 %collective-permute-done.56 = bf16[512,768]{1,0:T(8,128)(2,1)S(1)} collective-permute-done((bf16[512,768]{1,0:T(8,128)(2,1)S(1)}, bf16[512,768]{1,0:T(8,128)(2,1)S(1)}, u32[]{:S(2)}, u32[]{:S(2)}) %collective-permute-start.56) | collective-permute-done | bytes 786464 | tf_op jit(solution)/shard_map/ppermute | solution.py:49
  1260.4 5.4 gather_fusion.2
  (651 shorter events, 419.9 us)
Async XLA Ops:
  7.2 136.1 %all-gather.6.cloned.1.call-start = ((), (), s32[]{:S(2)}) async-start(), calls=%async_computation.7 | async-start | bytes 7151616 | tf_op jit(solution)/shard_map/all_gather | solution.py:39
  15.3 279.7 %all-gather.10.cloned.1.call-start = ((), (), s32[]{:S(2)}) async-start(), calls=%async_computation.9 | async-start | bytes 4718592 | tf_op jit(solution)/shard_map/all_gather | solution.py:39
  17.1 42.5 %collective-permute-start.3 = (bf16[512,1088]{0,1:T(8,128)(2,1)}, bf16[512,1088]{0,1:T(8,128)(2,1)}, u32[]{:S(2)}, u32[]{:S(2)}) collective-permute-start(bf16[512,1088]{0,1:T(8,128)(2,1)} %copy.61), channel_id=1, source_target_pairs={{0,8},{8,0},{16,24},{24,16},{1,9},{9,1},{17,25},{25,17},{2,10},{10... | collective-permute-start | bytes 3342344 | tf_op jit(solution)/shard_map/ppermute | solution.py:49
  17.6 40.2 %collective-permute-start.4 = (bf16[512,1088]{0,1:T(8,128)(2,1)}, bf16[512,1088]{0,1:T(8,128)(2,1)}, u32[]{:S(2)}, u32[]{:S(2)}) collective-permute-start(bf16[512,1088]{0,1:T(8,128)(2,1)} %copy.61), channel_id=1, source_target_pairs={{0,16},{8,24},{16,0},{24,8},{1,17},{9,25},{17,1},{25,9},{2,18},{10... | collective-permute-start | bytes 3342344 | tf_op jit(solution)/shard_map/ppermute | solution.py:49
  28.9 61.8 %collective-permute-start.1 = (bf16[2,512,1024]{2,1,0:T(8,128)(2,1)}, bf16[2,512,1024]{2,1,0:T(8,128)(2,1)}, u32[]{:S(2)}, u32[]{:S(2)}) collective-permute-start(bf16[2,512,1024]{2,1,0:T(8,128)(2,1)} %get-tuple-element.191), channel_id=1, source_target_pairs={{0,16},{8,24},{16,0},{24,8},{1,17},{9,25},{17,1},{25,9},{2,18},{10... | collective-permute-start | bytes 6291464 | tf_op jit(solution)/shard_map/ppermute | solution.py:49
  29.3 106.0 %collective-permute-start.2 = (bf16[2,512,1024]{2,1,0:T(8,128)(2,1)}, bf16[2,512,1024]{2,1,0:T(8,128)(2,1)}, u32[]{:S(2)}, u32[]{:S(2)}) collective-permute-start(bf16[2,512,1024]{2,1,0:T(8,128)(2,1)} %get-tuple-element.192), channel_id=1, source_target_pairs={{0,24},{8,16},{16,8},{24,0},{1,25},{9,17},{17,9},{25,1},{2,26},{10... | collective-permute-start | bytes 6291464 | tf_op jit(solution)/shard_map/ppermute | solution.py:49
  59.5 78.8 %collective-permute-start.5 = (bf16[512,1088]{0,1:T(8,128)(2,1)}, bf16[512,1088]{0,1:T(8,128)(2,1)}, u32[]{:S(2)}, u32[]{:S(2)}) collective-permute-start(bf16[512,1088]{0,1:T(8,128)(2,1)} %collective-permute-done.4), channel_id=1, source_target_pairs={{0,8},{8,0},{16,24},{24,16},{1,9},{9,1},{17,25},{25,17},{2,10},{10... | collective-permute-start | bytes 3342344 | tf_op jit(solution)/shard_map/ppermute | solution.py:49
  143.3 176.6 %all-gather.8.cloned.1.call-start = ((), (), s32[]{:S(2)}) async-start(), calls=%async_computation.8 | async-start | bytes 7077888 | tf_op jit(solution)/shard_map/all_gather | solution.py:39
  150.6 37.4 %collective-permute-start.7 = (bf16[1,512,1024]{2,1,0:T(8,128)(2,1)}, bf16[1,512,1024]{2,1,0:T(8,128)(2,1)}, u32[]{:S(2)}, u32[]{:S(2)}) collective-permute-start(bf16[1,512,1024]{2,1,0:T(8,128)(2,1)} %get-tuple-element.209), channel_id=1, source_target_pairs={{0,16},{8,24},{16,0},{24,8},{1,17},{9,25},{17,1},{25,9},{2,18},{10... | collective-permute-start | bytes 3145736 | tf_op jit(solution)/shard_map/ppermute | solution.py:49
  153.1 45.3 %collective-permute-start.8 = (bf16[1,512,1024]{2,1,0:T(8,128)(2,1)S(1)}, bf16[1,512,1024]{2,1,0:T(8,128)(2,1)}, u32[]{:S(2)}, u32[]{:S(2)}) collective-permute-start(bf16[1,512,1024]{2,1,0:T(8,128)(2,1)S(1)} %copy-done.46), channel_id=1, source_target_pairs={{0,24},{8,16},{16,8},{24,0},{1,25},{9,17},{17,9},{25,1},{2,26},{10... | collective-permute-start | bytes 3145736 | tf_op jit(solution)/shard_map/ppermute | solution.py:49
  200.7 219.3 %all-gather.12.cloned.1.call-start = ((), (), s32[]{:S(2)}) async-start(), calls=%async_computation.10 | async-start | bytes 7077888 | tf_op jit(solution)/shard_map/all_gather | solution.py:39
  201.6 48.8 %collective-permute-start.10 = (bf16[2,512,1024]{2,1,0:T(8,128)(2,1)}, bf16[2,512,1024]{2,1,0:T(8,128)(2,1)}, u32[]{:S(2)}, u32[]{:S(2)}) collective-permute-start(bf16[2,512,1024]{2,1,0:T(8,128)(2,1)} %get-tuple-element.223), channel_id=1, source_target_pairs={{0,16},{8,24},{16,0},{24,8},{1,17},{9,25},{17,1},{25,9},{2,18},{10... | collective-permute-start | bytes 6291464 | tf_op jit(solution)/shard_map/ppermute | solution.py:49
  203.1 90.4 %collective-permute-start.11 = (bf16[2,512,1024]{2,1,0:T(8,128)(2,1)}, bf16[2,512,1024]{2,1,0:T(8,128)(2,1)S(1)}, u32[]{:S(2)}, u32[]{:S(2)}) collective-permute-start(bf16[2,512,1024]{2,1,0:T(8,128)(2,1)} %get-tuple-element.224), channel_id=1, source_target_pairs={{0,24},{8,16},{16,8},{24,0},{1,25},{9,17},{17,9},{25,1},{2,26},{10... | collective-permute-start | bytes 6291464 | tf_op jit(solution)/shard_map/ppermute | solution.py:49
  328.6 69.6 %collective-permute-start.13 = (bf16[1,512,1024]{2,1,0:T(8,128)(2,1)}, bf16[1,512,1024]{2,1,0:T(8,128)(2,1)}, u32[]{:S(2)}, u32[]{:S(2)}) collective-permute-start(bf16[1,512,1024]{2,1,0:T(8,128)(2,1)} %get-tuple-element.242), channel_id=1, source_target_pairs={{0,8},{8,0},{16,24},{24,16},{1,9},{9,1},{17,25},{25,17},{2,10},{10... | collective-permute-start | bytes 3145736 | tf_op jit(solution)/shard_map/ppermute | solution.py:49
  328.6 73.1 %collective-permute-start.14 = (bf16[1,512,1024]{2,1,0:T(8,128)(2,1)}, bf16[1,512,1024]{2,1,0:T(8,128)(2,1)}, u32[]{:S(2)}, u32[]{:S(2)}) collective-permute-start(bf16[1,512,1024]{2,1,0:T(8,128)(2,1)} %get-tuple-element.243), channel_id=1, source_target_pairs={{0,16},{8,24},{16,0},{24,8},{1,17},{9,25},{17,1},{25,9},{2,18},{10... | collective-permute-start | bytes 3145736 | tf_op jit(solution)/shard_map/ppermute | solution.py:49
  330.0 73.9 %collective-permute-start.15 = (bf16[1,512,1024]{2,1,0:T(8,128)(2,1)S(1)}, bf16[1,512,1024]{2,1,0:T(8,128)(2,1)}, u32[]{:S(2)}, u32[]{:S(2)}) collective-permute-start(bf16[1,512,1024]{2,1,0:T(8,128)(2,1)S(1)} %copy-done.45), channel_id=1, source_target_pairs={{0,24},{8,16},{16,8},{24,0},{1,25},{9,17},{17,9},{25,1},{2,26},{10... | collective-permute-start | bytes 3145736 | tf_op jit(solution)/shard_map/ppermute | solution.py:49
  359.0 78.5 %collective-permute-start.19 = (bf16[240,2048]{1,0:T(8,128)(2,1)}, bf16[240,2048]{1,0:T(8,128)(2,1)}, u32[]{:S(2)}, u32[]{:S(2)}) collective-permute-start(bf16[240,2048]{1,0:T(8,128)(2,1)} %convolution_convert_fusion.17), channel_id=1, source_target_pairs={{0,8},{8,0},{16,24},{24,16},{1,9},{9,1},{17,25},{25,17},{2,10},{10... | collective-permute-start | bytes 2949128 | tf_op jit(solution)/shard_map/ppermute | solution.py:49
  361.9 81.9 %collective-permute-start.20 = (bf16[240,2048]{1,0:T(8,128)(2,1)}, bf16[240,2048]{1,0:T(8,128)(2,1)}, u32[]{:S(2)}, u32[]{:S(2)}) collective-permute-start(bf16[240,2048]{1,0:T(8,128)(2,1)} %convolution_convert_fusion.16), channel_id=1, source_target_pairs={{0,16},{8,24},{16,0},{24,8},{1,17},{9,25},{17,1},{25,9},{2,18},{10... | collective-permute-start | bytes 2949128 | tf_op jit(solution)/shard_map/ppermute | solution.py:49
  398.2 45.6 %collective-permute-start.21 = (bf16[240,2048]{1,0:T(8,128)(2,1)}, bf16[240,2048]{1,0:T(8,128)(2,1)}, u32[]{:S(2)}, u32[]{:S(2)}) collective-permute-start(bf16[240,2048]{1,0:T(8,128)(2,1)} %convolution_convert_fusion.15), channel_id=1, source_target_pairs={{0,24},{8,16},{16,8},{24,0},{1,25},{9,17},{17,9},{25,1},{2,26},{10... | collective-permute-start | bytes 2949128 | tf_op jit(solution)/shard_map/ppermute | solution.py:49
  406.3 37.6 %collective-permute-start.16 = (bf16[240,2048]{1,0:T(8,128)(2,1)}, bf16[240,2048]{1,0:T(8,128)(2,1)}, u32[]{:S(2)}, u32[]{:S(2)}) collective-permute-start(bf16[240,2048]{1,0:T(8,128)(2,1)} %convolution_convert_fusion.21), channel_id=1, source_target_pairs={{0,8},{8,0},{16,24},{24,16},{1,9},{9,1},{17,25},{25,17},{2,10},{10... | collective-permute-start | bytes 2949128 | tf_op jit(solution)/shard_map/ppermute | solution.py:49
  406.7 37.3 %collective-permute-start.17 = (bf16[240,2048]{1,0:T(8,128)(2,1)}, bf16[240,2048]{1,0:T(8,128)(2,1)}, u32[]{:S(2)}, u32[]{:S(2)}) collective-permute-start(bf16[240,2048]{1,0:T(8,128)(2,1)} %convolution_convert_fusion.20), channel_id=1, source_target_pairs={{0,16},{8,24},{16,0},{24,8},{1,17},{9,25},{17,1},{25,9},{2,18},{10... | collective-permute-start | bytes 2949128 | tf_op jit(solution)/shard_map/ppermute | solution.py:49
  469.1 40.9 %collective-permute-start.24 = (bf16[240,2048]{1,0:T(8,128)(2,1)}, bf16[240,2048]{1,0:T(8,128)(2,1)S(1)}, u32[]{:S(2)}, u32[]{:S(2)}) collective-permute-start(bf16[240,2048]{1,0:T(8,128)(2,1)} %convolution_convert_fusion.12), channel_id=1, source_target_pairs={{0,16},{8,24},{16,0},{24,8},{1,17},{9,25},{17,1},{25,9},{2,18},{10... | collective-permute-start | bytes 2949128 | tf_op jit(solution)/shard_map/ppermute | solution.py:49
  469.7 44.0 %collective-permute-start.22 = (bf16[240,2048]{1,0:T(8,128)(2,1)}, bf16[240,2048]{1,0:T(8,128)(2,1)S(1)}, u32[]{:S(2)}, u32[]{:S(2)}) collective-permute-start(bf16[240,2048]{1,0:T(8,128)(2,1)} %convolution_convert_fusion.13), channel_id=1, source_target_pairs={{0,8},{8,0},{16,24},{24,16},{1,9},{9,1},{17,25},{25,17},{2,10},{10... | collective-permute-start | bytes 2949128 | tf_op jit(solution)/shard_map/ppermute | solution.py:49
  469.8 82.5 %collective-permute-start.31 = (bf16[240,2048]{1,0:T(8,128)(2,1)}, bf16[240,2048]{1,0:T(8,128)(2,1)}, u32[]{:S(2)}, u32[]{:S(2)}) collective-permute-start(bf16[240,2048]{1,0:T(8,128)(2,1)} %convolution_convert_fusion.7), channel_id=1, source_target_pairs={{0,24},{8,16},{16,8},{24,0},{1,25},{9,17},{17,9},{25,1},{2,26},{10... | collective-permute-start | bytes 2949128 | tf_op jit(solution)/shard_map/ppermute | solution.py:49
  471.3 81.0 %collective-permute-start.30 = (bf16[240,2048]{1,0:T(8,128)(2,1)}, bf16[240,2048]{1,0:T(8,128)(2,1)}, u32[]{:S(2)}, u32[]{:S(2)}) collective-permute-start(bf16[240,2048]{1,0:T(8,128)(2,1)} %convolution_convert_fusion.8), channel_id=1, source_target_pairs={{0,16},{8,24},{16,0},{24,8},{1,17},{9,25},{17,1},{25,9},{2,18},{10... | collective-permute-start | bytes 2949128 | tf_op jit(solution)/shard_map/ppermute | solution.py:49
  488.4 85.5 %collective-permute-start.28 = (bf16[240,2048]{1,0:T(8,128)(2,1)}, bf16[240,2048]{1,0:T(8,128)(2,1)}, u32[]{:S(2)}, u32[]{:S(2)}) collective-permute-start(bf16[240,2048]{1,0:T(8,128)(2,1)} %convolution_convert_fusion.9), channel_id=1, source_target_pairs={{0,8},{8,0},{16,24},{24,16},{1,9},{9,1},{17,25},{25,17},{2,10},{10... | collective-permute-start | bytes 2949128 | tf_op jit(solution)/shard_map/ppermute | solution.py:49
  597.0 133.1 %all-to-all-start.1 = ((f32[4,2,240,2]{2,3,1,0:T(2,128)}), f32[4,2,240,2]{2,3,1,0:T(2,128)S(1)}, u32[]{:S(2)}, u32[]{:S(2)}) async-start(f32[4,2,240,2]{2,3,1,0:T(2,128)} %select_select_fusion), calls=%async_computation.2 | async-start | bytes 32768 | tf_op jit(solution)/shard_map/all_to_all | solution.py:498
  600.2 235.1 %reduce-scatter.4.cloned.1.call-start = ((), (), s32[]{:S(2)}) async-start(), calls=%async_computation.11 | async-start | bytes 7077888 | tf_op jit(solution)/shard_map/reduce_scatter | solution.py:43
  606.7 43.4 %collective-permute-start.27 = (bf16[240,2048]{1,0:T(8,128)(2,1)S(1)}, bf16[240,2048]{1,0:T(8,128)(2,1)S(1)}, u32[]{:S(2)}, u32[]{:S(2)}) collective-permute-start(bf16[240,2048]{1,0:T(8,128)(2,1)S(1)} %get-tuple-element.488), channel_id=1, source_target_pairs={{0,24},{8,16},{16,8},{24,0},{1,25},{9,17},{17,9},{25,1},{2,26},{10... | collective-permute-start | bytes 2949128 | tf_op jit(solution)/shard_map/ppermute | solution.py:49
  607.9 69.4 %collective-permute-start.32 = (bf16[240,2048]{1,0:T(8,128)(2,1)}, bf16[240,2048]{1,0:T(8,128)(2,1)}, u32[]{:S(2)}, u32[]{:S(2)}) collective-permute-start(bf16[240,2048]{1,0:T(8,128)(2,1)} %get-tuple-element.487), channel_id=1, source_target_pairs={{0,16},{8,24},{16,0},{24,8},{1,17},{9,25},{17,1},{25,9},{2,18},{10... | collective-permute-start | bytes 2949128 | tf_op jit(solution)/shard_map/ppermute | solution.py:49
  609.6 82.3 %collective-permute-start.33 = (bf16[240,2048]{1,0:T(8,128)(2,1)S(1)}, bf16[240,2048]{1,0:T(8,128)(2,1)}, u32[]{:S(2)}, u32[]{:S(2)}) collective-permute-start(bf16[240,2048]{1,0:T(8,128)(2,1)S(1)} %get-tuple-element.486), channel_id=1, source_target_pairs={{0,24},{8,16},{16,8},{24,0},{1,25},{9,17},{17,9},{25,1},{2,26},{10... | collective-permute-start | bytes 2949128 | tf_op jit(solution)/shard_map/ppermute | solution.py:49
  734.8 42.0 %all-to-all-start.2 = ((f32[8,9,1536]{2,1,0:T(8,128)}), f32[8,9,1536]{2,1,0:T(8,128)S(1)}, u32[]{:S(2)}, u32[]{:S(2)}) async-start(f32[8,9,1536]{2,1,0:T(8,128)} %broadcast_in_dim.639), calls=%async_computation.3 | async-start | bytes 1572864 | tf_op jit(solution)/shard_map/all_to_all | solution.py:622
  738.4 202.1 %all-gather.14.cloned.1.call-start = ((), (), s32[]{:S(2)}) async-start(), calls=%async_computation.12 | async-start | bytes 7077888 | tf_op jit(solution)/shard_map/all_gather | solution.py:39
  738.8 41.6 %collective-permute-start.34 = (bf16[2,240,2048]{2,1,0:T(8,128)(2,1)}, bf16[2,240,2048]{2,1,0:T(8,128)(2,1)}, u32[]{:S(2)}, u32[]{:S(2)}) collective-permute-start(bf16[2,240,2048]{2,1,0:T(8,128)(2,1)} %get-tuple-element.286), channel_id=1, source_target_pairs={{0,8},{8,0},{16,24},{24,16},{1,9},{9,1},{17,25},{25,17},{2,10},{10... | collective-permute-start | bytes 5898248 | tf_op jit(solution)/shard_map/ppermute | solution.py:49
  747.3 46.0 %collective-permute-start.35 = (bf16[2,240,2048]{2,1,0:T(8,128)(2,1)}, bf16[2,240,2048]{2,1,0:T(8,128)(2,1)}, u32[]{:S(2)}, u32[]{:S(2)}) collective-permute-start(bf16[2,240,2048]{2,1,0:T(8,128)(2,1)} %get-tuple-element.287), channel_id=1, source_target_pairs={{0,16},{8,24},{16,0},{24,8},{1,17},{9,25},{17,1},{25,9},{2,18},{10... | collective-permute-start | bytes 5898248 | tf_op jit(solution)/shard_map/ppermute | solution.py:49
  776.9 57.0 %collective-permute-start.36 = (bf16[2,240,2048]{2,1,0:T(8,128)(2,1)}, bf16[2,240,2048]{2,1,0:T(8,128)(2,1)S(1)}, u32[]{:S(2)}, u32[]{:S(2)}) collective-permute-start(bf16[2,240,2048]{2,1,0:T(8,128)(2,1)} %get-tuple-element.288), channel_id=1, source_target_pairs={{0,24},{8,16},{16,8},{24,0},{1,25},{9,17},{17,9},{25,1},{2,26},{10... | collective-permute-start | bytes 5898248 | tf_op jit(solution)/shard_map/ppermute | solution.py:49
  838.6 237.2 %reduce-scatter.6.cloned.1.call-start = ((), (), s32[]{:S(2)}) async-start(), calls=%async_computation.13 | async-start | bytes 7077888 | tf_op jit(solution)/shard_map/reduce_scatter | solution.py:43
  841.1 48.8 %collective-permute-start.38 = (bf16[2,512,1024]{2,1,0:T(8,128)(2,1)}, bf16[2,512,1024]{2,1,0:T(8,128)(2,1)}, u32[]{:S(2)}, u32[]{:S(2)}) collective-permute-start(bf16[2,512,1024]{2,1,0:T(8,128)(2,1)} %pad_maximum_fusion.11), channel_id=1, source_target_pairs={{0,16},{8,24},{16,0},{24,8},{1,17},{9,25},{17,1},{25,9},{2,18},{10... | collective-permute-start | bytes 6291464 | tf_op jit(solution)/shard_map/ppermute | solution.py:49
  842.9 90.3 %collective-permute-start.39 = (bf16[2,512,1024]{2,1,0:T(8,128)(2,1)}, bf16[2,512,1024]{2,1,0:T(8,128)(2,1)}, u32[]{:S(2)}, u32[]{:S(2)}) collective-permute-start(bf16[2,512,1024]{2,1,0:T(8,128)(2,1)} %pad_maximum_fusion.12), channel_id=1, source_target_pairs={{0,24},{8,16},{16,8},{24,0},{1,25},{9,17},{17,9},{25,1},{2,26},{10... | collective-permute-start | bytes 6291464 | tf_op jit(solution)/shard_map/ppermute | solution.py:49
  940.5 315.5 %reduce-scatter.8.cloned.1.call-start = ((), (), s32[]{:S(2)}) async-start(), calls=%async_computation.14 | async-start | bytes 7077888 | tf_op jit(solution)/shard_map/reduce_scatter | solution.py:43
  961.4 44.2 %collective-permute-start.40 = (bf16[2,512,1024]{2,1,0:T(8,128)(2,1)}, bf16[2,512,1024]{2,1,0:T(8,128)(2,1)}, u32[]{:S(2)}, u32[]{:S(2)}) collective-permute-start(bf16[2,512,1024]{2,1,0:T(8,128)(2,1)} %pad_maximum_fusion.14), channel_id=1, source_target_pairs={{0,8},{8,0},{16,24},{24,16},{1,9},{9,1},{17,25},{25,17},{2,10},{10... | collective-permute-start | bytes 6291464 | tf_op jit(solution)/shard_map/ppermute | solution.py:49
  961.4 48.7 %collective-permute-start.41 = (bf16[2,512,1024]{2,1,0:T(8,128)(2,1)}, bf16[2,512,1024]{2,1,0:T(8,128)(2,1)}, u32[]{:S(2)}, u32[]{:S(2)}) collective-permute-start(bf16[2,512,1024]{2,1,0:T(8,128)(2,1)} %pad_maximum_fusion.15), channel_id=1, source_target_pairs={{0,16},{8,24},{16,0},{24,8},{1,17},{9,25},{17,1},{25,9},{2,18},{10... | collective-permute-start | bytes 6291464 | tf_op jit(solution)/shard_map/ppermute | solution.py:49
  963.0 91.4 %collective-permute-start.42 = (bf16[2,512,1024]{2,1,0:T(8,128)(2,1)}, bf16[2,512,1024]{2,1,0:T(8,128)(2,1)}, u32[]{:S(2)}, u32[]{:S(2)}) collective-permute-start(bf16[2,512,1024]{2,1,0:T(8,128)(2,1)} %pad_maximum_fusion.16), channel_id=1, source_target_pairs={{0,24},{8,16},{16,8},{24,0},{1,25},{9,17},{17,9},{25,1},{2,26},{10... | collective-permute-start | bytes 6291464 | tf_op jit(solution)/shard_map/ppermute | solution.py:49
  1123.5 94.1 %collective-permute-start.52 = (bf16[2,512,1024]{2,1,0:T(8,128)(2,1)}, bf16[2,512,1024]{2,1,0:T(8,128)(2,1)}, u32[]{:S(2)}, u32[]{:S(2)}) collective-permute-start(bf16[2,512,1024]{2,1,0:T(8,128)(2,1)} %pad_maximum_fusion.18), channel_id=1, source_target_pairs={{0,8},{8,0},{16,24},{24,16},{1,9},{9,1},{17,25},{25,17},{2,10},{10... | collective-permute-start | bytes 6291464 | tf_op jit(solution)/shard_map/ppermute | solution.py:49
  1123.6 94.1 %collective-permute-start.53 = (bf16[2,512,1024]{2,1,0:T(8,128)(2,1)}, bf16[2,512,1024]{2,1,0:T(8,128)(2,1)}, u32[]{:S(2)}, u32[]{:S(2)}) collective-permute-start(bf16[2,512,1024]{2,1,0:T(8,128)(2,1)} %pad_maximum_fusion.19), channel_id=1, source_target_pairs={{0,16},{8,24},{16,0},{24,8},{1,17},{9,25},{17,1},{25,9},{2,18},{10... | collective-permute-start | bytes 6291464 | tf_op jit(solution)/shard_map/ppermute | solution.py:49
  1125.2 92.4 %collective-permute-start.54 = (bf16[2,512,1024]{2,1,0:T(8,128)(2,1)}, bf16[2,512,1024]{2,1,0:T(8,128)(2,1)}, u32[]{:S(2)}, u32[]{:S(2)}) collective-permute-start(bf16[2,512,1024]{2,1,0:T(8,128)(2,1)} %pad_maximum_fusion.20), channel_id=1, source_target_pairs={{0,24},{8,16},{16,8},{24,0},{1,25},{9,17},{17,9},{25,1},{2,26},{10... | collective-permute-start | bytes 6291464 | tf_op jit(solution)/shard_map/ppermute | solution.py:49
  1153.1 63.4 %collective-permute-start.51 = (f32[768]{0:T(1024)S(1)}, f32[768]{0:T(1024)S(1)}, u32[]{:S(2)}, u32[]{:S(2)}) collective-permute-start(f32[768]{0:T(1024)S(1)} %pad_maximum_fusion.35), channel_id=1, source_target_pairs={{0,24},{8,16},{16,8},{24,0},{1,25},{9,17},{17,9},{25,1},{2,26},{10... | collective-permute-start | bytes 9224 | tf_op jit(solution)/shard_map/ppermute | solution.py:49
  1156.7 60.3 %collective-permute-start.50 = (f32[768]{0:T(1024)S(1)}, f32[768]{0:T(1024)S(1)}, u32[]{:S(2)}, u32[]{:S(2)}) collective-permute-start(f32[768]{0:T(1024)S(1)} %pad_maximum_fusion.35), channel_id=1, source_target_pairs={{0,16},{8,24},{16,0},{24,8},{1,17},{9,25},{17,1},{25,9},{2,18},{10... | collective-permute-start | bytes 9224 | tf_op jit(solution)/shard_map/ppermute | solution.py:49
  (147 other events, 3766.2 us)
Sparse Core Ops, SparseCore 0:
  15.4 103.4 all-gather.5
  143.5 76.2 all-gather.9
  221.8 98.1 all-gather.7
  321.9 98.1 all-gather.11
  700.9 133.8 reduce-scatter.3
  838.7 101.7 all-gather.13
  944.7 116.5 reduce-scatter.5
  1086.3 118.5 reduce-scatter.7

commit v3 on v2

--- a/solution.py
+++ b/solution.py
@@ -363,6 +363,60 @@
     )(x, c, slot_gate, w, wd)
 
 
+def combine_kernel(*refs):
+    rank_ref, out_ref = refs[0], refs[-1]
+    pieces = refs[1:-1]
+    total = 0.0
+    for i, piece in enumerate(pieces):
+        shape = (piece.shape[0], out_ref.shape[0])
+        slots = lax.broadcasted_iota(jnp.int32, shape, 0)
+        hits = (slots == rank_ref[i : i + 1, :]).astype(BF16)
+        total = total + contract_first(hits, piece[...])
+    out_ref[...] = total.astype(BF16)
+
+
+def combine(ranks, pieces, block=256):
+    rows = ranks.shape[1]
+    width = 1024
+    whole = lambda a: pl.BlockSpec((a.shape[0], width), lambda j, i: (0, j))
+    return pl.pallas_call(
+        combine_kernel,
+        name="combine",
+        grid=(D // width, rows // block),
+        in_specs=[pl.BlockSpec((len(pieces), block), lambda j, i: (0, i))]
+        + [whole(piece) for piece in pieces],
+        out_specs=pl.BlockSpec((block, width), lambda j, i: (i, j)),
+        out_shape=jax.ShapeDtypeStruct((rows, D), BF16),
+        cost_estimate=cost(1000, 1000),
+    )(ranks, *pieces)
+
+
+def place_kernel(at_ref, *refs):
+    out_ref = refs[-1]
+    for i, piece in enumerate(refs[:-1]):
+        experts, _, units = piece.shape
+        first, unit = at_ref[2 * i], pl.multiple_of(at_ref[2 * i + 1], 128)
+        for e in range(experts):
+            out_ref[first + e, :, pl.ds(unit, units)] = piece[e].astype(F32)
+
+
+def place(places, pieces, experts, units, block=64):
+    rows = pieces[0].shape[1]
+    spec = lambda a: pl.BlockSpec((a.shape[0], block, a.shape[2]), lambda i, at: (0, i, 0))
+    return pl.pallas_call(
+        place_kernel,
+        name="place",
+        grid_spec=pltpu.PrefetchScalarGridSpec(
+            num_scalar_prefetch=1,
+            grid=(rows // block,),
+            in_specs=[spec(piece) for piece in pieces],
+            out_specs=pl.BlockSpec((experts, block, units), lambda i, at: (0, i, 0)),
+        ),
+        out_shape=jax.ShapeDtypeStruct((experts, rows, units), F32),
+        cost_estimate=cost(1000, 1000),
+    )(places, *pieces)
+
+
 def body(
     hidden_in,
     token_order,
@@ -395,6 +449,7 @@
     core = row % 2
     steps = range(n_row)
     peers = [row ^ step for step in steps]
+    near, far = list(steps)[:2], list(steps)[2:]
     rows_local = D // n_row
     unit_count = hidden_units // unit_split
     places = jnp.arange(tok_count, dtype=jnp.int32)
@@ -454,6 +509,7 @@
                     w_in[e] = lax.dynamic_update_slice(w_in[e], pieces[step][i], at)
                 else:
                     w_back[e] = lax.dynamic_update_slice(w_back[e], pieces[step][i], at)
+        return pieces
 
     def tied(value):
         value, w_in[:], w_back[:] = lax.optimization_barrier((value, w_in[:], w_back[:]))
@@ -462,10 +518,11 @@
     first_parts, second_parts = all_parts[:per_device], all_parts[per_device : per_device + 1]
     third_parts = all_parts[per_device + 1 : 2 * per_device + 1]
     last_parts = all_parts[2 * per_device + 1 :]
-    to_owner(first_parts, slices(first_parts))
+    first_pieces = to_owner(first_parts, slices(first_parts))
     second_pieces = after(slices(second_parts), *w_in)
     later = [slices(parts) for parts in (third_parts, last_parts)]
-    gathered, second_pieces, later = tied((gathered, second_pieces, later))
+    far_bases = far[::2]
+    gathered, second_pieces, later, cot_b = tied((gathered, second_pieces, later, cot_b))
     gains = gathered[tok_count : tok_count + 6].astype(F32).reshape(2, 3, D).sum(axis=1)
 
     expert_ids = jnp.arange(E, dtype=jnp.int32)
@@ -486,6 +543,8 @@
         for e in range(per_device)
     ]
     picks = [[hit.astype(BF16) for hit in hits[e]] for e in range(per_device)]
+
+    far_ranks = {base: trade(slot_rank.astype(F32), base, n_row) for base in far_bases}
 
     def swap_small(pieces):
         table = jnp.zeros((n_row,) + pieces[0].shape, pieces[0].dtype)
@@ -508,20 +567,24 @@
 
     half = D // 2
     out_half = lax.dynamic_slice_in_dim(w_out_own, core * half, half, 0)
-    out_half_all = gather_features(after(out_half, *w_in))
+    out_half_all = gather_features(after(out_half, *first_pieces[:-1]))
 
     to_owner(second_parts, second_pieces)
     attended_b = tied(attended_b)
-    attended_all = gather_features(attended_b)
-    to_owner(third_parts, later[0], attended_b)
+    attended_all = gather_features(after(attended_b, out_half_all))
+    far_cots = [trade(after(cot_b, *w_in), base, n_row) for base in far_bases]
+    to_owner(third_parts, later[0], attended_b, far_cots)
     other_half = trade(after(out_half_all, *w_back), 1, n_row)
-    cot_all = gather_features(after(cot_b, attended_all))
+    cot_alls = {
+        base: gather_features(after(cot, w_back[0])) for base, cot in zip(far_bases, far_cots)
+    }
     attended_all = tied(attended_all)
     if last_parts:
         to_owner(last_parts, later[1], w_back[0])
     normed2, scale_mid, mixed = run_branch(
         core, col, gathered, attended_all, out_half_all, other_half, gains[1:], feat_local
     )
+    cot_alls[0] = gather_features(after(cot_b, normed2))
     column_start = col * feat_local
 
     def chosen_rows(e, values):
@@ -530,9 +593,25 @@
     sent_rows = [chosen_rows(e, normed2) for e in range(per_device)]
     sent_rows[0] = tied(sent_rows[0])
     all_rows = [trade_all(pieces) for pieces in sent_rows]
-    sent_grads = [chosen_rows(e, cot_all) for e in range(per_device)]
-    all_rows, sent_grads = lax.optimization_barrier((all_rows, sent_grads))
-    all_grad_rows = [trade_all(pieces) for pieces in sent_grads]
+
+    def grad_rows_of(base, cots):
+        table = far_ranks[base] if base else slot_rank.astype(F32)
+        halves = []
+        for step in near:
+            held = []
+            for e in range(per_device):
+                pick = (of_peer(table, step, e) == slots[:, None].astype(F32)).astype(BF16)
+                held.append(plain_dot(pick, cots, BF16))
+            halves.append(jnp.stack(held))
+        return halves
+
+    grad_rows_at = {}
+
+    def hand_on(base, halves):
+        grad_rows_at[base], grad_rows_at[base + 1] = halves[0], trade(halves[1], 1, n_row)
+
+    for base in far_bases:
+        hand_on(base, grad_rows_of(base, after(cot_alls[base], sent_rows)))
 
     logits = lax.dot_general(
         router_all, normed2, (((0,), (1,)), ((), ())), preferred_element_type=F32
@@ -551,28 +630,58 @@
         slot_gates.append(jnp.stack(held))
     slot_gates = swap_small(slot_gates)
 
-    near, far = list(steps)[:2], list(steps)[2:]
-    branch_back, grads_back, scalars, weight_grads = [], [], [], []
+    both = range(per_device)
+    calls, grads_back = {}, [[None] * n_row for e in range(per_device)]
+
+    def expert_call(e, held):
+        rows = jnp.concatenate([all_rows[e][step] for step in held])
+        grad_rows = jnp.concatenate([grad_rows_at[step][e] for step in held])
+        slot_gate = jnp.concatenate([slot_gates[step][e] for step in held])[:, None]
+        results = run_expert(rows, grad_rows, slot_gate, w_in[e], w_back[e], 2 * capacity)
+        calls[e, held[0]] = [rows, grad_rows, *results]
+
+    def send_back(e, held):
+        grads = calls[e, held[0]][-1]
+        for i, step in enumerate(held):
+            piece = grads[i * capacity : (i + 1) * capacity]
+            grads_back[e][step] = trade(piece, step, n_row)
+
+    expert_call(0, far)
+    send_back(0, far)
+    for e in range(1, per_device):
+        all_rows[e] = after(all_rows[e], calls[0, 2])
+        expert_call(e, far)
+    near_halves = grad_rows_of(0, after(cot_alls[0], [calls[e, 2] for e in both]))
+    for e in range(1, per_device):
+        calls[e, 2], grads_back[e - 1], near_halves = lax.optimization_barrier(
+            (calls[e, 2], grads_back[e - 1], near_halves)
+        )
+        send_back(e, far)
+    hand_on(0, near_halves)
     for e in range(per_device):
-        rows, grad_rows, act, grad_pre, sums, grad_slot_rows = [], [], [], [], [], []
-        for held in (near, far):
-            rows.append(jnp.concatenate([all_rows[e][step] for step in held]))
-            grad_rows.append(jnp.concatenate([all_grad_rows[e][step] for step in held]))
-            slot_gate = jnp.concatenate([slot_gates[step][e] for step in held])[:, None]
-            results = run_expert(
-                rows[-1], grad_rows[-1], slot_gate, w_in[e], w_back[e], 2 * capacity
-            )
-            for total, result in zip((act, grad_pre, sums), results):
-                total.append(result)
-            grad_slot_rows += [
-                results[3][i * capacity : (i + 1) * capacity] for i in range(len(held))
-            ]
-        rows, grad_rows, act, grad_pre, sums = (
-            jnp.concatenate(parts) for parts in (rows, grad_rows, act, grad_pre, sums)
+        expert_call(e, near)
+        send_back(e, near)
+    last_near = (per_device - 1, 0)
+    calls[last_near], grads_back[-1] = lax.optimization_barrier((calls[last_near], grads_back[-1]))
+    scalars = [jnp.concatenate([calls[e, 0][4], calls[e, 2][4]]) for e in range(per_device)]
+    scalars = jnp.stack(scalars)
+    scalars_back = swap_small(
+        [scalars[:, step * capacity : (step + 1) * capacity] for step in steps]
+    )
+    every = [(e, step) for e in range(per_device) for step in steps]
+    ranks = jnp.concatenate([of_peer(slot_rank, step, e) for e, step in every])
+    grad_normed2_part = combine(ranks, [grads_back[e][step] for e, step in every])
+
+    calls = after(calls, grad_normed2_part)
+    branch_back, weight_grads = [], []
+    for e in range(per_device):
+        rows, grad_rows, act, grad_pre = (
+            jnp.concatenate([calls[e, 0][i], calls[e, 2][i]]) for i in range(4)
         )
-        scalars.append(sums)
-        grads_back.append(trade_all(grad_slot_rows))
-        branch_back.append(contract_last(act, w_back[e], BF16))
+        out = contract_last(act, w_back[e], BF16)
+        branch_back.append(
+            trade_all([out[step * capacity : (step + 1) * capacity] for step in steps])
+        )
         grad_in = contract_first(rows, grad_pre, BF16)
         weight_grads.append(
             (
@@ -581,29 +690,6 @@
                 contract_first(grad_rows, act, BF16),
             )
         )
-    scalars = jnp.stack(scalars)
-    scalars_back = swap_small(
-        [scalars[:, step * capacity : (step + 1) * capacity] for step in steps]
-    )
-    branch_back = jnp.stack(branch_back)
-    out_pieces = [branch_back[:, step * capacity : (step + 1) * capacity] for step in steps]
-
-    def to_tokens(back, which):
-        return contract_first(
-            jnp.concatenate([picks[e][step] for e, step in which]),
-            jnp.concatenate([back[e][step] for e, step in which]),
-        )
-
-    every = [(e, step) for e in range(per_device) for step in steps]
-    late = [(per_device - 1, step) for step in far]
-    early = [pair for pair in every if pair not in late]
-    grad_normed2_part = to_tokens(grads_back, early)
-    grads_back, out_pieces, grad_normed2_part = lax.optimization_barrier(
-        (grads_back, out_pieces, grad_normed2_part)
-    )
-    grad_normed2_part = (grad_normed2_part + to_tokens(grads_back, late)).astype(BF16)
-    branch_back = trade_all(out_pieces)
-    branch_back = [[piece[e] for piece in branch_back] for e in range(per_device)]
     grad_normed2 = scatter_partial(grad_normed2_part).astype(F32)
 
     grad_own = jnp.zeros((local_experts, tok_count), F32)
@@ -619,9 +705,11 @@
                 jnp.where(hits[e][step], back[:, 1:], 0.0), axis=0, keepdims=True
             )
     small = jnp.concatenate([grad_own, inner_own], axis=0)
+    small, branch_back[0] = lax.optimization_barrier((small, branch_back[0]))
     small = lax.all_to_all(
         jnp.broadcast_to(small[None], (n_col,) + small.shape), "col", 0, 0, tiled=True
     )
+    small, branch_back = lax.optimization_barrier((small, branch_back))
     grad_gates = small[:, :local_experts].reshape(E, tok_count)
     grad_logits = gate_probs * (
         grad_gates - jnp.sum(gate_probs * grad_gates, axis=0, keepdims=True)
@@ -642,43 +730,52 @@
     grad_norm2 = jnp.sum(grad_unit_mid * unit_mid, axis=0)
     scaled_mid = grad_unit_mid * norm2_gain
     grad_mixed = cot_b.astype(F32) + scale_mid * (scaled_mid - unit_mid * inner_mid)
-    def held_slices(which):
+    def held_slices(which, experts):
         return [
             jnp.stack(
                 [
                     lax.dynamic_slice_in_dim(
                         weight_grads[e][which], peers[step] * rows_local, rows_local, 0
                     )
-                    for e in range(per_device)
+                    for e in experts
                 ]
             )
             for step in steps
         ]
 
-    gate_slices, up_slices = held_slices(0), held_slices(1)
-    grad_mixed_b, branch_back, gate_slices, up_slices = lax.optimization_barrier(
-        (grad_mixed.astype(BF16), branch_back, gate_slices, up_slices)
-    )
-    grad_branch = gather_features(grad_mixed_b)
-
     def to_holders(pieces, *earlier):
         return trade_all(after(pieces, *earlier))
 
+    gate_slices, up_slices = held_slices(0, both), held_slices(1, both)
+    grad_mixed_b, gate_slices, up_slices, inverse = lax.optimization_barrier(
+        (grad_mixed.astype(BF16), gate_slices, up_slices, inverse)
+    )
+    grad_branch = gather_features(grad_mixed_b)
+    gate_pieces = to_holders(gate_slices)
+
     def to_rows(pieces):
-        grad = jnp.zeros((local_experts, rows_local, hidden_units), F32)
-        for step in steps:
-            grad = lax.dynamic_update_slice(grad, pieces[step].astype(F32), owned_at(peers[step]))
-        return grad
+        flat, places = [], []
+        for e, held in enumerate(pieces):
+            for step in steps:
+                first, _, unit = owned_at(peers[step])
+                flat.append(held[step])
+                places += [first + e, unit]
+        return place(jnp.stack(places), flat, local_experts, hidden_units)
 
     def sum_groups(grad, *earlier):
+        grad = after(grad, *earlier)
         parts = [
             lax.dynamic_slice_in_dim(grad, peers[step] * rows_local, rows_local, 0)
             for step in steps
         ]
-        return sum(part.astype(F32) for part in to_holders(parts, *earlier))
-
-    gate_pieces = to_holders(gate_slices)
-    combined_part = to_tokens(branch_back, every).astype(BF16)
+        other = trade(jnp.stack(parts[1::2]), 1, n_row).astype(F32)
+        sums = [part.astype(F32) + other[i] for i, part in enumerate(parts[::2])]
+        total = sums[0]
+        for i, base in enumerate(far_bases):
+            total = total + trade(sums[i + 1].astype(grad.dtype), base, n_row).astype(F32)
+        return total
+
+    combined_part = combine(ranks, [branch_back[e][step] for e, step in every])
     grad_branch, gate_pieces, combined_part = lax.optimization_barrier(
         (grad_branch, gate_pieces, combined_part)
     )
@@ -687,22 +784,30 @@
     combined = scatter_partial(combined_part)
 
     grad_w_out = contract_first(grad_branch, attended_b, BF16)
-    grad_attended = plain_dot(grad_branch, w_out_own, BF16)
+    grad_w_gate = to_rows([gate_pieces])
+    grad_attended = plain_dot(after(grad_branch, grad_w_gate), w_out_own, BF16)
     grad_q, grad_k, grad_v, grad_query_gain, grad_key_gain = attend_back(
         query_rot, key_rot, values_b, grad_attended, log_totals, seg_q, seg_k, raw_qk,
         q_gain, k_gain, cosine, sine,
     )
     grad_qkv = jnp.concatenate([grad_q, grad_k, grad_v], axis=1)
-    grad_w_out = sum_groups(grad_w_out, up_pieces)
-    grad_router = sum_groups(grad_router, up_pieces).T
-    down_pieces = held_slices(2)
-    grad_qkv, up_pieces, combined, down_pieces, grad_w_out, grad_router = (
+    grad_w_out = sum_groups(grad_w_out)
+    grad_router = sum_groups(grad_router, grad_branch).T
+    down_slices = [held_slices(2, [e]) for e in range(per_device)]
+    grad_qkv, up_pieces, combined, down_slices, grad_w_out, grad_router = (
         lax.optimization_barrier(
-            (grad_qkv, up_pieces, combined, down_pieces, grad_w_out, grad_router)
+            (grad_qkv, up_pieces, combined, down_slices, grad_w_out, grad_router)
         )
     )
+    down_pieces = [to_holders(down_slices[0])]
     grad_normed1_part = contract_last(grad_qkv, w_qkv, BF16)
     grad_unit_in = scatter_partial(grad_normed1_part)
+    output = (mixed + combined.astype(F32)).astype(BF16)[inverse]
+    grad_w_up = to_rows([up_pieces])
+    grad_normed1_part, down_pieces, output, grad_w_up = lax.optimization_barrier(
+        (grad_normed1_part, down_pieces, output, grad_w_up)
+    )
+    down_pieces += [to_holders(held, down_pieces) for held in down_slices[1:]]
     inner_in = jnp.sum(
         grad_qkv.astype(F32) * jnp.concatenate([raw_qk, values_b.astype(F32)], axis=1), axis=1
     )
@@ -710,7 +815,6 @@
     unit_in = packed * scale_in
     unit_all = gathered[:tok_count].astype(F32) * scale_in
     grad_norm1 = jnp.sum(grad_normed1_part.astype(F32) * unit_all, axis=0)
-    down_pieces = to_holders(down_pieces, grad_normed1_part)
     def for_all(vector):
         return jnp.broadcast_to(vector[None], (n_col,) + vector.shape)
 
@@ -723,26 +827,26 @@
         ],
         axis=1,
     )
+    heads_grad = contract_first(normed1, grad_qkv, BF16)
+    vectors, down_pieces, heads_grad = lax.optimization_barrier(
+        (vectors, down_pieces, heads_grad)
+    )
     vectors = jnp.sum(lax.all_to_all(vectors, "col", 0, 0, tiled=True), axis=0)
     inner_in = vectors[:tok_count, None] / D
     vectors = jnp.concatenate([vectors[tok_count:], grad_norm2])
     vectors = sum(trade(vectors, step, n_row) for step in steps)
-    grad_unit_in, vectors, inner_in = lax.optimization_barrier(
-        (grad_unit_in, vectors, inner_in)
+    grad_heads = sum_groups(heads_grad)
+    grad_unit_in, vectors, inner_in, grad_heads = lax.optimization_barrier(
+        (grad_unit_in, vectors, inner_in, grad_heads)
     )
     grad_unit_in = grad_unit_in.astype(F32)
     scaled_in = grad_unit_in * norm1_gain
     grad_input = (grad_mixed + scale_in * (scaled_in - unit_in * inner_in))[inverse]
 
-    output = (mixed + combined.astype(F32)).astype(BF16)[inverse]
-
-    grad_heads = sum_groups(contract_first(normed1, grad_qkv, BF16), down_pieces)
     grad_w_query, grad_w_key, grad_w_value = (
         grad_heads[:, i * width_local : (i + 1) * width_local] for i in range(3)
     )
-    grad_w_gate, grad_w_up, grad_w_down = (
-        to_rows(pieces) for pieces in (gate_pieces, up_pieces, down_pieces)
-    )
+    grad_w_down = to_rows(down_pieces)
 
     grad_query_gain, grad_key_gain = vectors[:DH], vectors[DH : 2 * DH]
     grad_norm1 = vectors[2 * DH : 2 * DH + feat_local]

time: 1290 us -> 1160 us (0.90)
  waiting for transfers between devices: 556 us -> 447 us
  Pallas kernels: 154 us -> 227 us
  other arithmetic: 141 us -> 76.4 us
  matrix products: 169 us -> 138 us
    ppermute x58 -> x59, waiting for transfers between devices: 487 us -> 382 us  [trade(): return lax.ppermute(value, 'row', [(r, r ^ step) for r in range(n_row)])]
    pallas_call x0 -> x5, Pallas kernels: none -> 72.4 us  [the longest x2 39.8 us: combine(): pl.pallas_call(combine_kernel, name='combine', grid=(D // width, rows //...]
    dot_general x9 -> x6, matrix products: 87.1 us -> 47.6 us  [contract_first(): lax.dot_general(left_op, right_op, (((0,), (0,)), ((), ())), preferred_el...]
    dynamic_update_slice x12 -> x0, other arithmetic: 36.7 us -> none  [to_rows(): lax.dynamic_update_slice(grad, pieces[step].astype(F32), owned_at(peers[s...]
    all_gather x5 -> x6, waiting for transfers between devices: 37.3 us -> 18.1 us  [gather_features(): return lax.all_gather(local_rows, 'col', axis=1, tiled=True)]
    concatenate x13 -> x8, other arithmetic: 23 us -> 6.18 us  [the longest x4 5.88 us: expert_call(): grad_rows = jnp.concatenate([grad_rows_at[step][e] for step in held])]
    another operation x6 -> x8, local copies, waits for them, and re-layouts: 28.2 us -> 12.2 us
    all_to_all x2, waiting for transfers between devices: 6.63 us -> 19.9 us  [swap_small(): table = lax.all_to_all(table, 'row', 0, 0, tiled=True)]
  transfers between devices with their start and end apart: 70 -> 72, of which waited for: 30 -> 27; matrix products, arithmetic and copies ran while one was open for 35% -> 31% of each run, Pallas kernels for 11% -> 18%
where the time goes in v3:
time: 1160 us; the launch traced here: 1150 us
  waiting for transfers between devices  447 us (39%)
  Pallas kernels  227 us (20%)
  local copies, waits for them, and re-layouts  189 us (16%)
  matrix products  138 us (12%)
  other arithmetic  76.4 us (7%)
  starting transfers between devices  56.7 us (5%)
  between operations  16.2 us (1%)
    ppermute x59, waiting for transfers between devices, trade(): return lax.ppermute(value, 'row', [(r, r ^ step) for r in range(n_row)])  382 us
    pallas_call x4, Pallas kernels, run_expert(): pl.pallas_call(expert_kernel, name='expert', grid=(rows // block,), in_sp...  73.4 us
    dot_general x18, matrix products, plain_dot(): return jnp.dot(left_op, right_op, preferred_element_type=F32).astype(kind)  56.5 us
    dot_general x6, matrix products, contract_first(): lax.dot_general(left_op, right_op, (((0,), (0,)), ((), ())), preferred_el...  47.6 us
    ppermute x59, starting transfers between devices, trade(): return lax.ppermute(value, 'row', [(r, r ^ step) for r in range(n_row)])  40.3 us
    pallas_call x2, Pallas kernels, combine(): pl.pallas_call(combine_kernel, name='combine', grid=(D // width, rows //...  39.8 us
    pallas_call x3, Pallas kernels, place(): pl.pallas_call(place_kernel, name='place', grid_spec=pltpu.PrefetchScalar...  32.7 us
    pallas_call x1, Pallas kernels, attend_back(): pl.pallas_call(attend_back_kernel, name='attend_back', grid=(heads, rows...  27.5 us
  transfers between devices with their start and end apart: 72, of which 27 were waited for; matrix products, arithmetic and copies ran while one was open for 31% of the time, Pallas kernels for 18%

profile of v3, /device:TPU:0, one launch (start us, length us, event | category | flops | bytes accessed | tf_op | source)
XLA Modules:
  0.0 1150.7 jit_solution(4403171276145332259)
XLA Ops:
  30.7 16.0 %collective-permute-done.4 = bf16[512,1088]{0,1:T(8,128)(2,1)} collective-permute-done((bf16[512,1088]{0,1:T(8,128)(2,1)}, bf16[512,1088]{0,1:T(8,128)(2,1)}, u32[]{:S(2)}, u32[]{:S(2)}) %collective-permute-start.4) | collective-permute-done | bytes 1114144 | tf_op jit(solution)/shard_map/ppermute | solution.py:49
  61.0 29.8 %collective-permute-done.1 = bf16[2,512,1024]{2,1,0:T(8,128)(2,1)} collective-permute-done((bf16[2,512,1024]{2,1,0:T(8,128)(2,1)}, bf16[2,512,1024]{2,1,0:T(8,128)(2,1)}, u32[]{:S(2)}, u32[]{:S(2)}) %collective-permute-start.1) | collective-permute-done | bytes 2097184 | tf_op jit(solution)/shard_map/ppermute | solution.py:49
  97.4 6.0 constant_dynamic-slice_fusion.41
  109.4 15.6 %gather_fusion.1 = bf16[1536,256]{1,0:T(8,128)(2,1)S(1)} fusion(bf16[1536,256]{1,0:T(8,128)(2,1)S(1)} %copy-done.3, s32[2048]{0:T(1024)S(1)} %pad_clamp_fusion.1), kind=kCustom, calls=%fused_computation.1 | custom fusion | bytes 1579008 | tf_op jit(solution)/shard_map/gather | solution.py:463
  154.7 14.1 %project.1 = (bf16[1536,2048]{1,0:T(8,128)(2,1)}, f32[1536,1]{1,0:T(8,128)}, f32[1536,512]{1,0:T(8,128)}, bf16[1536,256]{1,0:T(8,128)(2,1)}, bf16[1536,256]{1,0:T(8,128)(2,1)}, /*index=5*/bf16[1536,256]{1,0:T(8,128)(2,1)}) custom-call(bf16[1552,2048]{1,0:T(8,128)(2,1)} %all-gather.7.cloned.1.call-done.x_ref, f32[1,2048]{1,0:T(1,128)} %get-tuple-element.630.gain_ref, ...), custom_call_target="tpu_custom_call" | custom-call | flops 1000 | bytes 1000 | tf_op jit(solution)/shard_map/project/pallas_call | solution.py:117
  168.7 16.7 %attend.1 = (bf16[1536,256]{1,0:T(8,128)(2,1)}, f32[2,1536,1]{2,1,0:T(8,128)}) custom-call(bf16[1536,256]{1,0:T(8,128)(2,1)} %get-tuple-element.243.q_ref, bf16[1536,256]{1,0:T(8,128)(2,1)} %get-tuple-element.244.k_ref, bf16[1536,256]{1,0:T(8,128)(2,1)} %get-tuple-element.245.v_ref, s32[1536,1]{1,0:T(8,128)} %broadcast_in_dim.654.seg_q_ref, ...), custom_call_target="tpu_custom_call" | custom-call | flops 1000 | bytes 1000 | tf_op jit(solution)/shard_map/attend/pallas_call | solution.py:167
  191.1 7.7 collective-permute-done.8
  201.7 19.7 %collective-permute-done.9 = bf16[1536,256]{1,0:T(8,128)(2,1)S(1)} collective-permute-done((bf16[1536,256]{1,0:T(8,128)(2,1)S(1)}, bf16[1536,256]{1,0:T(8,128)(2,1)S(1)}, u32[]{:S(2)}, u32[]{:S(2)}) %collective-permute-start.9) | collective-permute-done | bytes 786464 | tf_op jit(solution)/shard_map/ppermute | solution.py:49
  230.2 39.9 %collective-permute-done.11 = bf16[2,512,1024]{2,1,0:T(8,128)(2,1)S(1)} collective-permute-done((bf16[2,512,1024]{2,1,0:T(8,128)(2,1)}, bf16[2,512,1024]{2,1,0:T(8,128)(2,1)S(1)}, u32[]{:S(2)}, u32[]{:S(2)}) %collective-permute-start.11) | collective-permute-done | bytes 2097184 | tf_op jit(solution)/shard_map/ppermute | solution.py:49
  271.6 42.6 %collective-permute-done.12 = bf16[2,512,1024]{2,1,0:T(8,128)(2,1)S(1)} collective-permute-done((bf16[2,512,1024]{2,1,0:T(8,128)(2,1)}, bf16[2,512,1024]{2,1,0:T(8,128)(2,1)S(1)}, u32[]{:S(2)}, u32[]{:S(2)}) %collective-permute-start.12) | collective-permute-done | bytes 2097184 | tf_op jit(solution)/shard_map/ppermute | solution.py:49
  323.3 23.2 %branch.1 = (bf16[1536,2048]{1,0:T(8,128)(2,1)}, f32[1536,1]{1,0:T(8,128)}, f32[1536,256]{1,0:T(8,128)}) custom-call(s32[2]{0:T(128)} %pad_add_fusion.at_ref, bf16[1552,2048]{1,0:T(8,128)(2,1)} %all-gather.7.cloned.1.call-done.x_ref, bf16[1536,2048]{1,0:T(8,128)(2,1)} %all-gather.11.cloned.1.call-done.att_ref, ...), custom_call_target="tpu_custom_call" | custom-call | flops 1000 | bytes 1000 | tf_op jit(solution)/shard_map/branch/pallas_call | solution.py:305
  358.4 5.8 convolution_convert_fusion.21
  389.2 6.5 all-to-all-done
  404.1 12.1 %all-gather.13.cloned.1.call-done = bf16[1536,2048]{1,0:T(8,128)(2,1)} async-done(((bf16[1536,256]{1,0:T(8,128)(2,1)}), bf16[1536,2048]{1,0:T(8,128)(2,1)}) %all-gather.13.cloned.1.call-update) | async-done | bytes 6291472 | tf_op jit(solution)/shard_map/all_gather | solution.py:39
  427.9 9.9 collective-permute-done.21
  440.0 17.6 %collective-permute-done.22 = bf16[240,2048]{1,0:T(8,128)(2,1)} collective-permute-done((bf16[240,2048]{1,0:T(8,128)(2,1)}, bf16[240,2048]{1,0:T(8,128)(2,1)}, u32[]{:S(2)}, u32[]{:S(2)}) %collective-permute-start.22) | collective-permute-done | bytes 983072 | tf_op jit(solution)/shard_map/ppermute | solution.py:49
  460.6 6.7 convolution_convert_fusion.12
  473.2 18.5 %expert.4 = (bf16[480,1024]{1,0:T(8,128)(2,1)}, bf16[480,2048]{1,0:T(8,128)(2,1)}, f32[480,2]{1,0:T(8,128)}, bf16[480,2048]{1,0:T(8,128)(2,1)}) custom-call(bf16[480,2048]{1,0:T(8,128)(2,1)} %copy-done.20, bf16[480,2048]{1,0:T(8,128)(2,1)} %pad_maximum_fusion.18.c_ref, f32[480,1]{1,0:T(8,128)} %copy.67.gate_ref, ...), custom_call_target="tpu_custom_call" | custom-call | flops 1000 | bytes 1000 | tf_op jit(solution)/shard_map/expert/pallas_call | solution.py:350
  500.6 18.3 %expert.5 = (bf16[480,1024]{1,0:T(8,128)(2,1)}, bf16[480,2048]{1,0:T(8,128)(2,1)}, f32[480,2]{1,0:T(8,128)}, bf16[480,2048]{1,0:T(8,128)(2,1)}) custom-call(bf16[480,2048]{1,0:T(8,128)(2,1)} %copy-done.23, bf16[480,2048]{1,0:T(8,128)(2,1)} %pad_maximum_fusion.19.c_ref, f32[480,1]{1,0:T(8,128)} %copy.68.gate_ref, ...), custom_call_target="tpu_custom_call" | custom-call | flops 1000 | bytes 1000 | tf_op jit(solution)/shard_map/expert/pallas_call | solution.py:350
  529.5 9.3 collective-permute-done.26.refs_4_
  549.4 18.2 %expert.7 = (bf16[480,1024]{1,0:T(8,128)(2,1)}, bf16[480,2048]{1,0:T(8,128)(2,1)}, f32[480,2]{1,0:T(8,128)}, bf16[480,2048]{1,0:T(8,128)(2,1)}) custom-call(bf16[480,2048]{1,0:T(8,128)(2,1)} %constant_dynamic-update-slice_fusion.10.x_ref, bf16[480,2048]{1,0:T(8,128)(2,1)} %pad_maximum_fusion.23.c_ref, f32[480,1]{1,0:T(8,128)} %copy.70.gate_ref, ...), custom_call_target="tpu_custom_call" | custom-call | flops 1000 | bytes 1000 | tf_op jit(solution)/shard_map/expert/pallas_call | solution.py:350
  572.9 18.4 %expert.6 = (bf16[480,1024]{1,0:T(8,128)(2,1)}, bf16[480,2048]{1,0:T(8,128)(2,1)}, f32[480,2]{1,0:T(8,128)}, bf16[480,2048]{1,0:T(8,128)(2,1)}) custom-call(bf16[480,2048]{1,0:T(8,128)(2,1)} %copy-done.22, bf16[480,2048]{1,0:T(8,128)(2,1)} %pad_maximum_fusion.22.c_ref, f32[480,1]{1,0:T(8,128)} %copy.69.gate_ref, ...), custom_call_target="tpu_custom_call" | custom-call | flops 1000 | bytes 1000 | tf_op jit(solution)/shard_map/expert/pallas_call | solution.py:350
  594.7 6.9 scatter_custom_fusion
  606.8 19.9 %combine.2 = bf16[1536,2048]{1,0:T(8,128)(2,1)} custom-call(s32[8,1536]{1,0:T(8,128)} %concatenate.137.refs_0_, bf16[240,2048]{1,0:T(8,128)(2,1)} %get-tuple-element.583.refs_1_, bf16[240,2048]{1,0:T(8,128)(2,1)} %collective-permute-done.28.refs_2_, bf16[240,2048]{1,0:T(8,128)(2,1)} %collective-permute-done.25.refs_3_, ...), custom_call_target="tpu_custom_call" | custom-call | flops 1000 | bytes 1000 | tf_op jit(solution)/shard_map/combine/pallas_call | solution.py:382
  628.3 7.5 convolution_convert_fusion.3
  639.1 7.5 convolution_convert_fusion.4
  655.0 11.4 convolution_convert_fusion.2
  669.1 11.5 convolution_convert_fusion.1
  691.2 13.4 %all-to-all-done.1 = f32[4,2,240,2]{2,3,1,0:T(2,128)S(1)} async-done(((f32[4,2,240,2]{2,3,1,0:T(2,128)}), f32[4,2,240,2]{2,3,1,0:T(2,128)S(1)}, u32[]{:S(2)}, u32[]{:S(2)}) %all-to-all-start.1) | async-done | bytes 15392 | tf_op jit(solution)/shard_map/all_to_all | solution.py:557
  709.6 6.0 all-to-all-start.2
  726.6 5.8 collective-permute-done.37.refs_8_
  732.4 24.2 %all-to-all-done.2 = f32[8,9,1536]{2,1,0:T(8,128)} async-done(((f32[8,9,1536]{2,1,0:T(8,128)}), f32[8,9,1536]{2,1,0:T(8,128)}, u32[]{:S(2)}, u32[]{:S(2)}) %all-to-all-start.2) | async-done | bytes 442400 | tf_op jit(solution)/shard_map/all_to_all | solution.py:709
  768.2 19.9 %combine.3 = bf16[1536,2048]{1,0:T(8,128)(2,1)} custom-call(s32[8,1536]{1,0:T(8,128)} %concatenate.137.refs_0_, bf16[240,2048]{1,0:T(8,128)(2,1)} %get-tuple-element.371.refs_1_, bf16[240,2048]{1,0:T(8,128)(2,1)} %collective-permute-done.32.refs_2_, bf16[240,2048]{1,0:T(8,128)(2,1)} %collective-permute-done.33.refs_3_, ...), custom_call_target="tpu_custom_call" | custom-call | flops 1000 | bytes 1000 | tf_op jit(solution)/shard_map/combine/pallas_call | solution.py:382
  788.1 27.1 %collective-permute-done.39.refs_2_ = bf16[2,512,1024]{2,1,0:T(8,128)(2,1)} collective-permute-done((bf16[2,512,1024]{2,1,0:T(8,128)(2,1)}, bf16[2,512,1024]{2,1,0:T(8,128)(2,1)}, u32[]{:S(2)}, u32[]{:S(2)}) %collective-permute-start.39) | collective-permute-done | bytes 2097184 | tf_op jit(solution)/shard_map/ppermute | solution.py:49
  815.1 44.0 %collective-permute-done.40.refs_3_ = bf16[2,512,1024]{2,1,0:T(8,128)(2,1)} collective-permute-done((bf16[2,512,1024]{2,1,0:T(8,128)(2,1)}, bf16[2,512,1024]{2,1,0:T(8,128)(2,1)}, u32[]{:S(2)}, u32[]{:S(2)}) %collective-permute-start.40) | collective-permute-done | bytes 2097184 | tf_op jit(solution)/shard_map/ppermute | solution.py:49
  859.2 6.0 all-gather.17.cloned.1.call-done
  865.8 7.4 fusion.22
  892.0 10.9 place.3
  903.0 5.9 convolution_convert_fusion.7.grad_ref
  908.9 27.5 %attend_back.1 = (bf16[1536,256]{1,0:T(8,128)(2,1)}, bf16[1536,256]{1,0:T(8,128)(2,1)}, bf16[1536,256]{1,0:T(8,128)(2,1)}, f32[1,128]{1,0:T(1,128)}, f32[1,128]{1,0:T(1,128)}) custom-call(bf16[1536,256]{1,0:T(8,128)(2,1)} %get-tuple-element.243.q_ref, bf16[1536,256]{1,0:T(8,128)(2,1)} %get-tuple-element.244.k_ref, ...), custom_call_target="tpu_custom_call" | custom-call | flops 1000 | bytes 1000 | tf_op jit(solution)/shard_map/attend_back/pallas_call | solution.py:250
  942.8 42.6 %collective-permute-done.47 = f32[512,64]{0,1:T(8,128)S(1)} collective-permute-done((f32[512,64]{0,1:T(8,128)S(1)}, f32[512,64]{0,1:T(8,128)S(1)}, u32[]{:S(2)}, u32[]{:S(2)}) %collective-permute-start.47) | collective-permute-done | bytes 131104 | tf_op jit(solution)/shard_map/ppermute | solution.py:49
  991.1 9.4 convolution_convert_fusion
  1006.2 10.8 place.4
  1027.3 10.0 convolution_convert_fusion.5
  1037.2 15.0 %collective-permute-done.50.refs_3_ = bf16[1,512,1024]{2,1,0:T(8,128)(2,1)} collective-permute-done((bf16[1,512,1024]{2,1,0:T(8,128)(2,1)}, bf16[1,512,1024]{2,1,0:T(8,128)(2,1)}, u32[]{:S(2)}, u32[]{:S(2)}) %collective-permute-start.50) | collective-permute-done | bytes 1048608 | tf_op jit(solution)/shard_map/ppermute | solution.py:49
  1057.8 21.4 %collective-permute-done.52.refs_6_ = bf16[1,512,1024]{2,1,0:T(8,128)(2,1)} collective-permute-done((bf16[1,512,1024]{2,1,0:T(8,128)(2,1)}, bf16[1,512,1024]{2,1,0:T(8,128)(2,1)}, u32[]{:S(2)}, u32[]{:S(2)}) %collective-permute-start.52) | collective-permute-done | bytes 1048608 | tf_op jit(solution)/shard_map/ppermute | solution.py:49
  1079.2 20.5 %collective-permute-done.53.refs_7_ = bf16[1,512,1024]{2,1,0:T(8,128)(2,1)} collective-permute-done((bf16[1,512,1024]{2,1,0:T(8,128)(2,1)S(1)}, bf16[1,512,1024]{2,1,0:T(8,128)(2,1)}, u32[]{:S(2)}, u32[]{:S(2)}) %collective-permute-start.53) | collective-permute-done | bytes 1048608 | tf_op jit(solution)/shard_map/ppermute | solution.py:49
  1115.0 10.9 place.5
  (617 shorter events, 358.3 us)
Async XLA Ops:
  7.2 143.1 %all-gather.7.cloned.1.call-start = ((), (), s32[]{:S(2)}) async-start(), calls=%async_computation.7 | async-start | bytes 7151616 | tf_op jit(solution)/shard_map/all_gather | solution.py:39
  15.9 185.1 %all-gather.9.cloned.1.call-start = ((), (), s32[]{:S(2)}) async-start(), calls=%async_computation.8 | async-start | bytes 4718592 | tf_op jit(solution)/shard_map/all_gather | solution.py:39
  30.2 60.6 %collective-permute-start.1 = (bf16[2,512,1024]{2,1,0:T(8,128)(2,1)}, bf16[2,512,1024]{2,1,0:T(8,128)(2,1)}, u32[]{:S(2)}, u32[]{:S(2)}) collective-permute-start(bf16[2,512,1024]{2,1,0:T(8,128)(2,1)} %get-tuple-element.236), channel_id=1, source_target_pairs={{0,16},{8,24},{16,0},{24,8},{1,17},{9,25},{17,1},{25,9},{2,18},{10... | collective-permute-start | bytes 6291464 | tf_op jit(solution)/shard_map/ppermute | solution.py:49
  90.9 230.2 %all-gather.11.cloned.1.call-start = ((), (), s32[]{:S(2)}) async-start(), calls=%async_computation.9 | async-start | bytes 7077888 | tf_op jit(solution)/shard_map/all_gather | solution.py:39
  90.9 56.3 %collective-permute-start.2 = (bf16[2,512,1024]{2,1,0:T(8,128)(2,1)}, bf16[2,512,1024]{2,1,0:T(8,128)(2,1)}, u32[]{:S(2)}, u32[]{:S(2)}) collective-permute-start(bf16[2,512,1024]{2,1,0:T(8,128)(2,1)} %get-tuple-element.237), channel_id=1, source_target_pairs={{0,24},{8,16},{16,8},{24,0},{1,25},{9,17},{17,9},{25,1},{2,26},{10... | collective-permute-start | bytes 6291464 | tf_op jit(solution)/shard_map/ppermute | solution.py:49
  150.3 36.3 %collective-permute-start.6 = (bf16[1,512,1024]{2,1,0:T(8,128)(2,1)}, bf16[1,512,1024]{2,1,0:T(8,128)(2,1)}, u32[]{:S(2)}, u32[]{:S(2)}) collective-permute-start(bf16[1,512,1024]{2,1,0:T(8,128)(2,1)} %get-tuple-element.254), channel_id=1, source_target_pairs={{0,8},{8,0},{16,24},{24,16},{1,9},{9,1},{17,25},{25,17},{2,10},{10... | collective-permute-start | bytes 3145736 | tf_op jit(solution)/shard_map/ppermute | solution.py:49
  151.9 36.9 %collective-permute-start.7 = (bf16[1,512,1024]{2,1,0:T(8,128)(2,1)}, bf16[1,512,1024]{2,1,0:T(8,128)(2,1)}, u32[]{:S(2)}, u32[]{:S(2)}) collective-permute-start(bf16[1,512,1024]{2,1,0:T(8,128)(2,1)} %get-tuple-element.255), channel_id=1, source_target_pairs={{0,16},{8,24},{16,0},{24,8},{1,17},{9,25},{17,1},{25,9},{2,18},{10... | collective-permute-start | bytes 3145736 | tf_op jit(solution)/shard_map/ppermute | solution.py:49
  152.1 46.7 %collective-permute-start.8 = (bf16[1,512,1024]{2,1,0:T(8,128)(2,1)}, bf16[1,512,1024]{2,1,0:T(8,128)(2,1)}, u32[]{:S(2)}, u32[]{:S(2)}) collective-permute-start(bf16[1,512,1024]{2,1,0:T(8,128)(2,1)} %get-tuple-element.256), channel_id=1, source_target_pairs={{0,24},{8,16},{16,8},{24,0},{1,25},{9,17},{17,9},{25,1},{2,26},{10... | collective-permute-start | bytes 3145736 | tf_op jit(solution)/shard_map/ppermute | solution.py:49
  201.1 215.2 %all-gather.13.cloned.1.call-start = ((), (), s32[]{:S(2)}) async-start(), calls=%async_computation.10 | async-start | bytes 7077888 | tf_op jit(solution)/shard_map/all_gather | solution.py:39
  221.4 48.6 %collective-permute-start.11 = (bf16[2,512,1024]{2,1,0:T(8,128)(2,1)}, bf16[2,512,1024]{2,1,0:T(8,128)(2,1)S(1)}, u32[]{:S(2)}, u32[]{:S(2)}) collective-permute-start(bf16[2,512,1024]{2,1,0:T(8,128)(2,1)} %get-tuple-element.272), channel_id=1, source_target_pairs={{0,16},{8,24},{16,0},{24,8},{1,17},{9,25},{17,1},{25,9},{2,18},{10... | collective-permute-start | bytes 6291464 | tf_op jit(solution)/shard_map/ppermute | solution.py:49
  221.8 92.4 %collective-permute-start.12 = (bf16[2,512,1024]{2,1,0:T(8,128)(2,1)}, bf16[2,512,1024]{2,1,0:T(8,128)(2,1)S(1)}, u32[]{:S(2)}, u32[]{:S(2)}) collective-permute-start(bf16[2,512,1024]{2,1,0:T(8,128)(2,1)} %get-tuple-element.273), channel_id=1, source_target_pairs={{0,24},{8,16},{16,8},{24,0},{1,25},{9,17},{17,9},{25,1},{2,26},{10... | collective-permute-start | bytes 6291464 | tf_op jit(solution)/shard_map/ppermute | solution.py:49
  315.7 203.1 %all-gather.15.cloned.1.call-start = ((), (), s32[]{:S(2)}) async-start(), calls=%async_computation.11 | async-start | bytes 7077888 | tf_op jit(solution)/shard_map/all_gather | solution.py:39
  346.6 49.1 %collective-permute-start.14 = (bf16[1,512,1024]{2,1,0:T(8,128)(2,1)}, bf16[1,512,1024]{2,1,0:T(8,128)(2,1)}, u32[]{:S(2)}, u32[]{:S(2)}) collective-permute-start(bf16[1,512,1024]{2,1,0:T(8,128)(2,1)} %get-tuple-element.289), channel_id=1, source_target_pairs={{0,8},{8,0},{16,24},{24,16},{1,9},{9,1},{17,25},{25,17},{2,10},{10... | collective-permute-start | bytes 3145736 | tf_op jit(solution)/shard_map/ppermute | solution.py:49
  346.9 51.1 %collective-permute-start.15 = (bf16[1,512,1024]{2,1,0:T(8,128)(2,1)}, bf16[1,512,1024]{2,1,0:T(8,128)(2,1)}, u32[]{:S(2)}, u32[]{:S(2)}) collective-permute-start(bf16[1,512,1024]{2,1,0:T(8,128)(2,1)} %get-tuple-element.290), channel_id=1, source_target_pairs={{0,16},{8,24},{16,0},{24,8},{1,17},{9,25},{17,1},{25,9},{2,18},{10... | collective-permute-start | bytes 3145736 | tf_op jit(solution)/shard_map/ppermute | solution.py:49
  347.5 52.8 %collective-permute-start.16 = (bf16[1,512,1024]{2,1,0:T(8,128)(2,1)}, bf16[1,512,1024]{2,1,0:T(8,128)(2,1)}, u32[]{:S(2)}, u32[]{:S(2)}) collective-permute-start(bf16[1,512,1024]{2,1,0:T(8,128)(2,1)} %get-tuple-element.291), channel_id=1, source_target_pairs={{0,24},{8,16},{16,8},{24,0},{1,25},{9,17},{17,9},{25,1},{2,26},{10... | collective-permute-start | bytes 3145736 | tf_op jit(solution)/shard_map/ppermute | solution.py:49
  384.7 378.0 %reduce-scatter.4.cloned.1.call-start = ((), (), s32[]{:S(2)}) async-start(), calls=%async_computation.12 | async-start | bytes 7077888 | tf_op jit(solution)/shard_map/reduce_scatter | solution.py:43
  384.8 106.9 %collective-permute-start.18 = (bf16[240,2048]{1,0:T(8,128)(2,1)}, bf16[240,2048]{1,0:T(8,128)(2,1)}, u32[]{:S(2)}, u32[]{:S(2)}) collective-permute-start(bf16[240,2048]{1,0:T(8,128)(2,1)} %convolution_convert_fusion.18), channel_id=1, source_target_pairs={{0,8},{8,0},{16,24},{24,16},{1,9},{9,1},{17,25},{25,17},{2,10},{10... | collective-permute-start | bytes 2949128 | tf_op jit(solution)/shard_map/ppermute | solution.py:49
  385.4 106.3 %collective-permute-start.19 = (bf16[240,2048]{1,0:T(8,128)(2,1)}, bf16[240,2048]{1,0:T(8,128)(2,1)}, u32[]{:S(2)}, u32[]{:S(2)}) collective-permute-start(bf16[240,2048]{1,0:T(8,128)(2,1)} %convolution_convert_fusion.17), channel_id=1, source_target_pairs={{0,16},{8,24},{16,0},{24,8},{1,17},{9,25},{17,1},{25,9},{2,18},{10... | collective-permute-start | bytes 2949128 | tf_op jit(solution)/shard_map/ppermute | solution.py:49
  402.6 35.2 %collective-permute-start.21 = (bf16[240,2048]{1,0:T(8,128)(2,1)S(1)}, bf16[240,2048]{1,0:T(8,128)(2,1)S(1)}, u32[]{:S(2)}, u32[]{:S(2)}) collective-permute-start(bf16[240,2048]{1,0:T(8,128)(2,1)S(1)} %copy-done.99), channel_id=1, source_target_pairs={{0,16},{8,24},{16,0},{24,8},{1,17},{9,25},{17,1},{25,9},{2,18},{10... | collective-permute-start | bytes 2949128 | tf_op jit(solution)/shard_map/ppermute | solution.py:49
  403.3 54.3 %collective-permute-start.22 = (bf16[240,2048]{1,0:T(8,128)(2,1)}, bf16[240,2048]{1,0:T(8,128)(2,1)}, u32[]{:S(2)}, u32[]{:S(2)}) collective-permute-start(bf16[240,2048]{1,0:T(8,128)(2,1)} %convolution_convert_fusion.20), channel_id=1, source_target_pairs={{0,24},{8,16},{16,8},{24,0},{1,25},{9,17},{17,9},{25,1},{2,26},{10... | collective-permute-start | bytes 2949128 | tf_op jit(solution)/shard_map/ppermute | solution.py:49
  424.2 45.0 %collective-permute-start.24 = (bf16[2,240,2048]{2,1,0:T(8,128)(2,1)}, bf16[2,240,2048]{2,1,0:T(8,128)(2,1)}, u32[]{:S(2)}, u32[]{:S(2)}) collective-permute-start(bf16[2,240,2048]{2,1,0:T(8,128)(2,1)} %pad_maximum_fusion.17), channel_id=1, source_target_pairs={{0,8},{8,0},{16,24},{24,16},{1,9},{9,1},{17,25},{25,17},{2,10},{10... | collective-permute-start | bytes 5898248 | tf_op jit(solution)/shard_map/ppermute | solution.py:49
  438.7 53.0 %collective-permute-start.20 = (bf16[240,2048]{1,0:T(8,128)(2,1)}, bf16[240,2048]{1,0:T(8,128)(2,1)}, u32[]{:S(2)}, u32[]{:S(2)}) collective-permute-start(bf16[240,2048]{1,0:T(8,128)(2,1)} %convolution_convert_fusion.16), channel_id=1, source_target_pairs={{0,24},{8,16},{16,8},{24,0},{1,25},{9,17},{17,9},{25,1},{2,26},{10... | collective-permute-start | bytes 2949128 | tf_op jit(solution)/shard_map/ppermute | solution.py:49
  457.6 82.1 %collective-permute-start.17 = (bf16[240,2048]{1,0:T(8,128)(2,1)}, bf16[240,2048]{1,0:T(8,128)(2,1)}, u32[]{:S(2)}, u32[]{:S(2)}) collective-permute-start(bf16[240,2048]{1,0:T(8,128)(2,1)} %convolution_convert_fusion.22), channel_id=1, source_target_pairs={{0,8},{8,0},{16,24},{24,16},{1,9},{9,1},{17,25},{25,17},{2,10},{10... | collective-permute-start | bytes 2949128 | tf_op jit(solution)/shard_map/ppermute | solution.py:49
  494.8 34.7 %collective-permute-start.25 = (bf16[240,2048]{1,0:T(8,128)(2,1)}, bf16[240,2048]{1,0:T(8,128)(2,1)}, u32[]{:S(2)}, u32[]{:S(2)}) collective-permute-start(bf16[240,2048]{1,0:T(8,128)(2,1)} %get-tuple-element.593), channel_id=1, source_target_pairs={{0,16},{8,24},{16,0},{24,8},{1,17},{9,25},{17,1},{25,9},{2,18},{10... | collective-permute-start | bytes 2949128 | tf_op jit(solution)/shard_map/ppermute | solution.py:49
  495.3 43.5 %collective-permute-start.26 = (bf16[240,2048]{1,0:T(8,128)(2,1)}, bf16[240,2048]{1,0:T(8,128)(2,1)}, u32[]{:S(2)}, u32[]{:S(2)}) collective-permute-start(bf16[240,2048]{1,0:T(8,128)(2,1)} %get-tuple-element.592), channel_id=1, source_target_pairs={{0,24},{8,16},{16,8},{24,0},{1,25},{9,17},{17,9},{25,1},{2,26},{10... | collective-permute-start | bytes 2949128 | tf_op jit(solution)/shard_map/ppermute | solution.py:49
  546.3 59.5 %collective-permute-start.30 = (bf16[240,2048]{1,0:T(8,128)(2,1)}, bf16[240,2048]{1,0:T(8,128)(2,1)}, u32[]{:S(2)}, u32[]{:S(2)}) collective-permute-start(bf16[240,2048]{1,0:T(8,128)(2,1)} %get-tuple-element.589), channel_id=1, source_target_pairs={{0,16},{8,24},{16,0},{24,8},{1,17},{9,25},{17,1},{25,9},{2,18},{10... | collective-permute-start | bytes 2949128 | tf_op jit(solution)/shard_map/ppermute | solution.py:49
  548.6 57.2 %collective-permute-start.31 = (bf16[240,2048]{1,0:T(8,128)(2,1)}, bf16[240,2048]{1,0:T(8,128)(2,1)}, u32[]{:S(2)}, u32[]{:S(2)}) collective-permute-start(bf16[240,2048]{1,0:T(8,128)(2,1)} %get-tuple-element.588), channel_id=1, source_target_pairs={{0,24},{8,16},{16,8},{24,0},{1,25},{9,17},{17,9},{25,1},{2,26},{10... | collective-permute-start | bytes 2949128 | tf_op jit(solution)/shard_map/ppermute | solution.py:49
  637.9 88.7 %collective-permute-start.35 = (bf16[240,2048]{1,0:T(8,128)(2,1)}, bf16[240,2048]{1,0:T(8,128)(2,1)}, u32[]{:S(2)}, u32[]{:S(2)}) collective-permute-start(bf16[240,2048]{1,0:T(8,128)(2,1)} %get-tuple-element.558), channel_id=1, source_target_pairs={{0,8},{8,0},{16,24},{24,16},{1,9},{9,1},{17,25},{25,17},{2,10},{10... | collective-permute-start | bytes 2949128 | tf_op jit(solution)/shard_map/ppermute | solution.py:49
  638.4 88.2 %collective-permute-start.36 = (bf16[240,2048]{1,0:T(8,128)(2,1)}, bf16[240,2048]{1,0:T(8,128)(2,1)}, u32[]{:S(2)}, u32[]{:S(2)}) collective-permute-start(bf16[240,2048]{1,0:T(8,128)(2,1)} %get-tuple-element.557), channel_id=1, source_target_pairs={{0,16},{8,24},{16,0},{24,8},{1,17},{9,25},{17,1},{25,9},{2,18},{10... | collective-permute-start | bytes 2949128 | tf_op jit(solution)/shard_map/ppermute | solution.py:49
  648.8 59.4 %collective-permute-start.32 = (bf16[240,2048]{1,0:T(8,128)(2,1)}, bf16[240,2048]{1,0:T(8,128)(2,1)}, u32[]{:S(2)}, u32[]{:S(2)}) collective-permute-start(bf16[240,2048]{1,0:T(8,128)(2,1)} %get-tuple-element.562), channel_id=1, source_target_pairs={{0,8},{8,0},{16,24},{24,16},{1,9},{9,1},{17,25},{25,17},{2,10},{10... | collective-permute-start | bytes 2949128 | tf_op jit(solution)/shard_map/ppermute | solution.py:49
  649.3 59.3 %collective-permute-start.33 = (bf16[240,2048]{1,0:T(8,128)(2,1)}, bf16[240,2048]{1,0:T(8,128)(2,1)}, u32[]{:S(2)}, u32[]{:S(2)}) collective-permute-start(bf16[240,2048]{1,0:T(8,128)(2,1)} %get-tuple-element.561), channel_id=1, source_target_pairs={{0,16},{8,24},{16,0},{24,8},{1,17},{9,25},{17,1},{25,9},{2,18},{10... | collective-permute-start | bytes 2949128 | tf_op jit(solution)/shard_map/ppermute | solution.py:49
  650.2 58.4 %collective-permute-start.34 = (bf16[240,2048]{1,0:T(8,128)(2,1)}, bf16[240,2048]{1,0:T(8,128)(2,1)}, u32[]{:S(2)}, u32[]{:S(2)}) collective-permute-start(bf16[240,2048]{1,0:T(8,128)(2,1)} %get-tuple-element.560), channel_id=1, source_target_pairs={{0,24},{8,16},{16,8},{24,0},{1,25},{9,17},{17,9},{25,1},{2,26},{10... | collective-permute-start | bytes 2949128 | tf_op jit(solution)/shard_map/ppermute | solution.py:49
  651.6 53.0 %all-to-all-start.1 = ((f32[4,2,240,2]{2,3,1,0:T(2,128)}), f32[4,2,240,2]{2,3,1,0:T(2,128)S(1)}, u32[]{:S(2)}, u32[]{:S(2)}) async-start(f32[4,2,240,2]{2,3,1,0:T(2,128)} %select_select_fusion), calls=%async_computation.2 | async-start | bytes 32768 | tf_op jit(solution)/shard_map/all_to_all | solution.py:557
  709.6 47.0 %all-to-all-start.2 = ((f32[8,9,1536]{2,1,0:T(8,128)}), f32[8,9,1536]{2,1,0:T(8,128)}, u32[]{:S(2)}, u32[]{:S(2)}) async-start(f32[8,9,1536]{2,1,0:T(8,128)} %broadcast_in_dim.647), calls=%async_computation.3 | async-start | bytes 1572864 | tf_op jit(solution)/shard_map/all_to_all | solution.py:709
  715.7 149.5 %all-gather.17.cloned.1.call-start = ((), (), s32[]{:S(2)}) async-start(), calls=%async_computation.13 | async-start | bytes 7077888 | tf_op jit(solution)/shard_map/all_gather | solution.py:39
  766.2 224.9 %reduce-scatter.6.cloned.1.call-start = ((), (), s32[]{:S(2)}) async-start(), calls=%async_computation.14 | async-start | bytes 7077888 | tf_op jit(solution)/shard_map/reduce_scatter | solution.py:43
  766.4 48.8 %collective-permute-start.39 = (bf16[2,512,1024]{2,1,0:T(8,128)(2,1)}, bf16[2,512,1024]{2,1,0:T(8,128)(2,1)}, u32[]{:S(2)}, u32[]{:S(2)}) collective-permute-start(bf16[2,512,1024]{2,1,0:T(8,128)(2,1)} %pad_maximum_fusion.11), channel_id=1, source_target_pairs={{0,16},{8,24},{16,0},{24,8},{1,17},{9,25},{17,1},{25,9},{2,18},{10... | collective-permute-start | bytes 6291464 | tf_op jit(solution)/shard_map/ppermute | solution.py:49
  767.7 91.4 %collective-permute-start.40 = (bf16[2,512,1024]{2,1,0:T(8,128)(2,1)}, bf16[2,512,1024]{2,1,0:T(8,128)(2,1)}, u32[]{:S(2)}, u32[]{:S(2)}) collective-permute-start(bf16[2,512,1024]{2,1,0:T(8,128)(2,1)} %pad_maximum_fusion.12), channel_id=1, source_target_pairs={{0,24},{8,16},{16,8},{24,0},{1,25},{9,17},{17,9},{25,1},{2,26},{10... | collective-permute-start | bytes 6291464 | tf_op jit(solution)/shard_map/ppermute | solution.py:49
  865.2 267.7 %reduce-scatter.8.cloned.1.call-start = ((), (), s32[]{:S(2)}) async-start(), calls=%async_computation.15 | async-start | bytes 7077888 | tf_op jit(solution)/shard_map/reduce_scatter | solution.py:43
  886.4 50.1 %collective-permute-start.46 = (f32[2,512,64]{1,2,0:T(8,128)}, f32[2,512,64]{1,2,0:T(8,128)S(1)}, u32[]{:S(2)}, u32[]{:S(2)}) collective-permute-start(f32[2,512,64]{1,2,0:T(8,128)} %pad_maximum_fusion.28), channel_id=1, source_target_pairs={{0,8},{8,0},{16,24},{24,16},{1,9},{9,1},{17,25},{25,17},{2,10},{10... | collective-permute-start | bytes 786440 | tf_op jit(solution)/shard_map/ppermute | solution.py:49
  888.4 102.6 %collective-permute-start.41 = (bf16[2,512,1024]{2,1,0:T(8,128)(2,1)}, bf16[2,512,1024]{2,1,0:T(8,128)(2,1)}, u32[]{:S(2)}, u32[]{:S(2)}) collective-permute-start(bf16[2,512,1024]{2,1,0:T(8,128)(2,1)} %pad_maximum_fusion.14), channel_id=1, source_target_pairs={{0,8},{8,0},{16,24},{24,16},{1,9},{9,1},{17,25},{25,17},{2,10},{10... | collective-permute-start | bytes 6291464 | tf_op jit(solution)/shard_map/ppermute | solution.py:49
  889.0 102.1 %collective-permute-start.42 = (bf16[2,512,1024]{2,1,0:T(8,128)(2,1)}, bf16[2,512,1024]{2,1,0:T(8,128)(2,1)}, u32[]{:S(2)}, u32[]{:S(2)}) collective-permute-start(bf16[2,512,1024]{2,1,0:T(8,128)(2,1)} %pad_maximum_fusion.15), channel_id=1, source_target_pairs={{0,16},{8,24},{16,0},{24,8},{1,17},{9,25},{17,1},{25,9},{2,18},{10... | collective-permute-start | bytes 6291464 | tf_op jit(solution)/shard_map/ppermute | solution.py:49
  890.5 100.6 %collective-permute-start.43 = (bf16[2,512,1024]{2,1,0:T(8,128)(2,1)}, bf16[2,512,1024]{2,1,0:T(8,128)(2,1)}, u32[]{:S(2)}, u32[]{:S(2)}) collective-permute-start(bf16[2,512,1024]{2,1,0:T(8,128)(2,1)} %pad_maximum_fusion.16), channel_id=1, source_target_pairs={{0,24},{8,16},{16,8},{24,0},{1,25},{9,17},{17,9},{25,1},{2,26},{10... | collective-permute-start | bytes 6291464 | tf_op jit(solution)/shard_map/ppermute | solution.py:49
  891.4 46.7 %collective-permute-start.44 = (bf16[2,512,256]{2,1,0:T(8,128)(2,1)}, bf16[2,512,256]{2,1,0:T(8,128)(2,1)}, u32[]{:S(2)}, u32[]{:S(2)}) collective-permute-start(bf16[2,512,256]{2,1,0:T(8,128)(2,1)} %pad_maximum_fusion.27), channel_id=1, source_target_pairs={{0,8},{8,0},{16,24},{24,16},{1,9},{9,1},{17,25},{25,17},{2,10},{10... | collective-permute-start | bytes 1572872 | tf_op jit(solution)/shard_map/ppermute | solution.py:49
  936.5 48.9 %collective-permute-start.47 = (f32[512,64]{0,1:T(8,128)S(1)}, f32[512,64]{0,1:T(8,128)S(1)}, u32[]{:S(2)}, u32[]{:S(2)}) collective-permute-start(f32[512,64]{0,1:T(8,128)S(1)} %fusion.98), channel_id=1, source_target_pairs={{0,16},{8,24},{16,0},{24,8},{1,17},{9,25},{17,1},{25,9},{2,18},{10... | collective-permute-start | bytes 393224 | tf_op jit(solution)/shard_map/ppermute | solution.py:49
  939.3 50.9 %collective-permute-start.45 = (bf16[512,256]{1,0:T(8,128)(2,1)S(1)}, bf16[512,256]{1,0:T(8,128)(2,1)S(1)}, u32[]{:S(2)}, u32[]{:S(2)}) collective-permute-start(bf16[512,256]{1,0:T(8,128)(2,1)S(1)} %fusion.89), channel_id=1, source_target_pairs={{0,16},{8,24},{16,0},{24,8},{1,17},{9,25},{17,1},{25,9},{2,18},{10... | collective-permute-start | bytes 786440 | tf_op jit(solution)/shard_map/ppermute | solution.py:49
  1005.9 46.4 %collective-permute-start.50 = (bf16[1,512,1024]{2,1,0:T(8,128)(2,1)}, bf16[1,512,1024]{2,1,0:T(8,128)(2,1)}, u32[]{:S(2)}, u32[]{:S(2)}) collective-permute-start(bf16[1,512,1024]{2,1,0:T(8,128)(2,1)} %get-tuple-element.412), channel_id=1, source_target_pairs={{0,24},{8,16},{16,8},{24,0},{1,25},{9,17},{17,9},{25,1},{2,26},{10... | collective-permute-start | bytes 3145736 | tf_op jit(solution)/shard_map/ppermute | solution.py:49
  1054.3 45.4 %collective-permute-start.53 = (bf16[1,512,1024]{2,1,0:T(8,128)(2,1)S(1)}, bf16[1,512,1024]{2,1,0:T(8,128)(2,1)}, u32[]{:S(2)}, u32[]{:S(2)}) collective-permute-start(bf16[1,512,1024]{2,1,0:T(8,128)(2,1)S(1)} %copy-done.37), channel_id=1, source_target_pairs={{0,24},{8,16},{16,8},{24,0},{1,25},{9,17},{17,9},{25,1},{2,26},{10... | collective-permute-start | bytes 3145736 | tf_op jit(solution)/shard_map/ppermute | solution.py:49
  (137 other events, 1962.1 us)
Sparse Core Ops, SparseCore 0:
  16.0 103.4 all-gather.6
  122.1 73.1 all-gather.8
  201.2 100.7 all-gather.10
  315.8 100.3 all-gather.12
  418.1 98.1 all-gather.14
  626.8 135.8 reduce-scatter.3
  766.3 98.8 all-gather.16
  869.3 116.5 reduce-scatter.5
  1000.6 116.7 reduce-scatter.7

commit v4 on v3

--- a/solution.py
+++ b/solution.py
@@ -324,7 +324,9 @@
 def expert_kernel(x_ref, c_ref, gate_ref, w_ref, wd_ref, act_ref, grad_ref, sums_ref, dx_ref):
     width = act_ref.shape[1]
     slot_gate = gate_ref[...]
-    pre = jnp.dot(x_ref[...], w_ref[...], preferred_element_type=F32)
+    pre = x_ref[...]
+    if pre.dtype == BF16:
+        pre = jnp.dot(pre, w_ref[...], preferred_element_type=F32)
     gate, up = pre[:, :width], pre[:, width:]
     grad = jnp.dot(c_ref[...], wd_ref[...], preferred_element_type=F32)
     opened = 1.0 / (1.0 + jnp.exp(-gate))
@@ -351,7 +353,7 @@
         expert_kernel,
         name="expert",
         grid=(rows // block,),
-        in_specs=[by_rows(D), by_rows(D), by_rows(1), whole(w), whole(wd)],
+        in_specs=[by_rows(x.shape[1]), by_rows(D), by_rows(1), whole(w), whole(wd)],
         out_specs=[by_rows(width), by_rows(2 * width), by_rows(2), by_rows(D)],
         out_shape=[
             jax.ShapeDtypeStruct((rows, width), BF16),
@@ -361,6 +363,27 @@
         ],
         cost_estimate=cost(1000, 1000),
     )(x, c, slot_gate, w, wd)
+
+
+def through_heads_kernel(grad_ref, w_ref, out_ref):
+    width = grad_ref.shape[1]
+    out_ref[...] = contract_last(grad_ref[...], w_ref[:, :width], BF16)
+
+
+def through_heads(grad, w, block=256):
+    rows, width = grad.shape
+    return pl.pallas_call(
+        through_heads_kernel,
+        name="through_heads",
+        grid=(rows // block,),
+        in_specs=[
+            pl.BlockSpec((block, width), lambda i: (i, 0)),
+            pl.BlockSpec(w.shape, lambda i: (0, 0)),
+        ],
+        out_specs=pl.BlockSpec((block, D), lambda i: (i, 0)),
+        out_shape=jax.ShapeDtypeStruct((rows, D), BF16),
+        cost_estimate=cost(1000, 1000),
+    )(grad, w)
 
 
 def combine_kernel(*refs):
@@ -501,7 +524,11 @@
         return pieces
 
     def to_owner(parts, pieces, *earlier):
-        pieces = trade_all(after(pieces, *earlier))
+        pieces = after(pieces, *earlier)
+        pieces = [
+            None if step == 1 else trade(pieces[step], step, n_row) for step in steps
+        ]
+        pieces[1] = jnp.stack([near_pieces[all_parts.index(part)] for part in parts])
         for i, (which, e) in enumerate(parts):
             for step in steps:
                 at = (peers[step] * rows_local, unit_count if which == 1 else 0)
@@ -518,11 +545,14 @@
     first_parts, second_parts = all_parts[:per_device], all_parts[per_device : per_device + 1]
     third_parts = all_parts[per_device + 1 : 2 * per_device + 1]
     last_parts = all_parts[2 * per_device + 1 :]
+    near_pieces = trade(slices(all_parts)[1], 1, n_row)
     first_pieces = to_owner(first_parts, slices(first_parts))
     second_pieces = after(slices(second_parts), *w_in)
     later = [slices(parts) for parts in (third_parts, last_parts)]
     far_bases = far[::2]
-    gathered, second_pieces, later, cot_b = tied((gathered, second_pieces, later, cot_b))
+    gathered, second_pieces, later, cot_b, inverse, near_pieces = tied(
+        (gathered, second_pieces, later, cot_b, inverse, near_pieces)
+    )
     gains = gathered[tok_count : tok_count + 6].astype(F32).reshape(2, 3, D).sum(axis=1)
 
     expert_ids = jnp.arange(E, dtype=jnp.int32)
@@ -570,13 +600,13 @@
     out_half_all = gather_features(after(out_half, *first_pieces[:-1]))
 
     to_owner(second_parts, second_pieces)
+    far_cots = [trade(cot_b, base, n_row) for base in far_bases]
     attended_b = tied(attended_b)
     attended_all = gather_features(after(attended_b, out_half_all))
-    far_cots = [trade(after(cot_b, *w_in), base, n_row) for base in far_bases]
-    to_owner(third_parts, later[0], attended_b, far_cots)
+    third_pieces = to_owner(third_parts, later[0], attended_b, far_cots)
     other_half = trade(after(out_half_all, *w_back), 1, n_row)
     cot_alls = {
-        base: gather_features(after(cot, w_back[0])) for base, cot in zip(far_bases, far_cots)
+        base: gather_features(after(cot, third_pieces[2])) for base, cot in zip(far_bases, far_cots)
     }
     attended_all = tied(attended_all)
     if last_parts:
@@ -585,13 +615,15 @@
         core, col, gathered, attended_all, out_half_all, other_half, gains[1:], feat_local
     )
     cot_alls[0] = gather_features(after(cot_b, normed2))
+    normed2 = tied(normed2)
     column_start = col * feat_local
 
     def chosen_rows(e, values):
         return [plain_dot(picks[e][step], values, BF16) for step in steps]
 
-    sent_rows = [chosen_rows(e, normed2) for e in range(per_device)]
-    sent_rows[0] = tied(sent_rows[0])
+    sent_rows = []
+    for e in range(per_device):
+        sent_rows.append(chosen_rows(e, after(normed2, sent_rows)))
     all_rows = [trade_all(pieces) for pieces in sent_rows]
 
     def grad_rows_of(base, cots):
@@ -611,10 +643,10 @@
         grad_rows_at[base], grad_rows_at[base + 1] = halves[0], trade(halves[1], 1, n_row)
 
     for base in far_bases:
-        hand_on(base, grad_rows_of(base, after(cot_alls[base], sent_rows)))
+        hand_on(base, grad_rows_of(base, after(cot_alls[base], sent_rows, all_rows[0])))
 
     logits = lax.dot_general(
-        router_all, normed2, (((0,), (1,)), ((), ())), preferred_element_type=F32
+        router_all, after(normed2, sent_rows), (((0,), (1,)), ((), ())), preferred_element_type=F32
     )
     top_logit = jnp.max(jnp.where(chosen, logits, -jnp.inf), axis=0, keepdims=True)
     raised = jnp.where(chosen, jnp.exp(logits - top_logit), 0.0)
@@ -633,11 +665,14 @@
     both = range(per_device)
     calls, grads_back = {}, [[None] * n_row for e in range(per_device)]
 
-    def expert_call(e, held):
+    def rows_and_gates(e, held):
         rows = jnp.concatenate([all_rows[e][step] for step in held])
+        return rows, jnp.concatenate([slot_gates[step][e] for step in held])[:, None]
+
+    def expert_call(e, held, rows, slot_gate, pre=None):
         grad_rows = jnp.concatenate([grad_rows_at[step][e] for step in held])
-        slot_gate = jnp.concatenate([slot_gates[step][e] for step in held])[:, None]
-        results = run_expert(rows, grad_rows, slot_gate, w_in[e], w_back[e], 2 * capacity)
+        first = rows if pre is None else pre
+        results = run_expert(first, grad_rows, slot_gate, w_in[e], w_back[e], 2 * capacity)
         calls[e, held[0]] = [rows, grad_rows, *results]
 
     def send_back(e, held):
@@ -646,12 +681,17 @@
             piece = grads[i * capacity : (i + 1) * capacity]
             grads_back[e][step] = trade(piece, step, n_row)
 
-    expert_call(0, far)
+    expert_call(0, far, *rows_and_gates(0, far))
     send_back(0, far)
     for e in range(1, per_device):
         all_rows[e] = after(all_rows[e], calls[0, 2])
-        expert_call(e, far)
-    near_halves = grad_rows_of(0, after(cot_alls[0], [calls[e, 2] for e in both]))
+        expert_call(e, far, *rows_and_gates(e, far))
+    near_inputs = [rows_and_gates(e, near) for e in both]
+    near_inputs = [(*held, plain_dot(held[0], w_in[e])) for e, held in enumerate(near_inputs)]
+    near_cots, near_inputs, _ = lax.optimization_barrier(
+        (cot_alls[0], near_inputs, [calls[e, 2] for e in both])
+    )
+    near_halves = grad_rows_of(0, near_cots)
     for e in range(1, per_device):
         calls[e, 2], grads_back[e - 1], near_halves = lax.optimization_barrier(
             (calls[e, 2], grads_back[e - 1], near_halves)
@@ -659,7 +699,7 @@
         send_back(e, far)
     hand_on(0, near_halves)
     for e in range(per_device):
-        expert_call(e, near)
+        expert_call(e, near, *near_inputs[e])
         send_back(e, near)
     last_near = (per_device - 1, 0)
     calls[last_near], grads_back[-1] = lax.optimization_barrier((calls[last_near], grads_back[-1]))
@@ -707,9 +747,10 @@
     small = jnp.concatenate([grad_own, inner_own], axis=0)
     small, branch_back[0] = lax.optimization_barrier((small, branch_back[0]))
     small = lax.all_to_all(
-        jnp.broadcast_to(small[None], (n_col,) + small.shape), "col", 0, 0, tiled=True
+        jnp.broadcast_to(small.astype(BF16)[None], (n_col,) + small.shape), "col", 0, 0, tiled=True
     )
     small, branch_back = lax.optimization_barrier((small, branch_back))
+    small = small.astype(F32)
     grad_gates = small[:, :local_experts].reshape(E, tok_count)
     grad_logits = gate_probs * (
         grad_gates - jnp.sum(gate_probs * grad_gates, axis=0, keepdims=True)
@@ -747,8 +788,8 @@
         return trade_all(after(pieces, *earlier))
 
     gate_slices, up_slices = held_slices(0, both), held_slices(1, both)
-    grad_mixed_b, gate_slices, up_slices, inverse = lax.optimization_barrier(
-        (grad_mixed.astype(BF16), gate_slices, up_slices, inverse)
+    grad_mixed_b, gate_slices, up_slices = lax.optimization_barrier(
+        (grad_mixed.astype(BF16), gate_slices, up_slices)
     )
     grad_branch = gather_features(grad_mixed_b)
     gate_pieces = to_holders(gate_slices)
@@ -762,18 +803,23 @@
                 places += [first + e, unit]
         return place(jnp.stack(places), flat, local_experts, hidden_units)
 
-    def sum_groups(grad, *earlier):
-        grad = after(grad, *earlier)
+    def sum_cores(grad):
         parts = [
             lax.dynamic_slice_in_dim(grad, peers[step] * rows_local, rows_local, 0)
             for step in steps
         ]
         other = trade(jnp.stack(parts[1::2]), 1, n_row).astype(F32)
         sums = [part.astype(F32) + other[i] for i, part in enumerate(parts[::2])]
+        return [sums[0]] + [part.astype(grad.dtype) for part in sums[1:]]
+
+    def sum_chips(sums):
         total = sums[0]
-        for i, base in enumerate(far_bases):
-            total = total + trade(sums[i + 1].astype(grad.dtype), base, n_row).astype(F32)
+        for part, base in zip(sums[1:], far_bases):
+            total = total + trade(part, base, n_row).astype(F32)
         return total
+
+    def sum_groups(grad, *earlier):
+        return sum_chips(sum_cores(after(grad, *earlier)))
 
     combined_part = combine(ranks, [branch_back[e][step] for e, step in every])
     grad_branch, gate_pieces, combined_part = lax.optimization_barrier(
@@ -800,7 +846,7 @@
         )
     )
     down_pieces = [to_holders(down_slices[0])]
-    grad_normed1_part = contract_last(grad_qkv, w_qkv, BF16)
+    grad_normed1_part = through_heads(grad_qkv, weight_heads)
     grad_unit_in = scatter_partial(grad_normed1_part)
     output = (mixed + combined.astype(F32)).astype(BF16)[inverse]
     grad_w_up = to_rows([up_pieces])
@@ -827,15 +873,16 @@
         ],
         axis=1,
     )
-    heads_grad = contract_first(normed1, grad_qkv, BF16)
-    vectors, down_pieces, heads_grad = lax.optimization_barrier(
-        (vectors, down_pieces, heads_grad)
-    )
+    heads_sums = sum_cores(contract_first(normed1, grad_qkv, BF16))
+    vectors, heads_sums = lax.optimization_barrier((vectors, heads_sums))
     vectors = jnp.sum(lax.all_to_all(vectors, "col", 0, 0, tiled=True), axis=0)
+    vectors, down_pieces, heads_sums = lax.optimization_barrier(
+        (vectors, down_pieces, heads_sums)
+    )
     inner_in = vectors[:tok_count, None] / D
     vectors = jnp.concatenate([vectors[tok_count:], grad_norm2])
     vectors = sum(trade(vectors, step, n_row) for step in steps)
-    grad_heads = sum_groups(heads_grad)
+    grad_heads = sum_chips(heads_sums)
     grad_unit_in, vectors, inner_in, grad_heads = lax.optimization_barrier(
         (grad_unit_in, vectors, inner_in, grad_heads)
     )

time: 1160 us -> 1120 us (0.966)
  waiting for transfers between devices: 447 us -> 396 us
    ppermute x59 -> x56, waiting for transfers between devices: 382 us -> 333 us  [trade(): return lax.ppermute(value, 'row', [(r, r ^ step) for r in range(n_row)])]
    all_to_all x2 -> x1, waiting for transfers between devices: 24.2 us -> 6.71 us  [body(): lax.all_to_all(jnp.broadcast_to(small.astype(BF16)[None], (n_col,) + smal...]
    dot_general x18 -> x20, matrix products: 56.5 us -> 70.1 us  [plain_dot(): return jnp.dot(left_op, right_op, preferred_element_type=F32).astype(kind)]
    reduce_scatter x3, waiting for transfers between devices: 2.95 us -> 15.7 us  [scatter_partial(): lax.psum_scatter(partial_rows, 'col', scatter_dimension=1, tiled=True)]
    dot_general x3 -> x2, matrix products: 24.3 us -> 15 us  [contract_last(): lax.dot_general(left_op, right_op, (((1,), (1,)), ((), ())), preferred_el...]
    unnamed x238 -> x272, local copies, waits for them, and re-layouts: 20.8 us -> 27.2 us
    ppermute x59 -> x56, starting transfers between devices: 40.3 us -> 41 us  [trade(): return lax.ppermute(value, 'row', [(r, r ^ step) for r in range(n_row)])]
  transfers between devices with their start and end apart: 72 -> 68, of which waited for: 27 -> 26; matrix products, arithmetic and copies ran while one was open for 31% -> 33% of each run, Pallas kernels for 18% -> 18%
where the time goes in v4:
time: 1120 us; the launch traced here: 1110 us
  waiting for transfers between devices  396 us (35%)
  Pallas kernels  230 us (21%)
  local copies, waits for them, and re-layouts  178 us (16%)
  matrix products  137 us (12%)
  other arithmetic  83.7 us (7%)
  starting transfers between devices  54.3 us (5%)
  between operations  16.5 us (1%)
    ppermute x56, waiting for transfers between devices, trade(): return lax.ppermute(value, 'row', [(r, r ^ step) for r in range(n_row)])  333 us
    dot_general x20, matrix products, plain_dot(): return jnp.dot(left_op, right_op, preferred_element_type=F32).astype(kind)  70.1 us
    pallas_call x4, Pallas kernels, run_expert(): pl.pallas_call(expert_kernel, name='expert', grid=(rows // block,), in_sp...  66.2 us
    dot_general x6, matrix products, contract_first(): lax.dot_general(left_op, right_op, (((0,), (0,)), ((), ())), preferred_el...  44.7 us
    ppermute x56, starting transfers between devices, trade(): return lax.ppermute(value, 'row', [(r, r ^ step) for r in range(n_row)])  41 us
    pallas_call x2, Pallas kernels, combine(): pl.pallas_call(combine_kernel, name='combine', grid=(D // width, rows //...  39.8 us
    pallas_call x3, Pallas kernels, place(): pl.pallas_call(place_kernel, name='place', grid_spec=pltpu.PrefetchScalar...  32.9 us
    all_to_all x2, waiting for transfers between devices, swap_small(): table = lax.all_to_all(table, 'row', 0, 0, tiled=True)  31 us
  transfers between devices with their start and end apart: 68, of which 26 were waited for; matrix products, arithmetic and copies ran while one was open for 33% of the time, Pallas kernels for 18%

profile of v4, /device:TPU:0, one launch (start us, length us, event | category | flops | bytes accessed | tf_op | source)
XLA Modules:
  0.0 1105.8 jit_solution(252321295989744183)
XLA Ops:
  22.9 6.1 constant_dynamic-slice_fusion.52
  60.8 30.1 %collective-permute-done.1 = bf16[2,512,1024]{2,1,0:T(8,128)(2,1)} collective-permute-done((bf16[2,512,1024]{2,1,0:T(8,128)(2,1)}, bf16[2,512,1024]{2,1,0:T(8,128)(2,1)}, u32[]{:S(2)}, u32[]{:S(2)}) %collective-permute-start.1) | collective-permute-done | bytes 2097184 | tf_op jit(solution)/shard_map/ppermute | solution.py:49
  104.2 7.2 scatter_custom_fusion
  133.6 5.4 collective-permute-done.2
  145.5 13.8 %project.1 = (bf16[1536,2048]{1,0:T(8,128)(2,1)}, f32[1536,1]{1,0:T(8,128)}, f32[1536,512]{1,0:T(8,128)}, bf16[1536,256]{1,0:T(8,128)(2,1)}, bf16[1536,256]{1,0:T(8,128)(2,1)}, /*index=5*/bf16[1536,256]{1,0:T(8,128)(2,1)}) custom-call(bf16[1552,2048]{1,0:T(8,128)(2,1)} %all-gather.7.cloned.1.call-done.x_ref, f32[1,2048]{1,0:T(1,128)} %get-tuple-element.636.gain_ref, ...), custom_call_target="tpu_custom_call" | custom-call | flops 1000 | bytes 1000 | tf_op jit(solution)/shard_map/project/pallas_call | solution.py:117
  159.3 16.8 %attend.1 = (bf16[1536,256]{1,0:T(8,128)(2,1)}, f32[2,1536,1]{2,1,0:T(8,128)}) custom-call(bf16[1536,256]{1,0:T(8,128)(2,1)} %get-tuple-element.242.q_ref, bf16[1536,256]{1,0:T(8,128)(2,1)} %get-tuple-element.243.k_ref, bf16[1536,256]{1,0:T(8,128)(2,1)} %get-tuple-element.244.v_ref, s32[1536,1]{1,0:T(8,128)} %broadcast_in_dim.654.seg_q_ref, ...), custom_call_target="tpu_custom_call" | custom-call | flops 1000 | bytes 1000 | tf_op jit(solution)/shard_map/attend/pallas_call | solution.py:167
  181.7 7.7 collective-permute-done.7
  196.3 17.4 %collective-permute-done.8 = bf16[1536,256]{1,0:T(8,128)(2,1)S(1)} collective-permute-done((bf16[1536,256]{1,0:T(8,128)(2,1)S(1)}, bf16[1536,256]{1,0:T(8,128)(2,1)S(1)}, u32[]{:S(2)}, u32[]{:S(2)}) %collective-permute-start.8) | collective-permute-done | bytes 786464 | tf_op jit(solution)/shard_map/ppermute | solution.py:49
  215.2 45.0 %collective-permute-done.9 = bf16[2,512,1024]{2,1,0:T(8,128)(2,1)S(1)} collective-permute-done((bf16[2,512,1024]{2,1,0:T(8,128)(2,1)}, bf16[2,512,1024]{2,1,0:T(8,128)(2,1)S(1)}, u32[]{:S(2)}, u32[]{:S(2)}) %collective-permute-start.9) | collective-permute-done | bytes 2097184 | tf_op jit(solution)/shard_map/ppermute | solution.py:49
  270.3 38.0 %collective-permute-done.10 = bf16[2,512,1024]{2,1,0:T(8,128)(2,1)S(1)} collective-permute-done((bf16[2,512,1024]{2,1,0:T(8,128)(2,1)}, bf16[2,512,1024]{2,1,0:T(8,128)(2,1)S(1)}, u32[]{:S(2)}, u32[]{:S(2)}) %collective-permute-start.10) | collective-permute-done | bytes 2097184 | tf_op jit(solution)/shard_map/ppermute | solution.py:49
  317.3 22.8 %branch.1 = (bf16[1536,2048]{1,0:T(8,128)(2,1)}, f32[1536,1]{1,0:T(8,128)}, f32[1536,256]{1,0:T(8,128)}) custom-call(s32[2]{0:T(128)} %pad_add_fusion.at_ref, bf16[1552,2048]{1,0:T(8,128)(2,1)} %all-gather.7.cloned.1.call-done.x_ref, bf16[1536,2048]{1,0:T(8,128)(2,1)} %all-gather.11.cloned.1.call-done.att_ref, ...), custom_call_target="tpu_custom_call" | custom-call | flops 1000 | bytes 1000 | tf_op jit(solution)/shard_map/branch/pallas_call | solution.py:305
  346.2 13.2 %collective-permute-done.13 = bf16[1,512,1024]{2,1,0:T(8,128)(2,1)} collective-permute-done((bf16[1,512,1024]{2,1,0:T(8,128)(2,1)S(1)}, bf16[1,512,1024]{2,1,0:T(8,128)(2,1)}, u32[]{:S(2)}, u32[]{:S(2)}) %collective-permute-start.13) | collective-permute-done | bytes 1048608 | tf_op jit(solution)/shard_map/ppermute | solution.py:49
  398.4 20.3 %all-to-all-done = f32[4,2,240]{2,1,0:T(2,128)S(1)} async-done(((f32[4,2,240]{2,1,0:T(2,128)}), f32[4,2,240]{2,1,0:T(2,128)S(1)}, u32[]{:S(2)}, u32[]{:S(2)}) %all-to-all-start) | async-done | bytes 7712 | tf_op jit(solution)/shard_map/all_to_all | solution.py:587
  436.2 10.0 fusion.137.x_ref
  453.4 18.3 %expert.4 = (bf16[480,1024]{1,0:T(8,128)(2,1)}, bf16[480,2048]{1,0:T(8,128)(2,1)}, f32[480,2]{1,0:T(8,128)}, bf16[480,2048]{1,0:T(8,128)(2,1)}) custom-call(bf16[480,2048]{1,0:T(8,128)(2,1)} %copy-done.23, bf16[480,2048]{1,0:T(8,128)(2,1)} %pad_maximum_fusion.17.c_ref, f32[480,1]{1,0:T(8,128)} %copy.67.gate_ref, ...), custom_call_target="tpu_custom_call" | custom-call | flops 1000 | bytes 1000 | tf_op jit(solution)/shard_map/expert/pallas_call | solution.py:352
  480.8 18.3 %expert.5 = (bf16[480,1024]{1,0:T(8,128)(2,1)}, bf16[480,2048]{1,0:T(8,128)(2,1)}, f32[480,2]{1,0:T(8,128)}, bf16[480,2048]{1,0:T(8,128)(2,1)}) custom-call(bf16[480,2048]{1,0:T(8,128)(2,1)} %copy-done.25, bf16[480,2048]{1,0:T(8,128)(2,1)} %pad_maximum_fusion.18.c_ref, f32[480,1]{1,0:T(8,128)} %copy.68.gate_ref, ...), custom_call_target="tpu_custom_call" | custom-call | flops 1000 | bytes 1000 | tf_op jit(solution)/shard_map/expert/pallas_call | solution.py:352
  502.9 9.5 fusion.168.x_ref
  535.6 14.8 %expert.7 = (bf16[480,1024]{1,0:T(8,128)(2,1)}, bf16[480,2048]{1,0:T(8,128)(2,1)}, f32[480,2]{1,0:T(8,128)}, bf16[480,2048]{1,0:T(8,128)(2,1)}) custom-call(f32[480,2048]{1,0:T(8,128)} %fusion.168.x_ref, bf16[480,2048]{1,0:T(8,128)(2,1)} %pad_maximum_fusion.22.c_ref, f32[480,1]{1,0:T(8,128)} %copy.70.gate_ref, bf16[2048,2048]{1,0:T(8,128)(2,1)} %get-tuple-element.299.w_ref, ...), custom_call_target="tpu_custom_call" | custom-call | flops 1000 | bytes 1000 | tf_op jit(solution)/shard_map/expert/pallas_call | solution.py:352
  555.3 14.9 %expert.6 = (bf16[480,1024]{1,0:T(8,128)(2,1)}, bf16[480,2048]{1,0:T(8,128)(2,1)}, f32[480,2]{1,0:T(8,128)}, bf16[480,2048]{1,0:T(8,128)(2,1)}) custom-call(f32[480,2048]{1,0:T(8,128)} %fusion.137.x_ref, bf16[480,2048]{1,0:T(8,128)(2,1)} %pad_maximum_fusion.21.c_ref, f32[480,1]{1,0:T(8,128)} %copy.69.gate_ref, ...), custom_call_target="tpu_custom_call" | custom-call | flops 1000 | bytes 1000 | tf_op jit(solution)/shard_map/expert/pallas_call | solution.py:352
  579.6 19.9 %combine.2 = bf16[1536,2048]{1,0:T(8,128)(2,1)} custom-call(s32[8,1536]{1,0:T(8,128)} %concatenate.135.refs_0_, bf16[240,2048]{1,0:T(8,128)(2,1)} %get-tuple-element.589.refs_1_, bf16[240,2048]{1,0:T(8,128)(2,1)} %collective-permute-done.25.refs_2_, bf16[240,2048]{1,0:T(8,128)(2,1)} %collective-permute-done.22.refs_3_, ...), custom_call_target="tpu_custom_call" | custom-call | flops 1000 | bytes 1000 | tf_op jit(solution)/shard_map/combine/pallas_call | solution.py:405
  601.1 7.5 convolution_convert_fusion.2
  612.3 7.5 convolution_convert_fusion.3
  628.2 11.4 %convolution_convert_fusion.1 = bf16[2048,2048]{1,0:T(8,128)(2,1)S(1)} fusion(bf16[480,2048]{1,0:T(8,128)(2,1)S(1)} %copy-done.24, bf16[480,2048]{1,0:T(8,128)(2,1)} %pad_maximum_fusion.15, bf16[480,2048]{1,0:T(8,128)(2,1)} %get-tuple-element.355, bf16[480,2048]{1,0:T(8,128)(2,1)} %get-tuple-element.354), kind=kOutput, calls=%fused_computation.9 | convolution fusion | flops 8072986624 | bytes 16252928 | tf_op jit(solution)/shard_map/dot_general | solution.py:63
  642.8 10.8 convolution_convert_fusion
  666.7 10.7 all-to-all-done.1
  682.8 6.2 all-to-all-start.2
  695.7 9.4 collective-permute-done.34.refs_8_
  705.1 6.7 all-to-all-done.2
  712.1 15.6 %reduce-scatter.4.cloned.1.call-done = bf16[1536,256]{1,0:T(8,128)(2,1)} async-done(((bf16[1536,2048]{1,0:T(8,128)(2,1)}), bf16[1536,256]{1,0:T(8,128)(2,1)}) %reduce-scatter.4.cloned.1.call-update) | async-done | bytes 786448 | tf_op jit(solution)/shard_map/reduce_scatter | solution.py:43
  733.0 19.9 %combine.3 = bf16[1536,2048]{1,0:T(8,128)(2,1)} custom-call(s32[8,1536]{1,0:T(8,128)} %concatenate.135.refs_0_, bf16[240,2048]{1,0:T(8,128)(2,1)} %get-tuple-element.369.refs_1_, bf16[240,2048]{1,0:T(8,128)(2,1)} %collective-permute-done.29.refs_2_, bf16[240,2048]{1,0:T(8,128)(2,1)} %collective-permute-done.30.refs_3_, ...), custom_call_target="tpu_custom_call" | custom-call | flops 1000 | bytes 1000 | tf_op jit(solution)/shard_map/combine/pallas_call | solution.py:405
  752.9 27.1 %collective-permute-done.36.refs_2_ = bf16[2,512,1024]{2,1,0:T(8,128)(2,1)} collective-permute-done((bf16[2,512,1024]{2,1,0:T(8,128)(2,1)}, bf16[2,512,1024]{2,1,0:T(8,128)(2,1)}, u32[]{:S(2)}, u32[]{:S(2)}) %collective-permute-start.36) | collective-permute-done | bytes 2097184 | tf_op jit(solution)/shard_map/ppermute | solution.py:49
  780.0 44.0 %collective-permute-done.37.refs_3_ = bf16[2,512,1024]{2,1,0:T(8,128)(2,1)} collective-permute-done((bf16[2,512,1024]{2,1,0:T(8,128)(2,1)}, bf16[2,512,1024]{2,1,0:T(8,128)(2,1)}, u32[]{:S(2)}, u32[]{:S(2)}) %collective-permute-start.37) | collective-permute-done | bytes 2097184 | tf_op jit(solution)/shard_map/ppermute | solution.py:49
  824.0 5.8 all-gather.17.cloned.1.call-done
  830.5 6.9 fusion.22
  855.8 11.0 place.3
  866.7 6.0 convolution_convert_fusion.6.grad_ref
  872.7 27.6 %attend_back.1 = (bf16[1536,256]{1,0:T(8,128)(2,1)}, bf16[1536,256]{1,0:T(8,128)(2,1)}, bf16[1536,256]{1,0:T(8,128)(2,1)}, f32[1,128]{1,0:T(1,128)}, f32[1,128]{1,0:T(1,128)}) custom-call(bf16[1536,256]{1,0:T(8,128)(2,1)} %get-tuple-element.242.q_ref, bf16[1536,256]{1,0:T(8,128)(2,1)} %get-tuple-element.243.k_ref, ...), custom_call_target="tpu_custom_call" | custom-call | flops 1000 | bytes 1000 | tf_op jit(solution)/shard_map/attend_back/pallas_call | solution.py:250
  906.5 42.7 %collective-permute-done.44 = f32[512,64]{0,1:T(8,128)S(1)} collective-permute-done((f32[512,64]{0,1:T(8,128)S(1)}, f32[512,64]{0,1:T(8,128)S(1)}, u32[]{:S(2)}, u32[]{:S(2)}) %collective-permute-start.44) | collective-permute-done | bytes 131104 | tf_op jit(solution)/shard_map/ppermute | solution.py:49
  954.8 10.4 through_heads.1
  971.1 8.6 convolution_convert_fusion.4
  985.2 11.0 place.4
  996.2 5.4 gather_fusion.2
  1001.6 15.5 %collective-permute-done.47.refs_3_ = bf16[1,512,1024]{2,1,0:T(8,128)(2,1)} collective-permute-done((bf16[1,512,1024]{2,1,0:T(8,128)(2,1)}, bf16[1,512,1024]{2,1,0:T(8,128)(2,1)}, u32[]{:S(2)}, u32[]{:S(2)}) %collective-permute-start.47) | collective-permute-done | bytes 1048608 | tf_op jit(solution)/shard_map/ppermute | solution.py:49
  1019.2 6.7 multiply_reduce_fusion
  1029.6 9.8 all_to_all.24
  1044.0 20.5 %collective-permute-done.51.refs_7_ = bf16[1,512,1024]{2,1,0:T(8,128)(2,1)} collective-permute-done((bf16[1,512,1024]{2,1,0:T(8,128)(2,1)S(1)}, bf16[1,512,1024]{2,1,0:T(8,128)(2,1)}, u32[]{:S(2)}, u32[]{:S(2)}) %collective-permute-start.51) | collective-permute-done | bytes 1048608 | tf_op jit(solution)/shard_map/ppermute | solution.py:49
  1069.0 11.0 place.5
  1080.1 5.1 collective-permute-done.53
  (646 shorter events, 359.1 us)
Async XLA Ops:
  7.2 134.9 %all-gather.7.cloned.1.call-start = ((), (), s32[]{:S(2)}) async-start(), calls=%async_computation.7 | async-start | bytes 7151616 | tf_op jit(solution)/shard_map/all_gather | solution.py:39
  15.3 179.4 %all-gather.9.cloned.1.call-start = ((), (), s32[]{:S(2)}) async-start(), calls=%async_computation.8 | async-start | bytes 4718592 | tf_op jit(solution)/shard_map/all_gather | solution.py:39
  17.5 34.0 %collective-permute-start.3 = (bf16[512,1088]{0,1:T(8,128)(2,1)}, bf16[512,1088]{0,1:T(8,128)(2,1)}, u32[]{:S(2)}, u32[]{:S(2)}) collective-permute-start(bf16[512,1088]{0,1:T(8,128)(2,1)} %copy.61), channel_id=1, source_target_pairs={{0,8},{8,0},{16,24},{24,16},{1,9},{9,1},{17,25},{25,17},{2,10},{10... | collective-permute-start | bytes 3342344 | tf_op jit(solution)/shard_map/ppermute | solution.py:49
  32.9 58.0 %collective-permute-start.1 = (bf16[2,512,1024]{2,1,0:T(8,128)(2,1)}, bf16[2,512,1024]{2,1,0:T(8,128)(2,1)}, u32[]{:S(2)}, u32[]{:S(2)}) collective-permute-start(bf16[2,512,1024]{2,1,0:T(8,128)(2,1)} %get-tuple-element.236), channel_id=1, source_target_pairs={{0,16},{8,24},{16,0},{24,8},{1,17},{9,25},{17,1},{25,9},{2,18},{10... | collective-permute-start | bytes 6291464 | tf_op jit(solution)/shard_map/ppermute | solution.py:49
  43.6 83.9 %collective-permute-start = (bf16[6,512,1024]{2,1,0:T(8,128)(2,1)}, bf16[6,512,1024]{2,1,0:T(8,128)(2,1)}, u32[]{:S(2)}, u32[]{:S(2)}) collective-permute-start(bf16[6,512,1024]{2,1,0:T(8,128)(2,1)} %get-tuple-element.519), channel_id=1, source_target_pairs={{0,8},{8,0},{16,24},{24,16},{1,9},{9,1},{17,25},{25,17},{2,10},{10... | collective-permute-start | bytes 18874376 | tf_op jit(solution)/shard_map/ppermute | solution.py:49
  91.0 220.4 %all-gather.11.cloned.1.call-start = ((), (), s32[]{:S(2)}) async-start(), calls=%async_computation.9 | async-start | bytes 7077888 | tf_op jit(solution)/shard_map/all_gather | solution.py:39
  91.0 48.0 %collective-permute-start.2 = (bf16[2,512,1024]{2,1,0:T(8,128)(2,1)}, bf16[2,512,1024]{2,1,0:T(8,128)(2,1)}, u32[]{:S(2)}, u32[]{:S(2)}) collective-permute-start(bf16[2,512,1024]{2,1,0:T(8,128)(2,1)} %pad_maximum_fusion.3), channel_id=1, source_target_pairs={{0,24},{8,16},{16,8},{24,0},{1,25},{9,17},{17,9},{25,1},{2,26},{10... | collective-permute-start | bytes 6291464 | tf_op jit(solution)/shard_map/ppermute | solution.py:49
  142.1 37.4 %collective-permute-start.6 = (bf16[1,512,1024]{2,1,0:T(8,128)(2,1)}, bf16[1,512,1024]{2,1,0:T(8,128)(2,1)}, u32[]{:S(2)}, u32[]{:S(2)}) collective-permute-start(bf16[1,512,1024]{2,1,0:T(8,128)(2,1)} %get-tuple-element.253), channel_id=1, source_target_pairs={{0,16},{8,24},{16,0},{24,8},{1,17},{9,25},{17,1},{25,9},{2,18},{10... | collective-permute-start | bytes 3145736 | tf_op jit(solution)/shard_map/ppermute | solution.py:49
  144.0 45.4 %collective-permute-start.7 = (bf16[1,512,1024]{2,1,0:T(8,128)(2,1)}, bf16[1,512,1024]{2,1,0:T(8,128)(2,1)}, u32[]{:S(2)}, u32[]{:S(2)}) collective-permute-start(bf16[1,512,1024]{2,1,0:T(8,128)(2,1)} %get-tuple-element.254), channel_id=1, source_target_pairs={{0,24},{8,16},{16,8},{24,0},{1,25},{9,17},{17,9},{25,1},{2,26},{10... | collective-permute-start | bytes 3145736 | tf_op jit(solution)/shard_map/ppermute | solution.py:49
  194.8 233.6 %all-gather.15.cloned.1.call-start = ((), (), s32[]{:S(2)}) async-start(), calls=%async_computation.11 | async-start | bytes 7077888 | tf_op jit(solution)/shard_map/all_gather | solution.py:39
  213.8 46.4 %collective-permute-start.9 = (bf16[2,512,1024]{2,1,0:T(8,128)(2,1)}, bf16[2,512,1024]{2,1,0:T(8,128)(2,1)S(1)}, u32[]{:S(2)}, u32[]{:S(2)}) collective-permute-start(bf16[2,512,1024]{2,1,0:T(8,128)(2,1)} %get-tuple-element.267), channel_id=1, source_target_pairs={{0,16},{8,24},{16,0},{24,8},{1,17},{9,25},{17,1},{25,9},{2,18},{10... | collective-permute-start | bytes 6291464 | tf_op jit(solution)/shard_map/ppermute | solution.py:49
  260.2 252.2 %all-gather.13.cloned.1.call-start = ((), (), s32[]{:S(2)}) async-start(), calls=%async_computation.10 | async-start | bytes 7077888 | tf_op jit(solution)/shard_map/all_gather | solution.py:39
  260.2 48.1 %collective-permute-start.10 = (bf16[2,512,1024]{2,1,0:T(8,128)(2,1)}, bf16[2,512,1024]{2,1,0:T(8,128)(2,1)S(1)}, u32[]{:S(2)}, u32[]{:S(2)}) collective-permute-start(bf16[2,512,1024]{2,1,0:T(8,128)(2,1)} %pad_maximum_fusion.6), channel_id=1, source_target_pairs={{0,24},{8,16},{16,8},{24,0},{1,25},{9,17},{17,9},{25,1},{2,26},{10... | collective-permute-start | bytes 6291464 | tf_op jit(solution)/shard_map/ppermute | solution.py:49
  310.6 85.2 %collective-permute-start.20 = (f32[8,1536]{1,0:T(8,128)S(1)}, f32[8,1536]{1,0:T(8,128)S(1)}, u32[]{:S(2)}, u32[]{:S(2)}) collective-permute-start(f32[8,1536]{1,0:T(8,128)S(1)} %get-tuple-element.676), channel_id=1, source_target_pairs={{0,16},{8,24},{16,0},{24,8},{1,17},{9,25},{17,1},{25,9},{2,18},{10... | collective-permute-start | bytes 147464 | tf_op jit(solution)/shard_map/ppermute | solution.py:49
  313.6 45.8 %collective-permute-start.13 = (bf16[1,512,1024]{2,1,0:T(8,128)(2,1)S(1)}, bf16[1,512,1024]{2,1,0:T(8,128)(2,1)}, u32[]{:S(2)}, u32[]{:S(2)}) collective-permute-start(bf16[1,512,1024]{2,1,0:T(8,128)(2,1)S(1)} %copy-done.42), channel_id=1, source_target_pairs={{0,24},{8,16},{16,8},{24,0},{1,25},{9,17},{17,9},{25,1},{2,26},{10... | collective-permute-start | bytes 3145736 | tf_op jit(solution)/shard_map/ppermute | solution.py:49
  372.6 51.1 %collective-permute-start.19 = (bf16[240,2048]{1,0:T(8,128)(2,1)}, bf16[240,2048]{1,0:T(8,128)(2,1)}, u32[]{:S(2)}, u32[]{:S(2)}) collective-permute-start(bf16[240,2048]{1,0:T(8,128)(2,1)} %convolution_convert_fusion.19), channel_id=1, source_target_pairs={{0,24},{8,16},{16,8},{24,0},{1,25},{9,17},{17,9},{25,1},{2,26},{10... | collective-permute-start | bytes 2949128 | tf_op jit(solution)/shard_map/ppermute | solution.py:49
  373.7 47.1 %collective-permute-start.18 = (bf16[240,2048]{1,0:T(8,128)(2,1)}, bf16[240,2048]{1,0:T(8,128)(2,1)S(1)}, u32[]{:S(2)}, u32[]{:S(2)}) collective-permute-start(bf16[240,2048]{1,0:T(8,128)(2,1)} %convolution_convert_fusion.20), channel_id=1, source_target_pairs={{0,16},{8,24},{16,0},{24,8},{1,17},{9,25},{17,1},{25,9},{2,18},{10... | collective-permute-start | bytes 2949128 | tf_op jit(solution)/shard_map/ppermute | solution.py:49
  395.7 332.0 %reduce-scatter.4.cloned.1.call-start = ((), (), s32[]{:S(2)}) async-start(), calls=%async_computation.12 | async-start | bytes 7077888 | tf_op jit(solution)/shard_map/reduce_scatter | solution.py:43
  396.4 75.2 %collective-permute-start.15 = (bf16[240,2048]{1,0:T(8,128)(2,1)}, bf16[240,2048]{1,0:T(8,128)(2,1)}, u32[]{:S(2)}, u32[]{:S(2)}) collective-permute-start(bf16[240,2048]{1,0:T(8,128)(2,1)} %convolution_convert_fusion.17), channel_id=1, source_target_pairs={{0,8},{8,0},{16,24},{24,16},{1,9},{9,1},{17,25},{25,17},{2,10},{10... | collective-permute-start | bytes 2949128 | tf_op jit(solution)/shard_map/ppermute | solution.py:49
  396.5 75.1 %collective-permute-start.16 = (bf16[240,2048]{1,0:T(8,128)(2,1)}, bf16[240,2048]{1,0:T(8,128)(2,1)}, u32[]{:S(2)}, u32[]{:S(2)}) collective-permute-start(bf16[240,2048]{1,0:T(8,128)(2,1)} %convolution_convert_fusion.16), channel_id=1, source_target_pairs={{0,16},{8,24},{16,0},{24,8},{1,17},{9,25},{17,1},{25,9},{2,18},{10... | collective-permute-start | bytes 2949128 | tf_op jit(solution)/shard_map/ppermute | solution.py:49
  421.7 49.9 %collective-permute-start.17 = (bf16[240,2048]{1,0:T(8,128)(2,1)}, bf16[240,2048]{1,0:T(8,128)(2,1)}, u32[]{:S(2)}, u32[]{:S(2)}) collective-permute-start(bf16[240,2048]{1,0:T(8,128)(2,1)} %convolution_convert_fusion.15), channel_id=1, source_target_pairs={{0,24},{8,16},{16,8},{24,0},{1,25},{9,17},{17,9},{25,1},{2,26},{10... | collective-permute-start | bytes 2949128 | tf_op jit(solution)/shard_map/ppermute | solution.py:49
  474.6 50.1 %collective-permute-start.22 = (bf16[240,2048]{1,0:T(8,128)(2,1)}, bf16[240,2048]{1,0:T(8,128)(2,1)}, u32[]{:S(2)}, u32[]{:S(2)}) collective-permute-start(bf16[240,2048]{1,0:T(8,128)(2,1)} %get-tuple-element.599), channel_id=1, source_target_pairs={{0,16},{8,24},{16,0},{24,8},{1,17},{9,25},{17,1},{25,9},{2,18},{10... | collective-permute-start | bytes 2949128 | tf_op jit(solution)/shard_map/ppermute | solution.py:49
  475.7 49.1 %collective-permute-start.23 = (bf16[240,2048]{1,0:T(8,128)(2,1)}, bf16[240,2048]{1,0:T(8,128)(2,1)}, u32[]{:S(2)}, u32[]{:S(2)}) collective-permute-start(bf16[240,2048]{1,0:T(8,128)(2,1)} %get-tuple-element.598), channel_id=1, source_target_pairs={{0,24},{8,16},{16,8},{24,0},{1,25},{9,17},{17,9},{25,1},{2,26},{10... | collective-permute-start | bytes 2949128 | tf_op jit(solution)/shard_map/ppermute | solution.py:49
  529.2 50.2 %collective-permute-start.27 = (bf16[240,2048]{1,0:T(8,128)(2,1)}, bf16[240,2048]{1,0:T(8,128)(2,1)}, u32[]{:S(2)}, u32[]{:S(2)}) collective-permute-start(bf16[240,2048]{1,0:T(8,128)(2,1)} %get-tuple-element.595), channel_id=1, source_target_pairs={{0,16},{8,24},{16,0},{24,8},{1,17},{9,25},{17,1},{25,9},{2,18},{10... | collective-permute-start | bytes 2949128 | tf_op jit(solution)/shard_map/ppermute | solution.py:49
  530.3 49.2 %collective-permute-start.28 = (bf16[240,2048]{1,0:T(8,128)(2,1)}, bf16[240,2048]{1,0:T(8,128)(2,1)}, u32[]{:S(2)}, u32[]{:S(2)}) collective-permute-start(bf16[240,2048]{1,0:T(8,128)(2,1)} %get-tuple-element.594), channel_id=1, source_target_pairs={{0,24},{8,16},{16,8},{24,0},{1,25},{9,17},{17,9},{25,1},{2,26},{10... | collective-permute-start | bytes 2949128 | tf_op jit(solution)/shard_map/ppermute | solution.py:49
  610.7 85.0 %collective-permute-start.32 = (bf16[240,2048]{1,0:T(8,128)(2,1)}, bf16[240,2048]{1,0:T(8,128)(2,1)}, u32[]{:S(2)}, u32[]{:S(2)}) collective-permute-start(bf16[240,2048]{1,0:T(8,128)(2,1)} %get-tuple-element.568), channel_id=1, source_target_pairs={{0,8},{8,0},{16,24},{24,16},{1,9},{9,1},{17,25},{25,17},{2,10},{10... | collective-permute-start | bytes 2949128 | tf_op jit(solution)/shard_map/ppermute | solution.py:49
  611.1 84.6 %collective-permute-start.33 = (bf16[240,2048]{1,0:T(8,128)(2,1)}, bf16[240,2048]{1,0:T(8,128)(2,1)}, u32[]{:S(2)}, u32[]{:S(2)}) collective-permute-start(bf16[240,2048]{1,0:T(8,128)(2,1)} %get-tuple-element.567), channel_id=1, source_target_pairs={{0,16},{8,24},{16,0},{24,8},{1,17},{9,25},{17,1},{25,9},{2,18},{10... | collective-permute-start | bytes 2949128 | tf_op jit(solution)/shard_map/ppermute | solution.py:49
  621.9 59.0 %collective-permute-start.29 = (bf16[240,2048]{1,0:T(8,128)(2,1)}, bf16[240,2048]{1,0:T(8,128)(2,1)}, u32[]{:S(2)}, u32[]{:S(2)}) collective-permute-start(bf16[240,2048]{1,0:T(8,128)(2,1)} %get-tuple-element.572), channel_id=1, source_target_pairs={{0,8},{8,0},{16,24},{24,16},{1,9},{9,1},{17,25},{25,17},{2,10},{10... | collective-permute-start | bytes 2949128 | tf_op jit(solution)/shard_map/ppermute | solution.py:49
  622.0 60.0 %collective-permute-start.30 = (bf16[240,2048]{1,0:T(8,128)(2,1)}, bf16[240,2048]{1,0:T(8,128)(2,1)}, u32[]{:S(2)}, u32[]{:S(2)}) collective-permute-start(bf16[240,2048]{1,0:T(8,128)(2,1)} %get-tuple-element.571), channel_id=1, source_target_pairs={{0,16},{8,24},{16,0},{24,8},{1,17},{9,25},{17,1},{25,9},{2,18},{10... | collective-permute-start | bytes 2949128 | tf_op jit(solution)/shard_map/ppermute | solution.py:49
  623.1 58.9 %collective-permute-start.31 = (bf16[240,2048]{1,0:T(8,128)(2,1)}, bf16[240,2048]{1,0:T(8,128)(2,1)}, u32[]{:S(2)}, u32[]{:S(2)}) collective-permute-start(bf16[240,2048]{1,0:T(8,128)(2,1)} %get-tuple-element.570), channel_id=1, source_target_pairs={{0,24},{8,16},{16,8},{24,0},{1,25},{9,17},{17,9},{25,1},{2,26},{10... | collective-permute-start | bytes 2949128 | tf_op jit(solution)/shard_map/ppermute | solution.py:49
  624.7 52.7 %all-to-all-start.1 = ((f32[4,2,240,2]{2,3,1,0:T(2,128)}), f32[4,2,240,2]{2,3,1,0:T(2,128)S(1)}, u32[]{:S(2)}, u32[]{:S(2)}) async-start(f32[4,2,240,2]{2,3,1,0:T(2,128)} %select_select_fusion), calls=%async_computation.2 | async-start | bytes 32768 | tf_op jit(solution)/shard_map/all_to_all | solution.py:587
  689.0 140.8 %all-gather.17.cloned.1.call-start = ((), (), s32[]{:S(2)}) async-start(), calls=%async_computation.13 | async-start | bytes 7077888 | tf_op jit(solution)/shard_map/all_gather | solution.py:39
  731.0 223.8 %reduce-scatter.6.cloned.1.call-start = ((), (), s32[]{:S(2)}) async-start(), calls=%async_computation.14 | async-start | bytes 7077888 | tf_op jit(solution)/shard_map/reduce_scatter | solution.py:43
  731.2 48.8 %collective-permute-start.36 = (bf16[2,512,1024]{2,1,0:T(8,128)(2,1)}, bf16[2,512,1024]{2,1,0:T(8,128)(2,1)}, u32[]{:S(2)}, u32[]{:S(2)}) collective-permute-start(bf16[2,512,1024]{2,1,0:T(8,128)(2,1)} %pad_maximum_fusion.9), channel_id=1, source_target_pairs={{0,16},{8,24},{16,0},{24,8},{1,17},{9,25},{17,1},{25,9},{2,18},{10... | collective-permute-start | bytes 6291464 | tf_op jit(solution)/shard_map/ppermute | solution.py:49
  732.4 91.6 %collective-permute-start.37 = (bf16[2,512,1024]{2,1,0:T(8,128)(2,1)}, bf16[2,512,1024]{2,1,0:T(8,128)(2,1)}, u32[]{:S(2)}, u32[]{:S(2)}) collective-permute-start(bf16[2,512,1024]{2,1,0:T(8,128)(2,1)} %pad_maximum_fusion.10), channel_id=1, source_target_pairs={{0,24},{8,16},{16,8},{24,0},{1,25},{9,17},{17,9},{25,1},{2,26},{10... | collective-permute-start | bytes 6291464 | tf_op jit(solution)/shard_map/ppermute | solution.py:49
  829.8 258.0 %reduce-scatter.8.cloned.1.call-start = ((), (), s32[]{:S(2)}) async-start(), calls=%async_computation.15 | async-start | bytes 7077888 | tf_op jit(solution)/shard_map/reduce_scatter | solution.py:43
  850.2 50.2 %collective-permute-start.43 = (f32[2,512,64]{1,2,0:T(8,128)}, f32[2,512,64]{1,2,0:T(8,128)}, u32[]{:S(2)}, u32[]{:S(2)}) collective-permute-start(f32[2,512,64]{1,2,0:T(8,128)} %pad_maximum_fusion.27), channel_id=1, source_target_pairs={{0,8},{8,0},{16,24},{24,16},{1,9},{9,1},{17,25},{25,17},{2,10},{10... | collective-permute-start | bytes 786440 | tf_op jit(solution)/shard_map/ppermute | solution.py:49
  852.2 102.6 %collective-permute-start.38 = (bf16[2,512,1024]{2,1,0:T(8,128)(2,1)}, bf16[2,512,1024]{2,1,0:T(8,128)(2,1)}, u32[]{:S(2)}, u32[]{:S(2)}) collective-permute-start(bf16[2,512,1024]{2,1,0:T(8,128)(2,1)} %pad_maximum_fusion.12), channel_id=1, source_target_pairs={{0,8},{8,0},{16,24},{24,16},{1,9},{9,1},{17,25},{25,17},{2,10},{10... | collective-permute-start | bytes 6291464 | tf_op jit(solution)/shard_map/ppermute | solution.py:49
  852.7 102.1 %collective-permute-start.39 = (bf16[2,512,1024]{2,1,0:T(8,128)(2,1)}, bf16[2,512,1024]{2,1,0:T(8,128)(2,1)}, u32[]{:S(2)}, u32[]{:S(2)}) collective-permute-start(bf16[2,512,1024]{2,1,0:T(8,128)(2,1)} %pad_maximum_fusion.13), channel_id=1, source_target_pairs={{0,16},{8,24},{16,0},{24,8},{1,17},{9,25},{17,1},{25,9},{2,18},{10... | collective-permute-start | bytes 6291464 | tf_op jit(solution)/shard_map/ppermute | solution.py:49
  854.3 100.5 %collective-permute-start.40 = (bf16[2,512,1024]{2,1,0:T(8,128)(2,1)S(1)}, bf16[2,512,1024]{2,1,0:T(8,128)(2,1)}, u32[]{:S(2)}, u32[]{:S(2)}) collective-permute-start(bf16[2,512,1024]{2,1,0:T(8,128)(2,1)S(1)} %copy-done.41), channel_id=1, source_target_pairs={{0,24},{8,16},{16,8},{24,0},{1,25},{9,17},{17,9},{25,1},{2,26},{10... | collective-permute-start | bytes 6291464 | tf_op jit(solution)/shard_map/ppermute | solution.py:49
  855.2 47.9 %collective-permute-start.41 = (bf16[2,512,256]{2,1,0:T(8,128)(2,1)}, bf16[2,512,256]{2,1,0:T(8,128)(2,1)S(1)}, u32[]{:S(2)}, u32[]{:S(2)}) collective-permute-start(bf16[2,512,256]{2,1,0:T(8,128)(2,1)} %pad_maximum_fusion.26), channel_id=1, source_target_pairs={{0,8},{8,0},{16,24},{24,16},{1,9},{9,1},{17,25},{25,17},{2,10},{10... | collective-permute-start | bytes 1572872 | tf_op jit(solution)/shard_map/ppermute | solution.py:49
  901.4 47.8 %collective-permute-start.44 = (f32[512,64]{0,1:T(8,128)S(1)}, f32[512,64]{0,1:T(8,128)S(1)}, u32[]{:S(2)}, u32[]{:S(2)}) collective-permute-start(f32[512,64]{0,1:T(8,128)S(1)} %fusion.91), channel_id=1, source_target_pairs={{0,16},{8,24},{16,0},{24,8},{1,17},{9,25},{17,1},{25,9},{2,18},{10... | collective-permute-start | bytes 393224 | tf_op jit(solution)/shard_map/ppermute | solution.py:49
  903.2 50.7 %collective-permute-start.42 = (bf16[512,256]{1,0:T(8,128)(2,1)S(1)}, bf16[512,256]{1,0:T(8,128)(2,1)S(1)}, u32[]{:S(2)}, u32[]{:S(2)}) collective-permute-start(bf16[512,256]{1,0:T(8,128)(2,1)S(1)} %fusion.85), channel_id=1, source_target_pairs={{0,16},{8,24},{16,0},{24,8},{1,17},{9,25},{17,1},{25,9},{2,18},{10... | collective-permute-start | bytes 786440 | tf_op jit(solution)/shard_map/ppermute | solution.py:49
  969.1 32.5 %collective-permute-start.45 = (bf16[1,512,1024]{2,1,0:T(8,128)(2,1)}, bf16[1,512,1024]{2,1,0:T(8,128)(2,1)}, u32[]{:S(2)}, u32[]{:S(2)}) collective-permute-start(bf16[1,512,1024]{2,1,0:T(8,128)(2,1)} %get-tuple-element.408), channel_id=1, source_target_pairs={{0,8},{8,0},{16,24},{24,16},{1,9},{9,1},{17,25},{25,17},{2,10},{10... | collective-permute-start | bytes 3145736 | tf_op jit(solution)/shard_map/ppermute | solution.py:49
  969.2 32.4 %collective-permute-start.46 = (bf16[1,512,1024]{2,1,0:T(8,128)(2,1)}, bf16[1,512,1024]{2,1,0:T(8,128)(2,1)}, u32[]{:S(2)}, u32[]{:S(2)}) collective-permute-start(bf16[1,512,1024]{2,1,0:T(8,128)(2,1)} %get-tuple-element.409), channel_id=1, source_target_pairs={{0,16},{8,24},{16,0},{24,8},{1,17},{9,25},{17,1},{25,9},{2,18},{10... | collective-permute-start | bytes 3145736 | tf_op jit(solution)/shard_map/ppermute | solution.py:49
  970.8 46.3 %collective-permute-start.47 = (bf16[1,512,1024]{2,1,0:T(8,128)(2,1)}, bf16[1,512,1024]{2,1,0:T(8,128)(2,1)}, u32[]{:S(2)}, u32[]{:S(2)}) collective-permute-start(bf16[1,512,1024]{2,1,0:T(8,128)(2,1)} %get-tuple-element.410), channel_id=1, source_target_pairs={{0,24},{8,16},{16,8},{24,0},{1,25},{9,17},{17,9},{25,1},{2,26},{10... | collective-permute-start | bytes 3145736 | tf_op jit(solution)/shard_map/ppermute | solution.py:49
  982.1 43.9 %collective-permute-start.48 = (bf16[2,512,768]{2,1,0:T(8,128)(2,1)}, bf16[2,512,768]{2,1,0:T(8,128)(2,1)}, u32[]{:S(2)}, u32[]{:S(2)}) collective-permute-start(bf16[2,512,768]{2,1,0:T(8,128)(2,1)} %pad_maximum_fusion.23), channel_id=1, source_target_pairs={{0,8},{8,0},{16,24},{24,16},{1,9},{9,1},{17,25},{25,17},{2,10},{10... | collective-permute-start | bytes 4718600 | tf_op jit(solution)/shard_map/ppermute | solution.py:49
  1019.2 45.4 %collective-permute-start.51 = (bf16[1,512,1024]{2,1,0:T(8,128)(2,1)S(1)}, bf16[1,512,1024]{2,1,0:T(8,128)(2,1)}, u32[]{:S(2)}, u32[]{:S(2)}) collective-permute-start(bf16[1,512,1024]{2,1,0:T(8,128)(2,1)S(1)} %copy-done.43), channel_id=1, source_target_pairs={{0,24},{8,16},{16,8},{24,0},{1,25},{9,17},{17,9},{25,1},{2,26},{10... | collective-permute-start | bytes 3145736 | tf_op jit(solution)/shard_map/ppermute | solution.py:49
  (149 other events, 2512.0 us)
Sparse Core Ops, SparseCore 0:
  15.5 103.4 all-gather.6
  121.5 73.1 all-gather.8
  196.8 98.1 all-gather.10
  296.9 98.1 all-gather.14
  396.9 98.1 all-gather.12
  599.7 128.0 reduce-scatter.3
  731.1 98.5 all-gather.16
  834.0 116.5 reduce-scatter.5
  965.4 117.5 reduce-scatter.7

commit v5 on v4

--- a/solution.py
+++ b/solution.py
@@ -321,14 +321,17 @@
     )(jnp.stack([core, col]), x, attended, own, other, gain)
 
 
-def expert_kernel(x_ref, c_ref, gate_ref, w_ref, wd_ref, act_ref, grad_ref, sums_ref, dx_ref):
+def expert_kernel(
+    x0_ref, x1_ref, c0_ref, c1_ref, gate_ref, w_ref, wd_ref,
+    act_ref, grad_ref, sums_ref, dx0_ref, dx1_ref,
+):
     width = act_ref.shape[1]
     slot_gate = gate_ref[...]
-    pre = x_ref[...]
-    if pre.dtype == BF16:
-        pre = jnp.dot(pre, w_ref[...], preferred_element_type=F32)
+    rows = jnp.concatenate([x0_ref[...], x1_ref[...]], axis=0)
+    pre = jnp.dot(rows, w_ref[...], preferred_element_type=F32)
     gate, up = pre[:, :width], pre[:, width:]
-    grad = jnp.dot(c_ref[...], wd_ref[...], preferred_element_type=F32)
+    cots = jnp.concatenate([c0_ref[...], c1_ref[...]], axis=0)
+    grad = jnp.dot(cots, wd_ref[...], preferred_element_type=F32)
     opened = 1.0 / (1.0 + jnp.exp(-gate))
     silu = gate * opened
     act = silu * up
@@ -342,27 +345,27 @@
     inner = jnp.sum(dgate.astype(F32) * gate + dup.astype(F32) * up, axis=1, keepdims=True)
     sums_ref[:, 0:1] = grad_gate
     sums_ref[:, 1:2] = inner
-    dx_ref[...] = contract_last(grad_ref[...], w_ref[...], BF16)
-
-
-def run_expert(x, c, slot_gate, w, wd, block):
-    rows, width = x.shape[0], wd.shape[1]
-    by_rows = lambda n: pl.BlockSpec((block, n), lambda i: (i, 0))
-    whole = lambda a: pl.BlockSpec(a.shape, lambda i: (0, 0), pipeline_mode=pl.Buffered(1))
+    back = contract_last(grad_ref[...], w_ref[...], BF16)
+    dx0_ref[...] = back[: dx0_ref.shape[0]]
+    dx1_ref[...] = back[dx0_ref.shape[0] :]
+
+
+def run_expert(xs, cs, slot_gate, w, wd):
+    capacity, width = xs[0].shape[0], wd.shape[1]
+    slots = 2 * capacity
+    operands = [*xs, *cs, slot_gate, w, wd]
+    outs = [(slots, width, BF16), (slots, 2 * width, BF16), (slots, 2, F32)]
+    outs += [(capacity, D, BF16)] * 2
+    whole = lambda shape: pl.BlockSpec(shape, lambda i: (0, 0), pipeline_mode=pl.Buffered(1))
     return pl.pallas_call(
         expert_kernel,
         name="expert",
-        grid=(rows // block,),
-        in_specs=[by_rows(x.shape[1]), by_rows(D), by_rows(1), whole(w), whole(wd)],
-        out_specs=[by_rows(width), by_rows(2 * width), by_rows(2), by_rows(D)],
-        out_shape=[
-            jax.ShapeDtypeStruct((rows, width), BF16),
-            jax.ShapeDtypeStruct((rows, 2 * width), BF16),
-            jax.ShapeDtypeStruct((rows, 2), F32),
-            jax.ShapeDtypeStruct((rows, D), BF16),
-        ],
+        grid=(1,),
+        in_specs=[whole(a.shape) for a in operands],
+        out_specs=[pl.BlockSpec(out[:2], lambda i: (0, 0)) for out in outs],
+        out_shape=[jax.ShapeDtypeStruct(out[:2], out[2]) for out in outs],
         cost_estimate=cost(1000, 1000),
-    )(x, c, slot_gate, w, wd)
+    )(*operands)
 
 
 def through_heads_kernel(grad_ref, w_ref, out_ref):
@@ -618,13 +621,17 @@
     normed2 = tied(normed2)
     column_start = col * feat_local
 
-    def chosen_rows(e, values):
-        return [plain_dot(picks[e][step], values, BF16) for step in steps]
-
-    sent_rows = []
-    for e in range(per_device):
-        sent_rows.append(chosen_rows(e, after(normed2, sent_rows)))
-    all_rows = [trade_all(pieces) for pieces in sent_rows]
+    all_rows = [[None] * n_row for e in range(per_device)]
+
+    def send_rows(e, held, values):
+        rows = [plain_dot(picks[e][step], values, BF16) for step in held]
+        for step, row_piece in zip(held, rows):
+            all_rows[e][step] = trade(row_piece, step, n_row)
+        return rows
+
+    sent = [send_rows(0, far, normed2)]
+    near_values = after(normed2, sent)
+    sent += [send_rows(e, near, near_values) for e in range(per_device)]
 
     def grad_rows_of(base, cots):
         table = far_ranks[base] if base else slot_rank.astype(F32)
@@ -634,19 +641,17 @@
             for e in range(per_device):
                 pick = (of_peer(table, step, e) == slots[:, None].astype(F32)).astype(BF16)
                 held.append(plain_dot(pick, cots, BF16))
-            halves.append(jnp.stack(held))
+            halves.append(held)
         return halves
 
     grad_rows_at = {}
 
     def hand_on(base, halves):
-        grad_rows_at[base], grad_rows_at[base + 1] = halves[0], trade(halves[1], 1, n_row)
-
-    for base in far_bases:
-        hand_on(base, grad_rows_of(base, after(cot_alls[base], sent_rows, all_rows[0])))
+        grad_rows_at[base] = halves[0]
+        grad_rows_at[base + 1] = [trade(piece, 1, n_row) for piece in halves[1]]
 
     logits = lax.dot_general(
-        router_all, after(normed2, sent_rows), (((0,), (1,)), ((), ())), preferred_element_type=F32
+        router_all, after(normed2, sent), (((0,), (1,)), ((), ())), preferred_element_type=F32
     )
     top_logit = jnp.max(jnp.where(chosen, logits, -jnp.inf), axis=0, keepdims=True)
     raised = jnp.where(chosen, jnp.exp(logits - top_logit), 0.0)
@@ -662,62 +667,76 @@
         slot_gates.append(jnp.stack(held))
     slot_gates = swap_small(slot_gates)
 
+    all_rows[0], slot_gates, later_rows = lax.optimization_barrier(
+        (all_rows[0], slot_gates, normed2)
+    )
+    for e in range(1, per_device):
+        sent.append(send_rows(e, far, later_rows))
+    far_cots = after([cot_alls[base] for base in far_bases], sent, later_rows)
+    for base, cots in zip(far_bases, far_cots):
+        hand_on(base, grad_rows_of(base, cots))
+
     both = range(per_device)
     calls, grads_back = {}, [[None] * n_row for e in range(per_device)]
 
-    def rows_and_gates(e, held):
-        rows = jnp.concatenate([all_rows[e][step] for step in held])
-        return rows, jnp.concatenate([slot_gates[step][e] for step in held])[:, None]
-
-    def expert_call(e, held, rows, slot_gate, pre=None):
-        grad_rows = jnp.concatenate([grad_rows_at[step][e] for step in held])
-        first = rows if pre is None else pre
-        results = run_expert(first, grad_rows, slot_gate, w_in[e], w_back[e], 2 * capacity)
-        calls[e, held[0]] = [rows, grad_rows, *results]
-
-    def send_back(e, held):
-        grads = calls[e, held[0]][-1]
-        for i, step in enumerate(held):
-            piece = grads[i * capacity : (i + 1) * capacity]
-            grads_back[e][step] = trade(piece, step, n_row)
-
-    expert_call(0, far, *rows_and_gates(0, far))
-    send_back(0, far)
+    def gates_of(e, step):
+        return jnp.concatenate([slot_gates[step][e], slot_gates[step + 1][e]])[:, None]
+
+    def expert_call(e, step, gates):
+        xs = [all_rows[e][step], all_rows[e][step + 1]]
+        cs = [grad_rows_at[step][e], grad_rows_at[step + 1][e]]
+        act, grad_pre, sums, *back = run_expert(xs, cs, gates, w_in[e], w_back[e])
+        calls[e, step] = [xs, cs, [act], [grad_pre], [sums], back]
+
+    def send_back(e, step):
+        for i, piece in enumerate(calls[e, step][-1]):
+            grads_back[e][step + i] = trade(piece, step + i, n_row)
+
+    def far_calls(e):
+        return [calls[e, step] for step in far_bases]
+
+    for step in far_bases:
+        expert_call(0, step, gates_of(0, step))
+        send_back(0, step)
     for e in range(1, per_device):
-        all_rows[e] = after(all_rows[e], calls[0, 2])
-        expert_call(e, far, *rows_and_gates(e, far))
-    near_inputs = [rows_and_gates(e, near) for e in both]
-    near_inputs = [(*held, plain_dot(held[0], w_in[e])) for e, held in enumerate(near_inputs)]
-    near_cots, near_inputs, _ = lax.optimization_barrier(
-        (cot_alls[0], near_inputs, [calls[e, 2] for e in both])
+        all_rows[e] = after(all_rows[e], far_calls(0))
+        for step in far_bases:
+            expert_call(e, step, gates_of(e, step))
+    every = [(e, step) for e in range(per_device) for step in steps]
+    ranks = jnp.concatenate([of_peer(slot_rank, step, e) for e, step in every])
+    near_gates = [gates_of(e, 0) for e in both]
+    near_cots, near_gates, ranks, _ = lax.optimization_barrier(
+        (cot_alls[0], near_gates, ranks, [far_calls(e) for e in both])
     )
     near_halves = grad_rows_of(0, near_cots)
     for e in range(1, per_device):
-        calls[e, 2], grads_back[e - 1], near_halves = lax.optimization_barrier(
-            (calls[e, 2], grads_back[e - 1], near_halves)
+        held, grads_back[e - 1], near_halves = lax.optimization_barrier(
+            (far_calls(e), grads_back[e - 1], near_halves)
         )
-        send_back(e, far)
+        for step, call in zip(far_bases, held):
+            calls[e, step] = call
+            send_back(e, step)
     hand_on(0, near_halves)
     for e in range(per_device):
-        expert_call(e, near, *near_inputs[e])
-        send_back(e, near)
+        expert_call(e, 0, near_gates[e])
+        send_back(e, 0)
     last_near = (per_device - 1, 0)
     calls[last_near], grads_back[-1] = lax.optimization_barrier((calls[last_near], grads_back[-1]))
-    scalars = [jnp.concatenate([calls[e, 0][4], calls[e, 2][4]]) for e in range(per_device)]
+
+    def joined(e, which):
+        return jnp.concatenate([piece for step in steps[::2] for piece in calls[e, step][which]])
+
+    scalars = [joined(e, 4) for e in range(per_device)]
     scalars = jnp.stack(scalars)
     scalars_back = swap_small(
         [scalars[:, step * capacity : (step + 1) * capacity] for step in steps]
     )
-    every = [(e, step) for e in range(per_device) for step in steps]
-    ranks = jnp.concatenate([of_peer(slot_rank, step, e) for e, step in every])
     grad_normed2_part = combine(ranks, [grads_back[e][step] for e, step in every])
 
     calls = after(calls, grad_normed2_part)
     branch_back, weight_grads = [], []
     for e in range(per_device):
-        rows, grad_rows, act, grad_pre = (
-            jnp.concatenate([calls[e, 0][i], calls[e, 2][i]]) for i in range(4)
-        )
+        rows, grad_rows, act, grad_pre = (joined(e, which) for which in range(4))
         out = contract_last(act, w_back[e], BF16)
         branch_back.append(
             trade_all([out[step * capacity : (step + 1) * capacity] for step in steps])

time: 1120 us -> 1090 us (0.973)
  local copies, waits for them, and re-layouts: 178 us -> 155 us
  waiting for transfers between devices: 396 us -> 413 us
  other arithmetic: 83.7 us -> 72.5 us
    all_gather x6, waiting for transfers between devices: 8.91 us -> 22 us  [gather_features(): return lax.all_gather(local_rows, 'col', axis=1, tiled=True)]
    dot_general x20 -> x18, matrix products: 70.1 us -> 58.3 us  [plain_dot(): return jnp.dot(left_op, right_op, preferred_element_type=F32).astype(kind)]
    slice x5 -> x4, local copies, waits for them, and re-layouts: 11.5 us -> 0.02 us  [the longest x2 0.01 us: gates_of(): slot_gates[step][e]]
    ppermute x56 -> x58, waiting for transfers between devices: 333 us -> 343 us  [trade(): return lax.ppermute(value, 'row', [(r, r ^ step) for r in range(n_row)])]
    unnamed x272 -> x237, local copies, waits for them, and re-layouts: 27.2 us -> 24.3 us
    ppermute x56 -> x58, starting transfers between devices: 41 us -> 41 us  [trade(): return lax.ppermute(value, 'row', [(r, r ^ step) for r in range(n_row)])]
  transfers between devices with their start and end apart: 68 -> 70, of which waited for: 26 -> 28; matrix products, arithmetic and copies ran while one was open for 33% -> 29% of each run, Pallas kernels for 18% -> 19%
where the time goes in v5:
time: 1090 us; the launch traced here: 1080 us
  waiting for transfers between devices  413 us (38%)
  Pallas kernels  238 us (22%)
  local copies, waits for them, and re-layouts  155 us (14%)
  matrix products  128 us (12%)
  other arithmetic  72.5 us (7%)
  starting transfers between devices  51.5 us (5%)
  between operations  16.1 us (1%)
    ppermute x58, waiting for transfers between devices, trade(): return lax.ppermute(value, 'row', [(r, r ^ step) for r in range(n_row)])  343 us
    pallas_call x4, Pallas kernels, run_expert(): pl.pallas_call(expert_kernel, name='expert', grid=(1,), in_specs=[whole(a...  73.4 us
    dot_general x18, matrix products, plain_dot(): return jnp.dot(left_op, right_op, preferred_element_type=F32).astype(kind)  58.3 us
    dot_general x6, matrix products, contract_first(): lax.dot_general(left_op, right_op, (((0,), (0,)), ((), ())), preferred_el...  46.9 us
    ppermute x58, starting transfers between devices, trade(): return lax.ppermute(value, 'row', [(r, r ^ step) for r in range(n_row)])  41 us
    pallas_call x2, Pallas kernels, combine(): pl.pallas_call(combine_kernel, name='combine', grid=(D // width, rows //...  39.8 us
    pallas_call x3, Pallas kernels, place(): pl.pallas_call(place_kernel, name='place', grid_spec=pltpu.PrefetchScalar...  32.9 us
    all_to_all x2, waiting for transfers between devices, swap_small(): table = lax.all_to_all(table, 'row', 0, 0, tiled=True)  28.7 us
  transfers between devices with their start and end apart: 70, of which 28 were waited for; matrix products, arithmetic and copies ran while one was open for 29% of the time, Pallas kernels for 19%

profile of v5, /device:TPU:0, one launch (start us, length us, event | category | flops | bytes accessed | tf_op | source)
XLA Modules:
  0.0 1083.8 jit_solution(14910565578697616607)
XLA Ops:
  22.9 6.1 constant_dynamic-slice_fusion.48
  60.7 30.2 %collective-permute-done.1 = bf16[2,512,1024]{2,1,0:T(8,128)(2,1)} collective-permute-done((bf16[2,512,1024]{2,1,0:T(8,128)(2,1)}, bf16[2,512,1024]{2,1,0:T(8,128)(2,1)}, u32[]{:S(2)}, u32[]{:S(2)}) %collective-permute-start.1) | collective-permute-done | bytes 2097184 | tf_op jit(solution)/shard_map/ppermute | solution.py:49
  104.1 7.2 scatter_custom_fusion
  133.5 5.5 collective-permute-done.2
  145.5 13.9 %project.1 = (bf16[1536,2048]{1,0:T(8,128)(2,1)}, f32[1536,1]{1,0:T(8,128)}, f32[1536,512]{1,0:T(8,128)}, bf16[1536,256]{1,0:T(8,128)(2,1)}, bf16[1536,256]{1,0:T(8,128)(2,1)}, /*index=5*/bf16[1536,256]{1,0:T(8,128)(2,1)}) custom-call(bf16[1552,2048]{1,0:T(8,128)(2,1)} %all-gather.7.cloned.1.call-done.x_ref, f32[1,2048]{1,0:T(1,128)} %get-tuple-element.672.gain_ref, ...), custom_call_target="tpu_custom_call" | custom-call | flops 1000 | bytes 1000 | tf_op jit(solution)/shard_map/project/pallas_call | solution.py:117
  159.4 16.8 %attend.1 = (bf16[1536,256]{1,0:T(8,128)(2,1)}, f32[2,1536,1]{2,1,0:T(8,128)}) custom-call(bf16[1536,256]{1,0:T(8,128)(2,1)} %get-tuple-element.267.q_ref, bf16[1536,256]{1,0:T(8,128)(2,1)} %get-tuple-element.268.k_ref, bf16[1536,256]{1,0:T(8,128)(2,1)} %get-tuple-element.269.v_ref, s32[1536,1]{1,0:T(8,128)} %broadcast_in_dim.654.seg_q_ref, ...), custom_call_target="tpu_custom_call" | custom-call | flops 1000 | bytes 1000 | tf_op jit(solution)/shard_map/attend/pallas_call | solution.py:167
  181.8 7.6 collective-permute-done.7
  196.4 17.3 %collective-permute-done.8 = bf16[1536,256]{1,0:T(8,128)(2,1)S(1)} collective-permute-done((bf16[1536,256]{1,0:T(8,128)(2,1)S(1)}, bf16[1536,256]{1,0:T(8,128)(2,1)S(1)}, u32[]{:S(2)}, u32[]{:S(2)}) %collective-permute-start.8) | collective-permute-done | bytes 786464 | tf_op jit(solution)/shard_map/ppermute | solution.py:49
  215.2 44.8 %collective-permute-done.9 = bf16[2,512,1024]{2,1,0:T(8,128)(2,1)S(1)} collective-permute-done((bf16[2,512,1024]{2,1,0:T(8,128)(2,1)}, bf16[2,512,1024]{2,1,0:T(8,128)(2,1)S(1)}, u32[]{:S(2)}, u32[]{:S(2)}) %collective-permute-start.9) | collective-permute-done | bytes 2097184 | tf_op jit(solution)/shard_map/ppermute | solution.py:49
  270.2 38.0 %collective-permute-done.10 = bf16[2,512,1024]{2,1,0:T(8,128)(2,1)S(1)} collective-permute-done((bf16[2,512,1024]{2,1,0:T(8,128)(2,1)}, bf16[2,512,1024]{2,1,0:T(8,128)(2,1)S(1)}, u32[]{:S(2)}, u32[]{:S(2)}) %collective-permute-start.10) | collective-permute-done | bytes 2097184 | tf_op jit(solution)/shard_map/ppermute | solution.py:49
  317.2 22.8 %branch.1 = (bf16[1536,2048]{1,0:T(8,128)(2,1)}, f32[1536,1]{1,0:T(8,128)}, f32[1536,256]{1,0:T(8,128)}) custom-call(s32[2]{0:T(128)} %pad_add_fusion.at_ref, bf16[1552,2048]{1,0:T(8,128)(2,1)} %all-gather.7.cloned.1.call-done.x_ref, bf16[1536,2048]{1,0:T(8,128)(2,1)} %all-gather.11.cloned.1.call-done.att_ref, ...), custom_call_target="tpu_custom_call" | custom-call | flops 1000 | bytes 1000 | tf_op jit(solution)/shard_map/branch/pallas_call | solution.py:305
  346.1 13.0 %collective-permute-done.13 = bf16[1,512,1024]{2,1,0:T(8,128)(2,1)} collective-permute-done((bf16[1,512,1024]{2,1,0:T(8,128)(2,1)S(1)}, bf16[1,512,1024]{2,1,0:T(8,128)(2,1)}, u32[]{:S(2)}, u32[]{:S(2)}) %collective-permute-start.13) | collective-permute-done | bytes 1048608 | tf_op jit(solution)/shard_map/ppermute | solution.py:49
  391.6 18.1 %all-to-all-done = f32[4,2,240]{2,1,0:T(2,128)S(1)} async-done(((f32[4,2,240]{2,1,0:T(2,128)}), f32[4,2,240]{2,1,0:T(2,128)S(1)}, u32[]{:S(2)}, u32[]{:S(2)}) %all-to-all-start) | async-done | bytes 7712 | tf_op jit(solution)/shard_map/all_to_all | solution.py:590
  411.6 5.6 convolution_convert_fusion.15
  436.5 18.7 %expert.4 = (bf16[480,1024]{1,0:T(8,128)(2,1)}, bf16[480,2048]{1,0:T(8,128)(2,1)}, f32[480,2]{1,0:T(8,128)}, bf16[240,2048]{1,0:T(8,128)(2,1)}, bf16[240,2048]{1,0:T(8,128)(2,1)}) custom-call(bf16[240,2048]{1,0:T(8,128)(2,1)} %collective-permute-done.15.x0_ref, bf16[240,2048]{1,0:T(8,128)(2,1)} %collective-permute-done.16.x1_ref, ...), custom_call_target="tpu_custom_call" | custom-call | flops 1000 | bytes 1000 | tf_op jit(solution)/shard_map/expert/pallas_call | solution.py:360
  456.6 6.3 collective-permute-done.20.x0_ref
  463.8 18.2 %expert.5 = (bf16[480,1024]{1,0:T(8,128)(2,1)}, bf16[480,2048]{1,0:T(8,128)(2,1)}, f32[480,2]{1,0:T(8,128)}, bf16[240,2048]{1,0:T(8,128)(2,1)}, bf16[240,2048]{1,0:T(8,128)(2,1)}) custom-call(bf16[240,2048]{1,0:T(8,128)(2,1)} %collective-permute-done.20.x0_ref, bf16[240,2048]{1,0:T(8,128)(2,1)} %collective-permute-done.21.x1_ref, ...), custom_call_target="tpu_custom_call" | custom-call | flops 1000 | bytes 1000 | tf_op jit(solution)/shard_map/expert/pallas_call | solution.py:360
  482.0 13.0 %all-gather.13.cloned.1.call-done = bf16[1536,2048]{1,0:T(8,128)(2,1)} async-done(((bf16[1536,256]{1,0:T(8,128)(2,1)}), bf16[1536,2048]{1,0:T(8,128)(2,1)}) %all-gather.13.cloned.1.call-update) | async-done | bytes 6291472 | tf_op jit(solution)/shard_map/all_gather | solution.py:39
  495.0 5.6 convolution_convert_fusion.7
  513.9 18.4 %expert.7 = (bf16[480,1024]{1,0:T(8,128)(2,1)}, bf16[480,2048]{1,0:T(8,128)(2,1)}, f32[480,2]{1,0:T(8,128)}, bf16[240,2048]{1,0:T(8,128)(2,1)}, bf16[240,2048]{1,0:T(8,128)(2,1)}) custom-call(bf16[240,2048]{1,0:T(8,128)(2,1)} %convolution_convert_fusion.18.x0_ref, bf16[240,2048]{1,0:T(8,128)(2,1)} %collective-permute-done.19.x1_ref, ...), custom_call_target="tpu_custom_call" | custom-call | flops 1000 | bytes 1000 | tf_op jit(solution)/shard_map/expert/pallas_call | solution.py:360
  534.8 18.1 %expert.6 = (bf16[480,1024]{1,0:T(8,128)(2,1)}, bf16[480,2048]{1,0:T(8,128)(2,1)}, f32[480,2]{1,0:T(8,128)}, bf16[240,2048]{1,0:T(8,128)(2,1)}, bf16[240,2048]{1,0:T(8,128)(2,1)}) custom-call(bf16[240,2048]{1,0:T(8,128)(2,1)} %convolution_convert_fusion.20.x0_ref, bf16[240,2048]{1,0:T(8,128)(2,1)} %collective-permute-done.14.x1_ref, ...), custom_call_target="tpu_custom_call" | custom-call | flops 1000 | bytes 1000 | tf_op jit(solution)/shard_map/expert/pallas_call | solution.py:360
  559.9 19.9 %combine.2 = bf16[1536,2048]{1,0:T(8,128)(2,1)} custom-call(s32[8,1536]{1,0:T(8,128)} %concatenate.113.refs_0_, bf16[240,2048]{1,0:T(8,128)(2,1)} %get-tuple-element.346.refs_1_, bf16[240,2048]{1,0:T(8,128)(2,1)} %copy-done.53, bf16[240,2048]{1,0:T(8,128)(2,1)} %copy-done.51, bf16[240,2048]{1,0:T(8,128)(2,1)} %collective-permute-done.24.refs_4_, ...), custom_call_target="tpu_custom_call" | custom-call | flops 1000 | bytes 1000 | tf_op jit(solution)/shard_map/combine/pallas_call | solution.py:408
  581.4 7.5 convolution_convert_fusion.2
  593.1 7.5 convolution_convert_fusion.3
  609.0 11.9 %convolution_convert_fusion.1 = bf16[2048,2048]{1,0:T(8,128)(2,1)S(1)} fusion(bf16[240,2048]{1,0:T(8,128)(2,1)} %collective-permute-done.16.x1_ref, bf16[240,2048]{1,0:T(8,128)(2,1)} %collective-permute-done.15.x0_ref, bf16[240,2048]{1,0:T(8,128)(2,1)} %collective-permute-done.14.x1_ref, bf16[240,2048]{1,0:T(8,128)(2,1)S(1)} %copy-done.46, ...), kind=kOutput, calls=%fused_computation.9 | convolution fusion | flops 8080850944 | bytes 16252928 | tf_op jit(solution)/shard_map/dot_general | solution.py:63
  622.4 12.0 %convolution_convert_fusion = bf16[2048,2048]{1,0:T(8,128)(2,1)S(1)} fusion(bf16[240,2048]{1,0:T(8,128)(2,1)} %collective-permute-done.21.x1_ref, bf16[240,2048]{1,0:T(8,128)(2,1)} %collective-permute-done.20.x0_ref, bf16[240,2048]{1,0:T(8,128)(2,1)} %collective-permute-done.19.x1_ref, bf16[240,2048]{1,0:T(8,128)(2,1)} %convolution_convert_fusion.18.x0_ref, ...), kind=kOutput, calls=%fused_computation.8 | convolution fusion | flops 8080850944 | bytes 16252928 | tf_op jit(solution)/shard_map/dot_general | solution.py:63
  647.0 10.7 all-to-all-done.1
  673.2 12.4 %collective-permute-done.36.refs_8_ = bf16[240,2048]{1,0:T(8,128)(2,1)} collective-permute-done((bf16[240,2048]{1,0:T(8,128)(2,1)}, bf16[240,2048]{1,0:T(8,128)(2,1)}, u32[]{:S(2)}, u32[]{:S(2)}) %collective-permute-start.36) | collective-permute-done | bytes 983072 | tf_op jit(solution)/shard_map/ppermute | solution.py:49
  689.9 15.3 %reduce-scatter.4.cloned.1.call-done = bf16[1536,256]{1,0:T(8,128)(2,1)} async-done(((bf16[1536,2048]{1,0:T(8,128)(2,1)}), bf16[1536,256]{1,0:T(8,128)(2,1)}) %reduce-scatter.4.cloned.1.call-update) | async-done | bytes 786448 | tf_op jit(solution)/shard_map/reduce_scatter | solution.py:43
  710.5 19.9 %combine.3 = bf16[1536,2048]{1,0:T(8,128)(2,1)} custom-call(s32[8,1536]{1,0:T(8,128)} %concatenate.113.refs_0_, bf16[240,2048]{1,0:T(8,128)(2,1)} %get-tuple-element.415.refs_1_, bf16[240,2048]{1,0:T(8,128)(2,1)} %collective-permute-done.31.refs_2_, bf16[240,2048]{1,0:T(8,128)(2,1)} %collective-permute-done.32.refs_3_, ...), custom_call_target="tpu_custom_call" | custom-call | flops 1000 | bytes 1000 | tf_op jit(solution)/shard_map/combine/pallas_call | solution.py:408
  730.4 27.0 %collective-permute-done.38.refs_2_ = bf16[2,512,1024]{2,1,0:T(8,128)(2,1)} collective-permute-done((bf16[2,512,1024]{2,1,0:T(8,128)(2,1)}, bf16[2,512,1024]{2,1,0:T(8,128)(2,1)}, u32[]{:S(2)}, u32[]{:S(2)}) %collective-permute-start.38) | collective-permute-done | bytes 2097184 | tf_op jit(solution)/shard_map/ppermute | solution.py:49
  757.4 44.0 %collective-permute-done.39.refs_3_ = bf16[2,512,1024]{2,1,0:T(8,128)(2,1)} collective-permute-done((bf16[2,512,1024]{2,1,0:T(8,128)(2,1)}, bf16[2,512,1024]{2,1,0:T(8,128)(2,1)}, u32[]{:S(2)}, u32[]{:S(2)}) %collective-permute-start.39) | collective-permute-done | bytes 2097184 | tf_op jit(solution)/shard_map/ppermute | solution.py:49
  801.5 6.0 all-gather.17.cloned.1.call-done
  808.1 7.4 fusion.38
  833.8 11.0 %place.3 = f32[8,512,1024]{2,1,0:T(8,128)} custom-call(s32[8]{0:T(128)} %stack.313.at_ref, bf16[2,512,1024]{2,1,0:T(8,128)(2,1)} %pad_maximum_fusion.7.refs_0_, bf16[2,512,1024]{2,1,0:T(8,128)(2,1)} %copy-done.33, bf16[2,512,1024]{2,1,0:T(8,128)(2,1)} %collective-permute-done.38.refs_2_, bf16[2,512,1024]{2,1,0:T(8,128)(2,1)} %collective-permute-done.39.refs_3_), custom_call_target="tpu_custom_call" | custom-call | flops 1000 | bytes 1000 | tf_op jit(solution)/shard_map/place/pallas_call | solution.py:432
  844.8 5.9 convolution_convert_fusion.6.grad_ref
  850.7 27.5 %attend_back.1 = (bf16[1536,256]{1,0:T(8,128)(2,1)}, bf16[1536,256]{1,0:T(8,128)(2,1)}, bf16[1536,256]{1,0:T(8,128)(2,1)}, f32[1,128]{1,0:T(1,128)}, f32[1,128]{1,0:T(1,128)}) custom-call(bf16[1536,256]{1,0:T(8,128)(2,1)} %get-tuple-element.267.q_ref, bf16[1536,256]{1,0:T(8,128)(2,1)} %get-tuple-element.268.k_ref, ...), custom_call_target="tpu_custom_call" | custom-call | flops 1000 | bytes 1000 | tf_op jit(solution)/shard_map/attend_back/pallas_call | solution.py:250
  884.4 42.9 %collective-permute-done.46 = f32[512,64]{0,1:T(8,128)S(1)} collective-permute-done((f32[512,64]{0,1:T(8,128)S(1)}, f32[512,64]{0,1:T(8,128)S(1)}, u32[]{:S(2)}, u32[]{:S(2)}) %collective-permute-start.46) | collective-permute-done | bytes 131104 | tf_op jit(solution)/shard_map/ppermute | solution.py:49
  932.9 10.4 through_heads.1
  949.1 8.6 convolution_convert_fusion.4
  963.3 11.0 %place.4 = f32[8,512,1024]{2,1,0:T(8,128)} custom-call(s32[8]{0:T(128)} %stack.313.at_ref, bf16[2,512,1024]{2,1,0:T(8,128)(2,1)} %pad_maximum_fusion.11.refs_0_, bf16[2,512,1024]{2,1,0:T(8,128)(2,1)} %collective-permute-done.40.refs_1_, bf16[2,512,1024]{2,1,0:T(8,128)(2,1)} %collective-permute-done.41.refs_2_, ...), custom_call_target="tpu_custom_call" | custom-call | flops 1000 | bytes 1000 | tf_op jit(solution)/shard_map/place/pallas_call | solution.py:432
  974.2 5.4 gather_fusion.2
  979.6 15.5 %collective-permute-done.49.refs_3_ = bf16[1,512,1024]{2,1,0:T(8,128)(2,1)} collective-permute-done((bf16[1,512,1024]{2,1,0:T(8,128)(2,1)}, bf16[1,512,1024]{2,1,0:T(8,128)(2,1)}, u32[]{:S(2)}, u32[]{:S(2)}) %collective-permute-start.49) | collective-permute-done | bytes 1048608 | tf_op jit(solution)/shard_map/ppermute | solution.py:49
  997.2 6.7 multiply_reduce_fusion
  1007.6 9.8 all_to_all.24
  1022.1 20.5 %collective-permute-done.53.refs_7_ = bf16[1,512,1024]{2,1,0:T(8,128)(2,1)} collective-permute-done((bf16[1,512,1024]{2,1,0:T(8,128)(2,1)S(1)}, bf16[1,512,1024]{2,1,0:T(8,128)(2,1)}, u32[]{:S(2)}, u32[]{:S(2)}) %collective-permute-start.53) | collective-permute-done | bytes 1048608 | tf_op jit(solution)/shard_map/ppermute | solution.py:49
  1047.0 11.0 %place.5 = f32[8,512,1024]{2,1,0:T(8,128)} custom-call(s32[16]{0:T(128)} %stack.335.at_ref, bf16[1,512,1024]{2,1,0:T(8,128)(2,1)} %get-tuple-element.498.refs_0_, bf16[1,512,1024]{2,1,0:T(8,128)(2,1)} %collective-permute-done.47.refs_1_, bf16[1,512,1024]{2,1,0:T(8,128)(2,1)} %collective-permute-done.48.refs_2_, ...), custom_call_target="tpu_custom_call" | custom-call | flops 1000 | bytes 1000 | tf_op jit(solution)/shard_map/place/pallas_call | solution.py:432
  1058.0 5.2 collective-permute-done.55
  (600 shorter events, 329.5 us)
Async XLA Ops:
  7.2 134.9 %all-gather.7.cloned.1.call-start = ((), (), s32[]{:S(2)}) async-start(), calls=%async_computation.7 | async-start | bytes 7151616 | tf_op jit(solution)/shard_map/all_gather | solution.py:39
  15.3 179.4 %all-gather.9.cloned.1.call-start = ((), (), s32[]{:S(2)}) async-start(), calls=%async_computation.8 | async-start | bytes 4718592 | tf_op jit(solution)/shard_map/all_gather | solution.py:39
  17.5 34.0 %collective-permute-start.3 = (bf16[512,1088]{0,1:T(8,128)(2,1)}, bf16[512,1088]{0,1:T(8,128)(2,1)}, u32[]{:S(2)}, u32[]{:S(2)}) collective-permute-start(bf16[512,1088]{0,1:T(8,128)(2,1)} %copy.61), channel_id=1, source_target_pairs={{0,8},{8,0},{16,24},{24,16},{1,9},{9,1},{17,25},{25,17},{2,10},{10... | collective-permute-start | bytes 3342344 | tf_op jit(solution)/shard_map/ppermute | solution.py:49
  32.8 58.1 %collective-permute-start.1 = (bf16[2,512,1024]{2,1,0:T(8,128)(2,1)}, bf16[2,512,1024]{2,1,0:T(8,128)(2,1)}, u32[]{:S(2)}, u32[]{:S(2)}) collective-permute-start(bf16[2,512,1024]{2,1,0:T(8,128)(2,1)} %get-tuple-element.261), channel_id=1, source_target_pairs={{0,16},{8,24},{16,0},{24,8},{1,17},{9,25},{17,1},{25,9},{2,18},{10... | collective-permute-start | bytes 6291464 | tf_op jit(solution)/shard_map/ppermute | solution.py:49
  43.5 83.9 %collective-permute-start = (bf16[6,512,1024]{2,1,0:T(8,128)(2,1)}, bf16[6,512,1024]{2,1,0:T(8,128)(2,1)}, u32[]{:S(2)}, u32[]{:S(2)}) collective-permute-start(bf16[6,512,1024]{2,1,0:T(8,128)(2,1)} %get-tuple-element.569), channel_id=1, source_target_pairs={{0,8},{8,0},{16,24},{24,16},{1,9},{9,1},{17,25},{25,17},{2,10},{10... | collective-permute-start | bytes 18874376 | tf_op jit(solution)/shard_map/ppermute | solution.py:49
  91.0 220.3 %all-gather.11.cloned.1.call-start = ((), (), s32[]{:S(2)}) async-start(), calls=%async_computation.9 | async-start | bytes 7077888 | tf_op jit(solution)/shard_map/all_gather | solution.py:39
  91.0 48.0 %collective-permute-start.2 = (bf16[2,512,1024]{2,1,0:T(8,128)(2,1)}, bf16[2,512,1024]{2,1,0:T(8,128)(2,1)}, u32[]{:S(2)}, u32[]{:S(2)}) collective-permute-start(bf16[2,512,1024]{2,1,0:T(8,128)(2,1)} %pad_maximum_fusion.3), channel_id=1, source_target_pairs={{0,24},{8,16},{16,8},{24,0},{1,25},{9,17},{17,9},{25,1},{2,26},{10... | collective-permute-start | bytes 6291464 | tf_op jit(solution)/shard_map/ppermute | solution.py:49
  142.0 37.5 %collective-permute-start.6 = (bf16[1,512,1024]{2,1,0:T(8,128)(2,1)}, bf16[1,512,1024]{2,1,0:T(8,128)(2,1)}, u32[]{:S(2)}, u32[]{:S(2)}) collective-permute-start(bf16[1,512,1024]{2,1,0:T(8,128)(2,1)} %get-tuple-element.278), channel_id=1, source_target_pairs={{0,16},{8,24},{16,0},{24,8},{1,17},{9,25},{17,1},{25,9},{2,18},{10... | collective-permute-start | bytes 3145736 | tf_op jit(solution)/shard_map/ppermute | solution.py:49
  144.0 45.4 %collective-permute-start.7 = (bf16[1,512,1024]{2,1,0:T(8,128)(2,1)}, bf16[1,512,1024]{2,1,0:T(8,128)(2,1)}, u32[]{:S(2)}, u32[]{:S(2)}) collective-permute-start(bf16[1,512,1024]{2,1,0:T(8,128)(2,1)} %get-tuple-element.279), channel_id=1, source_target_pairs={{0,24},{8,16},{16,8},{24,0},{1,25},{9,17},{17,9},{25,1},{2,26},{10... | collective-permute-start | bytes 3145736 | tf_op jit(solution)/shard_map/ppermute | solution.py:49
  194.7 227.0 %all-gather.15.cloned.1.call-start = ((), (), s32[]{:S(2)}) async-start(), calls=%async_computation.11 | async-start | bytes 7077888 | tf_op jit(solution)/shard_map/all_gather | solution.py:39
  213.7 46.3 %collective-permute-start.9 = (bf16[2,512,1024]{2,1,0:T(8,128)(2,1)}, bf16[2,512,1024]{2,1,0:T(8,128)(2,1)S(1)}, u32[]{:S(2)}, u32[]{:S(2)}) collective-permute-start(bf16[2,512,1024]{2,1,0:T(8,128)(2,1)} %get-tuple-element.292), channel_id=1, source_target_pairs={{0,16},{8,24},{16,0},{24,8},{1,17},{9,25},{17,1},{25,9},{2,18},{10... | collective-permute-start | bytes 6291464 | tf_op jit(solution)/shard_map/ppermute | solution.py:49
  260.1 235.0 %all-gather.13.cloned.1.call-start = ((), (), s32[]{:S(2)}) async-start(), calls=%async_computation.10 | async-start | bytes 7077888 | tf_op jit(solution)/shard_map/all_gather | solution.py:39
  260.1 48.1 %collective-permute-start.10 = (bf16[2,512,1024]{2,1,0:T(8,128)(2,1)}, bf16[2,512,1024]{2,1,0:T(8,128)(2,1)S(1)}, u32[]{:S(2)}, u32[]{:S(2)}) collective-permute-start(bf16[2,512,1024]{2,1,0:T(8,128)(2,1)} %pad_maximum_fusion.6), channel_id=1, source_target_pairs={{0,24},{8,16},{16,8},{24,0},{1,25},{9,17},{17,9},{25,1},{2,26},{10... | collective-permute-start | bytes 6291464 | tf_op jit(solution)/shard_map/ppermute | solution.py:49
  310.8 80.2 %collective-permute-start.17 = (f32[8,1536]{1,0:T(8,128)S(1)}, f32[8,1536]{1,0:T(8,128)S(1)}, u32[]{:S(2)}, u32[]{:S(2)}) collective-permute-start(f32[8,1536]{1,0:T(8,128)S(1)} %get-tuple-element.716), channel_id=1, source_target_pairs={{0,16},{8,24},{16,0},{24,8},{1,17},{9,25},{17,1},{25,9},{2,18},{10... | collective-permute-start | bytes 147464 | tf_op jit(solution)/shard_map/ppermute | solution.py:49
  313.1 46.0 %collective-permute-start.13 = (bf16[1,512,1024]{2,1,0:T(8,128)(2,1)S(1)}, bf16[1,512,1024]{2,1,0:T(8,128)(2,1)}, u32[]{:S(2)}, u32[]{:S(2)}) collective-permute-start(bf16[1,512,1024]{2,1,0:T(8,128)(2,1)S(1)} %copy-done.34), channel_id=1, source_target_pairs={{0,24},{8,16},{16,8},{24,0},{1,25},{9,17},{17,9},{25,1},{2,26},{10... | collective-permute-start | bytes 3145736 | tf_op jit(solution)/shard_map/ppermute | solution.py:49
  364.2 45.5 %collective-permute-start.16 = (bf16[240,2048]{1,0:T(8,128)(2,1)}, bf16[240,2048]{1,0:T(8,128)(2,1)}, u32[]{:S(2)}, u32[]{:S(2)}) collective-permute-start(bf16[240,2048]{1,0:T(8,128)(2,1)} %convolution_convert_fusion.21), channel_id=1, source_target_pairs={{0,24},{8,16},{16,8},{24,0},{1,25},{9,17},{17,9},{25,1},{2,26},{10... | collective-permute-start | bytes 2949128 | tf_op jit(solution)/shard_map/ppermute | solution.py:49
  368.1 41.6 %collective-permute-start.15 = (bf16[240,2048]{1,0:T(8,128)(2,1)}, bf16[240,2048]{1,0:T(8,128)(2,1)}, u32[]{:S(2)}, u32[]{:S(2)}) collective-permute-start(bf16[240,2048]{1,0:T(8,128)(2,1)} %convolution_convert_fusion.22), channel_id=1, source_target_pairs={{0,16},{8,24},{16,0},{24,8},{1,17},{9,25},{17,1},{25,9},{2,18},{10... | collective-permute-start | bytes 2949128 | tf_op jit(solution)/shard_map/ppermute | solution.py:49
  372.0 37.7 %collective-permute-start.14 = (bf16[240,2048]{1,0:T(8,128)(2,1)}, bf16[240,2048]{1,0:T(8,128)(2,1)}, u32[]{:S(2)}, u32[]{:S(2)}) collective-permute-start(bf16[240,2048]{1,0:T(8,128)(2,1)} %convolution_convert_fusion.19), channel_id=1, source_target_pairs={{0,8},{8,0},{16,24},{24,16},{1,9},{9,1},{17,25},{25,17},{2,10},{10... | collective-permute-start | bytes 2949128 | tf_op jit(solution)/shard_map/ppermute | solution.py:49
  390.1 315.1 %reduce-scatter.4.cloned.1.call-start = ((), (), s32[]{:S(2)}) async-start(), calls=%async_computation.12 | async-start | bytes 7077888 | tf_op jit(solution)/shard_map/reduce_scatter | solution.py:43
  391.0 64.6 %collective-permute-start.19 = (bf16[240,2048]{1,0:T(8,128)(2,1)}, bf16[240,2048]{1,0:T(8,128)(2,1)}, u32[]{:S(2)}, u32[]{:S(2)}) collective-permute-start(bf16[240,2048]{1,0:T(8,128)(2,1)} %convolution_convert_fusion.17), channel_id=1, source_target_pairs={{0,8},{8,0},{16,24},{24,16},{1,9},{9,1},{17,25},{25,17},{2,10},{10... | collective-permute-start | bytes 2949128 | tf_op jit(solution)/shard_map/ppermute | solution.py:49
  417.1 39.5 %collective-permute-start.21 = (bf16[240,2048]{1,0:T(8,128)(2,1)}, bf16[240,2048]{1,0:T(8,128)(2,1)}, u32[]{:S(2)}, u32[]{:S(2)}) collective-permute-start(bf16[240,2048]{1,0:T(8,128)(2,1)} %convolution_convert_fusion.15), channel_id=1, source_target_pairs={{0,24},{8,16},{16,8},{24,0},{1,25},{9,17},{17,9},{25,1},{2,26},{10... | collective-permute-start | bytes 2949128 | tf_op jit(solution)/shard_map/ppermute | solution.py:49
  420.2 42.7 %collective-permute-start.20 = (bf16[240,2048]{1,0:T(8,128)(2,1)}, bf16[240,2048]{1,0:T(8,128)(2,1)}, u32[]{:S(2)}, u32[]{:S(2)}) collective-permute-start(bf16[240,2048]{1,0:T(8,128)(2,1)} %convolution_convert_fusion.16), channel_id=1, source_target_pairs={{0,16},{8,24},{16,0},{24,8},{1,17},{9,25},{17,1},{25,9},{2,18},{10... | collective-permute-start | bytes 2949128 | tf_op jit(solution)/shard_map/ppermute | solution.py:49
  429.4 33.4 %collective-permute-start.22 = (bf16[240,2048]{1,0:T(8,128)(2,1)}, bf16[240,2048]{1,0:T(8,128)(2,1)S(1)}, u32[]{:S(2)}, u32[]{:S(2)}) collective-permute-start(bf16[240,2048]{1,0:T(8,128)(2,1)} %convolution_convert_fusion.11), channel_id=1, source_target_pairs={{0,8},{8,0},{16,24},{24,16},{1,9},{9,1},{17,25},{25,17},{2,10},{10... | collective-permute-start | bytes 2949128 | tf_op jit(solution)/shard_map/ppermute | solution.py:49
  455.2 53.9 %collective-permute-start.23 = (bf16[240,2048]{1,0:T(8,128)(2,1)}, bf16[240,2048]{1,0:T(8,128)(2,1)S(1)}, u32[]{:S(2)}, u32[]{:S(2)}) collective-permute-start(bf16[240,2048]{1,0:T(8,128)(2,1)} %get-tuple-element.328), channel_id=1, source_target_pairs={{0,16},{8,24},{16,0},{24,8},{1,17},{9,25},{17,1},{25,9},{2,18},{10... | collective-permute-start | bytes 2949128 | tf_op jit(solution)/shard_map/ppermute | solution.py:49
  455.6 53.5 %collective-permute-start.24 = (bf16[240,2048]{1,0:T(8,128)(2,1)}, bf16[240,2048]{1,0:T(8,128)(2,1)}, u32[]{:S(2)}, u32[]{:S(2)}) collective-permute-start(bf16[240,2048]{1,0:T(8,128)(2,1)} %get-tuple-element.329), channel_id=1, source_target_pairs={{0,24},{8,16},{16,8},{24,0},{1,25},{9,17},{17,9},{25,1},{2,26},{10... | collective-permute-start | bytes 2949128 | tf_op jit(solution)/shard_map/ppermute | solution.py:49
  511.5 47.1 %collective-permute-start.29 = (bf16[240,2048]{1,0:T(8,128)(2,1)}, bf16[240,2048]{1,0:T(8,128)(2,1)}, u32[]{:S(2)}, u32[]{:S(2)}) collective-permute-start(bf16[240,2048]{1,0:T(8,128)(2,1)} %get-tuple-element.360), channel_id=1, source_target_pairs={{0,16},{8,24},{16,0},{24,8},{1,17},{9,25},{17,1},{25,9},{2,18},{10... | collective-permute-start | bytes 2949128 | tf_op jit(solution)/shard_map/ppermute | solution.py:49
  512.9 45.7 %collective-permute-start.30 = (bf16[240,2048]{1,0:T(8,128)(2,1)}, bf16[240,2048]{1,0:T(8,128)(2,1)}, u32[]{:S(2)}, u32[]{:S(2)}) collective-permute-start(bf16[240,2048]{1,0:T(8,128)(2,1)} %get-tuple-element.361), channel_id=1, source_target_pairs={{0,24},{8,16},{16,8},{24,0},{1,25},{9,17},{17,9},{25,1},{2,26},{10... | collective-permute-start | bytes 2949128 | tf_op jit(solution)/shard_map/ppermute | solution.py:49
  591.0 82.2 %collective-permute-start.34 = (bf16[240,2048]{1,0:T(8,128)(2,1)}, bf16[240,2048]{1,0:T(8,128)(2,1)}, u32[]{:S(2)}, u32[]{:S(2)}) collective-permute-start(bf16[240,2048]{1,0:T(8,128)(2,1)} %get-tuple-element.618), channel_id=1, source_target_pairs={{0,8},{8,0},{16,24},{24,16},{1,9},{9,1},{17,25},{25,17},{2,10},{10... | collective-permute-start | bytes 2949128 | tf_op jit(solution)/shard_map/ppermute | solution.py:49
  591.5 81.7 %collective-permute-start.35 = (bf16[240,2048]{1,0:T(8,128)(2,1)}, bf16[240,2048]{1,0:T(8,128)(2,1)}, u32[]{:S(2)}, u32[]{:S(2)}) collective-permute-start(bf16[240,2048]{1,0:T(8,128)(2,1)} %get-tuple-element.617), channel_id=1, source_target_pairs={{0,16},{8,24},{16,0},{24,8},{1,17},{9,25},{17,1},{25,9},{2,18},{10... | collective-permute-start | bytes 2949128 | tf_op jit(solution)/shard_map/ppermute | solution.py:49
  602.8 58.4 %collective-permute-start.31 = (bf16[240,2048]{1,0:T(8,128)(2,1)}, bf16[240,2048]{1,0:T(8,128)(2,1)}, u32[]{:S(2)}, u32[]{:S(2)}) collective-permute-start(bf16[240,2048]{1,0:T(8,128)(2,1)} %get-tuple-element.622), channel_id=1, source_target_pairs={{0,8},{8,0},{16,24},{24,16},{1,9},{9,1},{17,25},{25,17},{2,10},{10... | collective-permute-start | bytes 2949128 | tf_op jit(solution)/shard_map/ppermute | solution.py:49
  602.8 59.5 %collective-permute-start.32 = (bf16[240,2048]{1,0:T(8,128)(2,1)}, bf16[240,2048]{1,0:T(8,128)(2,1)}, u32[]{:S(2)}, u32[]{:S(2)}) collective-permute-start(bf16[240,2048]{1,0:T(8,128)(2,1)} %get-tuple-element.621), channel_id=1, source_target_pairs={{0,16},{8,24},{16,0},{24,8},{1,17},{9,25},{17,1},{25,9},{2,18},{10... | collective-permute-start | bytes 2949128 | tf_op jit(solution)/shard_map/ppermute | solution.py:49
  603.9 58.5 %collective-permute-start.33 = (bf16[240,2048]{1,0:T(8,128)(2,1)}, bf16[240,2048]{1,0:T(8,128)(2,1)}, u32[]{:S(2)}, u32[]{:S(2)}) collective-permute-start(bf16[240,2048]{1,0:T(8,128)(2,1)} %get-tuple-element.620), channel_id=1, source_target_pairs={{0,24},{8,16},{16,8},{24,0},{1,25},{9,17},{17,9},{25,1},{2,26},{10... | collective-permute-start | bytes 2949128 | tf_op jit(solution)/shard_map/ppermute | solution.py:49
  605.5 52.1 %all-to-all-start.1 = ((f32[4,2,240,2]{2,3,1,0:T(2,128)}), f32[4,2,240,2]{2,3,1,0:T(2,128)S(1)}, u32[]{:S(2)}, u32[]{:S(2)}) async-start(f32[4,2,240,2]{2,3,1,0:T(2,128)} %select_select_fusion), calls=%async_computation.2 | async-start | bytes 32768 | tf_op jit(solution)/shard_map/all_to_all | solution.py:590
  666.6 140.8 %all-gather.17.cloned.1.call-start = ((), (), s32[]{:S(2)}) async-start(), calls=%async_computation.13 | async-start | bytes 7077888 | tf_op jit(solution)/shard_map/all_gather | solution.py:39
  708.5 224.4 %reduce-scatter.6.cloned.1.call-start = ((), (), s32[]{:S(2)}) async-start(), calls=%async_computation.14 | async-start | bytes 7077888 | tf_op jit(solution)/shard_map/reduce_scatter | solution.py:43
  708.6 48.8 %collective-permute-start.38 = (bf16[2,512,1024]{2,1,0:T(8,128)(2,1)}, bf16[2,512,1024]{2,1,0:T(8,128)(2,1)}, u32[]{:S(2)}, u32[]{:S(2)}) collective-permute-start(bf16[2,512,1024]{2,1,0:T(8,128)(2,1)} %pad_maximum_fusion.9), channel_id=1, source_target_pairs={{0,16},{8,24},{16,0},{24,8},{1,17},{9,25},{17,1},{25,9},{2,18},{10... | collective-permute-start | bytes 6291464 | tf_op jit(solution)/shard_map/ppermute | solution.py:49
  710.0 91.4 %collective-permute-start.39 = (bf16[2,512,1024]{2,1,0:T(8,128)(2,1)}, bf16[2,512,1024]{2,1,0:T(8,128)(2,1)}, u32[]{:S(2)}, u32[]{:S(2)}) collective-permute-start(bf16[2,512,1024]{2,1,0:T(8,128)(2,1)} %pad_maximum_fusion.10), channel_id=1, source_target_pairs={{0,24},{8,16},{16,8},{24,0},{1,25},{9,17},{17,9},{25,1},{2,26},{10... | collective-permute-start | bytes 6291464 | tf_op jit(solution)/shard_map/ppermute | solution.py:49
  807.5 258.4 %reduce-scatter.8.cloned.1.call-start = ((), (), s32[]{:S(2)}) async-start(), calls=%async_computation.15 | async-start | bytes 7077888 | tf_op jit(solution)/shard_map/reduce_scatter | solution.py:43
  828.3 50.0 %collective-permute-start.45 = (f32[2,512,64]{1,2,0:T(8,128)}, f32[2,512,64]{1,2,0:T(8,128)}, u32[]{:S(2)}, u32[]{:S(2)}) collective-permute-start(f32[2,512,64]{1,2,0:T(8,128)} %pad_maximum_fusion.19), channel_id=1, source_target_pairs={{0,8},{8,0},{16,24},{24,16},{1,9},{9,1},{17,25},{25,17},{2,10},{10... | collective-permute-start | bytes 786440 | tf_op jit(solution)/shard_map/ppermute | solution.py:49
  830.2 102.6 %collective-permute-start.40 = (bf16[2,512,1024]{2,1,0:T(8,128)(2,1)}, bf16[2,512,1024]{2,1,0:T(8,128)(2,1)}, u32[]{:S(2)}, u32[]{:S(2)}) collective-permute-start(bf16[2,512,1024]{2,1,0:T(8,128)(2,1)} %pad_maximum_fusion.12), channel_id=1, source_target_pairs={{0,8},{8,0},{16,24},{24,16},{1,9},{9,1},{17,25},{25,17},{2,10},{10... | collective-permute-start | bytes 6291464 | tf_op jit(solution)/shard_map/ppermute | solution.py:49
  830.8 102.1 %collective-permute-start.41 = (bf16[2,512,1024]{2,1,0:T(8,128)(2,1)}, bf16[2,512,1024]{2,1,0:T(8,128)(2,1)}, u32[]{:S(2)}, u32[]{:S(2)}) collective-permute-start(bf16[2,512,1024]{2,1,0:T(8,128)(2,1)} %pad_maximum_fusion.13), channel_id=1, source_target_pairs={{0,16},{8,24},{16,0},{24,8},{1,17},{9,25},{17,1},{25,9},{2,18},{10... | collective-permute-start | bytes 6291464 | tf_op jit(solution)/shard_map/ppermute | solution.py:49
  832.3 100.6 %collective-permute-start.42 = (bf16[2,512,1024]{2,1,0:T(8,128)(2,1)S(1)}, bf16[2,512,1024]{2,1,0:T(8,128)(2,1)}, u32[]{:S(2)}, u32[]{:S(2)}) collective-permute-start(bf16[2,512,1024]{2,1,0:T(8,128)(2,1)S(1)} %copy-done.32), channel_id=1, source_target_pairs={{0,24},{8,16},{16,8},{24,0},{1,25},{9,17},{17,9},{25,1},{2,26},{10... | collective-permute-start | bytes 6291464 | tf_op jit(solution)/shard_map/ppermute | solution.py:49
  833.2 47.8 %collective-permute-start.43 = (bf16[2,512,256]{2,1,0:T(8,128)(2,1)}, bf16[2,512,256]{2,1,0:T(8,128)(2,1)S(1)}, u32[]{:S(2)}, u32[]{:S(2)}) collective-permute-start(bf16[2,512,256]{2,1,0:T(8,128)(2,1)} %pad_maximum_fusion.18), channel_id=1, source_target_pairs={{0,8},{8,0},{16,24},{24,16},{1,9},{9,1},{17,25},{25,17},{2,10},{10... | collective-permute-start | bytes 1572872 | tf_op jit(solution)/shard_map/ppermute | solution.py:49
  879.4 47.9 %collective-permute-start.46 = (f32[512,64]{0,1:T(8,128)S(1)}, f32[512,64]{0,1:T(8,128)S(1)}, u32[]{:S(2)}, u32[]{:S(2)}) collective-permute-start(f32[512,64]{0,1:T(8,128)S(1)} %fusion.101), channel_id=1, source_target_pairs={{0,16},{8,24},{16,0},{24,8},{1,17},{9,25},{17,1},{25,9},{2,18},{10... | collective-permute-start | bytes 393224 | tf_op jit(solution)/shard_map/ppermute | solution.py:49
  881.1 50.9 %collective-permute-start.44 = (bf16[512,256]{1,0:T(8,128)(2,1)S(1)}, bf16[512,256]{1,0:T(8,128)(2,1)S(1)}, u32[]{:S(2)}, u32[]{:S(2)}) collective-permute-start(bf16[512,256]{1,0:T(8,128)(2,1)S(1)} %fusion.95), channel_id=1, source_target_pairs={{0,16},{8,24},{16,0},{24,8},{1,17},{9,25},{17,1},{25,9},{2,18},{10... | collective-permute-start | bytes 786440 | tf_op jit(solution)/shard_map/ppermute | solution.py:49
  948.8 46.4 %collective-permute-start.49 = (bf16[1,512,1024]{2,1,0:T(8,128)(2,1)}, bf16[1,512,1024]{2,1,0:T(8,128)(2,1)}, u32[]{:S(2)}, u32[]{:S(2)}) collective-permute-start(bf16[1,512,1024]{2,1,0:T(8,128)(2,1)} %get-tuple-element.460), channel_id=1, source_target_pairs={{0,24},{8,16},{16,8},{24,0},{1,25},{9,17},{17,9},{25,1},{2,26},{10... | collective-permute-start | bytes 3145736 | tf_op jit(solution)/shard_map/ppermute | solution.py:49
  960.1 43.8 %collective-permute-start.50 = (bf16[2,512,768]{2,1,0:T(8,128)(2,1)}, bf16[2,512,768]{2,1,0:T(8,128)(2,1)}, u32[]{:S(2)}, u32[]{:S(2)}) collective-permute-start(bf16[2,512,768]{2,1,0:T(8,128)(2,1)} %pad_maximum_fusion.15), channel_id=1, source_target_pairs={{0,8},{8,0},{16,24},{24,16},{1,9},{9,1},{17,25},{25,17},{2,10},{10... | collective-permute-start | bytes 4718600 | tf_op jit(solution)/shard_map/ppermute | solution.py:49
  997.2 45.4 %collective-permute-start.53 = (bf16[1,512,1024]{2,1,0:T(8,128)(2,1)S(1)}, bf16[1,512,1024]{2,1,0:T(8,128)(2,1)}, u32[]{:S(2)}, u32[]{:S(2)}) collective-permute-start(bf16[1,512,1024]{2,1,0:T(8,128)(2,1)S(1)} %copy-done.35), channel_id=1, source_target_pairs={{0,24},{8,16},{16,8},{24,0},{1,25},{9,17},{17,9},{25,1},{2,26},{10... | collective-permute-start | bytes 3145736 | tf_op jit(solution)/shard_map/ppermute | solution.py:49
  (135 other events, 2261.7 us)
Sparse Core Ops, SparseCore 0:
  15.4 103.4 all-gather.6
  121.5 73.1 all-gather.8
  196.8 98.1 all-gather.10
  296.8 98.1 all-gather.14
  396.9 98.1 all-gather.12
  579.9 125.2 reduce-scatter.3
  708.6 98.7 all-gather.16
  811.6 116.5 reduce-scatter.5
  943.4 117.4 reduce-scatter.7

commit v6 on v5

--- a/solution.py
+++ b/solution.py
@@ -373,7 +373,7 @@
     out_ref[...] = contract_last(grad_ref[...], w_ref[:, :width], BF16)
 
 
-def through_heads(grad, w, block=256):
+def through_heads(grad, w, block=768):
     rows, width = grad.shape
     return pl.pallas_call(
         through_heads_kernel,
@@ -389,6 +389,38 @@
     )(grad, w)
 
 
+def pick_kernel(rank_ref, value_ref, *refs):
+    hits_ref = refs[-1]
+    pieces = refs[:-1]
+    capacity = pieces[0].shape[0]
+
+    @pl.when(pl.program_id(0) == 0)
+    def _():
+        slots = lax.broadcasted_iota(jnp.int32, (capacity, hits_ref.shape[1]), 0)
+        for i in range(len(pieces)):
+            hits = (slots == rank_ref[i : i + 1, :]).astype(BF16)
+            hits_ref[i * capacity : (i + 1) * capacity, :] = hits
+
+    rows = jnp.dot(hits_ref[...], value_ref[...], preferred_element_type=F32).astype(BF16)
+    for i, piece in enumerate(pieces):
+        piece[...] = rows[i * capacity : (i + 1) * capacity]
+
+
+def pick(ranks, values, capacity, block=512):
+    pieces, rows = ranks.shape
+    by_width = lambda n: pl.BlockSpec((n, block), lambda j: (0, j))
+    return pl.pallas_call(
+        pick_kernel,
+        name="pick",
+        grid=(D // block,),
+        in_specs=[pl.BlockSpec(ranks.shape, lambda j: (0, 0)), by_width(rows)],
+        out_specs=[by_width(capacity)] * pieces,
+        out_shape=[jax.ShapeDtypeStruct((capacity, D), BF16)] * pieces,
+        scratch_shapes=[pltpu.VMEM((pieces * capacity, rows), BF16)],
+        cost_estimate=cost(1000, 1000),
+    )(ranks, values)
+
+
 def combine_kernel(*refs):
     rank_ref, out_ref = refs[0], refs[-1]
     pieces = refs[1:-1]
@@ -401,7 +433,7 @@
     out_ref[...] = total.astype(BF16)
 
 
-def combine(ranks, pieces, block=256):
+def combine(ranks, pieces, block=768):
     rows = ranks.shape[1]
     width = 1024
     whole = lambda a: pl.BlockSpec((a.shape[0], width), lambda j, i: (0, j))
@@ -634,13 +666,17 @@
     sent += [send_rows(e, near, near_values) for e in range(per_device)]
 
     def grad_rows_of(base, cots):
-        table = far_ranks[base] if base else slot_rank.astype(F32)
+        if not base:
+            wanted = [of_peer(slot_rank, step, e) for step in near for e in range(per_device)]
+            rows = pick(jnp.concatenate(wanted), cots, capacity)
+            return [rows[:per_device], rows[per_device:]]
+        table = far_ranks[base]
         halves = []
         for step in near:
             held = []
             for e in range(per_device):
-                pick = (of_peer(table, step, e) == slots[:, None].astype(F32)).astype(BF16)
-                held.append(plain_dot(pick, cots, BF16))
+                hit = (of_peer(table, step, e) == slots[:, None].astype(F32)).astype(BF16)
+                held.append(plain_dot(hit, cots, BF16))
             halves.append(held)
         return halves
 

time: 1090 us -> 1090 us (level)
  matrix products: 128 us -> 117 us
    dot_general x18 -> x14, matrix products: 58.3 us -> 47.1 us  [plain_dot(): return jnp.dot(left_op, right_op, preferred_element_type=F32).astype(kind)]
    unnamed x237 -> x235, local copies, waits for them, and re-layouts: 24.3 us -> 24.7 us
  transfers between devices with their start and end apart: 70 -> 70, of which waited for: 28 -> 28; matrix products, arithmetic and copies ran while one was open for 29% -> 29% of each run, Pallas kernels for 19% -> 20%
where the time goes in v6:
time: 1090 us; the launch traced here: 1080 us
  waiting for transfers between devices  410 us (38%)
  Pallas kernels  241 us (22%)
  local copies, waits for them, and re-layouts  158 us (14%)
  matrix products  117 us (11%)
  other arithmetic  75.7 us (7%)
  starting transfers between devices  51.9 us (5%)
  between operations  16.1 us (1%)
    ppermute x58, waiting for transfers between devices, trade(): return lax.ppermute(value, 'row', [(r, r ^ step) for r in range(n_row)])  341 us
    pallas_call x4, Pallas kernels, run_expert(): pl.pallas_call(expert_kernel, name='expert', grid=(1,), in_specs=[whole(a...  72.7 us
    dot_general x6, matrix products, contract_first(): lax.dot_general(left_op, right_op, (((0,), (0,)), ((), ())), preferred_el...  47.2 us
    dot_general x14, matrix products, plain_dot(): return jnp.dot(left_op, right_op, preferred_element_type=F32).astype(kind)  47.1 us
    ppermute x58, starting transfers between devices, trade(): return lax.ppermute(value, 'row', [(r, r ^ step) for r in range(n_row)])  41 us
    pallas_call x2, Pallas kernels, combine(): pl.pallas_call(combine_kernel, name='combine', grid=(D // width, rows //...  34.8 us
    pallas_call x3, Pallas kernels, place(): pl.pallas_call(place_kernel, name='place', grid_spec=pltpu.PrefetchScalar...  32.9 us
    pallas_call x1, Pallas kernels, attend_back(): pl.pallas_call(attend_back_kernel, name='attend_back', grid=(heads, rows...  27.5 us
  transfers between devices with their start and end apart: 70, of which 28 were waited for; matrix products, arithmetic and copies ran while one was open for 29% of the time, Pallas kernels for 20%

profile of v6, /device:TPU:0, one launch (start us, length us, event | category | flops | bytes accessed | tf_op | source)
XLA Modules:
  0.0 1079.8 jit_solution(13935798983912893203)
XLA Ops:
  22.9 6.1 constant_dynamic-slice_fusion.44
  60.8 30.1 %collective-permute-done.1 = bf16[2,512,1024]{2,1,0:T(8,128)(2,1)} collective-permute-done((bf16[2,512,1024]{2,1,0:T(8,128)(2,1)}, bf16[2,512,1024]{2,1,0:T(8,128)(2,1)}, u32[]{:S(2)}, u32[]{:S(2)}) %collective-permute-start.1) | collective-permute-done | bytes 2097184 | tf_op jit(solution)/shard_map/ppermute | solution.py:49
  104.1 7.2 scatter_custom_fusion
  133.5 5.5 collective-permute-done.2
  145.5 13.9 %project.1 = (bf16[1536,2048]{1,0:T(8,128)(2,1)}, f32[1536,1]{1,0:T(8,128)}, f32[1536,512]{1,0:T(8,128)}, bf16[1536,256]{1,0:T(8,128)(2,1)}, bf16[1536,256]{1,0:T(8,128)(2,1)}, /*index=5*/bf16[1536,256]{1,0:T(8,128)(2,1)}) custom-call(bf16[1552,2048]{1,0:T(8,128)(2,1)} %all-gather.7.cloned.1.call-done.x_ref, f32[1,2048]{1,0:T(1,128)} %get-tuple-element.676.gain_ref, ...), custom_call_target="tpu_custom_call" | custom-call | flops 1000 | bytes 1000 | tf_op jit(solution)/shard_map/project/pallas_call | solution.py:117
  159.3 16.8 %attend.1 = (bf16[1536,256]{1,0:T(8,128)(2,1)}, f32[2,1536,1]{2,1,0:T(8,128)}) custom-call(bf16[1536,256]{1,0:T(8,128)(2,1)} %get-tuple-element.271.q_ref, bf16[1536,256]{1,0:T(8,128)(2,1)} %get-tuple-element.272.k_ref, bf16[1536,256]{1,0:T(8,128)(2,1)} %get-tuple-element.273.v_ref, s32[1536,1]{1,0:T(8,128)} %broadcast_in_dim.650.seg_q_ref, ...), custom_call_target="tpu_custom_call" | custom-call | flops 1000 | bytes 1000 | tf_op jit(solution)/shard_map/attend/pallas_call | solution.py:167
  181.8 7.6 collective-permute-done.7
  196.4 17.4 %collective-permute-done.8 = bf16[1536,256]{1,0:T(8,128)(2,1)S(1)} collective-permute-done((bf16[1536,256]{1,0:T(8,128)(2,1)S(1)}, bf16[1536,256]{1,0:T(8,128)(2,1)S(1)}, u32[]{:S(2)}, u32[]{:S(2)}) %collective-permute-start.8) | collective-permute-done | bytes 786464 | tf_op jit(solution)/shard_map/ppermute | solution.py:49
  215.2 44.9 %collective-permute-done.9 = bf16[2,512,1024]{2,1,0:T(8,128)(2,1)S(1)} collective-permute-done((bf16[2,512,1024]{2,1,0:T(8,128)(2,1)}, bf16[2,512,1024]{2,1,0:T(8,128)(2,1)S(1)}, u32[]{:S(2)}, u32[]{:S(2)}) %collective-permute-start.9) | collective-permute-done | bytes 2097184 | tf_op jit(solution)/shard_map/ppermute | solution.py:49
  270.2 38.1 %collective-permute-done.10 = bf16[2,512,1024]{2,1,0:T(8,128)(2,1)S(1)} collective-permute-done((bf16[2,512,1024]{2,1,0:T(8,128)(2,1)}, bf16[2,512,1024]{2,1,0:T(8,128)(2,1)S(1)}, u32[]{:S(2)}, u32[]{:S(2)}) %collective-permute-start.10) | collective-permute-done | bytes 2097184 | tf_op jit(solution)/shard_map/ppermute | solution.py:49
  317.3 22.8 %branch.1 = (bf16[1536,2048]{1,0:T(8,128)(2,1)}, f32[1536,1]{1,0:T(8,128)}, f32[1536,256]{1,0:T(8,128)}) custom-call(s32[2]{0:T(128)} %pad_add_fusion.1.at_ref, bf16[1552,2048]{1,0:T(8,128)(2,1)} %all-gather.7.cloned.1.call-done.x_ref, bf16[1536,2048]{1,0:T(8,128)(2,1)} %all-gather.11.cloned.1.call-done.att_ref, ...), custom_call_target="tpu_custom_call" | custom-call | flops 1000 | bytes 1000 | tf_op jit(solution)/shard_map/branch/pallas_call | solution.py:305
  346.3 13.2 %collective-permute-done.13 = bf16[1,512,1024]{2,1,0:T(8,128)(2,1)} collective-permute-done((bf16[1,512,1024]{2,1,0:T(8,128)(2,1)S(1)}, bf16[1,512,1024]{2,1,0:T(8,128)(2,1)}, u32[]{:S(2)}, u32[]{:S(2)}) %collective-permute-start.13) | collective-permute-done | bytes 1048608 | tf_op jit(solution)/shard_map/ppermute | solution.py:49
  391.8 18.1 %all-to-all-done = f32[4,2,240]{2,1,0:T(2,128)S(1)} async-done(((f32[4,2,240]{2,1,0:T(2,128)}), f32[4,2,240]{2,1,0:T(2,128)S(1)}, u32[]{:S(2)}, u32[]{:S(2)}) %all-to-all-start) | async-done | bytes 7712 | tf_op jit(solution)/shard_map/all_to_all | solution.py:622
  410.9 5.6 convolution_convert_fusion.11
  433.0 18.2 %expert.4 = (bf16[480,1024]{1,0:T(8,128)(2,1)}, bf16[480,2048]{1,0:T(8,128)(2,1)}, f32[480,2]{1,0:T(8,128)}, bf16[240,2048]{1,0:T(8,128)(2,1)}, bf16[240,2048]{1,0:T(8,128)(2,1)}) custom-call(bf16[240,2048]{1,0:T(8,128)(2,1)} %collective-permute-done.15.x0_ref, bf16[240,2048]{1,0:T(8,128)(2,1)} %collective-permute-done.16.x1_ref, ...), custom_call_target="tpu_custom_call" | custom-call | flops 1000 | bytes 1000 | tf_op jit(solution)/shard_map/expert/pallas_call | solution.py:360
  453.7 5.5 convolution_convert_fusion.8.c0_ref
  463.3 18.4 %expert.5 = (bf16[480,1024]{1,0:T(8,128)(2,1)}, bf16[480,2048]{1,0:T(8,128)(2,1)}, f32[480,2]{1,0:T(8,128)}, bf16[240,2048]{1,0:T(8,128)(2,1)}, bf16[240,2048]{1,0:T(8,128)(2,1)}) custom-call(bf16[240,2048]{1,0:T(8,128)(2,1)} %collective-permute-done.20.x0_ref, bf16[240,2048]{1,0:T(8,128)(2,1)} %collective-permute-done.21.x1_ref, ...), custom_call_target="tpu_custom_call" | custom-call | flops 1000 | bytes 1000 | tf_op jit(solution)/shard_map/expert/pallas_call | solution.py:360
  481.7 13.3 %all-gather.13.cloned.1.call-done.value_ref = bf16[1536,2048]{1,0:T(8,128)(2,1)} async-done(((bf16[1536,256]{1,0:T(8,128)(2,1)}), bf16[1536,2048]{1,0:T(8,128)(2,1)}) %all-gather.13.cloned.1.call-update) | async-done | bytes 6291472 | tf_op jit(solution)/shard_map/all_gather | solution.py:39
  495.1 9.6 pick.1
  509.4 18.0 %expert.7 = (bf16[480,1024]{1,0:T(8,128)(2,1)}, bf16[480,2048]{1,0:T(8,128)(2,1)}, f32[480,2]{1,0:T(8,128)}, bf16[240,2048]{1,0:T(8,128)(2,1)}, bf16[240,2048]{1,0:T(8,128)(2,1)}) custom-call(bf16[240,2048]{1,0:T(8,128)(2,1)} %convolution_convert_fusion.14.x0_ref, bf16[240,2048]{1,0:T(8,128)(2,1)} %collective-permute-done.19.x1_ref, ...), custom_call_target="tpu_custom_call" | custom-call | flops 1000 | bytes 1000 | tf_op jit(solution)/shard_map/expert/pallas_call | solution.py:360
  529.8 18.1 %expert.6 = (bf16[480,1024]{1,0:T(8,128)(2,1)}, bf16[480,2048]{1,0:T(8,128)(2,1)}, f32[480,2]{1,0:T(8,128)}, bf16[240,2048]{1,0:T(8,128)(2,1)}, bf16[240,2048]{1,0:T(8,128)(2,1)}) custom-call(bf16[240,2048]{1,0:T(8,128)(2,1)} %convolution_convert_fusion.16.x0_ref, bf16[240,2048]{1,0:T(8,128)(2,1)} %collective-permute-done.14.x1_ref, ...), custom_call_target="tpu_custom_call" | custom-call | flops 1000 | bytes 1000 | tf_op jit(solution)/shard_map/expert/pallas_call | solution.py:360
  558.2 17.4 %combine.2 = bf16[1536,2048]{1,0:T(8,128)(2,1)} custom-call(s32[8,1536]{1,0:T(8,128)} %concatenate.116.refs_0_, bf16[240,2048]{1,0:T(8,128)(2,1)} %get-tuple-element.354.refs_1_, bf16[240,2048]{1,0:T(8,128)(2,1)} %copy-done.52, bf16[240,2048]{1,0:T(8,128)(2,1)} %copy-done.50, bf16[240,2048]{1,0:T(8,128)(2,1)} %collective-permute-done.24.refs_4_, ...), custom_call_target="tpu_custom_call" | custom-call | flops 1000 | bytes 1000 | tf_op jit(solution)/shard_map/combine/pallas_call | solution.py:440
  577.2 7.5 convolution_convert_fusion.2
  588.9 7.5 convolution_convert_fusion.3
  604.5 12.0 %convolution_convert_fusion.1 = bf16[2048,2048]{1,0:T(8,128)(2,1)S(1)} fusion(bf16[240,2048]{1,0:T(8,128)(2,1)} %collective-permute-done.16.x1_ref, bf16[240,2048]{1,0:T(8,128)(2,1)} %collective-permute-done.15.x0_ref, bf16[240,2048]{1,0:T(8,128)(2,1)} %collective-permute-done.14.x1_ref, bf16[240,2048]{1,0:T(8,128)(2,1)S(1)} %copy-done.45, ...), kind=kOutput, calls=%fused_computation.9 | convolution fusion | flops 8080850944 | bytes 16252928 | tf_op jit(solution)/shard_map/dot_general | solution.py:63
  618.9 12.0 %convolution_convert_fusion = bf16[2048,2048]{1,0:T(8,128)(2,1)S(1)} fusion(bf16[240,2048]{1,0:T(8,128)(2,1)} %collective-permute-done.21.x1_ref, bf16[240,2048]{1,0:T(8,128)(2,1)} %collective-permute-done.20.x0_ref, bf16[240,2048]{1,0:T(8,128)(2,1)} %collective-permute-done.19.x1_ref, bf16[240,2048]{1,0:T(8,128)(2,1)} %convolution_convert_fusion.14.x0_ref, ...), kind=kOutput, calls=%fused_computation.8 | convolution fusion | flops 8080850944 | bytes 16252928 | tf_op jit(solution)/shard_map/dot_general | solution.py:63
  644.1 9.3 all-to-all-done.1
  669.8 11.5 %collective-permute-done.36.refs_8_ = bf16[240,2048]{1,0:T(8,128)(2,1)} collective-permute-done((bf16[240,2048]{1,0:T(8,128)(2,1)}, bf16[240,2048]{1,0:T(8,128)(2,1)}, u32[]{:S(2)}, u32[]{:S(2)}) %collective-permute-start.36) | collective-permute-done | bytes 983072 | tf_op jit(solution)/shard_map/ppermute | solution.py:49
  687.5 14.5 %reduce-scatter.4.cloned.1.call-done = bf16[1536,256]{1,0:T(8,128)(2,1)} async-done(((bf16[1536,2048]{1,0:T(8,128)(2,1)}), bf16[1536,256]{1,0:T(8,128)(2,1)}) %reduce-scatter.4.cloned.1.call-update) | async-done | bytes 786448 | tf_op jit(solution)/shard_map/reduce_scatter | solution.py:43
  707.3 17.4 %combine.3 = bf16[1536,2048]{1,0:T(8,128)(2,1)} custom-call(s32[8,1536]{1,0:T(8,128)} %concatenate.116.refs_0_, bf16[240,2048]{1,0:T(8,128)(2,1)} %get-tuple-element.423.refs_1_, bf16[240,2048]{1,0:T(8,128)(2,1)} %collective-permute-done.31.refs_2_, bf16[240,2048]{1,0:T(8,128)(2,1)} %collective-permute-done.32.refs_3_, ...), custom_call_target="tpu_custom_call" | custom-call | flops 1000 | bytes 1000 | tf_op jit(solution)/shard_map/combine/pallas_call | solution.py:440
  724.8 29.5 %collective-permute-done.38.refs_2_ = bf16[2,512,1024]{2,1,0:T(8,128)(2,1)} collective-permute-done((bf16[2,512,1024]{2,1,0:T(8,128)(2,1)}, bf16[2,512,1024]{2,1,0:T(8,128)(2,1)}, u32[]{:S(2)}, u32[]{:S(2)}) %collective-permute-start.38) | collective-permute-done | bytes 2097184 | tf_op jit(solution)/shard_map/ppermute | solution.py:49
  754.3 44.0 %collective-permute-done.39.refs_3_ = bf16[2,512,1024]{2,1,0:T(8,128)(2,1)} collective-permute-done((bf16[2,512,1024]{2,1,0:T(8,128)(2,1)}, bf16[2,512,1024]{2,1,0:T(8,128)(2,1)}, u32[]{:S(2)}, u32[]{:S(2)}) %collective-permute-start.39) | collective-permute-done | bytes 2097184 | tf_op jit(solution)/shard_map/ppermute | solution.py:49
  798.3 5.4 all-gather.17.cloned.1.call-done
  804.4 7.4 fusion.38
  815.6 5.2 fusion.41
  830.3 11.0 %place.3 = f32[8,512,1024]{2,1,0:T(8,128)} custom-call(s32[8]{0:T(128)} %stack.313.at_ref, bf16[2,512,1024]{2,1,0:T(8,128)(2,1)} %pad_maximum_fusion.7.refs_0_, bf16[2,512,1024]{2,1,0:T(8,128)(2,1)} %copy-done.32, bf16[2,512,1024]{2,1,0:T(8,128)(2,1)} %collective-permute-done.38.refs_2_, bf16[2,512,1024]{2,1,0:T(8,128)(2,1)} %collective-permute-done.39.refs_3_), custom_call_target="tpu_custom_call" | custom-call | flops 1000 | bytes 1000 | tf_op jit(solution)/shard_map/place/pallas_call | solution.py:464
  841.3 5.9 convolution_convert_fusion.6.grad_ref
  847.2 27.5 %attend_back.1 = (bf16[1536,256]{1,0:T(8,128)(2,1)}, bf16[1536,256]{1,0:T(8,128)(2,1)}, bf16[1536,256]{1,0:T(8,128)(2,1)}, f32[1,128]{1,0:T(1,128)}, f32[1,128]{1,0:T(1,128)}) custom-call(bf16[1536,256]{1,0:T(8,128)(2,1)} %get-tuple-element.271.q_ref, bf16[1536,256]{1,0:T(8,128)(2,1)} %get-tuple-element.272.k_ref, ...), custom_call_target="tpu_custom_call" | custom-call | flops 1000 | bytes 1000 | tf_op jit(solution)/shard_map/attend_back/pallas_call | solution.py:250
  880.9 42.9 %collective-permute-done.46 = f32[512,64]{0,1:T(8,128)S(1)} collective-permute-done((f32[512,64]{0,1:T(8,128)S(1)}, f32[512,64]{0,1:T(8,128)S(1)}, u32[]{:S(2)}, u32[]{:S(2)}) %collective-permute-start.46) | collective-permute-done | bytes 131104 | tf_op jit(solution)/shard_map/ppermute | solution.py:49
  929.4 9.9 through_heads.1
  945.1 8.6 convolution_convert_fusion.4
  959.2 10.9 %place.4 = f32[8,512,1024]{2,1,0:T(8,128)} custom-call(s32[8]{0:T(128)} %stack.313.at_ref, bf16[2,512,1024]{2,1,0:T(8,128)(2,1)} %pad_maximum_fusion.11.refs_0_, bf16[2,512,1024]{2,1,0:T(8,128)(2,1)} %collective-permute-done.40.refs_1_, bf16[2,512,1024]{2,1,0:T(8,128)(2,1)} %collective-permute-done.41.refs_2_, ...), custom_call_target="tpu_custom_call" | custom-call | flops 1000 | bytes 1000 | tf_op jit(solution)/shard_map/place/pallas_call | solution.py:464
  970.2 5.4 gather_fusion.2
  975.6 15.6 %collective-permute-done.49.refs_3_ = bf16[1,512,1024]{2,1,0:T(8,128)(2,1)} collective-permute-done((bf16[1,512,1024]{2,1,0:T(8,128)(2,1)}, bf16[1,512,1024]{2,1,0:T(8,128)(2,1)}, u32[]{:S(2)}, u32[]{:S(2)}) %collective-permute-start.49) | collective-permute-done | bytes 1048608 | tf_op jit(solution)/shard_map/ppermute | solution.py:49
  993.2 6.7 multiply_reduce_fusion
  1003.5 9.8 all_to_all.24
  1018.0 20.5 %collective-permute-done.53.refs_7_ = bf16[1,512,1024]{2,1,0:T(8,128)(2,1)} collective-permute-done((bf16[1,512,1024]{2,1,0:T(8,128)(2,1)S(1)}, bf16[1,512,1024]{2,1,0:T(8,128)(2,1)}, u32[]{:S(2)}, u32[]{:S(2)}) %collective-permute-start.53) | collective-permute-done | bytes 1048608 | tf_op jit(solution)/shard_map/ppermute | solution.py:49
  1043.0 11.0 %place.5 = f32[8,512,1024]{2,1,0:T(8,128)} custom-call(s32[16]{0:T(128)} %stack.335.at_ref, bf16[1,512,1024]{2,1,0:T(8,128)(2,1)} %get-tuple-element.506.refs_0_, bf16[1,512,1024]{2,1,0:T(8,128)(2,1)} %collective-permute-done.47.refs_1_, bf16[1,512,1024]{2,1,0:T(8,128)(2,1)} %collective-permute-done.48.refs_2_, ...), custom_call_target="tpu_custom_call" | custom-call | flops 1000 | bytes 1000 | tf_op jit(solution)/shard_map/place/pallas_call | solution.py:464
  (595 shorter events, 328.9 us)
Async XLA Ops:
  7.2 134.9 %all-gather.7.cloned.1.call-start = ((), (), s32[]{:S(2)}) async-start(), calls=%async_computation.7 | async-start | bytes 7151616 | tf_op jit(solution)/shard_map/all_gather | solution.py:39
  15.3 179.4 %all-gather.9.cloned.1.call-start = ((), (), s32[]{:S(2)}) async-start(), calls=%async_computation.8 | async-start | bytes 4718592 | tf_op jit(solution)/shard_map/all_gather | solution.py:39
  17.5 34.0 %collective-permute-start.3 = (bf16[512,1088]{0,1:T(8,128)(2,1)}, bf16[512,1088]{0,1:T(8,128)(2,1)}, u32[]{:S(2)}, u32[]{:S(2)}) collective-permute-start(bf16[512,1088]{0,1:T(8,128)(2,1)} %copy.61), channel_id=1, source_target_pairs={{0,8},{8,0},{16,24},{24,16},{1,9},{9,1},{17,25},{25,17},{2,10},{10... | collective-permute-start | bytes 3342344 | tf_op jit(solution)/shard_map/ppermute | solution.py:49
  32.9 58.0 %collective-permute-start.1 = (bf16[2,512,1024]{2,1,0:T(8,128)(2,1)}, bf16[2,512,1024]{2,1,0:T(8,128)(2,1)}, u32[]{:S(2)}, u32[]{:S(2)}) collective-permute-start(bf16[2,512,1024]{2,1,0:T(8,128)(2,1)} %get-tuple-element.265), channel_id=1, source_target_pairs={{0,16},{8,24},{16,0},{24,8},{1,17},{9,25},{17,1},{25,9},{2,18},{10... | collective-permute-start | bytes 6291464 | tf_op jit(solution)/shard_map/ppermute | solution.py:49
  43.6 83.7 %collective-permute-start = (bf16[6,512,1024]{2,1,0:T(8,128)(2,1)}, bf16[6,512,1024]{2,1,0:T(8,128)(2,1)}, u32[]{:S(2)}, u32[]{:S(2)}) collective-permute-start(bf16[6,512,1024]{2,1,0:T(8,128)(2,1)} %get-tuple-element.573), channel_id=1, source_target_pairs={{0,8},{8,0},{16,24},{24,16},{1,9},{9,1},{17,25},{25,17},{2,10},{10... | collective-permute-start | bytes 18874376 | tf_op jit(solution)/shard_map/ppermute | solution.py:49
  91.0 220.4 %all-gather.11.cloned.1.call-start = ((), (), s32[]{:S(2)}) async-start(), calls=%async_computation.9 | async-start | bytes 7077888 | tf_op jit(solution)/shard_map/all_gather | solution.py:39
  91.0 48.0 %collective-permute-start.2 = (bf16[2,512,1024]{2,1,0:T(8,128)(2,1)}, bf16[2,512,1024]{2,1,0:T(8,128)(2,1)}, u32[]{:S(2)}, u32[]{:S(2)}) collective-permute-start(bf16[2,512,1024]{2,1,0:T(8,128)(2,1)} %pad_maximum_fusion.3), channel_id=1, source_target_pairs={{0,24},{8,16},{16,8},{24,0},{1,25},{9,17},{17,9},{25,1},{2,26},{10... | collective-permute-start | bytes 6291464 | tf_op jit(solution)/shard_map/ppermute | solution.py:49
  142.1 37.4 %collective-permute-start.6 = (bf16[1,512,1024]{2,1,0:T(8,128)(2,1)}, bf16[1,512,1024]{2,1,0:T(8,128)(2,1)}, u32[]{:S(2)}, u32[]{:S(2)}) collective-permute-start(bf16[1,512,1024]{2,1,0:T(8,128)(2,1)} %get-tuple-element.282), channel_id=1, source_target_pairs={{0,16},{8,24},{16,0},{24,8},{1,17},{9,25},{17,1},{25,9},{2,18},{10... | collective-permute-start | bytes 3145736 | tf_op jit(solution)/shard_map/ppermute | solution.py:49
  144.0 45.4 %collective-permute-start.7 = (bf16[1,512,1024]{2,1,0:T(8,128)(2,1)}, bf16[1,512,1024]{2,1,0:T(8,128)(2,1)}, u32[]{:S(2)}, u32[]{:S(2)}) collective-permute-start(bf16[1,512,1024]{2,1,0:T(8,128)(2,1)} %get-tuple-element.283), channel_id=1, source_target_pairs={{0,24},{8,16},{16,8},{24,0},{1,25},{9,17},{17,9},{25,1},{2,26},{10... | collective-permute-start | bytes 3145736 | tf_op jit(solution)/shard_map/ppermute | solution.py:49
  194.8 226.3 %all-gather.15.cloned.1.call-start = ((), (), s32[]{:S(2)}) async-start(), calls=%async_computation.11 | async-start | bytes 7077888 | tf_op jit(solution)/shard_map/all_gather | solution.py:39
  213.8 46.3 %collective-permute-start.9 = (bf16[2,512,1024]{2,1,0:T(8,128)(2,1)}, bf16[2,512,1024]{2,1,0:T(8,128)(2,1)S(1)}, u32[]{:S(2)}, u32[]{:S(2)}) collective-permute-start(bf16[2,512,1024]{2,1,0:T(8,128)(2,1)} %get-tuple-element.296), channel_id=1, source_target_pairs={{0,16},{8,24},{16,0},{24,8},{1,17},{9,25},{17,1},{25,9},{2,18},{10... | collective-permute-start | bytes 6291464 | tf_op jit(solution)/shard_map/ppermute | solution.py:49
  260.1 234.9 %all-gather.13.cloned.1.call-start = ((), (), s32[]{:S(2)}) async-start(), calls=%async_computation.10 | async-start | bytes 7077888 | tf_op jit(solution)/shard_map/all_gather | solution.py:39
  260.2 48.2 %collective-permute-start.10 = (bf16[2,512,1024]{2,1,0:T(8,128)(2,1)}, bf16[2,512,1024]{2,1,0:T(8,128)(2,1)S(1)}, u32[]{:S(2)}, u32[]{:S(2)}) collective-permute-start(bf16[2,512,1024]{2,1,0:T(8,128)(2,1)} %pad_maximum_fusion.6), channel_id=1, source_target_pairs={{0,24},{8,16},{16,8},{24,0},{1,25},{9,17},{17,9},{25,1},{2,26},{10... | collective-permute-start | bytes 6291464 | tf_op jit(solution)/shard_map/ppermute | solution.py:49
  310.8 80.4 %collective-permute-start.17 = (f32[8,1536]{1,0:T(8,128)S(1)}, f32[8,1536]{1,0:T(8,128)S(1)}, u32[]{:S(2)}, u32[]{:S(2)}) collective-permute-start(f32[8,1536]{1,0:T(8,128)S(1)} %get-tuple-element.720), channel_id=1, source_target_pairs={{0,16},{8,24},{16,0},{24,8},{1,17},{9,25},{17,1},{25,9},{2,18},{10... | collective-permute-start | bytes 147464 | tf_op jit(solution)/shard_map/ppermute | solution.py:49
  315.2 44.3 %collective-permute-start.13 = (bf16[1,512,1024]{2,1,0:T(8,128)(2,1)S(1)}, bf16[1,512,1024]{2,1,0:T(8,128)(2,1)}, u32[]{:S(2)}, u32[]{:S(2)}) collective-permute-start(bf16[1,512,1024]{2,1,0:T(8,128)(2,1)S(1)} %copy-done.33), channel_id=1, source_target_pairs={{0,24},{8,16},{16,8},{24,0},{1,25},{9,17},{17,9},{25,1},{2,26},{10... | collective-permute-start | bytes 3145736 | tf_op jit(solution)/shard_map/ppermute | solution.py:49
  364.5 45.5 %collective-permute-start.16 = (bf16[240,2048]{1,0:T(8,128)(2,1)}, bf16[240,2048]{1,0:T(8,128)(2,1)}, u32[]{:S(2)}, u32[]{:S(2)}) collective-permute-start(bf16[240,2048]{1,0:T(8,128)(2,1)} %convolution_convert_fusion.17), channel_id=1, source_target_pairs={{0,24},{8,16},{16,8},{24,0},{1,25},{9,17},{17,9},{25,1},{2,26},{10... | collective-permute-start | bytes 2949128 | tf_op jit(solution)/shard_map/ppermute | solution.py:49
  368.4 41.6 %collective-permute-start.15 = (bf16[240,2048]{1,0:T(8,128)(2,1)}, bf16[240,2048]{1,0:T(8,128)(2,1)}, u32[]{:S(2)}, u32[]{:S(2)}) collective-permute-start(bf16[240,2048]{1,0:T(8,128)(2,1)} %convolution_convert_fusion.18), channel_id=1, source_target_pairs={{0,16},{8,24},{16,0},{24,8},{1,17},{9,25},{17,1},{25,9},{2,18},{10... | collective-permute-start | bytes 2949128 | tf_op jit(solution)/shard_map/ppermute | solution.py:49
  372.3 37.7 %collective-permute-start.14 = (bf16[240,2048]{1,0:T(8,128)(2,1)}, bf16[240,2048]{1,0:T(8,128)(2,1)}, u32[]{:S(2)}, u32[]{:S(2)}) collective-permute-start(bf16[240,2048]{1,0:T(8,128)(2,1)} %convolution_convert_fusion.15), channel_id=1, source_target_pairs={{0,8},{8,0},{16,24},{24,16},{1,9},{9,1},{17,25},{25,17},{2,10},{10... | collective-permute-start | bytes 2949128 | tf_op jit(solution)/shard_map/ppermute | solution.py:49
  390.4 311.6 %reduce-scatter.4.cloned.1.call-start = ((), (), s32[]{:S(2)}) async-start(), calls=%async_computation.12 | async-start | bytes 7077888 | tf_op jit(solution)/shard_map/reduce_scatter | solution.py:43
  391.3 60.4 %collective-permute-start.19 = (bf16[240,2048]{1,0:T(8,128)(2,1)}, bf16[240,2048]{1,0:T(8,128)(2,1)}, u32[]{:S(2)}, u32[]{:S(2)}) collective-permute-start(bf16[240,2048]{1,0:T(8,128)(2,1)} %convolution_convert_fusion.13), channel_id=1, source_target_pairs={{0,8},{8,0},{16,24},{24,16},{1,9},{9,1},{17,25},{25,17},{2,10},{10... | collective-permute-start | bytes 2949128 | tf_op jit(solution)/shard_map/ppermute | solution.py:49
  416.5 42.6 %collective-permute-start.21 = (bf16[240,2048]{1,0:T(8,128)(2,1)}, bf16[240,2048]{1,0:T(8,128)(2,1)}, u32[]{:S(2)}, u32[]{:S(2)}) collective-permute-start(bf16[240,2048]{1,0:T(8,128)(2,1)} %convolution_convert_fusion.11), channel_id=1, source_target_pairs={{0,24},{8,16},{16,8},{24,0},{1,25},{9,17},{17,9},{25,1},{2,26},{10... | collective-permute-start | bytes 2949128 | tf_op jit(solution)/shard_map/ppermute | solution.py:49
  419.6 42.7 %collective-permute-start.20 = (bf16[240,2048]{1,0:T(8,128)(2,1)}, bf16[240,2048]{1,0:T(8,128)(2,1)}, u32[]{:S(2)}, u32[]{:S(2)}) collective-permute-start(bf16[240,2048]{1,0:T(8,128)(2,1)} %convolution_convert_fusion.12), channel_id=1, source_target_pairs={{0,16},{8,24},{16,0},{24,8},{1,17},{9,25},{17,1},{25,9},{2,18},{10... | collective-permute-start | bytes 2949128 | tf_op jit(solution)/shard_map/ppermute | solution.py:49
  428.8 33.5 %collective-permute-start.22 = (bf16[240,2048]{1,0:T(8,128)(2,1)}, bf16[240,2048]{1,0:T(8,128)(2,1)S(1)}, u32[]{:S(2)}, u32[]{:S(2)}) collective-permute-start(bf16[240,2048]{1,0:T(8,128)(2,1)} %convolution_convert_fusion.7), channel_id=1, source_target_pairs={{0,8},{8,0},{16,24},{24,16},{1,9},{9,1},{17,25},{25,17},{2,10},{10... | collective-permute-start | bytes 2949128 | tf_op jit(solution)/shard_map/ppermute | solution.py:49
  451.1 53.5 %collective-permute-start.23 = (bf16[240,2048]{1,0:T(8,128)(2,1)}, bf16[240,2048]{1,0:T(8,128)(2,1)S(1)}, u32[]{:S(2)}, u32[]{:S(2)}) collective-permute-start(bf16[240,2048]{1,0:T(8,128)(2,1)} %get-tuple-element.332), channel_id=1, source_target_pairs={{0,16},{8,24},{16,0},{24,8},{1,17},{9,25},{17,1},{25,9},{2,18},{10... | collective-permute-start | bytes 2949128 | tf_op jit(solution)/shard_map/ppermute | solution.py:49
  451.7 53.0 %collective-permute-start.24 = (bf16[240,2048]{1,0:T(8,128)(2,1)}, bf16[240,2048]{1,0:T(8,128)(2,1)}, u32[]{:S(2)}, u32[]{:S(2)}) collective-permute-start(bf16[240,2048]{1,0:T(8,128)(2,1)} %get-tuple-element.333), channel_id=1, source_target_pairs={{0,24},{8,16},{16,8},{24,0},{1,25},{9,17},{17,9},{25,1},{2,26},{10... | collective-permute-start | bytes 2949128 | tf_op jit(solution)/shard_map/ppermute | solution.py:49
  507.0 48.9 %collective-permute-start.29 = (bf16[240,2048]{1,0:T(8,128)(2,1)}, bf16[240,2048]{1,0:T(8,128)(2,1)}, u32[]{:S(2)}, u32[]{:S(2)}) collective-permute-start(bf16[240,2048]{1,0:T(8,128)(2,1)} %get-tuple-element.368), channel_id=1, source_target_pairs={{0,16},{8,24},{16,0},{24,8},{1,17},{9,25},{17,1},{25,9},{2,18},{10... | collective-permute-start | bytes 2949128 | tf_op jit(solution)/shard_map/ppermute | solution.py:49
  508.5 47.4 %collective-permute-start.30 = (bf16[240,2048]{1,0:T(8,128)(2,1)}, bf16[240,2048]{1,0:T(8,128)(2,1)}, u32[]{:S(2)}, u32[]{:S(2)}) collective-permute-start(bf16[240,2048]{1,0:T(8,128)(2,1)} %get-tuple-element.369), channel_id=1, source_target_pairs={{0,24},{8,16},{16,8},{24,0},{1,25},{9,17},{17,9},{25,1},{2,26},{10... | collective-permute-start | bytes 2949128 | tf_op jit(solution)/shard_map/ppermute | solution.py:49
  586.8 83.0 %collective-permute-start.34 = (bf16[240,2048]{1,0:T(8,128)(2,1)}, bf16[240,2048]{1,0:T(8,128)(2,1)}, u32[]{:S(2)}, u32[]{:S(2)}) collective-permute-start(bf16[240,2048]{1,0:T(8,128)(2,1)} %get-tuple-element.622), channel_id=1, source_target_pairs={{0,8},{8,0},{16,24},{24,16},{1,9},{9,1},{17,25},{25,17},{2,10},{10... | collective-permute-start | bytes 2949128 | tf_op jit(solution)/shard_map/ppermute | solution.py:49
  587.3 82.5 %collective-permute-start.35 = (bf16[240,2048]{1,0:T(8,128)(2,1)}, bf16[240,2048]{1,0:T(8,128)(2,1)}, u32[]{:S(2)}, u32[]{:S(2)}) collective-permute-start(bf16[240,2048]{1,0:T(8,128)(2,1)} %get-tuple-element.621), channel_id=1, source_target_pairs={{0,16},{8,24},{16,0},{24,8},{1,17},{9,25},{17,1},{25,9},{2,18},{10... | collective-permute-start | bytes 2949128 | tf_op jit(solution)/shard_map/ppermute | solution.py:49
  598.5 58.4 %collective-permute-start.31 = (bf16[240,2048]{1,0:T(8,128)(2,1)}, bf16[240,2048]{1,0:T(8,128)(2,1)}, u32[]{:S(2)}, u32[]{:S(2)}) collective-permute-start(bf16[240,2048]{1,0:T(8,128)(2,1)} %get-tuple-element.626), channel_id=1, source_target_pairs={{0,8},{8,0},{16,24},{24,16},{1,9},{9,1},{17,25},{25,17},{2,10},{10... | collective-permute-start | bytes 2949128 | tf_op jit(solution)/shard_map/ppermute | solution.py:49
  598.5 59.7 %collective-permute-start.32 = (bf16[240,2048]{1,0:T(8,128)(2,1)}, bf16[240,2048]{1,0:T(8,128)(2,1)}, u32[]{:S(2)}, u32[]{:S(2)}) collective-permute-start(bf16[240,2048]{1,0:T(8,128)(2,1)} %get-tuple-element.625), channel_id=1, source_target_pairs={{0,16},{8,24},{16,0},{24,8},{1,17},{9,25},{17,1},{25,9},{2,18},{10... | collective-permute-start | bytes 2949128 | tf_op jit(solution)/shard_map/ppermute | solution.py:49
  599.7 58.6 %collective-permute-start.33 = (bf16[240,2048]{1,0:T(8,128)(2,1)}, bf16[240,2048]{1,0:T(8,128)(2,1)}, u32[]{:S(2)}, u32[]{:S(2)}) collective-permute-start(bf16[240,2048]{1,0:T(8,128)(2,1)} %get-tuple-element.624), channel_id=1, source_target_pairs={{0,24},{8,16},{16,8},{24,0},{1,25},{9,17},{17,9},{25,1},{2,26},{10... | collective-permute-start | bytes 2949128 | tf_op jit(solution)/shard_map/ppermute | solution.py:49
  601.3 52.2 %all-to-all-start.1 = ((f32[4,2,240,2]{2,3,1,0:T(2,128)}), f32[4,2,240,2]{2,3,1,0:T(2,128)S(1)}, u32[]{:S(2)}, u32[]{:S(2)}) async-start(f32[4,2,240,2]{2,3,1,0:T(2,128)} %select_select_fusion), calls=%async_computation.2 | async-start | bytes 32768 | tf_op jit(solution)/shard_map/all_to_all | solution.py:622
  663.1 140.6 %all-gather.17.cloned.1.call-start = ((), (), s32[]{:S(2)}) async-start(), calls=%async_computation.13 | async-start | bytes 7077888 | tf_op jit(solution)/shard_map/all_gather | solution.py:39
  705.3 224.0 %reduce-scatter.6.cloned.1.call-start = ((), (), s32[]{:S(2)}) async-start(), calls=%async_computation.14 | async-start | bytes 7077888 | tf_op jit(solution)/shard_map/reduce_scatter | solution.py:43
  705.5 48.8 %collective-permute-start.38 = (bf16[2,512,1024]{2,1,0:T(8,128)(2,1)}, bf16[2,512,1024]{2,1,0:T(8,128)(2,1)}, u32[]{:S(2)}, u32[]{:S(2)}) collective-permute-start(bf16[2,512,1024]{2,1,0:T(8,128)(2,1)} %pad_maximum_fusion.9), channel_id=1, source_target_pairs={{0,16},{8,24},{16,0},{24,8},{1,17},{9,25},{17,1},{25,9},{2,18},{10... | collective-permute-start | bytes 6291464 | tf_op jit(solution)/shard_map/ppermute | solution.py:49
  706.3 92.0 %collective-permute-start.39 = (bf16[2,512,1024]{2,1,0:T(8,128)(2,1)}, bf16[2,512,1024]{2,1,0:T(8,128)(2,1)}, u32[]{:S(2)}, u32[]{:S(2)}) collective-permute-start(bf16[2,512,1024]{2,1,0:T(8,128)(2,1)} %pad_maximum_fusion.10), channel_id=1, source_target_pairs={{0,24},{8,16},{16,8},{24,0},{1,25},{9,17},{17,9},{25,1},{2,26},{10... | collective-permute-start | bytes 6291464 | tf_op jit(solution)/shard_map/ppermute | solution.py:49
  803.8 258.1 %reduce-scatter.8.cloned.1.call-start = ((), (), s32[]{:S(2)}) async-start(), calls=%async_computation.15 | async-start | bytes 7077888 | tf_op jit(solution)/shard_map/reduce_scatter | solution.py:43
  824.8 50.0 %collective-permute-start.45 = (f32[2,512,64]{1,2,0:T(8,128)}, f32[2,512,64]{1,2,0:T(8,128)}, u32[]{:S(2)}, u32[]{:S(2)}) collective-permute-start(f32[2,512,64]{1,2,0:T(8,128)} %pad_maximum_fusion.19), channel_id=1, source_target_pairs={{0,8},{8,0},{16,24},{24,16},{1,9},{9,1},{17,25},{25,17},{2,10},{10... | collective-permute-start | bytes 786440 | tf_op jit(solution)/shard_map/ppermute | solution.py:49
  826.7 102.6 %collective-permute-start.40 = (bf16[2,512,1024]{2,1,0:T(8,128)(2,1)}, bf16[2,512,1024]{2,1,0:T(8,128)(2,1)}, u32[]{:S(2)}, u32[]{:S(2)}) collective-permute-start(bf16[2,512,1024]{2,1,0:T(8,128)(2,1)} %pad_maximum_fusion.12), channel_id=1, source_target_pairs={{0,8},{8,0},{16,24},{24,16},{1,9},{9,1},{17,25},{25,17},{2,10},{10... | collective-permute-start | bytes 6291464 | tf_op jit(solution)/shard_map/ppermute | solution.py:49
  827.3 102.1 %collective-permute-start.41 = (bf16[2,512,1024]{2,1,0:T(8,128)(2,1)}, bf16[2,512,1024]{2,1,0:T(8,128)(2,1)}, u32[]{:S(2)}, u32[]{:S(2)}) collective-permute-start(bf16[2,512,1024]{2,1,0:T(8,128)(2,1)} %pad_maximum_fusion.13), channel_id=1, source_target_pairs={{0,16},{8,24},{16,0},{24,8},{1,17},{9,25},{17,1},{25,9},{2,18},{10... | collective-permute-start | bytes 6291464 | tf_op jit(solution)/shard_map/ppermute | solution.py:49
  828.8 100.6 %collective-permute-start.42 = (bf16[2,512,1024]{2,1,0:T(8,128)(2,1)S(1)}, bf16[2,512,1024]{2,1,0:T(8,128)(2,1)}, u32[]{:S(2)}, u32[]{:S(2)}) collective-permute-start(bf16[2,512,1024]{2,1,0:T(8,128)(2,1)S(1)} %copy-done.31), channel_id=1, source_target_pairs={{0,24},{8,16},{16,8},{24,0},{1,25},{9,17},{17,9},{25,1},{2,26},{10... | collective-permute-start | bytes 6291464 | tf_op jit(solution)/shard_map/ppermute | solution.py:49
  829.7 47.7 %collective-permute-start.43 = (bf16[2,512,256]{2,1,0:T(8,128)(2,1)}, bf16[2,512,256]{2,1,0:T(8,128)(2,1)S(1)}, u32[]{:S(2)}, u32[]{:S(2)}) collective-permute-start(bf16[2,512,256]{2,1,0:T(8,128)(2,1)} %pad_maximum_fusion.18), channel_id=1, source_target_pairs={{0,8},{8,0},{16,24},{24,16},{1,9},{9,1},{17,25},{25,17},{2,10},{10... | collective-permute-start | bytes 1572872 | tf_op jit(solution)/shard_map/ppermute | solution.py:49
  875.9 47.9 %collective-permute-start.46 = (f32[512,64]{0,1:T(8,128)S(1)}, f32[512,64]{0,1:T(8,128)S(1)}, u32[]{:S(2)}, u32[]{:S(2)}) collective-permute-start(f32[512,64]{0,1:T(8,128)S(1)} %fusion.89), channel_id=1, source_target_pairs={{0,16},{8,24},{16,0},{24,8},{1,17},{9,25},{17,1},{25,9},{2,18},{10... | collective-permute-start | bytes 393224 | tf_op jit(solution)/shard_map/ppermute | solution.py:49
  877.6 50.9 %collective-permute-start.44 = (bf16[512,256]{1,0:T(8,128)(2,1)S(1)}, bf16[512,256]{1,0:T(8,128)(2,1)S(1)}, u32[]{:S(2)}, u32[]{:S(2)}) collective-permute-start(bf16[512,256]{1,0:T(8,128)(2,1)S(1)} %fusion.83), channel_id=1, source_target_pairs={{0,16},{8,24},{16,0},{24,8},{1,17},{9,25},{17,1},{25,9},{2,18},{10... | collective-permute-start | bytes 786440 | tf_op jit(solution)/shard_map/ppermute | solution.py:49
  944.8 46.4 %collective-permute-start.49 = (bf16[1,512,1024]{2,1,0:T(8,128)(2,1)}, bf16[1,512,1024]{2,1,0:T(8,128)(2,1)}, u32[]{:S(2)}, u32[]{:S(2)}) collective-permute-start(bf16[1,512,1024]{2,1,0:T(8,128)(2,1)} %get-tuple-element.468), channel_id=1, source_target_pairs={{0,24},{8,16},{16,8},{24,0},{1,25},{9,17},{17,9},{25,1},{2,26},{10... | collective-permute-start | bytes 3145736 | tf_op jit(solution)/shard_map/ppermute | solution.py:49
  956.1 43.8 %collective-permute-start.50 = (bf16[2,512,768]{2,1,0:T(8,128)(2,1)}, bf16[2,512,768]{2,1,0:T(8,128)(2,1)}, u32[]{:S(2)}, u32[]{:S(2)}) collective-permute-start(bf16[2,512,768]{2,1,0:T(8,128)(2,1)} %pad_maximum_fusion.15), channel_id=1, source_target_pairs={{0,8},{8,0},{16,24},{24,16},{1,9},{9,1},{17,25},{25,17},{2,10},{10... | collective-permute-start | bytes 4718600 | tf_op jit(solution)/shard_map/ppermute | solution.py:49
  993.2 45.4 %collective-permute-start.53 = (bf16[1,512,1024]{2,1,0:T(8,128)(2,1)S(1)}, bf16[1,512,1024]{2,1,0:T(8,128)(2,1)}, u32[]{:S(2)}, u32[]{:S(2)}) collective-permute-start(bf16[1,512,1024]{2,1,0:T(8,128)(2,1)S(1)} %copy-done.34), channel_id=1, source_target_pairs={{0,24},{8,16},{16,8},{24,0},{1,25},{9,17},{17,9},{25,1},{2,26},{10... | collective-permute-start | bytes 3145736 | tf_op jit(solution)/shard_map/ppermute | solution.py:49
  (134 other events, 2162.2 us)
Sparse Core Ops, SparseCore 0:
  15.4 103.4 all-gather.6
  121.5 73.1 all-gather.8
  196.8 98.1 all-gather.10
  296.9 98.1 all-gather.14
  396.9 98.1 all-gather.12
  575.8 126.2 reduce-scatter.3
  705.5 98.2 all-gather.16
  807.9 116.5 reduce-scatter.5
  939.4 117.4 reduce-scatter.7

commit v7 on v6

--- a/solution.py
+++ b/solution.py
@@ -762,14 +762,14 @@
     def joined(e, which):
         return jnp.concatenate([piece for step in steps[::2] for piece in calls[e, step][which]])
 
+    grad_normed2_part = combine(ranks, [grads_back[e][step] for e, step in every])
+
+    calls = after(calls, grad_normed2_part)
     scalars = [joined(e, 4) for e in range(per_device)]
     scalars = jnp.stack(scalars)
     scalars_back = swap_small(
         [scalars[:, step * capacity : (step + 1) * capacity] for step in steps]
     )
-    grad_normed2_part = combine(ranks, [grads_back[e][step] for e, step in every])
-
-    calls = after(calls, grad_normed2_part)
     branch_back, weight_grads = [], []
     for e in range(per_device):
         rows, grad_rows, act, grad_pre = (joined(e, which) for which in range(4))

time: 1090 us -> 1080 us (level)
    unnamed x235 -> x191, local copies, waits for them, and re-layouts: 24.7 us -> 24.9 us
  transfers between devices with their start and end apart: 70 -> 70, of which waited for: 28 -> 29; matrix products, arithmetic and copies ran while one was open for 29% -> 28% of each run, Pallas kernels for 20% -> 20%
where the time goes in v7:
time: 1080 us; the launch traced here: 1070 us
  waiting for transfers between devices  411 us (38%)
  Pallas kernels  241 us (22%)
  local copies, waits for them, and re-layouts  156 us (14%)
  matrix products  117 us (11%)
  other arithmetic  72.6 us (7%)
  starting transfers between devices  52.4 us (5%)
  between operations  15.7 us (1%)
    ppermute x58, waiting for transfers between devices, trade(): return lax.ppermute(value, 'row', [(r, r ^ step) for r in range(n_row)])  340 us
    pallas_call x4, Pallas kernels, run_expert(): pl.pallas_call(expert_kernel, name='expert', grid=(1,), in_specs=[whole(a...  72.6 us
    dot_general x6, matrix products, contract_first(): lax.dot_general(left_op, right_op, (((0,), (0,)), ((), ())), preferred_el...  47.1 us
    dot_general x14, matrix products, plain_dot(): return jnp.dot(left_op, right_op, preferred_element_type=F32).astype(kind)  47 us
    ppermute x58, starting transfers between devices, trade(): return lax.ppermute(value, 'row', [(r, r ^ step) for r in range(n_row)])  41.4 us
    pallas_call x2, Pallas kernels, combine(): pl.pallas_call(combine_kernel, name='combine', grid=(D // width, rows //...  34.8 us
    pallas_call x3, Pallas kernels, place(): pl.pallas_call(place_kernel, name='place', grid_spec=pltpu.PrefetchScalar...  32.9 us
    pallas_call x1, Pallas kernels, attend_back(): pl.pallas_call(attend_back_kernel, name='attend_back', grid=(heads, rows...  27.6 us
  transfers between devices with their start and end apart: 70, of which 29 were waited for; matrix products, arithmetic and copies ran while one was open for 28% of the time, Pallas kernels for 20%

profile of v7, /device:TPU:0, one launch (start us, length us, event | category | flops | bytes accessed | tf_op | source)
XLA Modules:
  0.0 1074.1 jit_solution(13373211099757505503)
XLA Ops:
  22.9 6.1 constant_dynamic-slice_fusion.44
  60.9 30.1 %collective-permute-done.1 = bf16[2,512,1024]{2,1,0:T(8,128)(2,1)} collective-permute-done((bf16[2,512,1024]{2,1,0:T(8,128)(2,1)}, bf16[2,512,1024]{2,1,0:T(8,128)(2,1)}, u32[]{:S(2)}, u32[]{:S(2)}) %collective-permute-start.1) | collective-permute-done | bytes 2097184 | tf_op jit(solution)/shard_map/ppermute | solution.py:49
  104.2 7.2 scatter_custom_fusion
  133.6 5.5 collective-permute-done.2
  145.5 13.9 %project.1 = (bf16[1536,2048]{1,0:T(8,128)(2,1)}, f32[1536,1]{1,0:T(8,128)}, f32[1536,512]{1,0:T(8,128)}, bf16[1536,256]{1,0:T(8,128)(2,1)}, bf16[1536,256]{1,0:T(8,128)(2,1)}, /*index=5*/bf16[1536,256]{1,0:T(8,128)(2,1)}) custom-call(bf16[1552,2048]{1,0:T(8,128)(2,1)} %all-gather.7.cloned.1.call-done.x_ref, f32[1,2048]{1,0:T(1,128)} %get-tuple-element.684.gain_ref, ...), custom_call_target="tpu_custom_call" | custom-call | flops 1000 | bytes 1000 | tf_op jit(solution)/shard_map/project/pallas_call | solution.py:117
  159.4 16.8 %attend.1 = (bf16[1536,256]{1,0:T(8,128)(2,1)}, f32[2,1536,1]{2,1,0:T(8,128)}) custom-call(bf16[1536,256]{1,0:T(8,128)(2,1)} %get-tuple-element.275.q_ref, bf16[1536,256]{1,0:T(8,128)(2,1)} %get-tuple-element.276.k_ref, bf16[1536,256]{1,0:T(8,128)(2,1)} %get-tuple-element.277.v_ref, s32[1536,1]{1,0:T(8,128)} %broadcast_in_dim.650.seg_q_ref, ...), custom_call_target="tpu_custom_call" | custom-call | flops 1000 | bytes 1000 | tf_op jit(solution)/shard_map/attend/pallas_call | solution.py:167
  181.8 7.6 collective-permute-done.7
  196.3 17.5 %collective-permute-done.8 = bf16[1536,256]{1,0:T(8,128)(2,1)S(1)} collective-permute-done((bf16[1536,256]{1,0:T(8,128)(2,1)S(1)}, bf16[1536,256]{1,0:T(8,128)(2,1)S(1)}, u32[]{:S(2)}, u32[]{:S(2)}) %collective-permute-start.8) | collective-permute-done | bytes 786464 | tf_op jit(solution)/shard_map/ppermute | solution.py:49
  215.1 45.0 %collective-permute-done.9 = bf16[2,512,1024]{2,1,0:T(8,128)(2,1)S(1)} collective-permute-done((bf16[2,512,1024]{2,1,0:T(8,128)(2,1)}, bf16[2,512,1024]{2,1,0:T(8,128)(2,1)S(1)}, u32[]{:S(2)}, u32[]{:S(2)}) %collective-permute-start.9) | collective-permute-done | bytes 2097184 | tf_op jit(solution)/shard_map/ppermute | solution.py:49
  270.3 38.0 %collective-permute-done.10 = bf16[2,512,1024]{2,1,0:T(8,128)(2,1)S(1)} collective-permute-done((bf16[2,512,1024]{2,1,0:T(8,128)(2,1)}, bf16[2,512,1024]{2,1,0:T(8,128)(2,1)S(1)}, u32[]{:S(2)}, u32[]{:S(2)}) %collective-permute-start.10) | collective-permute-done | bytes 2097184 | tf_op jit(solution)/shard_map/ppermute | solution.py:49
  317.3 22.8 %branch.1 = (bf16[1536,2048]{1,0:T(8,128)(2,1)}, f32[1536,1]{1,0:T(8,128)}, f32[1536,256]{1,0:T(8,128)}) custom-call(s32[2]{0:T(128)} %pad_add_fusion.1.at_ref, bf16[1552,2048]{1,0:T(8,128)(2,1)} %all-gather.7.cloned.1.call-done.x_ref, bf16[1536,2048]{1,0:T(8,128)(2,1)} %all-gather.11.cloned.1.call-done.att_ref, ...), custom_call_target="tpu_custom_call" | custom-call | flops 1000 | bytes 1000 | tf_op jit(solution)/shard_map/branch/pallas_call | solution.py:305
  346.1 13.2 %collective-permute-done.13 = bf16[1,512,1024]{2,1,0:T(8,128)(2,1)} collective-permute-done((bf16[1,512,1024]{2,1,0:T(8,128)(2,1)S(1)}, bf16[1,512,1024]{2,1,0:T(8,128)(2,1)}, u32[]{:S(2)}, u32[]{:S(2)}) %collective-permute-start.13) | collective-permute-done | bytes 1048608 | tf_op jit(solution)/shard_map/ppermute | solution.py:49
  391.5 18.4 %all-to-all-done = f32[4,2,240]{2,1,0:T(2,128)S(1)} async-done(((f32[4,2,240]{2,1,0:T(2,128)}), f32[4,2,240]{2,1,0:T(2,128)S(1)}, u32[]{:S(2)}, u32[]{:S(2)}) %all-to-all-start) | async-done | bytes 7712 | tf_op jit(solution)/shard_map/all_to_all | solution.py:622
  410.8 5.6 convolution_convert_fusion.12
  432.6 18.1 %expert.4 = (bf16[480,1024]{1,0:T(8,128)(2,1)}, bf16[480,2048]{1,0:T(8,128)(2,1)}, f32[480,2]{1,0:T(8,128)}, bf16[240,2048]{1,0:T(8,128)(2,1)}, bf16[240,2048]{1,0:T(8,128)(2,1)}) custom-call(bf16[240,2048]{1,0:T(8,128)(2,1)} %collective-permute-done.15.x0_ref, bf16[240,2048]{1,0:T(8,128)(2,1)} %collective-permute-done.16.x1_ref, ...), custom_call_target="tpu_custom_call" | custom-call | flops 1000 | bytes 1000 | tf_op jit(solution)/shard_map/expert/pallas_call | solution.py:360
  453.7 5.5 convolution_convert_fusion.8.c0_ref
  461.8 18.4 %expert.5 = (bf16[480,1024]{1,0:T(8,128)(2,1)}, bf16[480,2048]{1,0:T(8,128)(2,1)}, f32[480,2]{1,0:T(8,128)}, bf16[240,2048]{1,0:T(8,128)(2,1)}, bf16[240,2048]{1,0:T(8,128)(2,1)}) custom-call(bf16[240,2048]{1,0:T(8,128)(2,1)} %collective-permute-done.20.x0_ref, bf16[240,2048]{1,0:T(8,128)(2,1)} %collective-permute-done.21.x1_ref, ...), custom_call_target="tpu_custom_call" | custom-call | flops 1000 | bytes 1000 | tf_op jit(solution)/shard_map/expert/pallas_call | solution.py:360
  480.2 14.9 %all-gather.13.cloned.1.call-done.value_ref = bf16[1536,2048]{1,0:T(8,128)(2,1)} async-done(((bf16[1536,256]{1,0:T(8,128)(2,1)}), bf16[1536,2048]{1,0:T(8,128)(2,1)}) %all-gather.13.cloned.1.call-update) | async-done | bytes 6291472 | tf_op jit(solution)/shard_map/all_gather | solution.py:39
  495.1 9.6 pick.1
  510.3 18.0 %expert.7 = (bf16[480,1024]{1,0:T(8,128)(2,1)}, bf16[480,2048]{1,0:T(8,128)(2,1)}, f32[480,2]{1,0:T(8,128)}, bf16[240,2048]{1,0:T(8,128)(2,1)}, bf16[240,2048]{1,0:T(8,128)(2,1)}) custom-call(bf16[240,2048]{1,0:T(8,128)(2,1)} %convolution_convert_fusion.14.x0_ref, bf16[240,2048]{1,0:T(8,128)(2,1)} %collective-permute-done.19.x1_ref, ...), custom_call_target="tpu_custom_call" | custom-call | flops 1000 | bytes 1000 | tf_op jit(solution)/shard_map/expert/pallas_call | solution.py:360
  529.8 18.1 %expert.6 = (bf16[480,1024]{1,0:T(8,128)(2,1)}, bf16[480,2048]{1,0:T(8,128)(2,1)}, f32[480,2]{1,0:T(8,128)}, bf16[240,2048]{1,0:T(8,128)(2,1)}, bf16[240,2048]{1,0:T(8,128)(2,1)}) custom-call(bf16[240,2048]{1,0:T(8,128)(2,1)} %convolution_convert_fusion.16.x0_ref, bf16[240,2048]{1,0:T(8,128)(2,1)} %collective-permute-done.14.x1_ref, ...), custom_call_target="tpu_custom_call" | custom-call | flops 1000 | bytes 1000 | tf_op jit(solution)/shard_map/expert/pallas_call | solution.py:360
  552.3 17.4 %combine.2 = bf16[1536,2048]{1,0:T(8,128)(2,1)} custom-call(s32[8,1536]{1,0:T(8,128)} %concatenate.116.refs_0_, bf16[240,2048]{1,0:T(8,128)(2,1)} %get-tuple-element.358.refs_1_, bf16[240,2048]{1,0:T(8,128)(2,1)} %copy-done.52, bf16[240,2048]{1,0:T(8,128)(2,1)} %copy-done.50, bf16[240,2048]{1,0:T(8,128)(2,1)} %collective-permute-done.24.refs_4_, ...), custom_call_target="tpu_custom_call" | custom-call | flops 1000 | bytes 1000 | tf_op jit(solution)/shard_map/combine/pallas_call | solution.py:440
  571.3 7.5 convolution_convert_fusion.2
  583.3 7.5 convolution_convert_fusion.3
  599.5 12.0 %convolution_convert_fusion.1 = bf16[2048,2048]{1,0:T(8,128)(2,1)S(1)} fusion(bf16[240,2048]{1,0:T(8,128)(2,1)} %collective-permute-done.16.x1_ref, bf16[240,2048]{1,0:T(8,128)(2,1)} %collective-permute-done.15.x0_ref, bf16[240,2048]{1,0:T(8,128)(2,1)} %collective-permute-done.14.x1_ref, bf16[240,2048]{1,0:T(8,128)(2,1)S(1)} %copy-done.45, ...), kind=kOutput, calls=%fused_computation.9 | convolution fusion | flops 8080850944 | bytes 16252928 | tf_op jit(solution)/shard_map/dot_general | solution.py:63
  613.9 12.0 %convolution_convert_fusion = bf16[2048,2048]{1,0:T(8,128)(2,1)S(1)} fusion(bf16[240,2048]{1,0:T(8,128)(2,1)} %collective-permute-done.21.x1_ref, bf16[240,2048]{1,0:T(8,128)(2,1)} %collective-permute-done.20.x0_ref, bf16[240,2048]{1,0:T(8,128)(2,1)} %collective-permute-done.19.x1_ref, bf16[240,2048]{1,0:T(8,128)(2,1)} %convolution_convert_fusion.14.x0_ref, ...), kind=kOutput, calls=%fused_computation.8 | convolution fusion | flops 8080850944 | bytes 16252928 | tf_op jit(solution)/shard_map/dot_general | solution.py:63
  639.2 8.7 all-to-all-done.1
  664.3 11.3 %collective-permute-done.36.refs_8_ = bf16[240,2048]{1,0:T(8,128)(2,1)} collective-permute-done((bf16[240,2048]{1,0:T(8,128)(2,1)}, bf16[240,2048]{1,0:T(8,128)(2,1)}, u32[]{:S(2)}, u32[]{:S(2)}) %collective-permute-start.36) | collective-permute-done | bytes 983072 | tf_op jit(solution)/shard_map/ppermute | solution.py:49
  675.6 5.2 all-to-all-done.2
  682.1 14.5 %reduce-scatter.4.cloned.1.call-done = bf16[1536,256]{1,0:T(8,128)(2,1)} async-done(((bf16[1536,2048]{1,0:T(8,128)(2,1)}), bf16[1536,256]{1,0:T(8,128)(2,1)}) %reduce-scatter.4.cloned.1.call-update) | async-done | bytes 786448 | tf_op jit(solution)/shard_map/reduce_scatter | solution.py:43
  701.9 17.4 %combine.3 = bf16[1536,2048]{1,0:T(8,128)(2,1)} custom-call(s32[8,1536]{1,0:T(8,128)} %concatenate.116.refs_0_, bf16[240,2048]{1,0:T(8,128)(2,1)} %get-tuple-element.431.refs_1_, bf16[240,2048]{1,0:T(8,128)(2,1)} %collective-permute-done.31.refs_2_, bf16[240,2048]{1,0:T(8,128)(2,1)} %collective-permute-done.32.refs_3_, ...), custom_call_target="tpu_custom_call" | custom-call | flops 1000 | bytes 1000 | tf_op jit(solution)/shard_map/combine/pallas_call | solution.py:440
  719.3 29.5 %collective-permute-done.38.refs_2_ = bf16[2,512,1024]{2,1,0:T(8,128)(2,1)} collective-permute-done((bf16[2,512,1024]{2,1,0:T(8,128)(2,1)}, bf16[2,512,1024]{2,1,0:T(8,128)(2,1)}, u32[]{:S(2)}, u32[]{:S(2)}) %collective-permute-start.38) | collective-permute-done | bytes 2097184 | tf_op jit(solution)/shard_map/ppermute | solution.py:49
  748.9 44.0 %collective-permute-done.39.refs_3_ = bf16[2,512,1024]{2,1,0:T(8,128)(2,1)} collective-permute-done((bf16[2,512,1024]{2,1,0:T(8,128)(2,1)}, bf16[2,512,1024]{2,1,0:T(8,128)(2,1)}, u32[]{:S(2)}, u32[]{:S(2)}) %collective-permute-start.39) | collective-permute-done | bytes 2097184 | tf_op jit(solution)/shard_map/ppermute | solution.py:49
  792.9 5.2 all-gather.17.cloned.1.call-done
  798.8 7.4 fusion.38
  824.7 11.0 %place.3 = f32[8,512,1024]{2,1,0:T(8,128)} custom-call(s32[8]{0:T(128)} %stack.313.at_ref, bf16[2,512,1024]{2,1,0:T(8,128)(2,1)} %pad_maximum_fusion.7.refs_0_, bf16[2,512,1024]{2,1,0:T(8,128)(2,1)} %copy-done.32, bf16[2,512,1024]{2,1,0:T(8,128)(2,1)} %collective-permute-done.38.refs_2_, bf16[2,512,1024]{2,1,0:T(8,128)(2,1)} %collective-permute-done.39.refs_3_), custom_call_target="tpu_custom_call" | custom-call | flops 1000 | bytes 1000 | tf_op jit(solution)/shard_map/place/pallas_call | solution.py:464
  835.6 5.9 convolution_convert_fusion.6.grad_ref
  841.6 27.6 %attend_back.1 = (bf16[1536,256]{1,0:T(8,128)(2,1)}, bf16[1536,256]{1,0:T(8,128)(2,1)}, bf16[1536,256]{1,0:T(8,128)(2,1)}, f32[1,128]{1,0:T(1,128)}, f32[1,128]{1,0:T(1,128)}) custom-call(bf16[1536,256]{1,0:T(8,128)(2,1)} %get-tuple-element.275.q_ref, bf16[1536,256]{1,0:T(8,128)(2,1)} %get-tuple-element.276.k_ref, ...), custom_call_target="tpu_custom_call" | custom-call | flops 1000 | bytes 1000 | tf_op jit(solution)/shard_map/attend_back/pallas_call | solution.py:250
  875.3 42.8 %collective-permute-done.46 = f32[512,64]{0,1:T(8,128)S(1)} collective-permute-done((f32[512,64]{0,1:T(8,128)S(1)}, f32[512,64]{0,1:T(8,128)S(1)}, u32[]{:S(2)}, u32[]{:S(2)}) %collective-permute-start.46) | collective-permute-done | bytes 131104 | tf_op jit(solution)/shard_map/ppermute | solution.py:49
  923.8 9.8 through_heads.1
  939.4 8.6 convolution_convert_fusion.4
  953.6 10.9 %place.4 = f32[8,512,1024]{2,1,0:T(8,128)} custom-call(s32[8]{0:T(128)} %stack.313.at_ref, bf16[2,512,1024]{2,1,0:T(8,128)(2,1)} %pad_maximum_fusion.11.refs_0_, bf16[2,512,1024]{2,1,0:T(8,128)(2,1)} %collective-permute-done.40.refs_1_, bf16[2,512,1024]{2,1,0:T(8,128)(2,1)} %collective-permute-done.41.refs_2_, ...), custom_call_target="tpu_custom_call" | custom-call | flops 1000 | bytes 1000 | tf_op jit(solution)/shard_map/place/pallas_call | solution.py:464
  964.5 5.4 gather_fusion.2
  969.9 15.6 %collective-permute-done.49.refs_3_ = bf16[1,512,1024]{2,1,0:T(8,128)(2,1)} collective-permute-done((bf16[1,512,1024]{2,1,0:T(8,128)(2,1)}, bf16[1,512,1024]{2,1,0:T(8,128)(2,1)}, u32[]{:S(2)}, u32[]{:S(2)}) %collective-permute-start.49) | collective-permute-done | bytes 1048608 | tf_op jit(solution)/shard_map/ppermute | solution.py:49
  987.5 6.7 multiply_reduce_fusion
  997.9 9.8 all_to_all.24
  1012.4 20.5 %collective-permute-done.53.refs_7_ = bf16[1,512,1024]{2,1,0:T(8,128)(2,1)} collective-permute-done((bf16[1,512,1024]{2,1,0:T(8,128)(2,1)S(1)}, bf16[1,512,1024]{2,1,0:T(8,128)(2,1)}, u32[]{:S(2)}, u32[]{:S(2)}) %collective-permute-start.53) | collective-permute-done | bytes 1048608 | tf_op jit(solution)/shard_map/ppermute | solution.py:49
  1037.3 11.0 %place.5 = f32[8,512,1024]{2,1,0:T(8,128)} custom-call(s32[16]{0:T(128)} %stack.335.at_ref, bf16[1,512,1024]{2,1,0:T(8,128)(2,1)} %get-tuple-element.514.refs_0_, bf16[1,512,1024]{2,1,0:T(8,128)(2,1)} %collective-permute-done.47.refs_1_, bf16[1,512,1024]{2,1,0:T(8,128)(2,1)} %collective-permute-done.48.refs_2_, ...), custom_call_target="tpu_custom_call" | custom-call | flops 1000 | bytes 1000 | tf_op jit(solution)/shard_map/place/pallas_call | solution.py:464
  (551 shorter events, 322.9 us)
Async XLA Ops:
  7.2 134.9 %all-gather.7.cloned.1.call-start = ((), (), s32[]{:S(2)}) async-start(), calls=%async_computation.7 | async-start | bytes 7151616 | tf_op jit(solution)/shard_map/all_gather | solution.py:39
  15.3 179.4 %all-gather.9.cloned.1.call-start = ((), (), s32[]{:S(2)}) async-start(), calls=%async_computation.8 | async-start | bytes 4718592 | tf_op jit(solution)/shard_map/all_gather | solution.py:39
  17.5 34.0 %collective-permute-start.3 = (bf16[512,1088]{0,1:T(8,128)(2,1)}, bf16[512,1088]{0,1:T(8,128)(2,1)}, u32[]{:S(2)}, u32[]{:S(2)}) collective-permute-start(bf16[512,1088]{0,1:T(8,128)(2,1)} %copy.61), channel_id=1, source_target_pairs={{0,8},{8,0},{16,24},{24,16},{1,9},{9,1},{17,25},{25,17},{2,10},{10... | collective-permute-start | bytes 3342344 | tf_op jit(solution)/shard_map/ppermute | solution.py:49
  32.9 58.0 %collective-permute-start.1 = (bf16[2,512,1024]{2,1,0:T(8,128)(2,1)}, bf16[2,512,1024]{2,1,0:T(8,128)(2,1)}, u32[]{:S(2)}, u32[]{:S(2)}) collective-permute-start(bf16[2,512,1024]{2,1,0:T(8,128)(2,1)} %get-tuple-element.269), channel_id=1, source_target_pairs={{0,16},{8,24},{16,0},{24,8},{1,17},{9,25},{17,1},{25,9},{2,18},{10... | collective-permute-start | bytes 6291464 | tf_op jit(solution)/shard_map/ppermute | solution.py:49
  43.6 83.8 %collective-permute-start = (bf16[6,512,1024]{2,1,0:T(8,128)(2,1)}, bf16[6,512,1024]{2,1,0:T(8,128)(2,1)}, u32[]{:S(2)}, u32[]{:S(2)}) collective-permute-start(bf16[6,512,1024]{2,1,0:T(8,128)(2,1)} %get-tuple-element.581), channel_id=1, source_target_pairs={{0,8},{8,0},{16,24},{24,16},{1,9},{9,1},{17,25},{25,17},{2,10},{10... | collective-permute-start | bytes 18874376 | tf_op jit(solution)/shard_map/ppermute | solution.py:49
  91.0 220.4 %all-gather.11.cloned.1.call-start = ((), (), s32[]{:S(2)}) async-start(), calls=%async_computation.9 | async-start | bytes 7077888 | tf_op jit(solution)/shard_map/all_gather | solution.py:39
  91.0 48.0 %collective-permute-start.2 = (bf16[2,512,1024]{2,1,0:T(8,128)(2,1)}, bf16[2,512,1024]{2,1,0:T(8,128)(2,1)}, u32[]{:S(2)}, u32[]{:S(2)}) collective-permute-start(bf16[2,512,1024]{2,1,0:T(8,128)(2,1)} %pad_maximum_fusion.3), channel_id=1, source_target_pairs={{0,24},{8,16},{16,8},{24,0},{1,25},{9,17},{17,9},{25,1},{2,26},{10... | collective-permute-start | bytes 6291464 | tf_op jit(solution)/shard_map/ppermute | solution.py:49
  142.1 37.5 %collective-permute-start.6 = (bf16[1,512,1024]{2,1,0:T(8,128)(2,1)}, bf16[1,512,1024]{2,1,0:T(8,128)(2,1)}, u32[]{:S(2)}, u32[]{:S(2)}) collective-permute-start(bf16[1,512,1024]{2,1,0:T(8,128)(2,1)} %get-tuple-element.286), channel_id=1, source_target_pairs={{0,16},{8,24},{16,0},{24,8},{1,17},{9,25},{17,1},{25,9},{2,18},{10... | collective-permute-start | bytes 3145736 | tf_op jit(solution)/shard_map/ppermute | solution.py:49
  144.0 45.4 %collective-permute-start.7 = (bf16[1,512,1024]{2,1,0:T(8,128)(2,1)}, bf16[1,512,1024]{2,1,0:T(8,128)(2,1)}, u32[]{:S(2)}, u32[]{:S(2)}) collective-permute-start(bf16[1,512,1024]{2,1,0:T(8,128)(2,1)} %get-tuple-element.287), channel_id=1, source_target_pairs={{0,24},{8,16},{16,8},{24,0},{1,25},{9,17},{17,9},{25,1},{2,26},{10... | collective-permute-start | bytes 3145736 | tf_op jit(solution)/shard_map/ppermute | solution.py:49
  194.8 225.8 %all-gather.15.cloned.1.call-start = ((), (), s32[]{:S(2)}) async-start(), calls=%async_computation.11 | async-start | bytes 7077888 | tf_op jit(solution)/shard_map/all_gather | solution.py:39
  213.8 46.4 %collective-permute-start.9 = (bf16[2,512,1024]{2,1,0:T(8,128)(2,1)}, bf16[2,512,1024]{2,1,0:T(8,128)(2,1)S(1)}, u32[]{:S(2)}, u32[]{:S(2)}) collective-permute-start(bf16[2,512,1024]{2,1,0:T(8,128)(2,1)} %get-tuple-element.300), channel_id=1, source_target_pairs={{0,16},{8,24},{16,0},{24,8},{1,17},{9,25},{17,1},{25,9},{2,18},{10... | collective-permute-start | bytes 6291464 | tf_op jit(solution)/shard_map/ppermute | solution.py:49
  260.2 234.9 %all-gather.13.cloned.1.call-start = ((), (), s32[]{:S(2)}) async-start(), calls=%async_computation.10 | async-start | bytes 7077888 | tf_op jit(solution)/shard_map/all_gather | solution.py:39
  260.2 48.1 %collective-permute-start.10 = (bf16[2,512,1024]{2,1,0:T(8,128)(2,1)}, bf16[2,512,1024]{2,1,0:T(8,128)(2,1)S(1)}, u32[]{:S(2)}, u32[]{:S(2)}) collective-permute-start(bf16[2,512,1024]{2,1,0:T(8,128)(2,1)} %pad_maximum_fusion.6), channel_id=1, source_target_pairs={{0,24},{8,16},{16,8},{24,0},{1,25},{9,17},{17,9},{25,1},{2,26},{10... | collective-permute-start | bytes 6291464 | tf_op jit(solution)/shard_map/ppermute | solution.py:49
  310.6 80.3 %collective-permute-start.17 = (f32[8,1536]{1,0:T(8,128)S(1)}, f32[8,1536]{1,0:T(8,128)S(1)}, u32[]{:S(2)}, u32[]{:S(2)}) collective-permute-start(f32[8,1536]{1,0:T(8,128)S(1)} %get-tuple-element.728), channel_id=1, source_target_pairs={{0,16},{8,24},{16,0},{24,8},{1,17},{9,25},{17,1},{25,9},{2,18},{10... | collective-permute-start | bytes 147464 | tf_op jit(solution)/shard_map/ppermute | solution.py:49
  314.8 44.5 %collective-permute-start.13 = (bf16[1,512,1024]{2,1,0:T(8,128)(2,1)S(1)}, bf16[1,512,1024]{2,1,0:T(8,128)(2,1)}, u32[]{:S(2)}, u32[]{:S(2)}) collective-permute-start(bf16[1,512,1024]{2,1,0:T(8,128)(2,1)S(1)} %copy-done.33), channel_id=1, source_target_pairs={{0,24},{8,16},{16,8},{24,0},{1,25},{9,17},{17,9},{25,1},{2,26},{10... | collective-permute-start | bytes 3145736 | tf_op jit(solution)/shard_map/ppermute | solution.py:49
  364.4 45.5 %collective-permute-start.16 = (bf16[240,2048]{1,0:T(8,128)(2,1)}, bf16[240,2048]{1,0:T(8,128)(2,1)}, u32[]{:S(2)}, u32[]{:S(2)}) collective-permute-start(bf16[240,2048]{1,0:T(8,128)(2,1)} %convolution_convert_fusion.17), channel_id=1, source_target_pairs={{0,24},{8,16},{16,8},{24,0},{1,25},{9,17},{17,9},{25,1},{2,26},{10... | collective-permute-start | bytes 2949128 | tf_op jit(solution)/shard_map/ppermute | solution.py:49
  368.2 41.7 %collective-permute-start.15 = (bf16[240,2048]{1,0:T(8,128)(2,1)}, bf16[240,2048]{1,0:T(8,128)(2,1)}, u32[]{:S(2)}, u32[]{:S(2)}) collective-permute-start(bf16[240,2048]{1,0:T(8,128)(2,1)} %convolution_convert_fusion.18), channel_id=1, source_target_pairs={{0,16},{8,24},{16,0},{24,8},{1,17},{9,25},{17,1},{25,9},{2,18},{10... | collective-permute-start | bytes 2949128 | tf_op jit(solution)/shard_map/ppermute | solution.py:49
  372.0 37.9 %collective-permute-start.14 = (bf16[240,2048]{1,0:T(8,128)(2,1)}, bf16[240,2048]{1,0:T(8,128)(2,1)}, u32[]{:S(2)}, u32[]{:S(2)}) collective-permute-start(bf16[240,2048]{1,0:T(8,128)(2,1)} %convolution_convert_fusion.15), channel_id=1, source_target_pairs={{0,8},{8,0},{16,24},{24,16},{1,9},{9,1},{17,25},{25,17},{2,10},{10... | collective-permute-start | bytes 2949128 | tf_op jit(solution)/shard_map/ppermute | solution.py:49
  390.0 306.6 %reduce-scatter.4.cloned.1.call-start = ((), (), s32[]{:S(2)}) async-start(), calls=%async_computation.12 | async-start | bytes 7077888 | tf_op jit(solution)/shard_map/reduce_scatter | solution.py:43
  390.9 60.6 %collective-permute-start.19 = (bf16[240,2048]{1,0:T(8,128)(2,1)}, bf16[240,2048]{1,0:T(8,128)(2,1)}, u32[]{:S(2)}, u32[]{:S(2)}) collective-permute-start(bf16[240,2048]{1,0:T(8,128)(2,1)} %convolution_convert_fusion.13), channel_id=1, source_target_pairs={{0,8},{8,0},{16,24},{24,16},{1,9},{9,1},{17,25},{25,17},{2,10},{10... | collective-permute-start | bytes 2949128 | tf_op jit(solution)/shard_map/ppermute | solution.py:49
  416.4 42.8 %collective-permute-start.20 = (bf16[240,2048]{1,0:T(8,128)(2,1)}, bf16[240,2048]{1,0:T(8,128)(2,1)}, u32[]{:S(2)}, u32[]{:S(2)}) collective-permute-start(bf16[240,2048]{1,0:T(8,128)(2,1)} %convolution_convert_fusion.12), channel_id=1, source_target_pairs={{0,16},{8,24},{16,0},{24,8},{1,17},{9,25},{17,1},{25,9},{2,18},{10... | collective-permute-start | bytes 2949128 | tf_op jit(solution)/shard_map/ppermute | solution.py:49
  419.8 41.0 %collective-permute-start.21 = (bf16[240,2048]{1,0:T(8,128)(2,1)}, bf16[240,2048]{1,0:T(8,128)(2,1)}, u32[]{:S(2)}, u32[]{:S(2)}) collective-permute-start(bf16[240,2048]{1,0:T(8,128)(2,1)} %convolution_convert_fusion.11), channel_id=1, source_target_pairs={{0,24},{8,16},{16,8},{24,0},{1,25},{9,17},{17,9},{25,1},{2,26},{10... | collective-permute-start | bytes 2949128 | tf_op jit(solution)/shard_map/ppermute | solution.py:49
  450.8 53.9 %collective-permute-start.23 = (bf16[240,2048]{1,0:T(8,128)(2,1)}, bf16[240,2048]{1,0:T(8,128)(2,1)S(1)}, u32[]{:S(2)}, u32[]{:S(2)}) collective-permute-start(bf16[240,2048]{1,0:T(8,128)(2,1)} %get-tuple-element.336), channel_id=1, source_target_pairs={{0,16},{8,24},{16,0},{24,8},{1,17},{9,25},{17,1},{25,9},{2,18},{10... | collective-permute-start | bytes 2949128 | tf_op jit(solution)/shard_map/ppermute | solution.py:49
  451.5 53.2 %collective-permute-start.24 = (bf16[240,2048]{1,0:T(8,128)(2,1)}, bf16[240,2048]{1,0:T(8,128)(2,1)}, u32[]{:S(2)}, u32[]{:S(2)}) collective-permute-start(bf16[240,2048]{1,0:T(8,128)(2,1)} %get-tuple-element.337), channel_id=1, source_target_pairs={{0,24},{8,16},{16,8},{24,0},{1,25},{9,17},{17,9},{25,1},{2,26},{10... | collective-permute-start | bytes 2949128 | tf_op jit(solution)/shard_map/ppermute | solution.py:49
  507.0 43.2 %collective-permute-start.29 = (bf16[240,2048]{1,0:T(8,128)(2,1)}, bf16[240,2048]{1,0:T(8,128)(2,1)}, u32[]{:S(2)}, u32[]{:S(2)}) collective-permute-start(bf16[240,2048]{1,0:T(8,128)(2,1)} %get-tuple-element.372), channel_id=1, source_target_pairs={{0,16},{8,24},{16,0},{24,8},{1,17},{9,25},{17,1},{25,9},{2,18},{10... | collective-permute-start | bytes 2949128 | tf_op jit(solution)/shard_map/ppermute | solution.py:49
  508.5 42.6 %collective-permute-start.30 = (bf16[240,2048]{1,0:T(8,128)(2,1)}, bf16[240,2048]{1,0:T(8,128)(2,1)}, u32[]{:S(2)}, u32[]{:S(2)}) collective-permute-start(bf16[240,2048]{1,0:T(8,128)(2,1)} %get-tuple-element.373), channel_id=1, source_target_pairs={{0,24},{8,16},{16,8},{24,0},{1,25},{9,17},{17,9},{25,1},{2,26},{10... | collective-permute-start | bytes 2949128 | tf_op jit(solution)/shard_map/ppermute | solution.py:49
  580.9 83.4 %collective-permute-start.34 = (bf16[240,2048]{1,0:T(8,128)(2,1)}, bf16[240,2048]{1,0:T(8,128)(2,1)}, u32[]{:S(2)}, u32[]{:S(2)}) collective-permute-start(bf16[240,2048]{1,0:T(8,128)(2,1)} %get-tuple-element.630), channel_id=1, source_target_pairs={{0,8},{8,0},{16,24},{24,16},{1,9},{9,1},{17,25},{25,17},{2,10},{10... | collective-permute-start | bytes 2949128 | tf_op jit(solution)/shard_map/ppermute | solution.py:49
  581.7 82.6 %collective-permute-start.35 = (bf16[240,2048]{1,0:T(8,128)(2,1)}, bf16[240,2048]{1,0:T(8,128)(2,1)}, u32[]{:S(2)}, u32[]{:S(2)}) collective-permute-start(bf16[240,2048]{1,0:T(8,128)(2,1)} %get-tuple-element.629), channel_id=1, source_target_pairs={{0,16},{8,24},{16,0},{24,8},{1,17},{9,25},{17,1},{25,9},{2,18},{10... | collective-permute-start | bytes 2949128 | tf_op jit(solution)/shard_map/ppermute | solution.py:49
  593.0 58.3 %collective-permute-start.31 = (bf16[240,2048]{1,0:T(8,128)(2,1)}, bf16[240,2048]{1,0:T(8,128)(2,1)}, u32[]{:S(2)}, u32[]{:S(2)}) collective-permute-start(bf16[240,2048]{1,0:T(8,128)(2,1)} %get-tuple-element.634), channel_id=1, source_target_pairs={{0,8},{8,0},{16,24},{24,16},{1,9},{9,1},{17,25},{25,17},{2,10},{10... | collective-permute-start | bytes 2949128 | tf_op jit(solution)/shard_map/ppermute | solution.py:49
  593.0 59.6 %collective-permute-start.32 = (bf16[240,2048]{1,0:T(8,128)(2,1)}, bf16[240,2048]{1,0:T(8,128)(2,1)}, u32[]{:S(2)}, u32[]{:S(2)}) collective-permute-start(bf16[240,2048]{1,0:T(8,128)(2,1)} %get-tuple-element.633), channel_id=1, source_target_pairs={{0,16},{8,24},{16,0},{24,8},{1,17},{9,25},{17,1},{25,9},{2,18},{10... | collective-permute-start | bytes 2949128 | tf_op jit(solution)/shard_map/ppermute | solution.py:49
  594.1 58.5 %collective-permute-start.33 = (bf16[240,2048]{1,0:T(8,128)(2,1)}, bf16[240,2048]{1,0:T(8,128)(2,1)}, u32[]{:S(2)}, u32[]{:S(2)}) collective-permute-start(bf16[240,2048]{1,0:T(8,128)(2,1)} %get-tuple-element.632), channel_id=1, source_target_pairs={{0,24},{8,16},{16,8},{24,0},{1,25},{9,17},{17,9},{25,1},{2,26},{10... | collective-permute-start | bytes 2949128 | tf_op jit(solution)/shard_map/ppermute | solution.py:49
  596.3 51.6 %all-to-all-start.1 = ((f32[4,2,240,2]{2,3,1,0:T(2,128)}), f32[4,2,240,2]{2,3,1,0:T(2,128)S(1)}, u32[]{:S(2)}, u32[]{:S(2)}) async-start(f32[4,2,240,2]{2,3,1,0:T(2,128)} %select_select_fusion), calls=%async_computation.2 | async-start | bytes 32768 | tf_op jit(solution)/shard_map/all_to_all | solution.py:622
  657.6 140.5 %all-gather.17.cloned.1.call-start = ((), (), s32[]{:S(2)}) async-start(), calls=%async_computation.13 | async-start | bytes 7077888 | tf_op jit(solution)/shard_map/all_gather | solution.py:39
  699.9 223.9 %reduce-scatter.6.cloned.1.call-start = ((), (), s32[]{:S(2)}) async-start(), calls=%async_computation.14 | async-start | bytes 7077888 | tf_op jit(solution)/shard_map/reduce_scatter | solution.py:43
  700.1 48.8 %collective-permute-start.38 = (bf16[2,512,1024]{2,1,0:T(8,128)(2,1)}, bf16[2,512,1024]{2,1,0:T(8,128)(2,1)}, u32[]{:S(2)}, u32[]{:S(2)}) collective-permute-start(bf16[2,512,1024]{2,1,0:T(8,128)(2,1)} %pad_maximum_fusion.9), channel_id=1, source_target_pairs={{0,16},{8,24},{16,0},{24,8},{1,17},{9,25},{17,1},{25,9},{2,18},{10... | collective-permute-start | bytes 6291464 | tf_op jit(solution)/shard_map/ppermute | solution.py:49
  700.6 92.2 %collective-permute-start.39 = (bf16[2,512,1024]{2,1,0:T(8,128)(2,1)}, bf16[2,512,1024]{2,1,0:T(8,128)(2,1)}, u32[]{:S(2)}, u32[]{:S(2)}) collective-permute-start(bf16[2,512,1024]{2,1,0:T(8,128)(2,1)} %pad_maximum_fusion.10), channel_id=1, source_target_pairs={{0,24},{8,16},{16,8},{24,0},{1,25},{9,17},{17,9},{25,1},{2,26},{10... | collective-permute-start | bytes 6291464 | tf_op jit(solution)/shard_map/ppermute | solution.py:49
  798.1 258.1 %reduce-scatter.8.cloned.1.call-start = ((), (), s32[]{:S(2)}) async-start(), calls=%async_computation.15 | async-start | bytes 7077888 | tf_op jit(solution)/shard_map/reduce_scatter | solution.py:43
  819.1 50.0 %collective-permute-start.45 = (f32[2,512,64]{1,2,0:T(8,128)}, f32[2,512,64]{1,2,0:T(8,128)}, u32[]{:S(2)}, u32[]{:S(2)}) collective-permute-start(f32[2,512,64]{1,2,0:T(8,128)} %pad_maximum_fusion.19), channel_id=1, source_target_pairs={{0,8},{8,0},{16,24},{24,16},{1,9},{9,1},{17,25},{25,17},{2,10},{10... | collective-permute-start | bytes 786440 | tf_op jit(solution)/shard_map/ppermute | solution.py:49
  821.1 102.6 %collective-permute-start.40 = (bf16[2,512,1024]{2,1,0:T(8,128)(2,1)}, bf16[2,512,1024]{2,1,0:T(8,128)(2,1)}, u32[]{:S(2)}, u32[]{:S(2)}) collective-permute-start(bf16[2,512,1024]{2,1,0:T(8,128)(2,1)} %pad_maximum_fusion.12), channel_id=1, source_target_pairs={{0,8},{8,0},{16,24},{24,16},{1,9},{9,1},{17,25},{25,17},{2,10},{10... | collective-permute-start | bytes 6291464 | tf_op jit(solution)/shard_map/ppermute | solution.py:49
  821.7 102.1 %collective-permute-start.41 = (bf16[2,512,1024]{2,1,0:T(8,128)(2,1)}, bf16[2,512,1024]{2,1,0:T(8,128)(2,1)}, u32[]{:S(2)}, u32[]{:S(2)}) collective-permute-start(bf16[2,512,1024]{2,1,0:T(8,128)(2,1)} %pad_maximum_fusion.13), channel_id=1, source_target_pairs={{0,16},{8,24},{16,0},{24,8},{1,17},{9,25},{17,1},{25,9},{2,18},{10... | collective-permute-start | bytes 6291464 | tf_op jit(solution)/shard_map/ppermute | solution.py:49
  823.1 100.6 %collective-permute-start.42 = (bf16[2,512,1024]{2,1,0:T(8,128)(2,1)S(1)}, bf16[2,512,1024]{2,1,0:T(8,128)(2,1)}, u32[]{:S(2)}, u32[]{:S(2)}) collective-permute-start(bf16[2,512,1024]{2,1,0:T(8,128)(2,1)S(1)} %copy-done.31), channel_id=1, source_target_pairs={{0,24},{8,16},{16,8},{24,0},{1,25},{9,17},{17,9},{25,1},{2,26},{10... | collective-permute-start | bytes 6291464 | tf_op jit(solution)/shard_map/ppermute | solution.py:49
  824.0 47.8 %collective-permute-start.43 = (bf16[2,512,256]{2,1,0:T(8,128)(2,1)}, bf16[2,512,256]{2,1,0:T(8,128)(2,1)S(1)}, u32[]{:S(2)}, u32[]{:S(2)}) collective-permute-start(bf16[2,512,256]{2,1,0:T(8,128)(2,1)} %pad_maximum_fusion.18), channel_id=1, source_target_pairs={{0,8},{8,0},{16,24},{24,16},{1,9},{9,1},{17,25},{25,17},{2,10},{10... | collective-permute-start | bytes 1572872 | tf_op jit(solution)/shard_map/ppermute | solution.py:49
  870.3 47.8 %collective-permute-start.46 = (f32[512,64]{0,1:T(8,128)S(1)}, f32[512,64]{0,1:T(8,128)S(1)}, u32[]{:S(2)}, u32[]{:S(2)}) collective-permute-start(f32[512,64]{0,1:T(8,128)S(1)} %fusion.89), channel_id=1, source_target_pairs={{0,16},{8,24},{16,0},{24,8},{1,17},{9,25},{17,1},{25,9},{2,18},{10... | collective-permute-start | bytes 393224 | tf_op jit(solution)/shard_map/ppermute | solution.py:49
  872.0 50.9 %collective-permute-start.44 = (bf16[512,256]{1,0:T(8,128)(2,1)S(1)}, bf16[512,256]{1,0:T(8,128)(2,1)S(1)}, u32[]{:S(2)}, u32[]{:S(2)}) collective-permute-start(bf16[512,256]{1,0:T(8,128)(2,1)S(1)} %fusion.83), channel_id=1, source_target_pairs={{0,16},{8,24},{16,0},{24,8},{1,17},{9,25},{17,1},{25,9},{2,18},{10... | collective-permute-start | bytes 786440 | tf_op jit(solution)/shard_map/ppermute | solution.py:49
  937.5 32.4 %collective-permute-start.47 = (bf16[1,512,1024]{2,1,0:T(8,128)(2,1)}, bf16[1,512,1024]{2,1,0:T(8,128)(2,1)}, u32[]{:S(2)}, u32[]{:S(2)}) collective-permute-start(bf16[1,512,1024]{2,1,0:T(8,128)(2,1)} %get-tuple-element.474), channel_id=1, source_target_pairs={{0,8},{8,0},{16,24},{24,16},{1,9},{9,1},{17,25},{25,17},{2,10},{10... | collective-permute-start | bytes 3145736 | tf_op jit(solution)/shard_map/ppermute | solution.py:49
  939.1 46.4 %collective-permute-start.49 = (bf16[1,512,1024]{2,1,0:T(8,128)(2,1)}, bf16[1,512,1024]{2,1,0:T(8,128)(2,1)}, u32[]{:S(2)}, u32[]{:S(2)}) collective-permute-start(bf16[1,512,1024]{2,1,0:T(8,128)(2,1)} %get-tuple-element.476), channel_id=1, source_target_pairs={{0,24},{8,16},{16,8},{24,0},{1,25},{9,17},{17,9},{25,1},{2,26},{10... | collective-permute-start | bytes 3145736 | tf_op jit(solution)/shard_map/ppermute | solution.py:49
  950.5 43.8 %collective-permute-start.50 = (bf16[2,512,768]{2,1,0:T(8,128)(2,1)}, bf16[2,512,768]{2,1,0:T(8,128)(2,1)}, u32[]{:S(2)}, u32[]{:S(2)}) collective-permute-start(bf16[2,512,768]{2,1,0:T(8,128)(2,1)} %pad_maximum_fusion.15), channel_id=1, source_target_pairs={{0,8},{8,0},{16,24},{24,16},{1,9},{9,1},{17,25},{25,17},{2,10},{10... | collective-permute-start | bytes 4718600 | tf_op jit(solution)/shard_map/ppermute | solution.py:49
  987.5 45.4 %collective-permute-start.53 = (bf16[1,512,1024]{2,1,0:T(8,128)(2,1)S(1)}, bf16[1,512,1024]{2,1,0:T(8,128)(2,1)}, u32[]{:S(2)}, u32[]{:S(2)}) collective-permute-start(bf16[1,512,1024]{2,1,0:T(8,128)(2,1)S(1)} %copy-done.34), channel_id=1, source_target_pairs={{0,24},{8,16},{16,8},{24,0},{1,25},{9,17},{17,9},{25,1},{2,26},{10... | collective-permute-start | bytes 3145736 | tf_op jit(solution)/shard_map/ppermute | solution.py:49
  (112 other events, 1340.2 us)
Sparse Core Ops, SparseCore 0:
  15.5 103.4 all-gather.6
  121.5 73.1 all-gather.8
  196.8 98.1 all-gather.10
  296.9 98.1 all-gather.14
  396.9 98.1 all-gather.12
  569.9 126.6 reduce-scatter.3
  700.0 98.0 all-gather.16
  802.3 116.5 reduce-scatter.5
  933.8 117.4 reduce-scatter.7
